TPU v7x, 32 devices: a whole 2x2x4 slice. The times are simulated.
32 devices in a mesh: dp: 2 (over x), row: 4 (over y, core), col: 4 (over z).
Axes of the slice: x: 2, y: 2, z: 4, core: 2. Of those that a mesh axis runs over, the one named last changes fastest.
Arguments:
- inputs: bfloat16 [2, 768, 4096], P(None, 'row', ('dp', 'col')), may hold values from -6 to 6
- cotangent: bfloat16 [2, 768, 4096], P(None, 'row', ('dp', 'col')), may hold values from -6 to 6
- lengths: int32 [2, 2], P('dp'), may hold values from 512 to 1536, as said below
- source: int32 [2, 4096], P(None, ('dp', 'col')), may hold values from 0 to 8191, as said below
- query_weight: bfloat16 [768, 768], P('row', 'col'), may hold values from -0.21875 to 0.21875
- key_weight: bfloat16 [768, 768], P('row', 'col'), may hold values from -0.21875 to 0.21875
- value_weight: bfloat16 [768, 768], P('row', 'col'), may hold values from -0.21875 to 0.21875
- output_weight: bfloat16 [768, 768], P('col', 'row'), may hold values from -6 to 6
- inner_weight: bfloat16 [768, 3072], P('row', 'col'), may hold values from -0.21875 to 0.21875
- outer_weight: bfloat16 [768, 3072], P('row', 'col'), may hold values from -0.109375 to 0.109375
- first_gain: float32 [768], P('row'), may hold values from 0.5 to 1.5
- first_shift: float32 [768], P('row'), may hold values from -3 to 3
- second_gain: float32 [768], P('row'), may hold values from 0.5 to 1.5
- second_shift: float32 [768], P('row'), may hold values from -3 to 3
Outputs:
- layer_out: bfloat16 [2, 768, 4096], P(None, 'row', ('dp', 'col'))
- input_grad: bfloat16 [2, 768, 4096], P(None, 'row', ('dp', 'col'))
- query_grad: float32 [768, 768], P('row', 'col')
- key_grad: float32 [768, 768], P('row', 'col')
- value_grad: float32 [768, 768], P('row', 'col')
- output_grad: float32 [768, 768], P('col', 'row')
- inner_grad: float32 [768, 3072], P('row', 'col')
- outer_grad: float32 [768, 3072], P('row', 'col')
- first_gain_grad: float32 [768], P('row')
- first_shift_grad: float32 [768], P('row')
- second_gain_grad: float32 [768], P('row')
- second_shift_grad: float32 [768], P('row')
Inputs may be any that keep to these rules, and one draw needn't show every extreme that they name: lengths is that of each pack's first sequence; the second takes the other 2048 - lengths tokens. source is a permutation of the 8192 flat loader positions, flat index m0 * 2 * 2048 + p0. A token keeps (p // 512) % 4; and for any d, s and col index, exactly 512 of the dealt positions with p // 2048 == d and that col index come from p0 // 2048 == s.
All inputs are finite; a program needn't handle non-finite values.
Results may differ from a plain program's by a relative error of at most 0.018.
Values may be sent and summed in bfloat16 or wider, within the bound.
No kernel may reach another device: no remote copies, remote signals or barrier semaphores. Data moves between devices by JAX's collectives and lax.ppermute only.
A program may use at most 192 MiB of HBM per device.

v0:
```python
import jax
import jax.numpy as jnp
from jax import lax
from jax.sharding import PartitionSpec as P

DH = 64


EPSILON = 1e-05
MASKED_SCORE = -1e30


def rotate(values, positions, rotation_sign):
    row_count, feature = values.shape
    paired = values.reshape(row_count, feature // DH, DH // 2, 2)
    frequency = 10000.0 ** (-2.0 * jnp.arange(DH // 2, dtype=jnp.float32) / DH)
    angles = positions.astype(jnp.float32)[:, None] * frequency[None, :]
    cosine = jnp.cos(angles)[:, None, :]
    sine_part = rotation_sign * jnp.sin(angles)[:, None, :]
    former = paired[..., 0]
    latter = paired[..., 1]
    turned = jnp.stack(
        [former * cosine - latter * sine_part, latter * cosine + former * sine_part], -1
    )
    return turned.reshape(row_count, feature)


def smooth_gate(values):
    return jax.nn.gelu(values, approximate=False)


def contract_last(left, right):
    return lax.dot_general(
        left, right, (((1,), (1,)), ((), ())), preferred_element_type=jnp.float32
    )


def contract_first(left, right):
    return lax.dot_general(
        left, right, (((0,), (0,)), ((), ())), preferred_element_type=jnp.float32
    )


def multiply(row_block, weight, flipped):
    if flipped:
        return contract_last(row_block, weight)
    return jnp.dot(row_block, weight, preferred_element_type=jnp.float32)


def spread_cols(values):
    return lax.all_gather(values, "col", axis=0, tiled=True)


def spread_rows(values):
    return lax.all_gather(values, "row", axis=0, tiled=True)


def reduce_rows(gathered, weight, flipped, share_rows):

    def partial_term(first_row, amount):
        return multiply(gathered, weight, flipped)

    return lax.psum_scatter(
        partial_term(jnp.int32(0), share_rows * lax.axis_size("row")),
        "row",
        scatter_dimension=0,
        tiled=True,
    )


def reduce_cols(gathered, weight, flipped, share_rows):

    def partial_term(first_row, amount):
        return multiply(gathered, weight, flipped)

    return lax.psum_scatter(
        partial_term(jnp.int32(0), share_rows * lax.axis_size("col")),
        "col",
        scatter_dimension=0,
        tiled=True,
    )


def feature_sums(first_sum, second_sum):
    return lax.psum((first_sum, second_sum), "row")


def norm_forward(values, gain, shift):
    feature = values.shape[1] * lax.axis_size("row")
    totals, squares = feature_sums(jnp.sum(values, 1), jnp.sum(values * values, 1))
    centre = totals / feature
    spread = squares / feature - centre * centre
    inverse = lax.rsqrt(spread + EPSILON)
    normed = (values - centre[:, None]) * inverse[:, None]
    return (normed * gain + shift, normed, inverse)


def norm_backward(grad_in, normed, inverse, gain):
    feature = grad_in.shape[1] * lax.axis_size("row")
    scaled = grad_in * gain
    first_sum, second_sum = feature_sums(jnp.sum(scaled, 1), jnp.sum(scaled * normed, 1))
    result = inverse[:, None] * (
        scaled - first_sum[:, None] / feature - normed * second_sum[:, None] / feature
    )
    return (result, jnp.sum(grad_in * normed, 0), jnp.sum(grad_in, 0))


def attend_forward(queries, keyval, same_seq):
    feature = queries.shape[1]
    scaling = DH ** (-0.5)
    results = []
    totals = []
    for head_index in range(feature // DH):
        low_col = head_index * DH
        high_col = low_col + DH
        scores = contract_last(queries[:, low_col:high_col], keyval[:, low_col:high_col]) * scaling
        masked = jnp.where(same_seq, scores, MASKED_SCORE)
        highest = jnp.max(masked, 1, keepdims=True)
        raised = jnp.exp(masked - highest)
        summed = jnp.sum(raised, 1, keepdims=True)
        weights_low = (raised / summed).astype(jnp.bfloat16)
        results.append(
            jnp.dot(
                weights_low,
                keyval[:, feature + low_col : feature + high_col],
                preferred_element_type=jnp.float32,
            )
        )
        totals.append(highest[:, 0] + jnp.log(summed[:, 0]))
    return (jnp.concatenate(results, 1), jnp.stack(totals))


def attend_backward(queries, keyval, grad_attended, totals, same_seq):
    feature = queries.shape[1]
    scaling = DH ** (-0.5)
    grad_queries = []
    grad_keys = []
    grad_values = []
    for head_index in range(feature // DH):
        low_col = head_index * DH
        high_col = low_col + DH
        head_queries = queries[:, low_col:high_col]
        head_keys = keyval[:, low_col:high_col]
        head_values = keyval[:, feature + low_col : feature + high_col]
        head_grad = grad_attended[:, low_col:high_col]
        scores = contract_last(head_queries, head_keys) * scaling
        masked = jnp.where(same_seq, scores, MASKED_SCORE)
        weights_full = jnp.exp(masked - totals[head_index][:, None])
        grad_weights = contract_last(head_grad, head_values)
        centre = jnp.sum(weights_full * grad_weights, 1, keepdims=True)
        grad_scores = (weights_full * (grad_weights - centre)).astype(jnp.bfloat16)
        grad_queries.append(
            jnp.dot(grad_scores, head_keys, preferred_element_type=jnp.float32) * scaling
        )
        grad_keys.append(contract_first(grad_scores, head_queries) * scaling)
        grad_values.append(contract_first(weights_full.astype(jnp.bfloat16), head_grad))
    return (jnp.concatenate(grad_queries, 1), jnp.concatenate(grad_keys + grad_values, 1))


def body(
    inputs,
    cotangent,
    lengths,
    source,
    query_weight,
    key_weight,
    value_weight,
    output_weight,
    inner_weight,
    outer_weight,
    first_gain,
    first_shift,
    second_gain,
    second_shift,
):
    micro, local_width, share_rows = inputs.shape
    dp_count = lax.axis_size("dp")
    pack_rows = share_rows * lax.axis_size("col")
    local_count = micro * share_rows
    sent_rows = local_count // dp_count
    anchor = source.reshape(local_count)
    anchor_pack = anchor % (dp_count * pack_rows)
    sender = anchor_pack // pack_rows
    wanted = anchor // (dp_count * pack_rows) * share_rows + anchor_pack % share_rows
    order = jnp.argsort(sender, stable=True)
    requested = lax.all_to_all(
        wanted[order].reshape(dp_count, sent_rows), "dp", split_axis=0, concat_axis=0, tiled=True
    )
    asked = requested.reshape(local_count)
    flat_in = inputs.transpose(0, 2, 1).reshape(local_count, local_width)
    flat_cot = cotangent.transpose(0, 2, 1).reshape(local_count, local_width)
    arrived_in, arrived_cot = (
        lax.all_to_all(flat_in[asked], "dp", split_axis=0, concat_axis=0, tiled=True),
        lax.all_to_all(flat_cot[asked], "dp", split_axis=0, concat_axis=0, tiled=True),
    )
    placing = jnp.argsort(order)
    dealt_in = arrived_in[placing]
    dealt_cot = arrived_cot[placing]
    head_width = query_weight.shape[1]
    qkv_weight = jnp.concatenate([query_weight, key_weight, value_weight], 1)
    own_pos = lax.axis_index("row") * share_rows + jnp.arange(share_rows, dtype=jnp.int32)
    all_pos = jnp.arange(pack_rows, dtype=jnp.int32)
    grad_qkv = jnp.zeros(qkv_weight.shape, jnp.float32)
    grad_output = jnp.zeros(output_weight.shape, jnp.float32)
    grad_inner = jnp.zeros(inner_weight.shape, jnp.float32)
    grad_outer = jnp.zeros(outer_weight.shape, jnp.float32)
    gain_one = jnp.zeros(first_gain.shape, jnp.float32)
    shift_one = jnp.zeros(first_gain.shape, jnp.float32)
    gain_two = jnp.zeros(first_gain.shape, jnp.float32)
    shift_two = jnp.zeros(first_gain.shape, jnp.float32)
    output_rows = []
    grad_rows = []
    for step_index in range(micro):
        boundary = lengths[0, step_index]
        own_side = own_pos >= boundary
        all_side = all_pos >= boundary
        own_place = own_pos - jnp.where(own_side, boundary, 0)
        block_in = dealt_in[step_index * share_rows : (step_index + 1) * share_rows]
        block_cot = dealt_cot[step_index * share_rows : (step_index + 1) * share_rows]
        tokens_full = spread_cols(block_in)
        projected = reduce_rows(tokens_full, qkv_weight, False, share_rows)
        queries = rotate(projected[:, :head_width], own_place, 1.0).astype(jnp.bfloat16)
        own_keys = rotate(projected[:, head_width : 2 * head_width], own_place, 1.0)
        own_kv = jnp.concatenate([own_keys, projected[:, 2 * head_width :]], 1).astype(jnp.bfloat16)
        keyval = spread_rows(own_kv)
        same_seq = own_side[:, None] == all_side[None, :]
        attended, log_totals = attend_forward(queries, keyval, same_seq)
        attended_full = spread_rows(attended.astype(jnp.bfloat16))
        branch = reduce_cols(attended_full, output_weight, False, share_rows)
        hidden, first_normed, first_inverse = norm_forward(
            block_in.astype(jnp.float32) + branch, first_gain, first_shift
        )
        hidden_full = spread_cols(hidden.astype(jnp.bfloat16))
        inner = reduce_rows(hidden_full, inner_weight, False, share_rows)
        activated_full = spread_rows(smooth_gate(inner).astype(jnp.bfloat16))
        outer = reduce_cols(activated_full, outer_weight, True, share_rows)
        result, second_normed, second_inverse = norm_forward(
            hidden + outer, second_gain, second_shift
        )
        output_rows.append(result.astype(jnp.bfloat16))
        grad_second, gain_piece, shift_piece = norm_backward(
            block_cot.astype(jnp.float32), second_normed, second_inverse, second_gain
        )
        gain_two = gain_two + gain_piece
        shift_two = shift_two + shift_piece
        outer_full = spread_cols(grad_second.astype(jnp.bfloat16))
        grad_outer = grad_outer + contract_first(outer_full, activated_full)
        grad_act = reduce_rows(outer_full, outer_weight, False, share_rows)
        inner_low = jax.vjp(smooth_gate, inner)[1](grad_act)[0].astype(jnp.bfloat16)
        inner_full = spread_rows(inner_low)
        grad_inner = grad_inner + contract_first(hidden_full, inner_full)
        grad_hidden = grad_second + reduce_cols(inner_full, inner_weight, True, share_rows)
        grad_first, gain_piece, shift_piece = norm_backward(
            grad_hidden, first_normed, first_inverse, first_gain
        )
        gain_one = gain_one + gain_piece
        shift_one = shift_one + shift_piece
        branch_full = spread_cols(grad_first.astype(jnp.bfloat16))
        grad_output = grad_output + contract_first(attended_full, branch_full)
        grad_attended = reduce_rows(branch_full, output_weight, True, share_rows).astype(
            jnp.bfloat16
        )
        grad_query, grad_keyval = attend_backward(
            queries, keyval, grad_attended, log_totals, same_seq
        )
        keyval_share = lax.psum_scatter(
            grad_keyval.astype(jnp.bfloat16), "row", scatter_dimension=0, tiled=True
        ).astype(jnp.float32)
        own_low = jnp.concatenate(
            [
                rotate(grad_query, own_place, -1.0),
                rotate(keyval_share[:, :head_width], own_place, -1.0),
                keyval_share[:, head_width:],
            ],
            1,
        ).astype(jnp.bfloat16)
        grads_full = spread_rows(own_low)
        grad_qkv = grad_qkv + contract_first(tokens_full, grads_full)
        grad_tokens = grad_first + reduce_cols(grads_full, qkv_weight, True, share_rows)
        grad_rows.append(grad_tokens.astype(jnp.bfloat16))
    summed_qkv, summed_output, summed_inner, summed_outer = (
        lax.psum(grad_qkv.astype(jnp.bfloat16), "dp").astype(jnp.float32),
        lax.psum(grad_output.astype(jnp.bfloat16), "dp").astype(jnp.float32),
        lax.psum(grad_inner.astype(jnp.bfloat16), "dp").astype(jnp.float32),
        lax.psum(grad_outer.astype(jnp.bfloat16), "dp").astype(jnp.float32),
    )
    gain_one, shift_one, gain_two, shift_two = lax.psum(
        (gain_one, shift_one, gain_two, shift_two), ("dp", "col")
    )
    results_all = jnp.concatenate(output_rows, 0)
    grads_all = jnp.concatenate(grad_rows, 0)
    returned_out, returned_grad = (
        lax.all_to_all(results_all[order], "dp", split_axis=0, concat_axis=0, tiled=True),
        lax.all_to_all(grads_all[order], "dp", split_axis=0, concat_axis=0, tiled=True),
    )
    restore = jnp.argsort(asked)
    final_out = returned_out[restore].reshape(micro, share_rows, local_width).transpose(0, 2, 1)
    final_grad = returned_grad[restore].reshape(micro, share_rows, local_width).transpose(0, 2, 1)
    return (
        final_out,
        final_grad,
        summed_qkv[:, :head_width],
        summed_qkv[:, head_width : 2 * head_width],
        summed_qkv[:, 2 * head_width :],
        summed_output,
        summed_inner,
        summed_outer,
        gain_one,
        shift_one,
        gain_two,
        shift_two,
    )


def solution(mesh):
    return jax.shard_map(
        body,
        mesh=mesh,
        in_specs=(
            P(None, "row", ("dp", "col")),
            P(None, "row", ("dp", "col")),
            P("dp", None),
            P(None, ("dp", "col")),
            P("row", "col"),
            P("row", "col"),
            P("row", "col"),
            P("col", "row"),
            P("row", "col"),
            P("row", "col"),
            P("row"),
            P("row"),
            P("row"),
            P("row"),
        ),
        out_specs=(
            P(None, "row", ("dp", "col")),
            P(None, "row", ("dp", "col")),
            P("row", "col"),
            P("row", "col"),
            P("row", "col"),
            P("col", "row"),
            P("row", "col"),
            P("row", "col"),
            P("row"),
            P("row"),
            P("row"),
            P("row"),
        ),
        check_vma=False,
    )
```

profile of v0, /device:TPU:0, one launch (start us, length us, event | category | flops | bytes accessed | tf_op | source)
XLA Modules:
  0.0 1248.0 jit_solution(11385265382036397583)
XLA Ops:
  8.0 4.4 sort.48
  12.3 8.8 gather_fusion
  25.4 4.4 sort.49
  39.0 7.0 all-to-all-done.1
  50.4 20.3 %all_gather.54 = bf16[2048,192]{0,1:T(8,128)(2,1)S(1)} all-gather(bf16[512,192]{0,1:T(8,128)(2,1)S(1)} %copy.64), channel_id=1, replica_groups=mesh['dp'=2,'row'=4,'col'=4] {'col'}, dimensions={0}, use_global_device_ids=true | all-gather | bytes 983040 | tf_op jit(solution)/shard_map/all_gather | solution.py:51
  75.0 17.7 %all_gather.59 = bf16[2048,192]{0,1:T(8,128)(2,1)S(1)} all-gather(bf16[512,192]{0,1:T(8,128)(2,1)S(1)} %copy.65), channel_id=1, replica_groups=mesh['dp'=2,'row'=4,'col'=4] {'col'}, dimensions={0}, use_global_device_ids=true | all-gather | bytes 983040 | tf_op jit(solution)/shard_map/all_gather | solution.py:51
  100.4 20.8 %reduce-scatter.19.cloned.1.call-done = f32[512,576]{0,1:T(8,128)} async-done(((f32[2048,576]{0,1:T(8,128)}), f32[512,576]{0,1:T(8,128)}) %reduce-scatter.19.cloned.1.call-update) | async-done | bytes 1179664 | tf_op jit(solution)/shard_map/reduce_scatter | solution.py:63
  129.5 42.3 %reduce-scatter.27.cloned.1.call-done = f32[512,576]{0,1:T(8,128)} async-done(((f32[2048,576]{0,1:T(8,128)}), f32[512,576]{0,1:T(8,128)}) %reduce-scatter.27.cloned.1.call-update) | async-done | bytes 1179664 | tf_op jit(solution)/shard_map/reduce_scatter | solution.py:63
  177.9 15.7 %all-gather.9.cloned.1.call-done = bf16[2048,384]{0,1:T(8,128)(2,1)} async-done(((bf16[512,384]{0,1:T(8,128)(2,1)}), bf16[2048,384]{0,1:T(8,128)(2,1)}) %all-gather.9.cloned.1.call-update) | async-done | bytes 1572880 | tf_op jit(solution)/shard_map/all_gather | solution.py:55
  204.4 13.3 %all_gather.56 = bf16[2048,192]{0,1:T(8,128)(2,1)S(1)} all-gather(bf16[512,192]{0,1:T(8,128)(2,1)S(1)} %pad_maximum_fusion.11), channel_id=1, replica_groups=mesh['dp'=2,'row'=4,'col'=4] {'row'}, dimensions={0}, use_global_device_ids=true | all-gather | bytes 983040 | tf_op jit(solution)/shard_map/all_gather | solution.py:55
  231.2 8.7 all_gather.61
  242.5 14.6 %reduce-scatter.21.cloned.1.call-done = f32[512,192]{0,1:T(8,128)} async-done(((f32[2048,192]{0,1:T(8,128)}), f32[512,192]{0,1:T(8,128)}) %reduce-scatter.21.cloned.1.call-update) | async-done | bytes 393232 | tf_op jit(solution)/shard_map/reduce_scatter | solution.py:76
  258.2 35.4 %reduce-scatter.29.cloned.1.call-done = f32[512,192]{0,1:T(8,128)} async-done(((f32[2048,192]{0,1:T(8,128)}), f32[512,192]{0,1:T(8,128)}) %reduce-scatter.29.cloned.1.call-update) | async-done | bytes 393232 | tf_op jit(solution)/shard_map/reduce_scatter | solution.py:76
  294.6 6.5 all-reduce.4
  301.3 18.0 %all_gather.57 = bf16[2048,192]{0,1:T(8,128)(2,1)S(1)} all-gather(bf16[512,192]{0,1:T(8,128)(2,1)S(1)} %fusion.85), channel_id=1, replica_groups=mesh['dp'=2,'row'=4,'col'=4] {'col'}, dimensions={0}, use_global_device_ids=true | all-gather | bytes 983040 | tf_op jit(solution)/shard_map/all_gather | solution.py:51
  324.0 57.4 %reduce-scatter.23.cloned.1.call-done = f32[512,768]{1,0:T(8,128)} async-done(((f32[2048,768]{1,0:T(8,128)}), f32[512,768]{1,0:T(8,128)}) %reduce-scatter.23.cloned.1.call-update) | async-done | bytes 1572880 | tf_op jit(solution)/shard_map/reduce_scatter | solution.py:63
  381.4 5.5 multiply_convert_fusion.7
  387.0 28.6 %all-gather.11.cloned.1.call-done = bf16[2048,768]{1,0:T(8,128)(2,1)} async-done(((bf16[512,768]{1,0:T(8,128)(2,1)}), bf16[2048,768]{1,0:T(8,128)(2,1)}) %all-gather.11.cloned.1.call-update) | async-done | bytes 3145744 | tf_op jit(solution)/shard_map/all_gather | solution.py:55
  415.7 4.3 fusion.186
  420.1 35.4 %reduce-scatter.25.cloned.1.call-done = f32[512,192]{0,1:T(8,128)} async-done(((f32[2048,192]{0,1:T(8,128)}), f32[512,192]{0,1:T(8,128)}) %reduce-scatter.25.cloned.1.call-update) | async-done | bytes 393232 | tf_op jit(solution)/shard_map/reduce_scatter | solution.py:76
  456.6 18.4 %all_gather.62 = bf16[2048,192]{0,1:T(8,128)(2,1)S(1)} all-gather(bf16[512,192]{0,1:T(8,128)(2,1)S(1)} %get-tuple-element.129), channel_id=1, replica_groups=mesh['dp'=2,'row'=4,'col'=4] {'col'}, dimensions={0}, use_global_device_ids=true | all-gather | bytes 983040 | tf_op jit(solution)/shard_map/all_gather | solution.py:51
  479.7 57.8 %reduce-scatter.31.cloned.1.call-done = f32[512,768]{1,0:T(8,128)} async-done(((f32[2048,768]{1,0:T(8,128)}), f32[512,768]{1,0:T(8,128)}) %reduce-scatter.31.cloned.1.call-update) | async-done | bytes 1572880 | tf_op jit(solution)/shard_map/reduce_scatter | solution.py:63
  537.4 5.5 multiply_convert_fusion.6
  543.0 28.6 %all-gather.15.cloned.1.call-done = bf16[2048,768]{1,0:T(8,128)(2,1)} async-done(((bf16[512,768]{1,0:T(8,128)(2,1)}), bf16[2048,768]{1,0:T(8,128)(2,1)}) %all-gather.15.cloned.1.call-update) | async-done | bytes 3145744 | tf_op jit(solution)/shard_map/all_gather | solution.py:55
  581.2 9.7 all_to_all.57
  595.4 16.0 %reduce-scatter.33.cloned.1.call-done = f32[512,192]{0,1:T(8,128)} async-done(((f32[2048,192]{0,1:T(8,128)}), f32[512,192]{0,1:T(8,128)}) %reduce-scatter.33.cloned.1.call-update) | async-done | bytes 393232 | tf_op jit(solution)/shard_map/reduce_scatter | solution.py:76
  612.5 6.5 all-reduce.3
  620.0 5.9 all-reduce.2
  626.2 18.0 %all_gather.68 = bf16[2048,192]{0,1:T(8,128)(2,1)S(1)} all-gather(bf16[512,192]{0,1:T(8,128)(2,1)S(1)} %get-tuple-element.139), channel_id=1, replica_groups=mesh['dp'=2,'row'=4,'col'=4] {'col'}, dimensions={0}, use_global_device_ids=true | all-gather | bytes 983040 | tf_op jit(solution)/shard_map/all_gather | solution.py:51
  648.9 17.5 %all_gather.64 = bf16[2048,192]{0,1:T(8,128)(2,1)S(1)} all-gather(bf16[512,192]{0,1:T(8,128)(2,1)S(1)} %get-tuple-element.138), channel_id=1, replica_groups=mesh['dp'=2,'row'=4,'col'=4] {'col'}, dimensions={0}, use_global_device_ids=true | all-gather | bytes 983040 | tf_op jit(solution)/shard_map/all_gather | solution.py:51
  671.2 34.9 %reduce-scatter.45.cloned.1.call-done = f32[512,768]{1,0:T(8,128)} async-done(((f32[2048,768]{1,0:T(8,128)}), f32[512,768]{1,0:T(8,128)}) %reduce-scatter.45.cloned.1.call-update) | async-done | bytes 1572880 | tf_op jit(solution)/shard_map/reduce_scatter | solution.py:63
  710.0 57.0 %reduce-scatter.35.cloned.1.call-done = f32[512,768]{1,0:T(8,128)} async-done(((f32[2048,768]{1,0:T(8,128)}), f32[512,768]{1,0:T(8,128)}) %reduce-scatter.35.cloned.1.call-update) | async-done | bytes 1572880 | tf_op jit(solution)/shard_map/reduce_scatter | solution.py:63
  771.1 26.0 %all-gather.21.cloned.1.call-done = bf16[2048,768]{1,0:T(8,128)(2,1)} async-done(((bf16[512,768]{1,0:T(8,128)(2,1)}), bf16[2048,768]{1,0:T(8,128)(2,1)}) %all-gather.21.cloned.1.call-update) | async-done | bytes 3145744 | tf_op jit(solution)/shard_map/all_gather | solution.py:55
  801.3 25.7 %all-gather.17.cloned.1.call-done = bf16[2048,768]{1,0:T(8,128)(2,1)} async-done(((bf16[512,768]{1,0:T(8,128)(2,1)}), bf16[2048,768]{1,0:T(8,128)(2,1)}) %all-gather.17.cloned.1.call-update) | async-done | bytes 3145744 | tf_op jit(solution)/shard_map/all_gather | solution.py:55
  831.7 32.8 %reduce-scatter.47.cloned.1.call-done = f32[512,192]{0,1:T(8,128)} async-done(((f32[2048,192]{0,1:T(8,128)}), f32[512,192]{0,1:T(8,128)}) %reduce-scatter.47.cloned.1.call-update) | async-done | bytes 393232 | tf_op jit(solution)/shard_map/reduce_scatter | solution.py:76
  866.5 34.4 %reduce-scatter.37.cloned.1.call-done = f32[512,192]{0,1:T(8,128)} async-done(((f32[2048,192]{0,1:T(8,128)}), f32[512,192]{0,1:T(8,128)}) %reduce-scatter.37.cloned.1.call-update) | async-done | bytes 393232 | tf_op jit(solution)/shard_map/reduce_scatter | solution.py:76
  903.5 6.5 all-reduce.1
  910.3 18.0 %all_gather.66 = bf16[2048,192]{0,1:T(8,128)(2,1)S(1)} all-gather(bf16[512,192]{0,1:T(8,128)(2,1)S(1)} %get-tuple-element.136), channel_id=1, replica_groups=mesh['dp'=2,'row'=4,'col'=4] {'col'}, dimensions={0}, use_global_device_ids=true | all-gather | bytes 983040 | tf_op jit(solution)/shard_map/all_gather | solution.py:51
  930.9 17.3 %all_gather.70 = bf16[2048,192]{0,1:T(8,128)(2,1)S(1)} all-gather(bf16[512,192]{0,1:T(8,128)(2,1)S(1)} %get-tuple-element.137), channel_id=1, replica_groups=mesh['dp'=2,'row'=4,'col'=4] {'col'}, dimensions={0}, use_global_device_ids=true | all-gather | bytes 983040 | tf_op jit(solution)/shard_map/all_gather | solution.py:51
  950.7 7.3 reduce-scatter.39.cloned.1.call-done
  976.4 12.4 reduce-scatter.49.cloned.1.call-done
  1033.8 16.7 %reduce-scatter.51.cloned.1.call-done = bf16[512,384]{0,1:T(8,128)(2,1)} async-done(((bf16[2048,384]{0,1:T(8,128)(2,1)}), bf16[512,384]{0,1:T(8,128)(2,1)}) %reduce-scatter.51.cloned.1.call-update) | async-done | bytes 393232 | tf_op jit(solution)/shard_map/reduce_scatter | solution.py:266
  1079.4 23.4 %all-gather.23.cloned.1.call-done = bf16[2048,576]{0,1:T(8,128)(2,1)} async-done(((bf16[512,576]{0,1:T(8,128)(2,1)}), bf16[2048,576]{0,1:T(8,128)(2,1)}) %all-gather.23.cloned.1.call-update) | async-done | bytes 2359312 | tf_op jit(solution)/shard_map/all_gather | solution.py:55
  1112.9 4.4 sort.50
  1126.1 22.8 %all-reduce = (f32[192]{0:T(256)}, f32[192]{0:T(256)}, f32[192]{0:T(256)}, f32[192]{0:T(256)}) all-reduce(f32[192]{0:T(256)S(1)} %add.349, f32[192]{0:T(256)S(1)} %add.350, f32[192]{0:T(256)S(1)} %add.351, f32[192]{0:T(256)S(1)} %add.352), channel_id=1, replica_groups=mesh['dp'=2,'row'=4,'col'=4] {'dp','col'}, use_global_device_ids=true, to_apply=%region_77.78 | all-reduce | flops 768 | bytes 6144 | tf_op jit(solution)/shard_map/psum | solution.py:287
  1159.3 23.1 %reduce-scatter.43.cloned.1.call-done = f32[512,192]{0,1:T(8,128)} async-done(((f32[2048,192]{0,1:T(8,128)}), f32[512,192]{0,1:T(8,128)}) %reduce-scatter.43.cloned.1.call-update) | async-done | bytes 393232 | tf_op jit(solution)/shard_map/reduce_scatter | solution.py:76
  1182.3 36.5 %reduce-scatter.53.cloned.1.call-done = f32[512,192]{0,1:T(8,128)} async-done(((f32[2048,192]{0,1:T(8,128)}), f32[512,192]{0,1:T(8,128)}) %reduce-scatter.53.cloned.1.call-update) | async-done | bytes 393232 | tf_op jit(solution)/shard_map/reduce_scatter | solution.py:76
  1229.8 5.8 all-to-all-done.4
  (448 shorter events, 273.7 us)
Async XLA Ops:
  7.2 408.5 %copy-start = (bf16[192,768]{1,0:T(8,128)(2,1)S(1)}, bf16[192,768]{1,0:T(8,128)(2,1)}, u32[]{:S(2)}) copy-start(bf16[192,768]{1,0:T(8,128)(2,1)} %param.23) | copy-start | bytes 884740
  21.2 8.8 all-to-all-start
  35.5 10.5 all-to-all-start.1
  38.9 82.3 %reduce-scatter.19.cloned.1.call-start = ((), (), s32[]{:S(2)}) async-start(), calls=%async_computation.23 | async-start | bytes 5898240 | tf_op jit(solution)/shard_map/reduce_scatter | solution.py:63
  74.8 97.0 %reduce-scatter.27.cloned.1.call-start = ((), (), s32[]{:S(2)}) async-start(), calls=%async_computation.29 | async-start | bytes 5898240 | tf_op jit(solution)/shard_map/reduce_scatter | solution.py:63
  96.7 96.9 %all-gather.9.cloned.1.call-start = ((), (), s32[]{:S(2)}) async-start(), calls=%async_computation.24 | async-start | bytes 1966080 | tf_op jit(solution)/shard_map/all_gather | solution.py:55
  126.2 94.2 %all-gather.13.cloned.1.call-start = ((), (), s32[]{:S(2)}) async-start(), calls=%async_computation.30 | async-start | bytes 1966080 | tf_op jit(solution)/shard_map/all_gather | solution.py:55
  129.5 69.4 %copy-start.69 = (bf16[512,192]{0,1:T(8,128)(2,1)}, bf16[512,192]{0,1:T(8,128)(2,1)S(1)}, u32[]{:S(2)}) copy-start(bf16[512,192]{0,1:T(8,128)(2,1)S(1)} %convert_element_type.178) | copy-start | bytes 589828
  175.0 50.7 %copy-start.67 = (bf16[512,192]{0,1:T(8,128)(2,1)}, bf16[512,192]{0,1:T(8,128)(2,1)S(1)}, u32[]{:S(2)}) copy-start(bf16[512,192]{0,1:T(8,128)(2,1)S(1)} %convert_element_type.187) | copy-start | bytes 589828
  177.4 79.6 %reduce-scatter.21.cloned.1.call-start = ((), (), s32[]{:S(2)}) async-start(), calls=%async_computation.25 | async-start | bytes 1966080 | tf_op jit(solution)/shard_map/reduce_scatter | solution.py:76
  220.2 73.3 %reduce-scatter.29.cloned.1.call-start = ((), (), s32[]{:S(2)}) async-start(), calls=%async_computation.31 | async-start | bytes 1966080 | tf_op jit(solution)/shard_map/reduce_scatter | solution.py:76
  242.4 58.7 %copy-start.81 = (f32[192]{0:T(256)S(1)}, f32[192]{0:T(256)}, u32[]{:S(2)}) copy-start(f32[192]{0:T(256)} %param.24) | copy-start | bytes 2308
  242.4 58.7 %copy-start.85 = (f32[192]{0:T(256)S(1)}, f32[192]{0:T(256)}, u32[]{:S(2)}) copy-start(f32[192]{0:T(256)} %param.25) | copy-start | bytes 2308
  242.5 77.8 %copy-start.50 = (bf16[192,768]{1,0:T(8,128)(2,1)S(1)}, bf16[192,768]{1,0:T(8,128)(2,1)}, u32[]{:S(2)}) copy-start(bf16[192,768]{1,0:T(8,128)(2,1)} %param.22) | copy-start | bytes 884740
  242.5 139.0 %reduce-scatter.23.cloned.1.call-start = ((), (), s32[]{:S(2)}) async-start(), calls=%async_computation.26 | async-start | bytes 7864320 | tf_op jit(solution)/shard_map/reduce_scatter | solution.py:63
  258.2 651.9 %copy-start.26 = (f32[512,192]{0,1:T(8,128)}, f32[512,192]{0,1:T(8,128)S(1)}, u32[]{:S(2)}) copy-start(f32[512,192]{0,1:T(8,128)S(1)} %get-tuple-element.74) | copy-start | bytes 1179652
  294.6 615.4 %copy-start.28 = (f32[512,192]{0,1:T(8,128)}, f32[512,192]{0,1:T(8,128)S(1)}, u32[]{:S(2)}) copy-start(f32[512,192]{0,1:T(8,128)S(1)} %get-tuple-element.75) | copy-start | bytes 1179652
  324.0 91.7 %all-gather.11.cloned.1.call-start = ((), (), s32[]{:S(2)}) async-start(), calls=%async_computation.27 | async-start | bytes 3932160 | tf_op jit(solution)/shard_map/all_gather | solution.py:55
  387.0 68.4 %reduce-scatter.25.cloned.1.call-start = ((), (), s32[]{:S(2)}) async-start(), calls=%async_computation.28 | async-start | bytes 1966080 | tf_op jit(solution)/shard_map/reduce_scatter | solution.py:76
  420.0 117.4 %reduce-scatter.31.cloned.1.call-start = ((), (), s32[]{:S(2)}) async-start(), calls=%async_computation.32 | async-start | bytes 7864320 | tf_op jit(solution)/shard_map/reduce_scatter | solution.py:63
  479.6 92.0 %all-gather.15.cloned.1.call-start = ((), (), s32[]{:S(2)}) async-start(), calls=%async_computation.33 | async-start | bytes 3932160 | tf_op jit(solution)/shard_map/all_gather | solution.py:55
  543.0 68.3 %reduce-scatter.33.cloned.1.call-start = ((), (), s32[]{:S(2)}) async-start(), calls=%async_computation.34 | async-start | bytes 1966080 | tf_op jit(solution)/shard_map/reduce_scatter | solution.py:76
  575.9 130.2 %reduce-scatter.45.cloned.1.call-start = ((), (), s32[]{:S(2)}) async-start(), calls=%async_computation.42 | async-start | bytes 7864320 | tf_op jit(solution)/shard_map/reduce_scatter | solution.py:63
  648.8 118.2 %reduce-scatter.35.cloned.1.call-start = ((), (), s32[]{:S(2)}) async-start(), calls=%async_computation.35 | async-start | bytes 7864320 | tf_op jit(solution)/shard_map/reduce_scatter | solution.py:63
  671.1 125.9 %all-gather.21.cloned.1.call-start = ((), (), s32[]{:S(2)}) async-start(), calls=%async_computation.43 | async-start | bytes 3932160 | tf_op jit(solution)/shard_map/all_gather | solution.py:55
  710.0 117.0 %all-gather.17.cloned.1.call-start = ((), (), s32[]{:S(2)}) async-start(), calls=%async_computation.36 | async-start | bytes 3932160 | tf_op jit(solution)/shard_map/all_gather | solution.py:55
  771.0 93.5 %reduce-scatter.47.cloned.1.call-start = ((), (), s32[]{:S(2)}) async-start(), calls=%async_computation.44 | async-start | bytes 1966080 | tf_op jit(solution)/shard_map/reduce_scatter | solution.py:76
  801.3 99.7 %reduce-scatter.37.cloned.1.call-start = ((), (), s32[]{:S(2)}) async-start(), calls=%async_computation.37 | async-start | bytes 1966080 | tf_op jit(solution)/shard_map/reduce_scatter | solution.py:76
  831.2 33.3 %copy-start.86 = (f32[192]{0:T(256)S(1)}, f32[192]{0:T(256)}, u32[]{:S(2)}) copy-start(f32[192]{0:T(256)} %param.27) | copy-start | bytes 2308
  831.2 126.8 %reduce-scatter.39.cloned.1.call-start = ((), (), s32[]{:S(2)}) async-start(), calls=%async_computation.38 | async-start | bytes 1966080 | tf_op jit(solution)/shard_map/reduce_scatter | solution.py:63
  866.5 43.8 %copy-start.51 = (f32[512,192]{0,1:T(8,128)}, f32[512,192]{0,1:T(8,128)S(1)}, u32[]{:S(2)}) copy-start(f32[512,192]{0,1:T(8,128)S(1)} %get-tuple-element.67) | copy-start | bytes 1179652
  903.5 27.2 %copy-start.53 = (f32[512,192]{0,1:T(8,128)}, f32[512,192]{0,1:T(8,128)S(1)}, u32[]{:S(2)}) copy-start(f32[512,192]{0,1:T(8,128)S(1)} %get-tuple-element.66) | copy-start | bytes 1179652
  930.8 58.0 %reduce-scatter.49.cloned.1.call-start = ((), (), s32[]{:S(2)}) async-start(), calls=%async_computation.45 | async-start | bytes 1966080 | tf_op jit(solution)/shard_map/reduce_scatter | solution.py:63
  950.7 68.9 %reduce-scatter.41.cloned.1.call-start = ((), (), s32[]{:S(2)}) async-start(), calls=%async_computation.39 | async-start | bytes 1966080 | tf_op jit(solution)/shard_map/reduce_scatter | solution.py:266
  976.2 74.3 %reduce-scatter.51.cloned.1.call-start = ((), (), s32[]{:S(2)}) async-start(), calls=%async_computation.46 | async-start | bytes 1966080 | tf_op jit(solution)/shard_map/reduce_scatter | solution.py:266
  1010.9 65.9 %all-gather.19.cloned.1.call-start = ((), (), s32[]{:S(2)}) async-start(), calls=%async_computation.40 | async-start | bytes 2949120 | tf_op jit(solution)/shard_map/all_gather | solution.py:55
  1027.5 75.3 %all-gather.23.cloned.1.call-start = ((), (), s32[]{:S(2)}) async-start(), calls=%async_computation.47 | async-start | bytes 2949120 | tf_op jit(solution)/shard_map/all_gather | solution.py:55
  1062.3 91.8 %all-reduce.8.cloned.1.call-start = ((), (), s32[]{:S(2)}) async-start(), calls=%async_computation.49 | async-start | bytes 1867776 | tf_op jit(solution)/shard_map/psum | solution.py:282
  1073.0 29.8 %copy-start.33 = (bf16[2048,192]{0,1:T(8,128)(2,1)S(1)}, bf16[2048,192]{0,1:T(8,128)(2,1)}, u32[]{:S(2)}) copy-start(bf16[2048,192]{0,1:T(8,128)(2,1)} %copy-done.32) | copy-start | bytes 2359300
  1079.4 26.9 %copy-start.58 = (bf16[192,192]{1,0:T(8,128)(2,1)S(1)}, bf16[192,192]{1,0:T(8,128)(2,1)}, u32[]{:S(2)}) copy-start(bf16[192,192]{1,0:T(8,128)(2,1)} %param.20) | copy-start | bytes 221188
  1106.3 76.1 %reduce-scatter.43.cloned.1.call-start = ((), (), s32[]{:S(2)}) async-start(), calls=%async_computation.41 | async-start | bytes 1966080 | tf_op jit(solution)/shard_map/reduce_scatter | solution.py:76
  1110.2 108.7 %reduce-scatter.53.cloned.1.call-start = ((), (), s32[]{:S(2)}) async-start(), calls=%async_computation.48 | async-start | bytes 1966080 | tf_op jit(solution)/shard_map/reduce_scatter | solution.py:76
  1122.5 26.4 %all-to-all-start.2 = ((bf16[2,512,192]{1,2,0:T(8,128)(2,1)}), bf16[2,512,192]{1,2,0:T(8,128)(2,1)S(1)}, u32[]{:S(2)}, u32[]{:S(2)}) async-start(bf16[2,512,192]{1,2,0:T(8,128)(2,1)} %copy.52), calls=%async_computation.10 | async-start | bytes 786432 | tf_op jit(solution)/shard_map/all_to_all | solution.py:293
  1153.1 65.8 %copy-start.27 = (f32[512,192]{0,1:T(8,128)S(1)}, f32[512,192]{0,1:T(8,128)}, u32[]{:S(2)}) copy-start(f32[512,192]{0,1:T(8,128)} %copy-done.26) | copy-start | bytes 1179652
  1153.1 65.8 %copy-start.29 = (f32[512,192]{0,1:T(8,128)S(1)}, f32[512,192]{0,1:T(8,128)}, u32[]{:S(2)}) copy-start(f32[512,192]{0,1:T(8,128)} %copy-done.28) | copy-start | bytes 1179652
  1153.1 65.8 %copy-start.52 = (f32[512,192]{0,1:T(8,128)S(1)}, f32[512,192]{0,1:T(8,128)}, u32[]{:S(2)}) copy-start(f32[512,192]{0,1:T(8,128)} %copy-done.51) | copy-start | bytes 1179652
  1153.1 65.8 %copy-start.54 = (f32[512,192]{0,1:T(8,128)S(1)}, f32[512,192]{0,1:T(8,128)}, u32[]{:S(2)}) copy-start(f32[512,192]{0,1:T(8,128)} %copy-done.53) | copy-start | bytes 1179652
  1225.5 10.2 all-to-all-start.4
  (76 other events, 404.2 us)
Sparse Core Ops, SparseCore 0:
  74.9 46.2 reduce-scatter.18
  123.9 47.8 reduce-scatter.26
  173.9 19.6 all-gather.8
  195.6 23.8 all-gather.12
  221.7 35.3 reduce-scatter.20
  259.2 34.2 reduce-scatter.28
  324.1 57.2 reduce-scatter.22
  387.1 28.5 all-gather.10
  420.1 35.2 reduce-scatter.24
  479.7 57.6 reduce-scatter.30
  543.1 28.5 all-gather.14
  576.0 35.2 reduce-scatter.32
  649.0 57.0 reduce-scatter.44
  708.6 58.3 reduce-scatter.34
  768.5 28.5 all-gather.20
  798.4 28.5 all-gather.16
  829.2 35.2 reduce-scatter.46
  866.6 34.2 reduce-scatter.36
  930.9 27.1 reduce-scatter.38
  960.6 28.1 reduce-scatter.48
  991.3 28.1 reduce-scatter.40
  1022.3 28.1 reduce-scatter.50
  1052.6 24.0 all-gather.18
  1078.7 24.0 all-gather.22
  1106.4 38.2 all-reduce.7
  1147.0 35.3 reduce-scatter.42
  1184.6 34.2 reduce-scatter.52
where the time goes:
time: 1260 us; the launch traced here: 1250 us
  waiting for transfers between devices  702 us (56%)
  blocking collectives  225 us (18%)
  matrix products  114 us (9%)
  other arithmetic  87.5 us (7%)
  local copies, waits for them, and re-layouts  85.6 us (7%)
  starting transfers between devices  17.4 us (1%)
  between operations  16.5 us (1%)
    reduce_scatter x8, waiting for transfers between devices, reduce_rows(): lax.psum_scatter(partial_term(jnp.int32(0), share_rows * lax.axis_size('r...  290 us
    reduce_scatter x8, waiting for transfers between devices, reduce_cols(): lax.psum_scatter(partial_term(jnp.int32(0), share_rows * lax.axis_size('c...  228 us
    all_gather x8, waiting for transfers between devices, spread_rows(): return lax.all_gather(values, 'row', axis=0, tiled=True)  152 us
    all_gather x8, blocking collectives, spread_cols(): return lax.all_gather(values, 'col', axis=0, tiled=True)  145 us
    dot_general x20, matrix products, contract_last(): lax.dot_general(left, right, (((1,), (1,)), ((), ())), preferred_element_...  45.9 us
    unnamed x191, local copies, waits for them, and re-layouts  26.9 us
    dot_general x20, matrix products, contract_first(): lax.dot_general(left, right, (((0,), (0,)), ((), ())), preferred_element_...  25.9 us
    psum x4, blocking collectives, feature_sums(): return lax.psum((first_sum, second_sum), 'row')  25.3 us
  transfers between devices with their start and end apart: 31, of which 27 were waited for; matrix products, arithmetic and copies ran while one was open for 14% of the time, Pallas kernels for 0%

commit v1 on v0

v1 whole, which is shorter than its diff:
```python
import jax
import jax.numpy as jnp
from jax import lax
from jax.experimental import pallas as pl
from jax.experimental.pallas import tpu as pltpu
from jax.sharding import Mesh, PartitionSpec as P

DH = 64
EPSILON = 1e-05
MASKED = -1e30
LOG2E = 1.4426950408889634
SWAP = ((0, 1), (1, 0))
ROWS = ("ya", "yb")
SHARDS = ("ya", "yb", "col")
bf16 = jnp.bfloat16
f32 = jnp.float32


def contract(left, right, dims):
    return lax.dot_general(left, right, ((dims[:1], dims[1:]), ((), ())), preferred_element_type=f32)


def swap(values, axis):
    return lax.ppermute(values, axis, SWAP)


def gather_rows(values):
    first, second = lax.axis_index("ya") == 0, lax.axis_index("yb") == 0
    other = swap(values, "ya")
    pair = jnp.stack([jnp.where(first, values, other), jnp.where(first, other, values)])
    twin = swap(pair, "yb")
    both = jnp.stack([jnp.where(second, pair, twin), jnp.where(second, twin, pair)], 1)
    return both.reshape((4,) + values.shape)


def spread_dp(values):
    if lax.axis_size("dp") == 2:
        other = swap(values, "dp")
        first = lax.axis_index("dp") == 0
        return jnp.stack([jnp.where(first, values, other), jnp.where(first, other, values)])
    return lax.all_gather(values, "dp", axis=0)


def turn(values, cosine, sine):
    lanes = values.shape[1]
    even = lax.broadcasted_iota(jnp.int32, values.shape, 1) % 2 == 0
    swapped = jnp.where(even, pltpu.roll(values, lanes - 1, 1), pltpu.roll(values, 1, 1))
    return values * cosine + swapped * sine


def project_kernel(x_ref, w_ref, cos_ref, sin_ref, q_ref, k_ref, kt_ref, v_ref, vt_ref):
    width = q_ref.shape[1]
    wide = jnp.dot(x_ref[...], w_ref[...], preferred_element_type=f32)
    turned = turn(wide[:, : 2 * width], cos_ref[...], sin_ref[...])
    q_ref[...] = turned[:, :width].astype(bf16)
    keys = turned[:, width:]
    k_ref[...] = keys.astype(bf16)
    kt_ref[...] = keys.T.astype(bf16)
    values = wide[:, 2 * width :]
    v_ref[...] = values.astype(bf16)
    vt_ref[...] = values.T.astype(bf16)


def project(tokens, weight, cosine, sine, block):
    count, feature = tokens.shape
    width = weight.shape[1] // 3
    by_row = lambda lanes: pl.BlockSpec((block, lanes), lambda i: (i, 0))
    by_col = pl.BlockSpec((width, block), lambda i: (0, i))
    row_shape = jax.ShapeDtypeStruct((count, width), bf16)
    col_shape = jax.ShapeDtypeStruct((width, count), bf16)
    return pl.pallas_call(
        project_kernel,
        grid=(count // block,),
        in_specs=[by_row(feature), pl.BlockSpec(weight.shape, lambda i: (0, 0)), by_row(2 * width), by_row(2 * width)],
        out_specs=[by_row(width), by_row(width), by_col, by_row(width), by_col],
        out_shape=[row_shape, row_shape, col_shape, row_shape, col_shape],
        name="project",
    )(tokens, weight, cosine, sine)


def head_rows(values, head):
    rows = lax.broadcasted_iota(jnp.int32, values.shape, 0)
    return jnp.where((rows >= head * DH) & (rows < (head + 1) * DH), values, jnp.zeros_like(values))


def head_lanes(values, head):
    lanes = lax.broadcasted_iota(jnp.int32, values.shape, 1)
    return jnp.where((lanes >= head * DH) & (lanes < (head + 1) * DH), values, jnp.zeros_like(values))


def forward_kernel(q_ref, k0_ref, k1_ref, vt0_ref, vt1_ref, side_q_ref, side0_ref, side1_ref, o_ref, lse_ref):
    queries = q_ref[...]
    scaling = DH ** (-0.5) * LOG2E
    same0 = side0_ref[...] == side_q_ref[...]
    same1 = side1_ref[...] == side_q_ref[...]
    for head in range(queries.shape[1] // DH):
        part = head_lanes(queries, head)
        s0 = jnp.where(same0, contract(k0_ref[...], part, (1, 1)) * scaling, MASKED)
        s1 = jnp.where(same1, contract(k1_ref[...], part, (1, 1)) * scaling, MASKED)
        highest = jnp.maximum(jnp.max(s0, 0, keepdims=True), jnp.max(s1, 0, keepdims=True))
        p0 = jnp.exp2(s0 - highest)
        p1 = jnp.exp2(s1 - highest)
        total = jnp.sum(p0, 0, keepdims=True) + jnp.sum(p1, 0, keepdims=True)
        rows = pl.ds(head * DH, DH)
        mixed = jnp.dot(vt0_ref[rows, :], p0.astype(bf16), preferred_element_type=f32) + jnp.dot(
            vt1_ref[rows, :], p1.astype(bf16), preferred_element_type=f32
        )
        o_ref[0, rows, :] = (mixed / total).astype(bf16)
        lse_ref[pl.ds(head, 1), :] = highest + jnp.log2(total)


def attend_forward(q, k, vt, side_row, side_col, block):
    count, width = q.shape
    heads = width // DH
    whole = lambda a: pl.BlockSpec(a.shape, lambda i: (0, 0))
    return pl.pallas_call(
        forward_kernel,
        grid=(count // block,),
        in_specs=[
            pl.BlockSpec((block, width), lambda i: (i, 0)),
            whole(k[0]),
            whole(k[1]),
            whole(vt[0]),
            whole(vt[1]),
            pl.BlockSpec((1, block), lambda i: (0, i)),
            whole(side_col[0]),
            whole(side_col[1]),
        ],
        out_specs=[
            pl.BlockSpec((1, width, block), lambda i: (i, 0, 0)),
            pl.BlockSpec((heads, block), lambda i: (0, i)),
        ],
        out_shape=[
            jax.ShapeDtypeStruct((count // block, width, block), bf16),
            jax.ShapeDtypeStruct((heads, count), f32),
        ],
        compiler_params=pltpu.CompilerParams(vmem_limit_bytes=50 << 20),
        name="attend_forward",
    )(q, k[0], k[1], vt[0], vt[1], side_row, side_col[0], side_col[1])


def backward_kernel(
    q_ref, k0_ref, k1_ref, kt0_ref, kt1_ref, v0_ref, v1_ref, g_ref, o_ref, lse_ref, side_q_ref, side0_ref, side1_ref,
    dq_ref, dk_ref, dv_ref,
):
    scaling = DH ** (-0.5)
    queries = q_ref[...]
    grad = g_ref[0]
    product = grad.astype(f32) * o_ref[0].astype(f32)
    sides = (side0_ref[...] == side_q_ref[...], side1_ref[...] == side_q_ref[...])

    @pl.when(pl.program_id(0) == 0)
    def _():
        dk_ref[...] = jnp.zeros_like(dk_ref)
        dv_ref[...] = jnp.zeros_like(dv_ref)

    pieces = []
    for head in range(queries.shape[1] // DH):
        part_q = head_lanes(queries, head)
        part_g = head_rows(grad, head)
        rows = pl.ds(head * DH, DH)
        delta = jnp.sum(product[head * DH : (head + 1) * DH], 0, keepdims=True)
        lse = lse_ref[pl.ds(head, 1), :]
        dq = None
        for half, (k, kt, v) in enumerate(((k0_ref, kt0_ref, v0_ref), (k1_ref, kt1_ref, v1_ref))):
            scores = jnp.where(sides[half], contract(k[...], part_q, (1, 1)) * (scaling * LOG2E), MASKED)
            probs = jnp.exp2(scores - lse)
            grad_probs = jnp.dot(v[...], part_g, preferred_element_type=f32)
            grad_scores = (probs * (grad_probs - delta)).astype(bf16)
            dv_ref[half] += contract(probs.astype(bf16), part_g, (1, 1))
            dk_ref[half] += jnp.dot(grad_scores, part_q, preferred_element_type=f32)
            piece = jnp.dot(kt[rows, :], grad_scores, preferred_element_type=f32)
            dq = piece if dq is None else dq + piece
        pieces.append(dq)
    dq_ref[...] = jnp.concatenate(pieces, 0).T * scaling


def attend_backward(q, k, kt, v, grad, out, lse, side_row, side_col, block):
    count, width = q.shape
    heads = width // DH
    whole = lambda a: pl.BlockSpec(a.shape, lambda i: (0, 0))
    turned = pl.BlockSpec((1, width, block), lambda i: (i, 0, 0))
    sums = pl.BlockSpec((2, count, width), lambda i: (0, 0, 0))
    return pl.pallas_call(
        backward_kernel,
        grid=(count // block,),
        in_specs=[
            pl.BlockSpec((block, width), lambda i: (i, 0)),
            whole(k[0]), whole(k[1]), whole(kt[0]), whole(kt[1]), whole(v[0]), whole(v[1]),
            turned, turned,
            pl.BlockSpec((heads, block), lambda i: (0, i)),
            pl.BlockSpec((1, block), lambda i: (0, i)),
            whole(side_col[0]), whole(side_col[1]),
        ],
        out_specs=[pl.BlockSpec((block, width), lambda i: (i, 0)), sums, sums],
        out_shape=[
            jax.ShapeDtypeStruct((count, width), f32),
            jax.ShapeDtypeStruct((2, count, width), f32),
            jax.ShapeDtypeStruct((2, count, width), f32),
        ],
        compiler_params=pltpu.CompilerParams(vmem_limit_bytes=56 << 20),
        name="attend_backward",
    )(q, k[0], k[1], kt[0], kt[1], v[0], v[1], grad, out, lse, side_row, side_col[0], side_col[1])


def norm_forward(values, gain, shift):
    centre = jnp.mean(values, 1, keepdims=True)
    centred = values - centre
    inverse = lax.rsqrt(jnp.mean(centred * centred, 1, keepdims=True) + EPSILON)
    normed = centred * inverse
    return normed * gain + shift, normed, inverse


def norm_backward(grad, normed, inverse, gain):
    scaled = grad * gain
    first = jnp.mean(scaled, 1, keepdims=True)
    second = jnp.mean(scaled * normed, 1, keepdims=True)
    return inverse * (scaled - first - normed * second)


def gelu_pair(values):
    cumulative = 0.5 * (1.0 + lax.erf(values * (0.5**0.5)))
    density = jnp.exp(-0.5 * values * values) * 0.3989422804014327
    return values * cumulative, cumulative + values * density


def split_three(values):
    high = values.astype(bf16)
    rest = values - high.astype(f32)
    middle = rest.astype(bf16)
    return jnp.stack([high, middle, (rest - middle.astype(f32)).astype(bf16)])


def body(
    inputs, cotangent, lengths, source, query_weight, key_weight, value_weight, output_weight, inner_weight, outer_weight,
    first_gain, first_shift, second_gain, second_shift,
):
    micro, quarter, share = inputs.shape
    dp_count, columns = lax.axis_size("dp"), lax.axis_size("col")
    pack, own = share * columns, share // 2
    feature, count = 4 * quarter, share * micro
    me, m, half, z = (lax.axis_index(a) for a in ("dp", "ya", "yb", "col"))

    qkv_weight = gather_rows(jnp.concatenate([query_weight, key_weight, value_weight], 1)).reshape(feature, -1)
    vectors = split_three(jnp.stack([first_gain, first_shift, second_gain, second_shift])).reshape(-1, inner_weight.shape[1])
    rows_of = lambda a: a.reshape(-1, inner_weight.shape[1])
    parcel = jnp.concatenate([inner_weight, outer_weight, rows_of(output_weight), vectors], 0)
    sizes = [inner_weight.shape[0], outer_weight.shape[0], rows_of(output_weight).shape[0], vectors.shape[0]]
    parcel = jnp.pad(parcel, ((0, -sum(sizes) % 16), (0, 0)))
    everywhere = lax.all_gather(parcel, SHARDS, axis=0).reshape((4, columns) + parcel.shape)
    ends = [sum(sizes[: i + 1]) for i in range(4)]
    full_inner = everywhere[:, :, : ends[0]].transpose(0, 2, 1, 3).reshape(feature, -1)
    full_outer = everywhere[:, :, ends[0] : ends[1]].transpose(0, 2, 1, 3).reshape(feature, -1)
    full_output = everywhere[:, :, ends[1] : ends[2]].reshape(4, columns, *output_weight.shape)
    full_output = full_output.transpose(1, 2, 0, 3).reshape(feature, feature)
    pieces = everywhere[:, 0, ends[2] : ends[3]].reshape(4, 3, 4, quarter).astype(f32)
    gain_one, shift_one, gain_two, shift_two = (
        (pieces[:, 0] + (pieces[:, 1] + pieces[:, 2])).transpose(1, 0, 2).reshape(4, 1, feature)
    )

    anchors = spread_dp(source)
    anchor = source.reshape(count)
    place = anchor // (dp_count * pack) * share + anchor % share
    holder = anchor % (dp_count * pack) // pack
    wide_in, wide_cot = spread_dp(inputs), spread_dp(cotangent)
    if dp_count == 2:
        pick = (holder * count + place)[:, None] == jnp.arange(dp_count * count, dtype=jnp.int32)[None, :]
        pick = pick.astype(bf16).reshape(count, dp_count, micro, share)
        deal = lambda wide: jnp.einsum("tsmj,smfj->tf", pick, wide, preferred_element_type=f32).astype(bf16)
    else:
        deal = lambda wide: wide.transpose(0, 1, 3, 2).reshape(-1, quarter)[holder * count + place]

    def to_tokens(dealt):
        moved = lax.all_to_all(dealt.reshape(4, own, quarter), ROWS, split_axis=0, concat_axis=0, tiled=True)
        return moved.transpose(1, 0, 2).reshape(own, feature)

    tokens = to_tokens(deal(wide_in))
    cot = to_tokens(deal(wide_cot))

    boundary = jnp.where(m == 0, lengths[0, 0], lengths[0, 1])
    spots = jnp.arange(columns, dtype=jnp.int32)[:, None] * share + jnp.arange(own, dtype=jnp.int32)[None, :]
    mine = (spots + half * own).reshape(-1)
    twin = (spots + (1 - half) * own).reshape(-1)
    side = lambda where: (where >= boundary).astype(f32)
    side_row = side(mine)[None, :]
    side_col = (side(mine)[:, None], side(twin)[:, None])
    frequency = 10000.0 ** (-2.0 * jnp.arange(DH // 2, dtype=f32) / DH)
    angles = (mine - jnp.where(mine >= boundary, boundary, 0)).astype(f32)[:, None] * jnp.repeat(frequency, 2)[None, :]
    signs = jnp.where(jnp.arange(DH) % 2 == 0, -1.0, 1.0)
    width = query_weight.shape[1]
    copies = 2 * width // DH
    cosine, sine = jnp.tile(jnp.cos(angles), (1, copies)), jnp.tile(jnp.sin(angles) * signs, (1, copies))

    parts = [lax.all_gather(tokens[i * own // 2 : (i + 1) * own // 2], "col", axis=0) for i in range(2)]
    tokens_full = jnp.concatenate(parts, 1).reshape(columns * own, feature)
    q, k, kt, v, vt = project(tokens_full, qkv_weight, cosine, sine, own)
    k_pair, vt_pair = (k, swap(k, "yb")), (vt, swap(vt, "yb"))
    kt_pair, v_pair = (kt, swap(kt, "yb")), (v, swap(v, "yb"))
    attended, lse = attend_forward(q, k_pair, vt_pair, side_row, side_col, own)
    over_cols = lambda a: lax.all_to_all(a, "col", split_axis=0, concat_axis=0, tiled=True)
    attended_t = over_cols(attended).reshape(feature, own)

    branch = contract(attended_t, full_output, (0, 0))
    hidden, normed_one, inverse_one = norm_forward(tokens.astype(f32) + branch, gain_one, shift_one)
    hidden_low = hidden.astype(bf16)
    inner = jnp.dot(hidden_low, full_inner, preferred_element_type=f32)
    activated, slope = gelu_pair(inner)
    activated = activated.astype(bf16)
    outer = contract(activated, full_outer, (1, 1))
    result, normed_two, inverse_two = norm_forward(hidden + outer, gain_two, shift_two)
    cot_wide = cot.astype(f32)
    grad_two = norm_backward(cot_wide, normed_two, inverse_two, gain_two)
    grad_two_low = grad_two.astype(bf16)
    grad_outer = contract(grad_two_low, activated, (0, 0))
    grad_inner_low = (jnp.dot(grad_two_low, full_outer, preferred_element_type=f32) * slope).astype(bf16)
    grad_inner = contract(hidden_low, grad_inner_low, (0, 0))
    grad_hidden = grad_two + contract(grad_inner_low, full_inner, (1, 1))
    grad_one = norm_backward(grad_hidden, normed_one, inverse_one, gain_one)
    grad_one_low = grad_one.astype(bf16)
    grad_output = jnp.dot(attended_t, grad_one_low, preferred_element_type=f32)
    grad_vectors = jnp.stack(
        [jnp.sum(grad_hidden * normed_one, 0), jnp.sum(grad_hidden, 0), jnp.sum(cot_wide * normed_two, 0), jnp.sum(cot_wide, 0)]
    )

    def shards(grad):
        cut = grad.astype(bf16).reshape(4, quarter, columns, -1).transpose(0, 2, 1, 3)
        return cut

    output_cut = grad_output.astype(bf16).reshape(columns, -1, 4, quarter).transpose(2, 0, 1, 3)
    output_cut = output_cut.reshape(4, columns, -1, inner_weight.shape[1])
    vector_cut = grad_vectors.astype(bf16).reshape(4, 4, quarter).transpose(1, 0, 2).reshape(4, 1, -1, inner_weight.shape[1])
    vector_cut = jnp.broadcast_to(vector_cut, (4, columns) + vector_cut.shape[2:])
    parcel = jnp.concatenate([shards(grad_inner), shards(grad_outer), output_cut, vector_cut], 2)
    sizes[3] = vector_cut.shape[2]
    parcel = jnp.pad(parcel, ((0, 0), (0, 0), (0, -sum(sizes) % 16), (0, 0)))
    parcel = parcel.reshape((4 * columns,) + parcel.shape[2:])
    summed = lax.psum_scatter(parcel, SHARDS, scatter_dimension=0, tiled=False)
    summed = (
        summed.astype(f32) + swap(summed, "dp").astype(f32) if dp_count == 2 else lax.psum(summed, "dp").astype(f32)
    )
    ends = [sum(sizes[: i + 1]) for i in range(4)]
    sum_inner, sum_outer = summed[: ends[0]], summed[ends[0] : ends[1]]
    sum_output = summed[ends[1] : ends[2]].reshape(output_weight.shape)
    sum_vectors = summed[ends[2] : ends[3]].reshape(4, quarter)

    grad_att = contract(full_output, grad_one_low, (1, 1)).astype(bf16).reshape(columns, width, own)
    grad_att = over_cols(grad_att)
    dq, dk, dv = attend_backward(q, k_pair, kt_pair, v_pair, grad_att, attended, lse, side_row, side_col, own)
    dk_low, dv_low = dk.astype(bf16), dv.astype(bf16)
    dk = dk[0] + swap(dk_low[1], "yb").astype(f32)
    dv = dv[0] + swap(dv_low[1], "yb").astype(f32)
    dk = dk * DH ** (-0.5)
    even = (jnp.arange(width) % 2 == 0)[None, :]

    def turn_back(values):
        swapped = jnp.where(even, jnp.roll(values, -1, 1), jnp.roll(values, 1, 1))
        return values * cosine[:, :width] - swapped * sine[:, :width]

    grad_low = jnp.concatenate([turn_back(dq), turn_back(dk), dv], 1).astype(bf16)
    grad_qkv = contract(tokens_full, grad_low, (0, 0)).astype(bf16).reshape(4, quarter, -1)
    grad_qkv = lax.psum_scatter(grad_qkv, ROWS, scatter_dimension=0, tiled=False)
    grad_qkv = (
        grad_qkv.astype(f32) + swap(grad_qkv, "dp").astype(f32) if dp_count == 2 else lax.psum(grad_qkv, "dp").astype(f32)
    )
    partial = contract(grad_low, qkv_weight, (1, 1)).astype(bf16).reshape(columns, own, feature)
    grad_tokens = grad_one + jnp.sum(over_cols(partial).astype(f32), 0)

    def to_loader(rows):
        cut = rows.astype(bf16).reshape(own, 4, quarter).transpose(1, 0, 2)
        moved = lax.all_to_all(cut, ROWS, split_axis=0, concat_axis=0, tiled=True).reshape(count, quarter)
        return spread_dp(moved)

    spot = jnp.arange(count, dtype=jnp.int32)
    wanted = spot // share * (dp_count * pack) + me * pack + z * share + spot % share
    if dp_count == 2:
        put = (anchors.reshape(-1)[:, None] == wanted[None, :]).astype(bf16)
        settle = lambda wide: contract(wide.reshape(-1, quarter), put, (0, 0)).astype(bf16)
    else:
        order = jnp.argsort(anchors.reshape(-1))
        spots_in = jnp.searchsorted(anchors.reshape(-1)[order], wanted)
        settle = lambda wide: wide.reshape(-1, quarter)[order[spots_in]].T
    shape = lambda a: a.reshape(quarter, micro, share).transpose(1, 0, 2)
    final_out = shape(settle(to_loader(result)))
    final_grad = shape(settle(to_loader(grad_tokens)))
    return (
        final_out, final_grad, grad_qkv[:, :width], grad_qkv[:, width : 2 * width], grad_qkv[:, 2 * width :],
        sum_output, sum_inner, sum_outer, sum_vectors[0], sum_vectors[1], sum_vectors[2], sum_vectors[3],
    )


def solution(mesh):
    dp, row, col = (mesh.shape[a] for a in ("dp", "row", "col"))
    fine = Mesh(mesh.devices.reshape(dp, 2, row // 2, col), ("dp", "ya", "yb", "col"))
    tokens, matrix = P(None, ROWS, ("dp", "col")), P(ROWS, "col")
    weights = (matrix, matrix, matrix, P("col", ROWS), matrix, matrix, P(ROWS), P(ROWS), P(ROWS), P(ROWS))
    return jax.shard_map(
        body,
        mesh=fine,
        in_specs=(tokens, tokens, P("dp", None), P(None, ("dp", "col"))) + weights,
        out_specs=(tokens, tokens) + weights,
        check_vma=False,
    )
```

time: 1260 us -> 464 us (0.37)
  waiting for transfers between devices: 702 us -> 124 us
  blocking collectives: 225 us -> 58.5 us
  matrix products: 114 us -> 31.9 us
  other arithmetic: 87.5 us -> 28.4 us
  Pallas kernels: 0 us -> 42.8 us
  starting transfers between devices: 17.4 us -> 43.3 us
  local copies, waits for them, and re-layouts: 85.6 us -> 111 us
    reduce_scatter x18 -> x2, waiting for transfers between devices: 537 us -> 47.7 us  [the longest x1 47.7 us: body(): summed = lax.psum_scatter(parcel, SHARDS, scatter_dimension=0, tiled=False)]
    all_gather x8 -> x1, waiting for transfers between devices: 152 us -> 0.02 us  [body(): lax.all_gather(parcel, SHARDS, axis=0).reshape((4, columns) + parcel.shape)]
    all_gather x10 -> x2, blocking collectives: 167 us -> 58.5 us  [body(): lax.all_gather(tokens[i * own // 2:(i + 1) * own // 2], 'col', axis=0)]
    dot_general x60 -> x15, matrix products: 114 us -> 31.9 us  [the longest x10 22.8 us: contract(): lax.dot_general(left, right, ((dims[:1], dims[1:]), ((), ())), preferred_...]
    psum x5 -> x0, blocking collectives: 48.2 us -> none  [the longest x4 25.3 us: feature_sums(): return lax.psum((first_sum, second_sum), 'row')]
    pallas_call x0 -> x3, Pallas kernels: none -> 42.8 us  [the longest x1 23.1 us: attend_backward(): pl.pallas_call(backward_kernel, grid=(count // block,), in_specs=[pl.Bloc...]
    all_to_all x4 -> x7, waiting for transfers between devices: 12.8 us -> 53.2 us  [the longest x3 34.3 us: body(): lax.all_to_all(a, 'col', split_axis=0, concat_axis=0, tiled=True)]
    gather x9 -> x0, local copies, waits for them, and re-layouts: 40.4 us -> none  [the longest x1 8.84 us: body(): wanted[order].reshape(dp_count, sent_rows)]
  transfers between devices with their start and end apart: 31 -> 25, of which waited for: 27 -> 10; matrix products, arithmetic and copies ran while one was open for 14% -> 33% of each run, Pallas kernels for 0% -> 4%
where the time goes in v1:
time: 464 us; the launch traced here: 456 us
  waiting for transfers between devices  124 us (27%)
  local copies, waits for them, and re-layouts  111 us (24%)
  blocking collectives  58.5 us (13%)
  starting transfers between devices  43.3 us (9%)
  Pallas kernels  42.8 us (9%)
  matrix products  31.9 us (7%)
  other arithmetic  28.4 us (6%)
  between operations  16.2 us (3%)
    all_gather x2, blocking collectives, body(): lax.all_gather(tokens[i * own // 2:(i + 1) * own // 2], 'col', axis=0)  58.5 us
    reduce_scatter x1, waiting for transfers between devices, body(): summed = lax.psum_scatter(parcel, SHARDS, scatter_dimension=0, tiled=False)  47.7 us
    all_to_all x3, waiting for transfers between devices, body(): lax.all_to_all(a, 'col', split_axis=0, concat_axis=0, tiled=True)  34.3 us
    unnamed x99, local copies, waits for them, and re-layouts  26.9 us
    ppermute x15, waiting for transfers between devices, swap(): return lax.ppermute(values, axis, SWAP)  23.3 us
    pallas_call x1, Pallas kernels, attend_backward(): pl.pallas_call(backward_kernel, grid=(count // block,), in_specs=[pl.Bloc...  23.1 us
    dot_general x10, matrix products, contract(): lax.dot_general(left, right, ((dims[:1], dims[1:]), ((), ())), preferred_...  22.8 us
    reshape x2, local copies, waits for them, and re-layouts, shards(): grad.astype(bf16).reshape(4, quarter, columns, -1).transpose(0, 2, 1, 3)  19.6 us
  transfers between devices with their start and end apart: 25, of which 10 were waited for; matrix products, arithmetic and copies ran while one was open for 33% of the time, Pallas kernels for 4%

profile of v1, /device:TPU:0, one launch (start us, length us, event | category | flops | bytes accessed | tf_op | source)
XLA Modules:
  0.0 456.4 jit_solution(1300242189430171577)
XLA Ops:
  9.3 3.7 concatenate.39
  14.7 3.0 collective-permute-start.1
  30.9 1.8 fusion.30
  33.5 3.5 all-to-all-start
  38.1 1.8 fusion.27
  42.0 2.3 all-to-all-done
  44.4 3.5 all-to-all-start.3
  48.2 27.7 %all_gather.21 = bf16[4,128,768]{2,1,0:T(8,128)(2,1)S(1)} all-gather(bf16[1,128,768]{2,1,0:T(8,128)(2,1)S(1)} %copy.107), channel_id=1, replica_groups=mesh['dp'=2,'ya'=2,'yb'=2,'col'=4] {'col'}, dimensions={0}, use_global_device_ids=true | all-gather | bytes 983040 | tf_op jit(solution)/shard_map/all_gather | solution.py:294
  75.9 30.8 %all_gather.19 = bf16[4,128,768]{2,1,0:T(8,128)(2,1)S(1)} all-gather(bf16[1,128,768]{2,1,0:T(8,128)(2,1)S(1)} %copy.106), channel_id=1, replica_groups=mesh['dp'=2,'ya'=2,'yb'=2,'col'=4] {'col'}, dimensions={0}, use_global_device_ids=true | all-gather | bytes 983040 | tf_op jit(solution)/shard_map/all_gather | solution.py:294
  108.0 6.2 %project.1 = (bf16[1024,192]{1,0:T(8,128)(2,1)}, bf16[1024,192]{1,0:T(8,128)(2,1)}, bf16[192,1024]{1,0:T(8,128)(2,1)}, bf16[1024,192]{1,0:T(8,128)(2,1)}, bf16[192,1024]{1,0:T(8,128)(2,1)}) custom-call(bf16[1024,768]{1,0:T(8,128)(2,1)} %bitcast.215, bf16[768,576]{1,0:T(8,128)(2,1)} %bitcast.224, f32[1024,384]{1,0:T(8,128)} %copy.109.cos_ref, ...), custom_call_target="tpu_custom_call" | custom-call | tf_op jit(solution)/shard_map/project/pallas_call | solution.py:71
  116.5 2.5 copy.124
  119.1 1.9 bitcast_convert_fusion
  121.0 2.3 copy.114
  123.8 1.8 bitcast_reduce_fusion
  125.7 13.4 %attend_forward.1 = (bf16[4,192,256]{2,1,0:T(8,128)(2,1)}, f32[3,1024]{1,0:T(4,128)S(1)}) custom-call(bf16[1024,192]{1,0:T(8,128)(2,1)S(1)} %copy-done.2, bf16[1024,192]{1,0:T(8,128)(2,1)S(1)} %copy-done.3, bf16[1024,192]{1,0:T(8,128)(2,1)S(1)} %collective-permute-done.3.k1_ref, bf16[192,1024]{1,0:T(8,128)(2,1)S(1)} %copy-done.5, ...), custom_call_target="tpu_custom_call" | custom-call | tf_op jit(solution)/shard_map/attend_forward/pallas_call | solution.py:116
  139.7 5.9 %all-to-all-start.1 = ((bf16[4,192,256]{2,1,0:T(8,128)(2,1)}), bf16[4,192,256]{2,1,0:T(8,128)(2,1)S(1)}, u32[]{:S(2)}, u32[]{:S(2)}) async-start(bf16[4,192,256]{2,1,0:T(8,128)(2,1)} %get-tuple-element.25.o_ref), calls=%async_computation.1 | async-start | bytes 786432 | tf_op jit(solution)/shard_map/all_to_all | solution.py:300
  146.5 8.3 %fusion.92 = (bf16[4,4,192,768]{3,2,1,0:T(8,128)(2,1)}, bf16[4,4,192,768]{3,2,1,0:T(8,128)(2,1)}) fusion(bf16[4,4,448,768]{3,2,1,0:T(8,128)(2,1)} %bitcast.211), kind=kLoop, calls=%fused_computation.196 | loop fusion | bytes 18874368 | tf_op jit(solution)/shard_map/slice | solution.py:253
  157.3 6.0 %copy.144 = bf16[4,4,192,768]{3,1,2,0:T(4,128)(2,1)S(1)} copy(bf16[4,4,192,768]{3,2,1,0:T(8,128)(2,1)} %get-tuple-element.42) | data formatting | bytes 9437184
  163.3 3.3 copy.162
  168.1 2.4 copy.113
  170.4 3.4 reshape.631
  174.9 6.0 %copy.143 = bf16[4,4,192,768]{3,1,2,0:T(4,128)(2,1)S(1)} copy(bf16[4,4,192,768]{3,2,1,0:T(8,128)(2,1)} %get-tuple-element.43) | data formatting | bytes 9437184
  187.1 2.2 fusion.16
  189.4 2.5 multiply_reduce_fusion.1
  191.9 3.8 convolution_convert_fusion.1
  198.7 5.1 %all-to-all-start.4 = ((bf16[4,192,256]{2,1,0:T(8,128)(2,1)}), bf16[4,192,256]{2,1,0:T(8,128)(2,1)}, u32[]{:S(2)}, u32[]{:S(2)}) async-start(bf16[4,192,256]{2,1,0:T(8,128)(2,1)} %bitcast.44), calls=%async_computation.4 | async-start | bytes 786432 | tf_op jit(solution)/shard_map/all_to_all | solution.py:300
  205.3 3.7 reshape.648
  210.5 3.1 reshape.649
  215.2 9.9 %reshape.646 = bf16[4,192,4,768]{3,2,1,0:T(4,128)(2,1)} reshape(bf16[768,3072]{1,0:T(8,128)(2,1)} %convolution_convert_fusion.1) | data formatting | bytes 9437184 | tf_op jit(solution)/shard_map/reshape | solution.py:326
  225.1 3.7 convolution_convert_fusion
  228.7 9.7 %reshape.647 = bf16[4,192,4,768]{3,2,1,0:T(4,128)(2,1)} reshape(bf16[768,3072]{1,0:T(8,128)(2,1)} %convolution_convert_fusion) | data formatting | bytes 9437184 | tf_op jit(solution)/shard_map/reshape | solution.py:326
  238.5 23.1 %attend_backward.1 = (f32[1024,192]{1,0:T(8,128)}, f32[2,1024,192]{2,1,0:T(8,128)}, f32[2,1024,192]{2,1,0:T(8,128)}) custom-call(bf16[1024,192]{1,0:T(8,128)(2,1)} %get-tuple-element.22.q_ref, bf16[1024,192]{1,0:T(8,128)(2,1)} %get-tuple-element.23.k0_ref, bf16[1024,192]{1,0:T(8,128)(2,1)} %copy-done.4, bf16[192,1024]{1,0:T(8,128)(2,1)} %get-tuple-element.26.kt0_ref, ...), custom_call_target="tpu_custom_call" | custom-call | tf_op jit(solution)/shard_map/attend_backward/pallas_call | solution.py:184
  271.5 2.3 convolution_convert_fusion.4
  273.8 2.3 copy.133
  276.2 9.7 %pad_maximum_fusion = bf16[4,4,433,768]{3,1,2,0:T(4,128)(2,1)S(1)} fusion(bf16[4,4,1,768]{3,1,2,0:T(4,128)(2,1)S(1)} %broadcast_in_dim.36, bf16[4,4,48,768]{3,1,2,0:T(4,128)(2,1)S(1)} %copy-done.17, bf16[4,4,192,768]{3,1,2,0:T(4,128)(2,1)} %bitcast.209, bf16[4,4,192,768]{3,1,2,0:T(4,128)(2,1)} %bitcast.208), kind=kLoop, calls=%fused_computation | loop fusion | flops 15962112 | bytes 21282816 | tf_op jit(solution)/shard_map/concatenate | solution.py:333
  285.9 4.2 copy.145
  290.2 5.2 %pad.9.clone = bf16[4,4,448,768]{3,2,1,0:T(8,128)(2,1)} pad(bf16[4,4,433,768]{3,2,1,0:T(8,128)(2,1)S(1)} %copy.145, bf16[]{:T(256)} %constant.147.clone.1), padding=0_0x0_0x0_15x0_0 | pad | bytes 21651458 | tf_op jit(solution)/shard_map/jit(_pad)/pad | solution.py:335
  296.5 3.7 convolution_convert_fusion.2
  300.2 5.2 %all-to-all-start.5 = ((bf16[4,256,768]{2,1,0:T(8,128)(2,1)}), bf16[4,256,768]{2,1,0:T(8,128)(2,1)S(1)}, u32[]{:S(2)}, u32[]{:S(2)}) async-start(bf16[4,256,768]{2,1,0:T(8,128)(2,1)} %bitcast.230), calls=%async_computation.5 | async-start | bytes 3145728 | tf_op jit(solution)/shard_map/all_to_all | solution.py:300
  308.4 34.3 %all-to-all-done.5 = bf16[4,256,768]{2,1,0:T(8,128)(2,1)S(1)} async-done(((bf16[4,256,768]{2,1,0:T(8,128)(2,1)}), bf16[4,256,768]{2,1,0:T(8,128)(2,1)S(1)}, u32[]{:S(2)}, u32[]{:S(2)}) %all-to-all-start.5) | async-done | bytes 1572896 | tf_op jit(solution)/shard_map/all_to_all | solution.py:300
  342.8 3.5 all-to-all-start.2
  347.5 10.7 %all-to-all-done.2 = bf16[4,256,192]{1,2,0:T(8,128)(2,1)S(1)} async-done(((bf16[4,256,192]{1,2,0:T(8,128)(2,1)}), bf16[4,256,192]{1,2,0:T(8,128)(2,1)S(1)}, u32[]{:S(2)}, u32[]{:S(2)}) %all-to-all-start.2) | async-done | bytes 393248 | tf_op jit(solution)/shard_map/all_to_all | solution.py:370
  358.2 3.6 all-to-all-start.6
  363.3 5.9 %all-to-all-done.6 = bf16[4,256,192]{1,2,0:T(8,128)(2,1)S(1)} async-done(((bf16[4,256,192]{1,2,0:T(8,128)(2,1)}), bf16[4,256,192]{1,2,0:T(8,128)(2,1)S(1)}, u32[]{:S(2)}, u32[]{:S(2)}) %all-to-all-start.6) | async-done | bytes 393248 | tf_op jit(solution)/shard_map/all_to_all | solution.py:370
  371.6 2.3 collective-permute-done.5
  373.9 8.0 %collective-permute-done.12 = bf16[1024,192]{0,1:T(8,128)(2,1)S(1)} collective-permute-done((bf16[1024,192]{0,1:T(8,128)(2,1)S(1)}, bf16[1024,192]{0,1:T(8,128)(2,1)S(1)}, u32[]{:S(2)}, u32[]{:S(2)}) %collective-permute-start.12) | collective-permute-done | bytes 393248 | tf_op jit(solution)/shard_map/ppermute | solution.py:24
  382.1 47.7 %reduce-scatter.5.cloned.1.call-done = bf16[1,448,768]{2,1,0:T(8,128)(2,1)} async-done(((bf16[16,448,768]{2,1,0:T(8,128)(2,1)}), bf16[1,448,768]{2,1,0:T(8,128)(2,1)}) %reduce-scatter.5.cloned.1.call-update) | async-done | bytes 688144 | tf_op jit(solution)/shard_map/reduce_scatter | solution.py:337
  436.4 10.6 %collective-permute-done.14 = bf16[448,768]{1,0:T(8,128)(2,1)S(1)} collective-permute-done((bf16[448,768]{1,0:T(8,128)(2,1)}, bf16[448,768]{1,0:T(8,128)(2,1)S(1)}, u32[]{:S(2)}, u32[]{:S(2)}) %collective-permute-start.14) | collective-permute-done | bytes 688160 | tf_op jit(solution)/shard_map/ppermute | solution.py:24
  (243 shorter events, 72.8 us)
Async XLA Ops:
  7.2 6.7 %copy-start.29 = (bf16[192,192]{1,0:T(8,128)(2,1)S(1)}, bf16[192,192]{1,0:T(8,128)(2,1)}, u32[]{:S(2)}) copy-start(bf16[192,192]{1,0:T(8,128)(2,1)} %param.20) | copy-start | bytes 221188
  7.2 6.7 %copy-start.31 = (bf16[192,192]{1,0:T(8,128)(2,1)S(1)}, bf16[192,192]{1,0:T(8,128)(2,1)}, u32[]{:S(2)}) copy-start(bf16[192,192]{1,0:T(8,128)(2,1)} %param.19) | copy-start | bytes 221188
  7.2 6.7 %copy-start.33 = (bf16[192,192]{1,0:T(8,128)(2,1)S(1)}, bf16[192,192]{1,0:T(8,128)(2,1)}, u32[]{:S(2)}) copy-start(bf16[192,192]{1,0:T(8,128)(2,1)} %param.18) | copy-start | bytes 221188
  7.2 10.5 %copy-start.28 = (bf16[2,192,512]{2,1,0:T(8,128)(2,1)S(1)}, bf16[2,192,512]{2,1,0:T(8,128)(2,1)}, u32[]{:S(2)}) copy-start(bf16[2,192,512]{2,1,0:T(8,128)(2,1)} %param.14) | copy-start | bytes 1179652
  7.2 12.6 %copy-start.36 = (s32[2,512]{1,0:T(2,128)S(1)}, s32[2,512]{1,0:T(2,128)}, u32[]{:S(2)}) copy-start(s32[2,512]{1,0:T(2,128)} %param.17) | copy-start | bytes 12292
  7.2 12.8 %copy-start.39 = (s32[1,2]{1,0:T(1,128)S(1)}, s32[1,2]{1,0:T(1,128)}, u32[]{:S(2)}) copy-start(s32[1,2]{1,0:T(1,128)} %param.16) | copy-start | bytes 28
  7.2 138.4 %all-gather.3.cloned.1.call-start = ((), (), s32[]{:S(2)}) async-start(), calls=%async_computation.11 | async-start | bytes 11698176 | tf_op jit(solution)/shard_map/all_gather | solution.py:250
  14.7 13.0 %collective-permute-start.1 = (bf16[192,576]{1,0:T(8,128)(2,1)}, bf16[192,576]{1,0:T(8,128)(2,1)}, u32[]{:S(2)}, u32[]{:S(2)}) collective-permute-start(bf16[192,576]{1,0:T(8,128)(2,1)} %pad_maximum_fusion.8), channel_id=1, source_target_pairs={{0,8},{8,0},{1,9},{9,1},{2,10},{10,2},{3,11},{11,3},{4,12},{12,4},... | collective-permute-start | bytes 663560 | tf_op jit(solution)/shard_map/ppermute | solution.py:24
  17.7 12.1 %collective-permute-start = (bf16[2,192,512]{2,1,0:T(8,128)(2,1)S(1)}, bf16[2,192,512]{2,1,0:T(8,128)(2,1)}, u32[]{:S(2)}, u32[]{:S(2)}) collective-permute-start(bf16[2,192,512]{2,1,0:T(8,128)(2,1)S(1)} %copy-done.28), channel_id=1, source_target_pairs={{0,16},{16,0},{1,17},{17,1},{2,18},{18,2},{3,19},{19,3},{4,20},{20... | collective-permute-start | bytes 1179656 | tf_op jit(solution)/shard_map/ppermute | solution.py:24
  19.2 17.8 %collective-permute-start.7 = (bf16[2,192,512]{2,1,0:T(8,128)(2,1)}, bf16[2,192,512]{2,1,0:T(8,128)(2,1)}, u32[]{:S(2)}, u32[]{:S(2)}) collective-permute-start(bf16[2,192,512]{2,1,0:T(8,128)(2,1)} %param.15), channel_id=1, source_target_pairs={{0,16},{16,0},{1,17},{17,1},{2,18},{18,2},{3,19},{19,3},{4,20},{20... | collective-permute-start | bytes 1179656 | tf_op jit(solution)/shard_map/ppermute | solution.py:24
  23.6 102.1 %copy-start.6 = (f32[1,1,4,256]{3,1,2,0:T(1,128)}, f32[1,1,4,256]{3,1,2,0:T(1,128)S(1)}, u32[]{:S(2)}) copy-start(f32[1,1,4,256]{3,1,2,0:T(1,128)S(1)} %copy.156) | copy-start | bytes 12292
  23.8 101.8 %copy-start = (f32[1,1024]{0,1:T(8,128)}, f32[1,1024]{0,1:T(8,128)S(1)}, u32[]{:S(2)}) copy-start(f32[1,1024]{0,1:T(8,128)S(1)} %copy.160) | copy-start | bytes 12292
  24.1 101.6 %copy-start.1 = (f32[1,1024]{0,1:T(8,128)}, f32[1,1024]{0,1:T(8,128)S(1)}, u32[]{:S(2)}) copy-start(f32[1,1024]{0,1:T(8,128)S(1)} %copy.158) | copy-start | bytes 12292
  29.0 11.7 %collective-permute-start.2 = (bf16[2,192,576]{2,1,0:T(8,128)(2,1)S(1)}, bf16[2,192,576]{2,1,0:T(8,128)(2,1)S(1)}, u32[]{:S(2)}, u32[]{:S(2)}) collective-permute-start(bf16[2,192,576]{2,1,0:T(8,128)(2,1)S(1)} %pad_maximum_fusion.5), channel_id=1, source_target_pairs={{0,4},{4,0},{1,5},{5,1},{2,6},{6,2},{3,7},{7,3},{8,12},{12,8},{9,1... | collective-permute-start | bytes 1327112 | tf_op jit(solution)/shard_map/ppermute | solution.py:24
  33.5 10.9 %all-to-all-start = ((bf16[4,256,192]{1,2,0:T(8,128)(2,1)}), bf16[4,256,192]{1,2,0:T(8,128)(2,1)S(1)}, u32[]{:S(2)}, u32[]{:S(2)}) async-start(bf16[4,256,192]{1,2,0:T(8,128)(2,1)} %bitcast.194), calls=%async_computation | async-start | bytes 786432 | tf_op jit(solution)/shard_map/all_to_all | solution.py:274
  44.3 63.7 %copy-start.21 = (bf16[4,256,192]{1,2,0:T(8,128)(2,1)}, bf16[4,256,192]{1,2,0:T(8,128)(2,1)S(1)}, u32[]{:S(2)}) copy-start(bf16[4,256,192]{1,2,0:T(8,128)(2,1)S(1)} %all-to-all-done) | copy-start | bytes 1179652
  44.4 70.5 %all-to-all-start.3 = ((bf16[4,256,192]{1,2,0:T(8,128)(2,1)}), bf16[4,256,192]{1,2,0:T(8,128)(2,1)S(1)}, u32[]{:S(2)}, u32[]{:S(2)}) async-start(bf16[4,256,192]{1,2,0:T(8,128)(2,1)} %bitcast.191), calls=%async_computation.3 | async-start | bytes 786432 | tf_op jit(solution)/shard_map/all_to_all | solution.py:274
  114.3 11.4 %collective-permute-start.4 = (bf16[192,1024]{1,0:T(8,128)(2,1)}, bf16[192,1024]{1,0:T(8,128)(2,1)S(1)}, u32[]{:S(2)}, u32[]{:S(2)}) collective-permute-start(bf16[192,1024]{1,0:T(8,128)(2,1)} %get-tuple-element.24.vt0_ref), channel_id=1, source_target_pairs={{0,4},{4,0},{1,5},{5,1},{2,6},{6,2},{3,7},{7,3},{8,12},{12,8},{9,1... | collective-permute-start | bytes 1179656 | tf_op jit(solution)/shard_map/ppermute | solution.py:24
  114.3 11.3 %collective-permute-start.3 = (bf16[1024,192]{1,0:T(8,128)(2,1)}, bf16[1024,192]{1,0:T(8,128)(2,1)S(1)}, u32[]{:S(2)}, u32[]{:S(2)}) collective-permute-start(bf16[1024,192]{1,0:T(8,128)(2,1)} %get-tuple-element.23.k0_ref), channel_id=1, source_target_pairs={{0,4},{4,0},{1,5},{5,1},{2,6},{6,2},{3,7},{7,3},{8,12},{12,8},{9,1... | collective-permute-start | bytes 1179656 | tf_op jit(solution)/shard_map/ppermute | solution.py:24
  116.5 9.1 %copy-start.2 = (bf16[1024,192]{1,0:T(8,128)(2,1)S(1)}, bf16[1024,192]{1,0:T(8,128)(2,1)}, u32[]{:S(2)}) copy-start(bf16[1024,192]{1,0:T(8,128)(2,1)} %get-tuple-element.22.q_ref) | copy-start | bytes 1179652
  116.5 9.1 %copy-start.3 = (bf16[1024,192]{1,0:T(8,128)(2,1)S(1)}, bf16[1024,192]{1,0:T(8,128)(2,1)}, u32[]{:S(2)}) copy-start(bf16[1024,192]{1,0:T(8,128)(2,1)} %get-tuple-element.23.k0_ref) | copy-start | bytes 1179652
  116.5 9.1 %copy-start.5 = (bf16[192,1024]{1,0:T(8,128)(2,1)S(1)}, bf16[192,1024]{1,0:T(8,128)(2,1)}, u32[]{:S(2)}) copy-start(bf16[192,1024]{1,0:T(8,128)(2,1)} %get-tuple-element.24.vt0_ref) | copy-start | bytes 1179652
  123.3 115.2 %collective-permute-start.8 = (bf16[192,1024]{1,0:T(8,128)(2,1)}, bf16[192,1024]{1,0:T(8,128)(2,1)}, u32[]{:S(2)}, u32[]{:S(2)}) collective-permute-start(bf16[192,1024]{1,0:T(8,128)(2,1)} %get-tuple-element.26.kt0_ref), channel_id=1, source_target_pairs={{0,4},{4,0},{1,5},{5,1},{2,6},{6,2},{3,7},{7,3},{8,12},{12,8},{9,1... | collective-permute-start | bytes 1179656 | tf_op jit(solution)/shard_map/ppermute | solution.py:24
  123.4 115.1 %collective-permute-start.9 = (bf16[1024,192]{1,0:T(8,128)(2,1)}, bf16[1024,192]{1,0:T(8,128)(2,1)}, u32[]{:S(2)}, u32[]{:S(2)}) collective-permute-start(bf16[1024,192]{1,0:T(8,128)(2,1)} %get-tuple-element.27.v0_ref), channel_id=1, source_target_pairs={{0,4},{4,0},{1,5},{5,1},{2,6},{6,2},{3,7},{7,3},{8,12},{12,8},{9,1... | collective-permute-start | bytes 1179656 | tf_op jit(solution)/shard_map/ppermute | solution.py:24
  125.6 29.2 %copy-start.4 = (bf16[1024,192]{1,0:T(8,128)(2,1)}, bf16[1024,192]{1,0:T(8,128)(2,1)S(1)}, u32[]{:S(2)}) copy-start(bf16[1024,192]{1,0:T(8,128)(2,1)S(1)} %collective-permute-done.3.k1_ref) | copy-start | bytes 1179652
  139.7 34.3 %all-to-all-start.1 = ((bf16[4,192,256]{2,1,0:T(8,128)(2,1)}), bf16[4,192,256]{2,1,0:T(8,128)(2,1)S(1)}, u32[]{:S(2)}, u32[]{:S(2)}) async-start(bf16[4,192,256]{2,1,0:T(8,128)(2,1)} %get-tuple-element.25.o_ref), calls=%async_computation.1 | async-start | bytes 786432 | tf_op jit(solution)/shard_map/all_to_all | solution.py:300
  168.0 5.8 %copy-start.13 = (bf16[4,256,192]{1,2,0:T(8,128)(2,1)S(1)}, bf16[4,256,192]{1,2,0:T(8,128)(2,1)}, u32[]{:S(2)}) copy-start(bf16[4,256,192]{1,2,0:T(8,128)(2,1)} %copy-done.12) | copy-start | bytes 1179652
  168.0 5.8 %copy-start.35 = (f32[1,4,192]{2,1,0:T(4,128)S(1)}, f32[1,4,192]{2,1,0:T(4,128)}, u32[]{:S(2)}) copy-start(f32[1,4,192]{2,1,0:T(4,128)} %copy.178) | copy-start | bytes 9220
  170.4 3.6 copy-start.22
  198.7 39.8 %all-to-all-start.4 = ((bf16[4,192,256]{2,1,0:T(8,128)(2,1)}), bf16[4,192,256]{2,1,0:T(8,128)(2,1)}, u32[]{:S(2)}, u32[]{:S(2)}) async-start(bf16[4,192,256]{2,1,0:T(8,128)(2,1)} %bitcast.44), calls=%async_computation.4 | async-start | bytes 786432 | tf_op jit(solution)/shard_map/all_to_all | solution.py:300
  203.8 104.0 %reduce-scatter.3.cloned.1.call-start = ((), (), s32[]{:S(2)}) async-start(), calls=%async_computation.9 | async-start | bytes 1228800 | tf_op jit(solution)/shard_map/reduce_scatter | solution.py:361
  215.2 9.9 %copy-start.16 = (bf16[256,3072]{1,0:T(8,128)(2,1)S(1)}, bf16[256,3072]{1,0:T(8,128)(2,1)}, u32[]{:S(2)}) copy-start(bf16[256,3072]{1,0:T(8,128)(2,1)} %copy-done.15) | copy-start | bytes 4718596
  215.2 9.9 %copy-start.19 = (f32[256,768]{1,0:T(8,128)S(1)}, f32[256,768]{1,0:T(8,128)}, u32[]{:S(2)}) copy-start(f32[256,768]{1,0:T(8,128)} %copy-done.18) | copy-start | bytes 2359300
  264.2 5.7 %collective-permute-start.11 = (bf16[1024,192]{1,0:T(8,128)(2,1)S(1)}, bf16[1024,192]{1,0:T(8,128)(2,1)S(1)}, u32[]{:S(2)}, u32[]{:S(2)}) collective-permute-start(bf16[1024,192]{1,0:T(8,128)(2,1)S(1)} %fusion.53), channel_id=1, source_target_pairs={{0,4},{4,0},{1,5},{5,1},{2,6},{6,2},{3,7},{7,3},{8,12},{12,8},{9,1... | collective-permute-start | bytes 1179656 | tf_op jit(solution)/shard_map/ppermute | solution.py:24
  264.3 2.6 collective-permute-start.10
  276.2 153.6 %reduce-scatter.5.cloned.1.call-start = ((), (), s32[]{:S(2)}) async-start(), calls=%async_computation.10 | async-start | bytes 11698176 | tf_op jit(solution)/shard_map/reduce_scatter | solution.py:337
  300.2 5.2 %copy-start.37 = (s32[2,512]{1,0:T(2,128)S(1)}, s32[2,512]{1,0:T(2,128)}, u32[]{:S(2)}) copy-start(s32[2,512]{1,0:T(2,128)} %param.17) | copy-start | bytes 12292
  300.2 6.6 %copy-start.23 = (bf16[256,768]{1,0:T(8,128)(2,1)S(1)}, bf16[256,768]{1,0:T(8,128)(2,1)}, u32[]{:S(2)}) copy-start(bf16[256,768]{1,0:T(8,128)(2,1)} %get-tuple-element.63) | copy-start | bytes 1179652
  300.2 42.5 %all-to-all-start.5 = ((bf16[4,256,768]{2,1,0:T(8,128)(2,1)}), bf16[4,256,768]{2,1,0:T(8,128)(2,1)S(1)}, u32[]{:S(2)}, u32[]{:S(2)}) async-start(bf16[4,256,768]{2,1,0:T(8,128)(2,1)} %bitcast.230), calls=%async_computation.5 | async-start | bytes 3145728 | tf_op jit(solution)/shard_map/all_to_all | solution.py:300
  305.5 56.4 %collective-permute-start.6 = (s32[2,512]{1,0:T(2,128)S(1)}, s32[2,512]{1,0:T(2,128)S(1)}, u32[]{:S(2)}, u32[]{:S(2)}) collective-permute-start(s32[2,512]{1,0:T(2,128)S(1)} %copy-done.37), channel_id=1, source_target_pairs={{0,16},{16,0},{1,17},{17,1},{2,18},{18,2},{3,19},{19,3},{4,20},{20... | collective-permute-start | bytes 12296 | tf_op jit(solution)/shard_map/ppermute | solution.py:24
  307.8 62.9 %collective-permute-start.13 = (bf16[192,576]{1,0:T(8,128)(2,1)}, bf16[192,576]{1,0:T(8,128)(2,1)S(1)}, u32[]{:S(2)}, u32[]{:S(2)}) collective-permute-start(bf16[192,576]{1,0:T(8,128)(2,1)} %bitcast.248), channel_id=1, source_target_pairs={{0,16},{16,0},{1,17},{17,1},{2,18},{18,2},{3,19},{19,3},{4,20},{20... | collective-permute-start | bytes 663560 | tf_op jit(solution)/shard_map/ppermute | solution.py:24
  342.8 15.4 %all-to-all-start.2 = ((bf16[4,256,192]{1,2,0:T(8,128)(2,1)}), bf16[4,256,192]{1,2,0:T(8,128)(2,1)S(1)}, u32[]{:S(2)}, u32[]{:S(2)}) async-start(bf16[4,256,192]{1,2,0:T(8,128)(2,1)} %bitcast.32), calls=%async_computation.2 | async-start | bytes 786432 | tf_op jit(solution)/shard_map/all_to_all | solution.py:370
  346.5 24.2 %copy-start.34 = (bf16[1,192,576]{2,1,0:T(8,128)(2,1)S(1)}, bf16[1,192,576]{2,1,0:T(8,128)(2,1)}, u32[]{:S(2)}) copy-start(bf16[1,192,576]{2,1,0:T(8,128)(2,1)} %reduce-scatter.3.cloned.1.call-done) | copy-start | bytes 663556
  358.2 11.0 %all-to-all-start.6 = ((bf16[4,256,192]{1,2,0:T(8,128)(2,1)}), bf16[4,256,192]{1,2,0:T(8,128)(2,1)S(1)}, u32[]{:S(2)}, u32[]{:S(2)}) async-start(bf16[4,256,192]{1,2,0:T(8,128)(2,1)} %bitcast.51), calls=%async_computation.6 | async-start | bytes 786432 | tf_op jit(solution)/shard_map/all_to_all | solution.py:370
  361.9 12.0 %collective-permute-start.5 = (bf16[1024,192]{0,1:T(8,128)(2,1)S(1)}, bf16[1024,192]{0,1:T(8,128)(2,1)S(1)}, u32[]{:S(2)}, u32[]{:S(2)}) collective-permute-start(bf16[1024,192]{0,1:T(8,128)(2,1)S(1)} %bitcast.233), channel_id=1, source_target_pairs={{0,16},{16,0},{1,17},{17,1},{2,18},{18,2},{3,19},{19,3},{4,20},{20... | collective-permute-start | bytes 1179656 | tf_op jit(solution)/shard_map/ppermute | solution.py:24
  369.3 12.6 %collective-permute-start.12 = (bf16[1024,192]{0,1:T(8,128)(2,1)S(1)}, bf16[1024,192]{0,1:T(8,128)(2,1)S(1)}, u32[]{:S(2)}, u32[]{:S(2)}) collective-permute-start(bf16[1024,192]{0,1:T(8,128)(2,1)S(1)} %bitcast.235), channel_id=1, source_target_pairs={{0,16},{16,0},{1,17},{17,1},{2,18},{18,2},{3,19},{19,3},{4,20},{20... | collective-permute-start | bytes 1179656 | tf_op jit(solution)/shard_map/ppermute | solution.py:24
  429.8 17.2 %collective-permute-start.14 = (bf16[448,768]{1,0:T(8,128)(2,1)}, bf16[448,768]{1,0:T(8,128)(2,1)S(1)}, u32[]{:S(2)}, u32[]{:S(2)}) collective-permute-start(bf16[448,768]{1,0:T(8,128)(2,1)} %bitcast.241), channel_id=1, source_target_pairs={{0,16},{16,0},{1,17},{17,1},{2,18},{18,2},{3,19},{19,3},{4,20},{20... | collective-permute-start | bytes 2064392 | tf_op jit(solution)/shard_map/ppermute | solution.py:24
  434.0 13.0 %copy-start.26 = (bf16[1,448,768]{2,1,0:T(8,128)(2,1)S(1)}, bf16[1,448,768]{2,1,0:T(8,128)(2,1)}, u32[]{:S(2)}) copy-start(bf16[1,448,768]{2,1,0:T(8,128)(2,1)} %reduce-scatter.5.cloned.1.call-done) | copy-start | bytes 2064388
  (20 other events, 37.4 us)
Sparse Core Ops, SparseCore 0:
  14.0 112.3 all-gather.2
  276.3 26.0 reduce-scatter.2
  307.0 122.7 reduce-scatter.4

commit v2 on v1

v2 whole, which is shorter than its diff:
```python
import jax
import jax.numpy as jnp
from jax import lax
from jax.experimental import pallas as pl
from jax.experimental.pallas import tpu as pltpu
from jax.sharding import Mesh, PartitionSpec as P

DH = 64
EPSILON = 1e-05
MASKED = -1e30
LOG2E = 1.4426950408889634
SWAP = ((0, 1), (1, 0))
ROWS = ("ya", "yb")
SHARDS = ("ya", "yb", "col")
bf16 = jnp.bfloat16
f32 = jnp.float32


def contract(left, right, dims):
    return lax.dot_general(left, right, ((dims[:1], dims[1:]), ((), ())), preferred_element_type=f32)


def swap(values, axis):
    return lax.ppermute(values, axis, SWAP)


def gather_rows(values):
    first, second = lax.axis_index("ya") == 0, lax.axis_index("yb") == 0
    other = swap(values, "ya")
    pair = jnp.stack([jnp.where(first, values, other), jnp.where(first, other, values)])
    twin = swap(pair, "yb")
    both = jnp.stack([jnp.where(second, pair, twin), jnp.where(second, twin, pair)], 1)
    return both.reshape((4,) + values.shape)


def spread_dp(values):
    if lax.axis_size("dp") == 2:
        other = swap(values, "dp")
        first = lax.axis_index("dp") == 0
        return jnp.stack([jnp.where(first, values, other), jnp.where(first, other, values)])
    return lax.all_gather(values, "dp", axis=0)


def turn(values, cosine, sine):
    lanes = values.shape[1]
    even = lax.broadcasted_iota(jnp.int32, values.shape, 1) % 2 == 0
    swapped = jnp.where(even, pltpu.roll(values, lanes - 1, 1), pltpu.roll(values, 1, 1))
    return values * cosine + swapped * sine


def project_kernel(x_ref, w_ref, cos_ref, sin_ref, q_ref, k_ref, kt_ref, v_ref, vt_ref):
    width = q_ref.shape[1]
    wide = jnp.dot(x_ref[...], w_ref[...], preferred_element_type=f32)
    turned = turn(wide[:, : 2 * width], cos_ref[...], sin_ref[...])
    q_ref[...] = turned[:, :width].astype(bf16)
    keys = turned[:, width:]
    k_ref[0] = keys.astype(bf16)
    kt_ref[0] = keys.T.astype(bf16)
    values = wide[:, 2 * width :]
    v_ref[0] = values.astype(bf16)
    vt_ref[0] = values.T.astype(bf16)


def project(tokens, weight, cosine, sine, block):
    count, feature = tokens.shape
    width = weight.shape[1] // 3
    by_row = lambda lanes: pl.BlockSpec((block, lanes), lambda i: (i, 0))
    by_block = pl.BlockSpec((1, block, width), lambda i: (i, 0, 0))
    by_col = pl.BlockSpec((1, width, block), lambda i: (i, 0, 0))
    row_shape = jax.ShapeDtypeStruct((count // block, block, width), bf16)
    col_shape = jax.ShapeDtypeStruct((count // block, width, block), bf16)
    return pl.pallas_call(
        project_kernel,
        grid=(count // block,),
        in_specs=[by_row(feature), pl.BlockSpec(weight.shape, lambda i: (0, 0)), by_row(2 * width), by_row(2 * width)],
        out_specs=[by_row(width), by_block, by_col, by_block, by_col],
        out_shape=[jax.ShapeDtypeStruct((count, width), bf16), row_shape, col_shape, row_shape, col_shape],
        name="project",
    )(tokens, weight, cosine, sine)


def head_rows(values, head):
    rows = lax.broadcasted_iota(jnp.int32, values.shape, 0)
    return jnp.where((rows >= head * DH) & (rows < (head + 1) * DH), values, jnp.zeros_like(values))


def head_lanes(values, head):
    lanes = lax.broadcasted_iota(jnp.int32, values.shape, 1)
    return jnp.where((lanes >= head * DH) & (lanes < (head + 1) * DH), values, jnp.zeros_like(values))


def block_sides(info_ref, query_block, key_block, columns, share, own):
    boundary, half = info_ref[0], info_ref[1]
    low_q = query_block * share + half * own
    low_k = key_block % columns * share + jnp.where(key_block < columns, half, 1 - half) * own
    first_q, second_q = low_q < boundary, low_q + own > boundary
    first_k, second_k = low_k < boundary, low_k + own > boundary
    meets = (first_q & first_k) | (second_q & second_k)
    mixed = (first_q & second_q) | (first_k & second_k)
    side_q = low_q + lax.broadcasted_iota(jnp.int32, (1, own), 1) >= boundary
    side_k = low_k + lax.broadcasted_iota(jnp.int32, (own, 1), 0) >= boundary
    return meets, mixed, side_q.astype(f32), side_k.astype(f32)


def forward_kernel(share, info_ref, q_ref, k_ref, vt_ref, o_ref, lse_ref, parts, top, total, mixed_sum):
    own, width = q_ref.shape
    columns = k_ref.shape[0] // 2
    heads = width // DH
    scaling = DH ** (-0.5) * LOG2E
    query_block = pl.program_id(0)
    for head in range(heads):
        parts[head] = head_lanes(q_ref[...], head)
    top[...] = jnp.full_like(top, MASKED)
    total[...] = jnp.zeros_like(total)
    mixed_sum[...] = jnp.zeros_like(mixed_sum)

    def visit(key_block, same):
        for head in range(heads):
            rows = pl.ds(head * DH, DH)
            line = pl.ds(head, 1)
            scores = contract(k_ref[key_block], parts[head], (1, 1)) * scaling
            if same is not None:
                scores = jnp.where(same, scores, MASKED)
            before = top[line, :]
            highest = jnp.maximum(before, jnp.max(scores, 0, keepdims=True))
            fade = jnp.exp2(before - highest)
            raised = jnp.exp2(scores - highest)
            if same is not None:
                raised = jnp.where(same, raised, 0.0)
            top[line, :] = highest
            total[line, :] = total[line, :] * fade + jnp.sum(raised, 0, keepdims=True)
            product = jnp.dot(vt_ref[key_block, rows, :], raised.astype(bf16), preferred_element_type=f32)
            mixed_sum[rows, :] = mixed_sum[rows, :] * fade + product

    def step(key_block, carry):
        meets, mixed, side_q, side_k = block_sides(info_ref, query_block, key_block, columns, share, own)

        @pl.when(meets & mixed)
        def _():
            visit(key_block, side_q == side_k)

        @pl.when(meets & jnp.logical_not(mixed))
        def _():
            visit(key_block, None)

        return carry

    lax.fori_loop(0, 2 * columns, step, 0)
    for head in range(heads):
        rows = pl.ds(head * DH, DH)
        line = pl.ds(head, 1)
        o_ref[0, rows, :] = (mixed_sum[rows, :] / total[line, :]).astype(bf16)
        lse_ref[0, line, :] = top[line, :] + jnp.log2(total[line, :])


def attend_forward(info, q, k, vt, share, own):
    count, width = q.shape
    heads = width // DH
    blocks = count // own
    whole = lambda a: pl.BlockSpec(a.shape, lambda i, s: (0, 0, 0))
    return pl.pallas_call(
        lambda *refs: forward_kernel(share, *refs),
        grid_spec=pltpu.PrefetchScalarGridSpec(
            num_scalar_prefetch=1,
            grid=(blocks,),
            in_specs=[pl.BlockSpec((own, width), lambda i, s: (i, 0)), whole(k), whole(vt)],
            out_specs=[
                pl.BlockSpec((1, width, own), lambda i, s: (i, 0, 0)),
                pl.BlockSpec((1, heads, own), lambda i, s: (i, 0, 0)),
            ],
            scratch_shapes=[
                pltpu.VMEM((heads, own, width), bf16),
                pltpu.VMEM((heads, own), f32),
                pltpu.VMEM((heads, own), f32),
                pltpu.VMEM((width, own), f32),
            ],
        ),
        out_shape=[
            jax.ShapeDtypeStruct((blocks, width, own), bf16),
            jax.ShapeDtypeStruct((blocks, heads, own), f32),
        ],
        compiler_params=pltpu.CompilerParams(vmem_limit_bytes=40 << 20),
        name="attend_forward",
    )(info, q, k, vt)


def backward_kernel(
    share, info_ref, q_ref, k_ref, kt_ref, v_ref, g_ref, o_ref, lse_ref, dq_ref, dk_ref, dv_ref, far_k_ref, far_v_ref,
    part_q, part_g, delta, sum_q, sum_k, sum_v,
):
    own, width = q_ref.shape
    columns = k_ref.shape[0] // 2
    heads = width // DH
    scaling = DH ** (-0.5)
    query_block = pl.program_id(0)
    product = g_ref[0].astype(f32) * o_ref[0].astype(f32)
    for head in range(heads):
        part_q[pl.ds(head * own, own), :] = head_lanes(q_ref[...], head)
        part_g[:, pl.ds(head * own, own)] = head_rows(g_ref[0], head)
        delta[pl.ds(head, 1), :] = jnp.sum(product[head * DH : (head + 1) * DH], 0, keepdims=True)
    sum_q[...] = jnp.zeros_like(sum_q)

    @pl.when(query_block == 0)
    def _():
        sum_k[...] = jnp.zeros_like(sum_k)
        sum_v[...] = jnp.zeros_like(sum_v)

    def visit(key_block, same):
        all_probs, all_grads = [], []
        for head in range(heads):
            scores = contract(k_ref[key_block], part_q[pl.ds(head * own, own), :], (1, 1)) * (scaling * LOG2E)
            probs = jnp.exp2(scores - lse_ref[0, pl.ds(head, 1), :])
            if same is not None:
                probs = jnp.where(same, probs, 0.0)
            slopes = jnp.dot(v_ref[key_block], part_g[:, pl.ds(head * own, own)], preferred_element_type=f32)
            grads = (probs * (slopes - delta[pl.ds(head, 1), :])).astype(bf16)
            rows = pl.ds(head * DH, DH)
            sum_q[rows, :] += jnp.dot(kt_ref[key_block, rows, :], grads, preferred_element_type=f32)
            all_probs.append(probs.astype(bf16))
            all_grads.append(grads)
        sum_v[key_block] += contract(jnp.concatenate(all_probs, 1), part_g[...], (1, 1))
        sum_k[key_block] += jnp.dot(jnp.concatenate(all_grads, 1), part_q[...], preferred_element_type=f32)

    def step(key_block, carry):
        meets, mixed, side_q, side_k = block_sides(info_ref, query_block, key_block, columns, share, own)

        @pl.when(meets & mixed)
        def _():
            visit(key_block, side_q == side_k)

        @pl.when(meets & jnp.logical_not(mixed))
        def _():
            visit(key_block, None)

        return carry

    lax.fori_loop(0, 2 * columns, step, 0)
    dq_ref[...] = sum_q[...].T * scaling

    @pl.when(query_block == pl.num_programs(0) - 1)
    def _():
        dk_ref[...] = sum_k[:columns]
        dv_ref[...] = sum_v[:columns]
        far_k_ref[...] = sum_k[columns:].astype(bf16)
        far_v_ref[...] = sum_v[columns:].astype(bf16)


def attend_backward(info, q, k, kt, v, grad, out, lse, share, own):
    count, width = q.shape
    heads = width // DH
    blocks = count // own
    whole = lambda a: pl.BlockSpec(a.shape, lambda i, s: (0, 0, 0))
    turned = pl.BlockSpec((1, width, own), lambda i, s: (i, 0, 0))
    sums = pl.BlockSpec((blocks, own, width), lambda i, s: (0, 0, 0))
    sum_shape = lambda kind: jax.ShapeDtypeStruct((blocks, own, width), kind)
    return pl.pallas_call(
        lambda *refs: backward_kernel(share, *refs),
        grid_spec=pltpu.PrefetchScalarGridSpec(
            num_scalar_prefetch=1,
            grid=(blocks,),
            in_specs=[
                pl.BlockSpec((own, width), lambda i, s: (i, 0)),
                whole(k), whole(kt), whole(v), turned, turned,
                pl.BlockSpec((1, heads, own), lambda i, s: (i, 0, 0)),
            ],
            out_specs=[pl.BlockSpec((own, width), lambda i, s: (i, 0)), sums, sums, sums, sums],
            scratch_shapes=[
                pltpu.VMEM((heads * own, width), bf16),
                pltpu.VMEM((width, heads * own), bf16),
                pltpu.VMEM((heads, own), f32),
                pltpu.VMEM((width, own), f32),
                pltpu.VMEM((2 * blocks, own, width), f32),
                pltpu.VMEM((2 * blocks, own, width), f32),
            ],
        ),
        out_shape=[jax.ShapeDtypeStruct((count, width), f32), sum_shape(f32), sum_shape(f32), sum_shape(bf16), sum_shape(bf16)],
        compiler_params=pltpu.CompilerParams(vmem_limit_bytes=50 << 20),
        name="attend_backward",
    )(info, q, k, kt, v, grad, out, lse)


def unproject_kernel(
    dq_ref, dk_ref, far_k_ref, dv_ref, far_v_ref, x_ref, w_ref, cos_ref, sin_ref, part_ref, grad_ref, total
):
    width = dq_ref.shape[1]
    step = pl.program_id(0)

    def turn_back(values):
        lanes = lax.broadcasted_iota(jnp.int32, values.shape, 1)
        ahead = jnp.concatenate([values[:, 1:], values[:, :1]], 1)
        behind = jnp.concatenate([values[:, -1:], values[:, :-1]], 1)
        return values * cos_ref[:, :width] - jnp.where(lanes % 2 == 0, ahead, behind) * sin_ref[:, :width]

    dk = (dk_ref[0] + far_k_ref[0].astype(f32)) * DH ** (-0.5)
    dv = dv_ref[0] + far_v_ref[0].astype(f32)
    low = jnp.concatenate([turn_back(dq_ref[...]), turn_back(dk), dv], 1).astype(bf16)
    part_ref[0] = contract(low, w_ref[...], (1, 1)).astype(bf16)
    piece = contract(x_ref[...], low, (0, 0))

    @pl.when(step == 0)
    def _():
        total[...] = piece

    @pl.when(step > 0)
    def _():
        total[...] += piece

    @pl.when(step == pl.num_programs(0) - 1)
    def _():
        grad_ref[...] = total[...].astype(bf16)


def unproject(dq, dk, far_k, dv, far_v, tokens, weight, cosine, sine, own):
    count, width = dq.shape
    feature = tokens.shape[1]
    flat = lambda a: pl.BlockSpec((own, a.shape[1]), lambda i: (i, 0))
    block = pl.BlockSpec((1, own, width), lambda i: (i, 0, 0))
    whole = pl.BlockSpec(weight.shape, lambda i: (0, 0))
    return pl.pallas_call(
        unproject_kernel,
        grid=(count // own,),
        in_specs=[flat(dq), block, block, block, block, flat(tokens), whole, flat(cosine), flat(sine)],
        out_specs=[pl.BlockSpec((1, own, feature), lambda i: (i, 0, 0)), whole],
        out_shape=[jax.ShapeDtypeStruct((count // own, own, feature), bf16), jax.ShapeDtypeStruct(weight.shape, bf16)],
        scratch_shapes=[pltpu.VMEM(weight.shape, f32)],
        compiler_params=pltpu.CompilerParams(vmem_limit_bytes=40 << 20),
        name="unproject",
    )(dq, dk, far_k, dv, far_v, tokens, weight, cosine, sine)


def mean_lanes(values):
    return jnp.sum(values, 1, keepdims=True) * (1.0 / values.shape[1])


def norm_forward(values, gain, shift):
    centred = values - mean_lanes(values)
    inverse = lax.rsqrt(mean_lanes(centred * centred) + EPSILON)
    normed = centred * inverse
    return normed * gain + shift, normed, inverse


def norm_backward(grad, normed, inverse, gain):
    scaled = grad * gain
    return inverse * (scaled - mean_lanes(scaled) - normed * mean_lanes(scaled * normed))


def unit(size):
    rows = lax.broadcasted_iota(jnp.int32, (size, size), 0)
    return (rows == lax.broadcasted_iota(jnp.int32, (size, size), 1)).astype(bf16)


def feed_kernel(
    att_ref, x_ref, cot_ref, w_ref,
    result_ref, grad_att_ref, grad_one_ref, hidden_ref, act_ref, gin_ref, gtwo_ref, gone_ref, sums_ref,
    w, slopes, outer, sems,
):
    rows, columns, quarter, _ = w.shape
    hidden_cols = act_ref.shape[2]
    both = 2 * hidden_cols
    spans = ((0, hidden_cols), (hidden_cols, hidden_cols), (both, w.shape[3] - both))

    def copy(kind, column):
        lanes = pl.ds(*spans[kind])
        if kind == 2:
            return pltpu.make_async_copy(w_ref.at[:, :, :, lanes], w.at[:, :, :, lanes], sems.at[kind, 0])
        return pltpu.make_async_copy(w_ref.at[:, column, :, lanes], w.at[:, column, :, lanes], sems.at[kind, column])

    copy(2, 0).start()
    for column in range(columns):
        copy(0, column).start()
        copy(1, column).start()

    def block(kind, column):
        lanes = pl.ds(*spans[kind])
        return jnp.concatenate([w[row, column, :, lanes] for row in range(rows)], 0)

    copy(2, 0).wait()
    mix = pl.ds(both, quarter)
    attended = att_ref[...]
    branch = []
    for row in range(rows):
        weight = jnp.concatenate([w[row, column, :, mix] for column in range(columns)], 0)
        branch.append(contract(attended, weight, (0, 0)))
    branch = jnp.concatenate(branch, 1)
    eye = unit(quarter)
    small = [contract(w[row, 0, :, pl.ds(both + quarter, 12)], eye, (0, 0)) for row in range(rows)]
    small = jnp.concatenate(small, 1)
    vectors = small[0:4] + (small[4:8] + small[8:12])
    gain_one, shift_one, gain_two, shift_two = (vectors[i : i + 1] for i in range(4))

    hidden, normed_one, inverse_one = norm_forward(x_ref[...].astype(f32) + branch, gain_one, shift_one)
    hidden_ref[...] = hidden.astype(bf16)
    outer[...] = jnp.zeros_like(outer)

    def forward(column, carry):
        copy(0, column).wait()
        inner = jnp.dot(hidden_ref[...], block(0, column), preferred_element_type=f32)
        cumulative = 0.5 * (1.0 + lax.erf(inner * (0.5**0.5)))
        slopes[column] = cumulative + inner * (jnp.exp(-0.5 * inner * inner) * 0.3989422804014327)
        act_ref[column] = (inner * cumulative).astype(bf16)
        copy(1, column).wait()
        outer[...] += contract(act_ref[column], block(1, column), (1, 1))
        return carry

    lax.fori_loop(0, columns, forward, 0)
    result, normed_two, inverse_two = norm_forward(hidden + outer[...], gain_two, shift_two)
    result_ref[...] = result.astype(bf16)
    cot = cot_ref[...].astype(f32)
    grad_two = norm_backward(cot, normed_two, inverse_two, gain_two)
    gtwo_ref[...] = grad_two.astype(bf16)
    outer[...] = grad_two

    def backward(column, carry):
        grad = jnp.dot(gtwo_ref[...], block(1, column), preferred_element_type=f32)
        gin_ref[column] = (grad * slopes[column]).astype(bf16)
        outer[...] += contract(gin_ref[column], block(0, column), (1, 1))
        return carry

    lax.fori_loop(0, columns, backward, 0)
    grad_hidden = outer[...]
    grad_one = norm_backward(grad_hidden, normed_one, inverse_one, gain_one)
    grad_one_ref[...] = grad_one
    gone_ref[...] = grad_one.astype(bf16)
    for column in range(columns):
        weight = jnp.concatenate([w[row, column, :, mix] for row in range(rows)], 1)
        grad_att_ref[column] = contract(weight, gone_ref[...], (1, 1)).astype(bf16)
    sums_ref[0:1, :] = jnp.sum(grad_hidden * normed_one, 0, keepdims=True)
    sums_ref[1:2, :] = jnp.sum(grad_hidden, 0, keepdims=True)
    sums_ref[2:3, :] = jnp.sum(cot * normed_two, 0, keepdims=True)
    sums_ref[3:4, :] = jnp.sum(cot, 0, keepdims=True)


def feed(attended, tokens, cot, weights):
    own, feature = tokens.shape
    rows, columns, quarter, lanes = weights.shape
    hidden_cols = feature
    vmem = pl.BlockSpec(memory_space=pltpu.VMEM)
    wide = jax.ShapeDtypeStruct((columns, own, hidden_cols), bf16)
    flat = lambda kind: jax.ShapeDtypeStruct((own, feature), kind)
    return pl.pallas_call(
        feed_kernel,
        in_specs=[vmem, vmem, vmem, pl.BlockSpec(memory_space=pl.ANY)],
        out_specs=[vmem] * 9,
        out_shape=[
            flat(bf16), jax.ShapeDtypeStruct((columns, quarter, own), bf16), flat(f32), flat(bf16), wide, wide,
            flat(bf16), flat(bf16), jax.ShapeDtypeStruct((4, feature), f32),
        ],
        scratch_shapes=[
            pltpu.VMEM(weights.shape, bf16),
            pltpu.VMEM((columns, own, hidden_cols), f32),
            pltpu.VMEM((own, feature), f32),
            pltpu.SemaphoreType.DMA((3, columns)),
        ],
        compiler_params=pltpu.CompilerParams(vmem_limit_bytes=58 << 20),
        name="feed",
    )(attended, tokens, cot, weights)


def weigh_kernel(att_ref, hidden_ref, act_ref, gin_ref, gtwo_ref, gone_ref, sums_ref, out_ref):
    rows, _, quarter, _ = out_ref.shape
    hidden_cols = act_ref.shape[2]
    inner = contract(hidden_ref[...], gin_ref[0], (0, 0)).astype(bf16)
    outer = contract(gtwo_ref[...], act_ref[0], (0, 0)).astype(bf16)
    mixed = jnp.dot(att_ref[...], gone_ref[...], preferred_element_type=f32).astype(bf16)
    eye = unit(quarter)
    for row in range(rows):
        mine = slice(row * quarter, (row + 1) * quarter)
        out_ref[row, 0, :, 0:hidden_cols] = inner[mine]
        out_ref[row, 0, :, hidden_cols : 2 * hidden_cols] = outer[mine]
        vector = contract(eye, sums_ref[:, mine].astype(bf16), (1, 1)).astype(bf16)
        rest = jnp.zeros((quarter, out_ref.shape[3] - 2 * hidden_cols - quarter - 4), bf16)
        out_ref[row, 0, :, 2 * hidden_cols :] = jnp.concatenate([mixed[:, mine], vector, rest], 1)


def weigh(attended, hidden, act, gin, gtwo, gone, sums, lanes):
    own, feature = hidden.shape
    columns = act.shape[0]
    quarter = attended.shape[0] // columns
    whole = lambda a: pl.BlockSpec(a.shape, lambda i: (0, 0))
    piece = pl.BlockSpec((1,) + act.shape[1:], lambda i: (i, 0, 0))
    return pl.pallas_call(
        weigh_kernel,
        grid=(columns,),
        in_specs=[
            pl.BlockSpec((quarter, own), lambda i: (i, 0)),
            whole(hidden), piece, piece, whole(gtwo), whole(gone), whole(sums),
        ],
        out_specs=pl.BlockSpec((feature // quarter, 1, quarter, lanes), lambda i: (0, i, 0, 0)),
        out_shape=jax.ShapeDtypeStruct((feature // quarter, columns, quarter, lanes), bf16),
        compiler_params=pltpu.CompilerParams(vmem_limit_bytes=40 << 20),
        name="weigh",
    )(attended, hidden, act, gin, gtwo, gone, sums)


def parcel_kernel(inner_ref, outer_ref, output_ref, small_ref, out_ref):
    columns = inner_ref.shape[1]
    quarter = output_ref.shape[1]
    rest = jnp.zeros((quarter, out_ref.shape[1] - 2 * columns - quarter - 12), bf16)
    out_ref[:, 0:columns] = inner_ref[...]
    out_ref[:, columns : 2 * columns] = outer_ref[...]
    small = contract(unit(quarter), small_ref[...], (1, 1)).astype(bf16)
    out_ref[:, 2 * columns :] = jnp.concatenate([output_ref[...], small, rest], 1)


def parcel(inner, outer, output, small, lanes):
    return pl.pallas_call(
        parcel_kernel,
        out_shape=jax.ShapeDtypeStruct((inner.shape[0], lanes), bf16),
        name="parcel",
    )(inner, outer, output, small)


def split_three(values):
    high = values.astype(bf16)
    rest = values - high.astype(f32)
    middle = rest.astype(bf16)
    return jnp.concatenate([high, middle, (rest - middle.astype(f32)).astype(bf16)], 0)


def keep(values, index, axis=0):
    first, second = lax.index_in_dim(values, 0, axis, False), lax.index_in_dim(values, 1, axis, False)
    chosen = index == 0
    return jnp.where(chosen, first, second), jnp.where(chosen, second, first)


def body(
    inputs, cotangent, lengths, source, query_weight, key_weight, value_weight, output_weight, inner_weight, outer_weight,
    first_gain, first_shift, second_gain, second_shift,
):
    micro, quarter, share = inputs.shape
    dp_count, columns = lax.axis_size("dp"), lax.axis_size("col")
    pack, own = share * columns, share // 2
    feature, count = 4 * quarter, share * micro
    width, hidden_cols = query_weight.shape[1], inner_weight.shape[1]
    lanes = -(-(2 * hidden_cols + quarter + 12) // 128) * 128
    me, m, half, z = (lax.axis_index(a) for a in ("dp", "ya", "yb", "col"))

    vectors = split_three(jnp.stack([first_gain, first_shift, second_gain, second_shift]))
    packed = parcel(inner_weight, outer_weight, output_weight, vectors, lanes)
    everywhere = lax.all_gather(packed, SHARDS, axis=0).reshape(4, columns, quarter, lanes)
    qkv_weight = gather_rows(jnp.concatenate([query_weight, key_weight, value_weight], 1)).reshape(feature, -1)

    anchors = spread_dp(source)
    anchor = source.reshape(count)
    place = anchor // (dp_count * pack) * share + anchor % share
    holder = anchor % (dp_count * pack) // pack
    wide_in, wide_cot = spread_dp(inputs), spread_dp(cotangent)
    if dp_count == 2:
        pick = (holder * count + place)[:, None] == jnp.arange(dp_count * count, dtype=jnp.int32)[None, :]
        pick = pick.astype(bf16).reshape(count, dp_count, micro, share)
        deal = lambda wide: jnp.einsum("tsmj,smfj->tf", pick, wide, preferred_element_type=f32).astype(bf16)
    else:
        deal = lambda wide: wide.transpose(0, 1, 3, 2).reshape(-1, quarter)[holder * count + place]

    def to_tokens(dealt):
        moved = lax.all_to_all(dealt.reshape(4, own, quarter), ROWS, split_axis=0, concat_axis=0, tiled=True)
        return moved.transpose(1, 0, 2).reshape(own, feature)

    tokens = to_tokens(deal(wide_in))
    cot = to_tokens(deal(wide_cot))

    boundary = jnp.where(m == 0, lengths[0, 0], lengths[0, 1])
    info = jnp.stack([boundary, half]).astype(jnp.int32)
    spots = jnp.arange(columns, dtype=jnp.int32)[:, None] * share + jnp.arange(own, dtype=jnp.int32)[None, :]
    mine = (spots + half * own).reshape(-1)
    frequency = 10000.0 ** (-2.0 * jnp.arange(DH // 2, dtype=f32) / DH)
    angles = (mine - jnp.where(mine >= boundary, boundary, 0)).astype(f32)[:, None] * jnp.repeat(frequency, 2)[None, :]
    signs = jnp.where(jnp.arange(DH) % 2 == 0, -1.0, 1.0)
    copies = 2 * width // DH
    cosine, sine = jnp.tile(jnp.cos(angles), (1, copies)), jnp.tile(jnp.sin(angles) * signs, (1, copies))

    parts = [lax.all_gather(tokens[i * own // 2 : (i + 1) * own // 2], "col", axis=0) for i in range(2)]
    tokens_full = jnp.concatenate(parts, 1).reshape(columns * own, feature)
    q, k, kt, v, vt = project(tokens_full, qkv_weight, cosine, sine, own)
    with_twin = lambda a: jnp.concatenate([a, swap(a, "yb")], 0)
    k, kt, v, vt = (with_twin(a) for a in (k, kt, v, vt))
    attended, lse = attend_forward(info, q, k, vt, share, own)
    over_cols = lambda a: lax.all_to_all(a, "col", split_axis=0, concat_axis=0, tiled=True)
    attended_t = over_cols(attended).reshape(feature, own)

    result, grad_att, grad_one, hidden, act, gin, gtwo, gone, sums = feed(attended_t, tokens, cot, everywhere)
    grad_att = over_cols(grad_att)
    cut = weigh(attended_t, hidden, act, gin, gtwo, gone, sums, lanes)
    summed = lax.psum_scatter(cut.reshape(4 * columns, quarter, lanes), SHARDS, scatter_dimension=0, tiled=False)

    dq, dk, dv, far_k, far_v = attend_backward(info, q, k, kt, v, grad_att, attended, lse, share, own)
    far_k, far_v = swap(far_k, "yb"), swap(far_v, "yb")
    partial, grad_qkv = unproject(dq, dk, far_k, dv, far_v, tokens_full, qkv_weight, cosine, sine, own)
    partial = over_cols(partial)
    grad_tokens = grad_one + jnp.sum(partial.astype(f32), 0)

    grad_qkv = grad_qkv.reshape(2, 2, quarter, 3 * width)
    for axis, index, place_axis in (("yb", half, 1), ("ya", m, 0)):
        kept, sent = keep(grad_qkv, index, place_axis)
        grad_qkv = (kept.astype(f32) + swap(sent, axis).astype(f32)).astype(bf16)

    def over_dp(values):
        if dp_count == 2:
            return values.astype(f32) + swap(values, "dp").astype(f32)
        return lax.psum(values, "dp").astype(f32)

    grad_qkv = over_dp(grad_qkv)
    summed = over_dp(summed)
    sum_inner, sum_outer = summed[:, :hidden_cols], summed[:, hidden_cols : 2 * hidden_cols]
    sum_output = summed[:, 2 * hidden_cols : 2 * hidden_cols + quarter]
    sum_vectors = summed[:, 2 * hidden_cols + quarter : 2 * hidden_cols + quarter + 4].T

    def to_loader(rows):
        cut = rows.astype(bf16).reshape(own, 4, quarter).transpose(1, 0, 2)
        moved = lax.all_to_all(cut, ROWS, split_axis=0, concat_axis=0, tiled=True).reshape(count, quarter)
        return spread_dp(moved)

    spot = jnp.arange(count, dtype=jnp.int32)
    wanted = spot // share * (dp_count * pack) + me * pack + z * share + spot % share
    if dp_count == 2:
        put = (anchors.reshape(-1)[:, None] == wanted[None, :]).astype(bf16)
        settle = lambda wide: contract(wide.reshape(-1, quarter), put, (0, 0)).astype(bf16)
    else:
        order = jnp.argsort(anchors.reshape(-1))
        spots_in = jnp.searchsorted(anchors.reshape(-1)[order], wanted)
        settle = lambda wide: wide.reshape(-1, quarter)[order[spots_in]].T
    shape = lambda a: a.reshape(quarter, micro, share).transpose(1, 0, 2)
    final_out = shape(settle(to_loader(result)))
    final_grad = shape(settle(to_loader(grad_tokens)))
    return (
        final_out, final_grad, grad_qkv[:, :width], grad_qkv[:, width : 2 * width], grad_qkv[:, 2 * width :],
        sum_output, sum_inner, sum_outer, sum_vectors[0], sum_vectors[1], sum_vectors[2], sum_vectors[3],
    )


def solution(mesh):
    dp, row, col = (mesh.shape[a] for a in ("dp", "row", "col"))
    fine = Mesh(mesh.devices.reshape(dp, 2, row // 2, col), ("dp", "ya", "yb", "col"))
    tokens, matrix = P(None, ROWS, ("dp", "col")), P(ROWS, "col")
    weights = (matrix, matrix, matrix, P("col", ROWS), matrix, matrix, P(ROWS), P(ROWS), P(ROWS), P(ROWS))
    return jax.shard_map(
        body,
        mesh=fine,
        in_specs=(tokens, tokens, P("dp", None), P(None, ("dp", "col"))) + weights,
        out_specs=(tokens, tokens) + weights,
        check_vma=False,
    )
```

time: 464 us -> 352 us (0.76); the launches traced: 456 us -> 350 us
  local copies, waits for them, and re-layouts: 111 us -> 32.8 us
  Pallas kernels: 42.8 us -> 78 us
  matrix products: 31.9 us -> 6.91 us
  waiting for transfers between devices: 124 us -> 106 us
  other arithmetic: 28.4 us -> 14 us
  blocking collectives: 58.5 us -> 51 us
    reduce_scatter x2 -> x1, waiting for transfers between devices: 47.7 us -> 0.02 us  [body(): lax.psum_scatter(cut.reshape(4 * columns, quarter, lanes), SHARDS, scatte...]
    pallas_call x2 -> x6, Pallas kernels: 36.5 us -> 71.8 us  [the longest x1 27.8 us: attend_backward(): pl.pallas_call(lambda *refs: backward_kernel(share, *refs), grid_spec=plt...]
    reshape x10 -> x2, local copies, waits for them, and re-layouts: 36.2 us -> 1.84 us  [to_tokens(): return moved.transpose(1, 0, 2).reshape(own, feature)]
    all_to_all x3, waiting for transfers between devices: 34.3 us -> 59.6 us  [body(): lax.all_to_all(a, 'col', split_axis=0, concat_axis=0, tiled=True)]
    dot_general x10 -> x2, matrix products: 22.8 us -> 3.31 us  [contract(): lax.dot_general(left, right, ((dims[:1], dims[1:]), ((), ())), preferred_...]
    unnamed x99 -> x70, local copies, waits for them, and re-layouts: 26.9 us -> 14.2 us
    slice x9 -> x2, local copies, waits for them, and re-layouts: 12.7 us -> 1.78 us  [the longest x1 1.09 us: body(): summed[:, hidden_cols:2 * hidden_cols]]
    all_gather x2, blocking collectives: 58.5 us -> 51 us  [body(): lax.all_gather(tokens[i * own // 2:(i + 1) * own // 2], 'col', axis=0)]
  transfers between devices with their start and end apart: 25 -> 26, of which waited for: 10 -> 15; matrix products, arithmetic and copies ran while one was open for 33% -> 10% of each run, Pallas kernels for 4% -> 15%
where the time goes in v2:
time: 352 us; the launch traced here: 350 us
  waiting for transfers between devices  106 us (30%)
  Pallas kernels  78 us (22%)
  blocking collectives  51 us (14%)
  starting transfers between devices  44.9 us (13%)
  local copies, waits for them, and re-layouts  32.8 us (9%)
  between operations  16 us (5%)
  other arithmetic  14 us (4%)
  matrix products  6.91 us (2%)
    all_to_all x3, waiting for transfers between devices, body(): lax.all_to_all(a, 'col', split_axis=0, concat_axis=0, tiled=True)  59.6 us
    all_gather x2, blocking collectives, body(): lax.all_gather(tokens[i * own // 2:(i + 1) * own // 2], 'col', axis=0)  51 us
    ppermute x17, waiting for transfers between devices, swap(): return lax.ppermute(values, axis, SWAP)  29.7 us
    pallas_call x1, Pallas kernels, attend_backward(): pl.pallas_call(lambda *refs: backward_kernel(share, *refs), grid_spec=plt...  27.8 us
    ppermute x17, starting transfers between devices, swap(): return lax.ppermute(values, axis, SWAP)  18.7 us
    pallas_call x1, Pallas kernels, feed(): pl.pallas_call(feed_kernel, in_specs=[vmem, vmem, vmem, pl.BlockSpec(memo...  16 us
    unnamed x70, local copies, waits for them, and re-layouts  14.2 us
    pallas_call x1, Pallas kernels, attend_forward(): pl.pallas_call(lambda *refs: forward_kernel(share, *refs), grid_spec=pltp...  13.7 us
  transfers between devices with their start and end apart: 26, of which 15 were waited for; matrix products, arithmetic and copies ran while one was open for 10% of the time, Pallas kernels for 15%

profile of v2, /device:TPU:0, one launch (start us, length us, event | category | flops | bytes accessed | tf_op | source)
XLA Modules:
  0.0 349.9 jit_solution(6767849289551643280)
XLA Ops:
  9.5 2.2 parcel.1
  12.5 3.0 collective-permute-start.1
  15.5 1.5 collective-permute-start
  21.0 1.7 copy.82.cos_ref
  22.9 1.6 copy.83.sin_ref
  25.8 1.9 collective-permute-done
  28.7 1.8 fusion.25
  31.3 3.5 all-to-all-start
  36.9 5.2 %all-to-all-done = bf16[4,256,192]{1,2,0:T(8,128)(2,1)S(1)} async-done(((bf16[4,256,192]{1,2,0:T(8,128)(2,1)}), bf16[4,256,192]{1,2,0:T(8,128)(2,1)S(1)}, u32[]{:S(2)}, u32[]{:S(2)}) %all-to-all-start) | async-done | bytes 393248 | tf_op jit(solution)/shard_map/all_to_all | solution.py:556
  42.5 21.6 %all_gather.19 = bf16[4,128,768]{2,1,0:T(8,128)(2,1)S(1)} all-gather(bf16[1,128,768]{2,1,0:T(8,128)(2,1)S(1)} %copy.79), channel_id=1, replica_groups=mesh['dp'=2,'ya'=2,'yb'=2,'col'=4] {'col'}, dimensions={0}, use_global_device_ids=true | all-gather | bytes 983040 | tf_op jit(solution)/shard_map/all_gather | solution.py:572
  64.2 29.4 %all_gather.21 = bf16[4,128,768]{2,1,0:T(8,128)(2,1)S(1)} all-gather(bf16[1,128,768]{2,1,0:T(8,128)(2,1)S(1)} %copy.80), channel_id=1, replica_groups=mesh['dp'=2,'ya'=2,'yb'=2,'col'=4] {'col'}, dimensions={0}, use_global_device_ids=true | all-gather | bytes 983040 | tf_op jit(solution)/shard_map/all_gather | solution.py:572
  94.9 6.3 %project.1 = (bf16[1024,192]{1,0:T(8,128)(2,1)}, bf16[4,256,192]{2,1,0:T(8,128)(2,1)}, bf16[4,192,256]{2,1,0:T(8,128)(2,1)}, bf16[4,256,192]{2,1,0:T(8,128)(2,1)}, bf16[4,192,256]{2,1,0:T(8,128)(2,1)}) custom-call(bf16[1024,768]{1,0:T(8,128)(2,1)} %bitcast.140, bf16[768,576]{1,0:T(8,128)(2,1)} %bitcast.142, f32[1024,384]{1,0:T(8,128)} %copy.82.cos_ref, ...), custom_call_target="tpu_custom_call" | custom-call | tf_op jit(solution)/shard_map/project/pallas_call | solution.py:72
  101.7 1.8 fusion.22
  104.3 3.6 %all-to-all-start.2 = ((bf16[4,256,192]{1,2,0:T(8,128)(2,1)}), bf16[4,256,192]{1,2,0:T(8,128)(2,1)S(1)}, u32[]{:S(2)}, u32[]{:S(2)}) async-start(bf16[4,256,192]{1,2,0:T(8,128)(2,1)} %bitcast.138), calls=%async_computation.2 | async-start | bytes 786432 | tf_op jit(solution)/shard_map/all_to_all | solution.py:556
  110.6 13.7 %attend_forward.1 = (bf16[4,192,256]{2,1,0:T(8,128)(2,1)}, f32[4,3,256]{2,1,0:T(4,128)S(1)}) custom-call(s32[2]{0:T(128)S(1)} %pad_add_fusion.refs_0_, bf16[1024,192]{1,0:T(8,128)(2,1)S(1)} %copy-done.7, bf16[8,256,192]{2,1,0:T(8,128)(2,1)S(1)} %constant_dynamic-update-slice_fusion.refs_2_, bf16[8,192,256]{2,1,0:T(8,128)(2,1)S(1)} %pad_maximum_fusion.3.refs_3_), custom_call_target="tpu_custom_call" | custom-call | tf_op jit(solution)/shard_map/attend_forward/pallas_call | solution.py:161
  124.3 4.9 %all-to-all-start.1 = ((bf16[4,192,256]{2,1,0:T(8,128)(2,1)}), bf16[4,192,256]{2,1,0:T(8,128)(2,1)S(1)}, u32[]{:S(2)}, u32[]{:S(2)}) async-start(bf16[4,192,256]{2,1,0:T(8,128)(2,1)} %get-tuple-element.38.refs_6_), calls=%async_computation.1 | async-start | bytes 786432 | tf_op jit(solution)/shard_map/all_to_all | solution.py:578
  131.1 10.4 %all-to-all-done.1 = bf16[4,192,256]{2,1,0:T(8,128)(2,1)S(1)} async-done(((bf16[4,192,256]{2,1,0:T(8,128)(2,1)}), bf16[4,192,256]{2,1,0:T(8,128)(2,1)S(1)}, u32[]{:S(2)}, u32[]{:S(2)}) %all-to-all-start.1) | async-done | bytes 393248 | tf_op jit(solution)/shard_map/all_to_all | solution.py:578
  142.3 16.0 %feed.1 = (bf16[256,768]{1,0:T(8,128)(2,1)}, bf16[4,192,256]{2,1,0:T(8,128)(2,1)}, f32[256,768]{1,0:T(8,128)}, bf16[256,768]{1,0:T(8,128)(2,1)}, bf16[4,256,768]...) custom-call(bf16[768,256]{1,0:T(8,128)(2,1)} %bitcast.146, ...), custom_call_target="tpu_custom_call" | custom-call | tf_op jit(solution)/shard_map/feed/pallas_call | solution.py:440
  159.3 1.4 copy-done.9
  160.7 1.4 copy-done.10
  165.8 6.3 %weigh.1 = bf16[4,4,192,1792]{3,2,1,0:T(8,128)(2,1)} custom-call(bf16[768,256]{1,0:T(8,128)(2,1)S(1)} %bitcast.147, bf16[256,768]{1,0:T(8,128)(2,1)S(1)} %copy-done.14, bf16[4,256,768]{2,1,0:T(8,128)(2,1)S(1)} %copy-done.9, bf16[4,256,768]{2,1,0:T(8,128)(2,1)S(1)} %copy-done.10, bf16[256,768]{1,0:T(8,128)(2,1)S(1)} %copy-done.15, ...), custom_call_target="tpu_custom_call" | custom-call | tf_op jit(solution)/shard_map/weigh/pallas_call | solution.py:481
  173.1 3.5 all-to-all-start.4
  177.3 1.5 collective-permute-done.9
  178.7 2.5 pad_maximum_fusion.1.refs_4_
  181.2 8.0 %all-to-all-done.4.refs_5_ = bf16[4,192,256]{2,1,0:T(8,128)(2,1)S(1)} async-done(((bf16[4,192,256]{2,1,0:T(8,128)(2,1)}), bf16[4,192,256]{2,1,0:T(8,128)(2,1)S(1)}, u32[]{:S(2)}, u32[]{:S(2)}) %all-to-all-start.4) | async-done | bytes 393248 | tf_op jit(solution)/shard_map/all_to_all | solution.py:578
  189.2 27.8 %attend_backward.1 = (f32[1024,192]{1,0:T(8,128)}, f32[4,256,192]{2,1,0:T(8,128)}, f32[4,256,192]{2,1,0:T(8,128)}, bf16[4,256,192]{2,1,0:T(8,128)(2,1)S(1)}, bf16[4,256,192]{2,1,0:T(8,128)(2,1)S(1)}) custom-call(s32[2]{0:T(128)S(1)} %pad_add_fusion.refs_0_, bf16[1024,192]{1,0:T(8,128)(2,1)S(1)} %copy-done.7, bf16[8,256,192]{2,1,0:T(8,128)(2,1)} %copy-done.4, ...), custom_call_target="tpu_custom_call" | custom-call | tf_op jit(solution)/shard_map/attend_backward/pallas_call | solution.py:256
  217.5 1.4 collective-permute-done.10.far_k_ref
  223.3 5.8 %unproject.1 = (bf16[4,256,768]{2,1,0:T(8,128)(2,1)S(1)}, bf16[768,576]{1,0:T(8,128)(2,1)S(1)}) custom-call(f32[1024,192]{1,0:T(8,128)S(1)} %copy-done.11, f32[4,256,192]{2,1,0:T(8,128)S(1)} %copy-done.12, bf16[4,256,192]{2,1,0:T(8,128)(2,1)S(1)} %collective-permute-done.10.far_k_ref, f32[4,256,192]{2,1,0:T(8,128)S(1)} %copy-done.13, ...), custom_call_target="tpu_custom_call" | custom-call | tf_op jit(solution)/shard_map/unproject/pallas_call | solution.py:319
  230.3 3.6 %all-to-all-start.5 = ((bf16[4,256,768]{2,1,0:T(8,128)(2,1)}), bf16[4,256,768]{2,1,0:T(8,128)(2,1)S(1)}, u32[]{:S(2)}, u32[]{:S(2)}) async-start(bf16[4,256,768]{2,1,0:T(8,128)(2,1)} %copy-done.8), calls=%async_computation.5 | async-start | bytes 3145728 | tf_op jit(solution)/shard_map/all_to_all | solution.py:578
  234.1 1.8 collective-permute-done.13
  236.1 1.7 collective-permute-start.14
  237.8 2.5 collective-permute-start.7
  240.3 1.9 copy.88
  242.2 1.9 collective-permute-done.14
  244.3 3.0 collective-permute-start.15
  247.3 41.1 %all-to-all-done.5 = bf16[4,256,768]{2,1,0:T(8,128)(2,1)S(1)} async-done(((bf16[4,256,768]{2,1,0:T(8,128)(2,1)}), bf16[4,256,768]{2,1,0:T(8,128)(2,1)S(1)}, u32[]{:S(2)}, u32[]{:S(2)}) %all-to-all-start.5) | async-done | bytes 1572896 | tf_op jit(solution)/shard_map/all_to_all | solution.py:578
  288.5 3.5 all-to-all-start.3
  293.2 6.1 %all-to-all-done.3 = bf16[4,256,192]{1,2,0:T(8,128)(2,1)S(1)} async-done(((bf16[4,256,192]{1,2,0:T(8,128)(2,1)}), bf16[4,256,192]{1,2,0:T(8,128)(2,1)S(1)}, u32[]{:S(2)}, u32[]{:S(2)}) %all-to-all-start.3) | async-done | bytes 393248 | tf_op jit(solution)/shard_map/all_to_all | solution.py:610
  299.3 3.7 %all-to-all-start.6 = ((bf16[4,256,192]{1,2,0:T(8,128)(2,1)}), bf16[4,256,192]{1,2,0:T(8,128)(2,1)S(1)}, u32[]{:S(2)}, u32[]{:S(2)}) async-start(bf16[4,256,192]{1,2,0:T(8,128)(2,1)} %bitcast.41), calls=%async_computation.6 | async-start | bytes 786432 | tf_op jit(solution)/shard_map/all_to_all | solution.py:610
  303.1 1.5 collective-permute-start.6
  304.7 5.6 %all-to-all-done.6 = bf16[4,256,192]{1,2,0:T(8,128)(2,1)S(1)} async-done(((bf16[4,256,192]{1,2,0:T(8,128)(2,1)}), bf16[4,256,192]{1,2,0:T(8,128)(2,1)S(1)}, u32[]{:S(2)}, u32[]{:S(2)}) %all-to-all-start.6) | async-done | bytes 393248 | tf_op jit(solution)/shard_map/all_to_all | solution.py:610
  310.3 1.5 collective-permute-start.12
  312.7 2.4 collective-permute-done.6
  315.1 7.7 %collective-permute-done.12 = bf16[1024,192]{0,1:T(8,128)(2,1)S(1)} collective-permute-done((bf16[1024,192]{0,1:T(8,128)(2,1)S(1)}, bf16[1024,192]{0,1:T(8,128)(2,1)S(1)}, u32[]{:S(2)}, u32[]{:S(2)}) %collective-permute-start.12) | collective-permute-done | bytes 393248 | tf_op jit(solution)/shard_map/ppermute | solution.py:24
  323.1 1.5 collective-permute-start.16
  324.7 1.7 fusion.31
  327.3 1.7 fusion.28
  329.7 10.3 %collective-permute-done.16 = bf16[192,1792]{1,0:T(8,128)(2,1)S(1)} collective-permute-done((bf16[192,1792]{1,0:T(8,128)(2,1)}, bf16[192,1792]{1,0:T(8,128)(2,1)S(1)}, u32[]{:S(2)}, u32[]{:S(2)}) %collective-permute-start.16) | collective-permute-done | bytes 688160 | tf_op jit(solution)/shard_map/ppermute | solution.py:24
  (155 shorter events, 39.5 us)
Async XLA Ops:
  7.2 4.5 %copy-start.29 = (bf16[192,192]{1,0:T(8,128)(2,1)S(1)}, bf16[192,192]{1,0:T(8,128)(2,1)}, u32[]{:S(2)}) copy-start(bf16[192,192]{1,0:T(8,128)(2,1)} %param.18) | copy-start | bytes 221188
  7.2 4.5 %copy-start.28 = (bf16[192,192]{1,0:T(8,128)(2,1)S(1)}, bf16[192,192]{1,0:T(8,128)(2,1)}, u32[]{:S(2)}) copy-start(bf16[192,192]{1,0:T(8,128)(2,1)} %param.19) | copy-start | bytes 221188
  7.2 4.5 %copy-start.27 = (bf16[192,192]{1,0:T(8,128)(2,1)S(1)}, bf16[192,192]{1,0:T(8,128)(2,1)}, u32[]{:S(2)}) copy-start(bf16[192,192]{1,0:T(8,128)(2,1)} %param.20) | copy-start | bytes 221188
  7.2 8.3 %copy-start.22 = (bf16[2,192,512]{2,1,0:T(8,128)(2,1)S(1)}, bf16[2,192,512]{2,1,0:T(8,128)(2,1)}, u32[]{:S(2)}) copy-start(bf16[2,192,512]{2,1,0:T(8,128)(2,1)} %param.14) | copy-start | bytes 1179652
  7.2 9.8 %copy-start.23 = (bf16[2,192,512]{2,1,0:T(8,128)(2,1)S(1)}, bf16[2,192,512]{2,1,0:T(8,128)(2,1)}, u32[]{:S(2)}) copy-start(bf16[2,192,512]{2,1,0:T(8,128)(2,1)} %param.15) | copy-start | bytes 1179652
  7.2 10.3 %copy-start.31 = (s32[2,512]{1,0:T(2,128)S(1)}, s32[2,512]{1,0:T(2,128)}, u32[]{:S(2)}) copy-start(s32[2,512]{1,0:T(2,128)} %param.17) | copy-start | bytes 12292
  7.2 10.6 %copy-start.32 = (s32[1,2]{1,0:T(1,128)S(1)}, s32[1,2]{1,0:T(1,128)}, u32[]{:S(2)}) copy-start(s32[1,2]{1,0:T(1,128)} %param.16) | copy-start | bytes 28
  7.3 134.3 %all-gather.3.cloned.1.call-start = ((), (), s32[]{:S(2)}) async-start(), calls=%async_computation.9 | async-start | bytes 11698176 | tf_op jit(solution)/shard_map/all_gather | solution.py:540
  12.5 12.0 %collective-permute-start.1 = (bf16[192,576]{1,0:T(8,128)(2,1)}, bf16[192,576]{1,0:T(8,128)(2,1)}, u32[]{:S(2)}, u32[]{:S(2)}) collective-permute-start(bf16[192,576]{1,0:T(8,128)(2,1)} %pad_maximum_fusion.7), channel_id=1, source_target_pairs={{0,8},{8,0},{1,9},{9,1},{2,10},{10,2},{3,11},{11,3},{4,12},{12,4},... | collective-permute-start | bytes 663560 | tf_op jit(solution)/shard_map/ppermute | solution.py:24
  15.5 12.1 %collective-permute-start = (bf16[2,192,512]{2,1,0:T(8,128)(2,1)S(1)}, bf16[2,192,512]{2,1,0:T(8,128)(2,1)}, u32[]{:S(2)}, u32[]{:S(2)}) collective-permute-start(bf16[2,192,512]{2,1,0:T(8,128)(2,1)S(1)} %copy-done.22), channel_id=1, source_target_pairs={{0,16},{16,0},{1,17},{17,1},{2,18},{18,2},{3,19},{19,3},{4,20},{20... | collective-permute-start | bytes 1179656 | tf_op jit(solution)/shard_map/ppermute | solution.py:24
  17.0 17.8 %collective-permute-start.5 = (bf16[2,192,512]{2,1,0:T(8,128)(2,1)S(1)}, bf16[2,192,512]{2,1,0:T(8,128)(2,1)S(1)}, u32[]{:S(2)}, u32[]{:S(2)}) collective-permute-start(bf16[2,192,512]{2,1,0:T(8,128)(2,1)S(1)} %copy-done.23), channel_id=1, source_target_pairs={{0,16},{16,0},{1,17},{17,1},{2,18},{18,2},{3,19},{19,3},{4,20},{20... | collective-permute-start | bytes 1179656 | tf_op jit(solution)/shard_map/ppermute | solution.py:24
  22.7 1.8 copy-start.30
  25.7 9.9 %collective-permute-start.2 = (bf16[2,192,576]{2,1,0:T(8,128)(2,1)S(1)}, bf16[2,192,576]{2,1,0:T(8,128)(2,1)S(1)}, u32[]{:S(2)}, u32[]{:S(2)}) collective-permute-start(bf16[2,192,576]{2,1,0:T(8,128)(2,1)S(1)} %pad_maximum_fusion.6), channel_id=1, source_target_pairs={{0,4},{4,0},{1,5},{5,1},{2,6},{6,2},{3,7},{7,3},{8,12},{12,8},{9,1... | collective-permute-start | bytes 1327112 | tf_op jit(solution)/shard_map/ppermute | solution.py:24
  31.3 10.9 %all-to-all-start = ((bf16[4,256,192]{1,2,0:T(8,128)(2,1)}), bf16[4,256,192]{1,2,0:T(8,128)(2,1)S(1)}, u32[]{:S(2)}, u32[]{:S(2)}) async-start(bf16[4,256,192]{1,2,0:T(8,128)(2,1)} %bitcast.139), calls=%async_computation | async-start | bytes 786432 | tf_op jit(solution)/shard_map/all_to_all | solution.py:556
  94.9 6.8 %copy-start.25 = (bf16[1,2,192,512]{3,2,1,0:T(8,128)(2,1)S(1)}, bf16[1,2,192,512]{3,2,1,0:T(8,128)(2,1)}, u32[]{:S(2)}) copy-start(bf16[1,2,192,512]{3,2,1,0:T(8,128)(2,1)} %get-tuple-element.71) | copy-start | bytes 1179652
  101.2 8.0 %collective-permute-start.4 = (bf16[4,192,256]{2,1,0:T(8,128)(2,1)}, bf16[4,192,256]{2,1,0:T(8,128)(2,1)}, u32[]{:S(2)}, u32[]{:S(2)}) collective-permute-start(bf16[4,192,256]{2,1,0:T(8,128)(2,1)} %get-tuple-element.37), channel_id=1, source_target_pairs={{0,4},{4,0},{1,5},{5,1},{2,6},{6,2},{3,7},{7,3},{8,12},{12,8},{9,1... | collective-permute-start | bytes 1179656 | tf_op jit(solution)/shard_map/ppermute | solution.py:24
  101.2 6.8 %collective-permute-start.3 = (bf16[4,256,192]{2,1,0:T(8,128)(2,1)}, bf16[4,256,192]{2,1,0:T(8,128)(2,1)}, u32[]{:S(2)}, u32[]{:S(2)}) collective-permute-start(bf16[4,256,192]{2,1,0:T(8,128)(2,1)} %get-tuple-element.36), channel_id=1, source_target_pairs={{0,4},{4,0},{1,5},{5,1},{2,6},{6,2},{3,7},{7,3},{8,12},{12,8},{9,1... | collective-permute-start | bytes 1179656 | tf_op jit(solution)/shard_map/ppermute | solution.py:24
  101.7 6.2 %copy-start.20 = (bf16[4,256,192]{2,1,0:T(8,128)(2,1)S(1)}, bf16[4,256,192]{2,1,0:T(8,128)(2,1)}, u32[]{:S(2)}) copy-start(bf16[4,256,192]{2,1,0:T(8,128)(2,1)} %get-tuple-element.36) | copy-start | bytes 1179652
  103.5 5.7 %copy-start.26 = (bf16[4,192,256]{2,1,0:T(8,128)(2,1)S(1)}, bf16[4,192,256]{2,1,0:T(8,128)(2,1)}, u32[]{:S(2)}) copy-start(bf16[4,192,256]{2,1,0:T(8,128)(2,1)} %get-tuple-element.37) | copy-start | bytes 1179652
  104.3 6.2 %copy-start.7 = (bf16[1024,192]{1,0:T(8,128)(2,1)S(1)}, bf16[1024,192]{1,0:T(8,128)(2,1)}, u32[]{:S(2)}) copy-start(bf16[1024,192]{1,0:T(8,128)(2,1)} %get-tuple-element.35.refs_1_) | copy-start | bytes 1179652
  104.3 20.0 %all-to-all-start.2 = ((bf16[4,256,192]{1,2,0:T(8,128)(2,1)}), bf16[4,256,192]{1,2,0:T(8,128)(2,1)S(1)}, u32[]{:S(2)}, u32[]{:S(2)}) async-start(bf16[4,256,192]{1,2,0:T(8,128)(2,1)} %bitcast.138), calls=%async_computation.2 | async-start | bytes 786432 | tf_op jit(solution)/shard_map/all_to_all | solution.py:556
  109.2 15.1 %copy-start.4 = (bf16[8,256,192]{2,1,0:T(8,128)(2,1)}, bf16[8,256,192]{2,1,0:T(8,128)(2,1)S(1)}, u32[]{:S(2)}) copy-start(bf16[8,256,192]{2,1,0:T(8,128)(2,1)S(1)} %constant_dynamic-update-slice_fusion.refs_2_) | copy-start | bytes 2359300
  124.3 17.2 %all-to-all-start.1 = ((bf16[4,192,256]{2,1,0:T(8,128)(2,1)}), bf16[4,192,256]{2,1,0:T(8,128)(2,1)S(1)}, u32[]{:S(2)}, u32[]{:S(2)}) async-start(bf16[4,192,256]{2,1,0:T(8,128)(2,1)} %get-tuple-element.38.refs_6_), calls=%async_computation.1 | async-start | bytes 786432 | tf_op jit(solution)/shard_map/all_to_all | solution.py:578
  129.2 193.8 %reduce-scatter.2.cloned.1.call-start = ((), (), s32[]{:S(2)}) async-start(), calls=%async_computation.8 | async-start | bytes 11698176 | tf_op jit(solution)/shard_map/reduce_scatter | solution.py:584
  159.3 1.4 copy-start.9
  160.7 1.4 copy-start.10
  172.1 4.5 %copy-start.21 = (bf16[4,256,192]{2,1,0:T(8,128)(2,1)S(1)}, bf16[4,256,192]{2,1,0:T(8,128)(2,1)}, u32[]{:S(2)}) copy-start(bf16[4,256,192]{2,1,0:T(8,128)(2,1)} %get-tuple-element.42) | copy-start | bytes 1179652
  173.1 4.1 %collective-permute-start.8 = (bf16[4,192,256]{2,1,0:T(8,128)(2,1)S(1)}, bf16[4,192,256]{2,1,0:T(8,128)(2,1)S(1)}, u32[]{:S(2)}, u32[]{:S(2)}) collective-permute-start(bf16[4,192,256]{2,1,0:T(8,128)(2,1)S(1)} %copy-done.24), channel_id=1, source_target_pairs={{0,4},{4,0},{1,5},{5,1},{2,6},{6,2},{3,7},{7,3},{8,12},{12,8},{9,1... | collective-permute-start | bytes 1179656 | tf_op jit(solution)/shard_map/ppermute | solution.py:24
  173.1 16.1 %all-to-all-start.4 = ((bf16[4,192,256]{2,1,0:T(8,128)(2,1)}), bf16[4,192,256]{2,1,0:T(8,128)(2,1)S(1)}, u32[]{:S(2)}, u32[]{:S(2)}) async-start(bf16[4,192,256]{2,1,0:T(8,128)(2,1)} %get-tuple-element.43), calls=%async_computation.4 | async-start | bytes 786432 | tf_op jit(solution)/shard_map/all_to_all | solution.py:578
  176.6 2.1 collective-permute-start.9
  178.7 40.9 %copy-start.2 = (bf16[4,256,768]{2,1,0:T(8,128)(2,1)S(1)}, bf16[4,256,768]{2,1,0:T(8,128)(2,1)}, u32[]{:S(2)}) copy-start(bf16[4,256,768]{2,1,0:T(8,128)(2,1)} %pad_maximum_fusion) | copy-start | bytes 4718596
  189.2 30.4 %copy-start = (f32[1024,384]{1,0:T(8,128)S(1)}, f32[1024,384]{1,0:T(8,128)}, u32[]{:S(2)}) copy-start(f32[1024,384]{1,0:T(8,128)} %copy.82.cos_ref) | copy-start | bytes 4718596
  189.2 30.4 %copy-start.1 = (f32[1024,384]{1,0:T(8,128)S(1)}, f32[1024,384]{1,0:T(8,128)}, u32[]{:S(2)}) copy-start(f32[1024,384]{1,0:T(8,128)} %copy.83.sin_ref) | copy-start | bytes 4718596
  189.2 30.4 %copy-start.3 = (bf16[2,2,192,576]{3,2,1,0:T(8,128)(2,1)S(1)}, bf16[2,2,192,576]{3,2,1,0:T(8,128)(2,1)}, u32[]{:S(2)}) copy-start(bf16[2,2,192,576]{3,2,1,0:T(8,128)(2,1)} %copy.81) | copy-start | bytes 2654212
  217.0 1.9 collective-permute-start.10
  217.0 2.7 collective-permute-start.11
  230.3 58.1 %all-to-all-start.5 = ((bf16[4,256,768]{2,1,0:T(8,128)(2,1)}), bf16[4,256,768]{2,1,0:T(8,128)(2,1)S(1)}, u32[]{:S(2)}, u32[]{:S(2)}) async-start(bf16[4,256,768]{2,1,0:T(8,128)(2,1)} %copy-done.8), calls=%async_computation.5 | async-start | bytes 3145728 | tf_op jit(solution)/shard_map/all_to_all | solution.py:578
  234.0 1.9 collective-permute-start.13
  236.1 8.1 %collective-permute-start.14 = (bf16[192,576]{1,0:T(8,128)(2,1)S(1)}, bf16[192,576]{1,0:T(8,128)(2,1)S(1)}, u32[]{:S(2)}, u32[]{:S(2)}) collective-permute-start(bf16[192,576]{1,0:T(8,128)(2,1)S(1)} %select_bitcast_fusion.11), channel_id=1, source_target_pairs={{0,8},{8,0},{1,9},{9,1},{2,10},{10,2},{3,11},{11,3},{4,12},{12,4},... | collective-permute-start | bytes 663560 | tf_op jit(solution)/shard_map/ppermute | solution.py:24
  237.8 65.2 %collective-permute-start.7 = (s32[2,512]{1,0:T(2,128)S(1)}, s32[2,512]{1,0:T(2,128)S(1)}, u32[]{:S(2)}, u32[]{:S(2)}) collective-permute-start(s32[2,512]{1,0:T(2,128)S(1)} %copy-done.31), channel_id=1, source_target_pairs={{0,16},{16,0},{1,17},{17,1},{2,18},{18,2},{3,19},{19,3},{4,20},{20... | collective-permute-start | bytes 12296 | tf_op jit(solution)/shard_map/ppermute | solution.py:24
  242.2 49.9 %copy-start.18 = (f32[256,768]{1,0:T(8,128)S(1)}, f32[256,768]{1,0:T(8,128)}, u32[]{:S(2)}) copy-start(f32[256,768]{1,0:T(8,128)} %get-tuple-element.40) | copy-start | bytes 2359300
  244.3 67.5 %collective-permute-start.15 = (bf16[192,576]{1,0:T(8,128)(2,1)S(1)}, bf16[192,576]{1,0:T(8,128)(2,1)S(1)}, u32[]{:S(2)}, u32[]{:S(2)}) collective-permute-start(bf16[192,576]{1,0:T(8,128)(2,1)S(1)} %fusion.39), channel_id=1, source_target_pairs={{0,16},{16,0},{1,17},{17,1},{2,18},{18,2},{3,19},{19,3},{4,20},{20... | collective-permute-start | bytes 663560 | tf_op jit(solution)/shard_map/ppermute | solution.py:24
  288.5 10.9 %all-to-all-start.3 = ((bf16[4,256,192]{1,2,0:T(8,128)(2,1)}), bf16[4,256,192]{1,2,0:T(8,128)(2,1)S(1)}, u32[]{:S(2)}, u32[]{:S(2)}) async-start(bf16[4,256,192]{1,2,0:T(8,128)(2,1)} %bitcast.34), calls=%async_computation.3 | async-start | bytes 786432 | tf_op jit(solution)/shard_map/all_to_all | solution.py:610
  299.3 10.9 %all-to-all-start.6 = ((bf16[4,256,192]{1,2,0:T(8,128)(2,1)}), bf16[4,256,192]{1,2,0:T(8,128)(2,1)S(1)}, u32[]{:S(2)}, u32[]{:S(2)}) async-start(bf16[4,256,192]{1,2,0:T(8,128)(2,1)} %bitcast.41), calls=%async_computation.6 | async-start | bytes 786432 | tf_op jit(solution)/shard_map/all_to_all | solution.py:610
  303.1 12.0 %collective-permute-start.6 = (bf16[1024,192]{0,1:T(8,128)(2,1)S(1)}, bf16[1024,192]{0,1:T(8,128)(2,1)S(1)}, u32[]{:S(2)}, u32[]{:S(2)}) collective-permute-start(bf16[1024,192]{0,1:T(8,128)(2,1)S(1)} %bitcast.157), channel_id=1, source_target_pairs={{0,16},{16,0},{1,17},{17,1},{2,18},{18,2},{3,19},{19,3},{4,20},{20... | collective-permute-start | bytes 1179656 | tf_op jit(solution)/shard_map/ppermute | solution.py:24
  310.3 12.6 %collective-permute-start.12 = (bf16[1024,192]{0,1:T(8,128)(2,1)S(1)}, bf16[1024,192]{0,1:T(8,128)(2,1)S(1)}, u32[]{:S(2)}, u32[]{:S(2)}) collective-permute-start(bf16[1024,192]{0,1:T(8,128)(2,1)S(1)} %bitcast.159), channel_id=1, source_target_pairs={{0,16},{16,0},{1,17},{17,1},{2,18},{18,2},{3,19},{19,3},{4,20},{20... | collective-permute-start | bytes 1179656 | tf_op jit(solution)/shard_map/ppermute | solution.py:24
  323.1 17.0 %collective-permute-start.16 = (bf16[192,1792]{1,0:T(8,128)(2,1)}, bf16[192,1792]{1,0:T(8,128)(2,1)S(1)}, u32[]{:S(2)}, u32[]{:S(2)}) collective-permute-start(bf16[192,1792]{1,0:T(8,128)(2,1)} %bitcast.165), channel_id=1, source_target_pairs={{0,16},{16,0},{1,17},{17,1},{2,18},{18,2},{3,19},{19,3},{4,20},{20... | collective-permute-start | bytes 2064392 | tf_op jit(solution)/shard_map/ppermute | solution.py:24
  327.3 12.8 %copy-start.19 = (bf16[1,192,1792]{2,1,0:T(8,128)(2,1)S(1)}, bf16[1,192,1792]{2,1,0:T(8,128)(2,1)}, u32[]{:S(2)}) copy-start(bf16[1,192,1792]{2,1,0:T(8,128)(2,1)} %reduce-scatter.2.cloned.1.call-done) | copy-start | bytes 2064388
  (11 other events, 11.3 us)
Sparse Core Ops, SparseCore 0:
  11.8 109.0 all-gather.2
  172.2 136.1 reduce-scatter.1

commit v3 on v2

v3 whole, which is shorter than its diff:
```python
import jax
import jax.numpy as jnp
from jax import lax
from jax.experimental import pallas as pl
from jax.experimental.pallas import tpu as pltpu
from jax.sharding import Mesh, PartitionSpec as P

DH = 64
EPSILON = 1e-05
MASKED = -1e30
LOG2E = 1.4426950408889634
SWAP = ((0, 1), (1, 0))
ROWS = ("ya", "yb")
SHARDS = ("ya", "yb", "col")
bf16 = jnp.bfloat16
f32 = jnp.float32


def cost(microseconds):
    return pl.CostEstimate(flops=int(microseconds * 1e9), bytes_accessed=int(microseconds * 3e6), transcendentals=0)


def contract(left, right, dims):
    return lax.dot_general(left, right, ((dims[:1], dims[1:]), ((), ())), preferred_element_type=f32)


def swap(values, axis):
    return lax.ppermute(values, axis, SWAP)


def gather_rows(values):
    first, second = lax.axis_index("ya") == 0, lax.axis_index("yb") == 0
    other = swap(values, "ya")
    pair = jnp.stack([jnp.where(first, values, other), jnp.where(first, other, values)])
    twin = swap(pair, "yb")
    both = jnp.stack([jnp.where(second, pair, twin), jnp.where(second, twin, pair)], 1)
    return both.reshape((4,) + values.shape)


def spread_dp(values):
    if lax.axis_size("dp") == 2:
        other = swap(values, "dp")
        first = lax.axis_index("dp") == 0
        return jnp.stack([jnp.where(first, values, other), jnp.where(first, other, values)])
    return lax.all_gather(values, "dp", axis=0)


def widen(table, lanes):
    return jnp.concatenate([table] * (lanes // table.shape[1]), 1)


def turn(values, cosine, sine):
    lanes = values.shape[1]
    even = lax.broadcasted_iota(jnp.int32, values.shape, 1) % 2 == 0
    swapped = jnp.where(even, pltpu.roll(values, lanes - 1, 1), pltpu.roll(values, 1, 1))
    return values * widen(cosine, lanes) + swapped * widen(sine, lanes)


def project_kernel(blocks, *refs):
    x_refs, (w_ref, cos_ref, sin_ref) = refs[:blocks], refs[blocks : blocks + 3]
    q_ref, kv_ref, turned_ref, xt_ref = refs[-4:]
    width = q_ref.shape[2]
    for index, x_ref in enumerate(x_refs):
        wide = jnp.dot(x_ref[...], w_ref[...], preferred_element_type=f32)
        xt_ref[index] = x_ref[...].T
        turned = turn(wide[:, : 2 * width], cos_ref[index], sin_ref[index])
        q_ref[index] = turned[:, :width].astype(bf16)
        for place, part in ((index, turned[:, width:]), (blocks + index, wide[:, 2 * width :])):
            kv_ref[place] = part.astype(bf16)
            turned_ref[place] = part.T.astype(bf16)


def project(blocks, weight, cosine, sine):
    own, width, count = blocks[0].shape[0], weight.shape[1] // 3, len(blocks)
    return pl.pallas_call(
        lambda *refs: project_kernel(count, *refs),
        out_shape=[
            jax.ShapeDtypeStruct((count, own, width), bf16),
            jax.ShapeDtypeStruct((2 * count, own, width), bf16),
            jax.ShapeDtypeStruct((2 * count, width, own), bf16),
            jax.ShapeDtypeStruct((count, blocks[0].shape[1], own), bf16),
        ],
        compiler_params=pltpu.CompilerParams(vmem_limit_bytes=16 << 20),
        cost_estimate=cost(0.001),
        name="project",
    )(*blocks, weight, cosine, sine)


def head_rows(values, head):
    rows = lax.broadcasted_iota(jnp.int32, values.shape, 0)
    return jnp.where((rows >= head * DH) & (rows < (head + 1) * DH), values, jnp.zeros_like(values))


def head_lanes(values, head):
    lanes = lax.broadcasted_iota(jnp.int32, values.shape, 1)
    return jnp.where((lanes >= head * DH) & (lanes < (head + 1) * DH), values, jnp.zeros_like(values))


def block_sides(info_ref, query_block, key_block, columns, share, own):
    boundary, half, column = info_ref[0], info_ref[1], info_ref[2]
    place = lambda block: jnp.where(column >= block, column - block, column - block + columns) * share
    low_q = place(query_block) + half * own
    low_k = place(key_block)
    first_q, second_q = low_q < boundary, low_q + own > boundary
    first_k, second_k = low_k < boundary, low_k + share > boundary
    meets = (first_q & first_k) | (second_q & second_k)
    mixed = (first_q & second_q) | (first_k & second_k)
    side_q = low_q + lax.broadcasted_iota(jnp.int32, (1, own), 1) >= boundary
    rows = lax.broadcasted_iota(jnp.int32, (share, 1), 0)
    shift = jnp.where(rows < own, half * own, (1 - half) * own - own)
    side_k = low_k + rows + shift >= boundary
    return meets, mixed, side_q.astype(f32), side_k.astype(f32)


def visit_blocks(info_ref, query_block, columns, share, own, visit):
    def step(key_block, carry):
        meets, mixed, side_q, side_k = block_sides(info_ref, query_block, key_block, columns, share, own)

        @pl.when(meets & mixed)
        def _():
            visit(key_block, side_q == side_k)

        @pl.when(meets & jnp.logical_not(mixed))
        def _():
            visit(key_block, None)

        return carry

    lax.fori_loop(0, columns, step, 0)


def forward_kernel(first, share, info_ref, q_ref, k0_ref, k1_ref, vt0_ref, vt1_ref, *refs):
    columns, own, width = k0_ref.shape
    heads = width // DH
    count = (len(refs) - 4) // 2
    outs, lses, (parts, top, total, sums) = refs[:count], refs[count : 2 * count], refs[2 * count :]
    scaling = DH ** (-0.5) * LOG2E

    def visit(key_block, same):
        keys = jnp.concatenate([k0_ref[key_block], k1_ref[key_block]], 0)
        values = jnp.concatenate([vt0_ref[key_block], vt1_ref[key_block]], 1)
        for head in range(heads):
            rows = pl.ds(head * DH, DH)
            line = pl.ds(head, 1)
            scores = contract(keys, parts[head], (1, 1)) * scaling
            if same is not None:
                scores = jnp.where(same, scores, MASKED)
            before = top[line, :]
            highest = jnp.maximum(before, jnp.max(scores, 0, keepdims=True))
            fade = jnp.exp2(before - highest)
            raised = jnp.exp2(scores - highest)
            if same is not None:
                raised = jnp.where(same, raised, 0.0)
            top[line, :] = highest
            total[line, :] = total[line, :] * fade + jnp.sum(raised, 0, keepdims=True)
            product = jnp.dot(values[head * DH : (head + 1) * DH], raised.astype(bf16), preferred_element_type=f32)
            sums[rows, :] = sums[rows, :] * fade + product

    for index in range(count):
        for head in range(heads):
            parts[head] = head_lanes(q_ref[first + index], head)
        top[...] = jnp.full_like(top, MASKED)
        total[...] = jnp.zeros_like(total)
        sums[...] = jnp.zeros_like(sums)
        visit_blocks(info_ref, first + index, columns, share, own, visit)
        for head in range(heads):
            rows = pl.ds(head * DH, DH)
            line = pl.ds(head, 1)
            outs[index][rows, :] = (sums[rows, :] / total[line, :]).astype(bf16)
            lses[index][line, :] = top[line, :] + jnp.log2(total[line, :])


def attend_forward(first, count, info, q, kv, kv_twin, turned, turned_twin, share):
    columns, own, width = q.shape
    heads = width // DH
    keys = pl.BlockSpec((columns, own, width), lambda i, s: (0, 0, 0))
    values = pl.BlockSpec((columns, width, own), lambda i, s: (1, 0, 0))
    flat = lambda rows: pl.BlockSpec((rows, own), lambda i, s: (0, 0))
    outs = pl.pallas_call(
        lambda *refs: forward_kernel(first, share, *refs),
        grid_spec=pltpu.PrefetchScalarGridSpec(
            num_scalar_prefetch=1,
            grid=(1,),
            in_specs=[keys, keys, keys, values, values],
            out_specs=[flat(width)] * count + [flat(heads)] * count,
            scratch_shapes=[
                pltpu.VMEM((heads, own, width), bf16),
                pltpu.VMEM((heads, own), f32),
                pltpu.VMEM((heads, own), f32),
                pltpu.VMEM((width, own), f32),
            ],
        ),
        out_shape=[jax.ShapeDtypeStruct((width, own), bf16)] * count + [jax.ShapeDtypeStruct((heads, own), f32)] * count,
        compiler_params=pltpu.CompilerParams(vmem_limit_bytes=16 << 20),
        cost_estimate=cost(0.001),
        name="attend_forward",
    )(info, q, kv, kv_twin, turned, turned_twin)
    return outs[:count], outs[count:]


def backward_kernel(columns, share, info_ref, q_ref, kv0_ref, kv1_ref, kt0_ref, kt1_ref, *refs):
    grads, outs, lses, refs = refs[:columns], refs[columns : 2 * columns], refs[2 * columns : 3 * columns], refs[3 * columns :]
    dq_ref, dk_ref, dv_ref, far_k_ref, far_v_ref, part_q, part_g, delta, lse, sum_q, sum_k, sum_v = refs
    _, own, width = q_ref.shape
    heads = width // DH
    scaling = DH ** (-0.5)
    sum_k[...] = jnp.zeros_like(sum_k)
    sum_v[...] = jnp.zeros_like(sum_v)
    for block in range(columns):
        lse[block] = lses[block][...]
        grad = grads[block][...]
        product = grad.astype(f32) * outs[block][...].astype(f32)
        for head in range(heads):
            part_q[block, pl.ds(head * own, own), :] = head_lanes(q_ref[block], head)
            part_g[block, :, pl.ds(head * own, own)] = head_rows(grad, head)
            delta[block, pl.ds(head, 1), :] = jnp.sum(product[head * DH : (head + 1) * DH], 0, keepdims=True)

    def query_step(block, carry):
        sum_q[...] = jnp.zeros_like(sum_q)

        def visit(key_block, same):
            keys = jnp.concatenate([kv0_ref[key_block], kv1_ref[key_block]], 0)
            turned = jnp.concatenate([kt0_ref[key_block], kt1_ref[key_block]], 1)
            values = jnp.concatenate([kv0_ref[columns + key_block], kv1_ref[columns + key_block]], 0)
            all_probs, all_grads = [], []
            for head in range(heads):
                span = pl.ds(head * own, own)
                scores = contract(keys, part_q[block, span, :], (1, 1)) * (scaling * LOG2E)
                probs = jnp.exp2(scores - lse[block, pl.ds(head, 1), :])
                if same is not None:
                    probs = jnp.where(same, probs, 0.0)
                slopes = jnp.dot(values, part_g[block, :, span], preferred_element_type=f32)
                grads = (probs * (slopes - delta[block, pl.ds(head, 1), :])).astype(bf16)
                all_probs.append(probs.astype(bf16))
                all_grads.append(grads)
            for head in range(heads):
                rows = pl.ds(head * DH, DH)
                part = turned[head * DH : (head + 1) * DH]
                sum_q[rows, :] += jnp.dot(part, all_grads[head], preferred_element_type=f32)
            sum_v[key_block] += contract(jnp.concatenate(all_probs, 1), part_g[block], (1, 1))
            sum_k[key_block] += jnp.dot(jnp.concatenate(all_grads, 1), part_q[block], preferred_element_type=f32)

        visit_blocks(info_ref, block, columns, share, own, visit)
        dq_ref[block] = sum_q[...].T * scaling
        return carry

    lax.fori_loop(0, columns, query_step, 0)
    for block in range(columns):
        dk_ref[block] = sum_k[block, :own]
        dv_ref[block] = sum_v[block, :own]
        far_k_ref[block] = sum_k[block, own:].astype(bf16)
        far_v_ref[block] = sum_v[block, own:].astype(bf16)


def attend_backward(info, q, kv, kv_twin, turned, turned_twin, grads, outs, lses, share):
    columns, own, width = q.shape
    heads = width // DH
    vmem = pl.BlockSpec(memory_space=pltpu.VMEM)
    shape = lambda kind: jax.ShapeDtypeStruct((columns, own, width), kind)
    operands = [q, kv, kv_twin, turned, turned_twin, *grads, *outs, *lses]
    return pl.pallas_call(
        lambda *refs: backward_kernel(columns, share, *refs),
        in_specs=[pl.BlockSpec(memory_space=pltpu.SMEM)] + [vmem] * len(operands),
        out_specs=[vmem] * 5,
        out_shape=[shape(f32), shape(f32), shape(f32), shape(bf16), shape(bf16)],
        scratch_shapes=[
            pltpu.VMEM((columns, heads * own, width), bf16),
            pltpu.VMEM((columns, width, heads * own), bf16),
            pltpu.VMEM((columns, heads, own), f32),
            pltpu.VMEM((columns, heads, own), f32),
            pltpu.VMEM((width, own), f32),
            pltpu.VMEM((columns, share, width), f32),
            pltpu.VMEM((columns, share, width), f32),
        ],
        compiler_params=pltpu.CompilerParams(vmem_limit_bytes=28 << 20),
        cost_estimate=cost(0.001),
        name="attend_backward",
    )(info, *operands)


def unproject_kernel(
    info_ref, dq_ref, dk_ref, far_k_ref, dv_ref, far_v_ref, w_ref, cos_ref, sin_ref, xt_ref, part_ref, grad_ref, total
):
    columns = dq_ref.shape[0]
    width = dq_ref.shape[2]
    lanes = 2 * width
    even = lax.broadcasted_iota(jnp.int32, (dq_ref.shape[1], lanes), 1) % 2 == 0
    for block in range(columns):
        dk = (dk_ref[block] + far_k_ref[block].astype(f32)) * DH ** (-0.5)
        dv = dv_ref[block] + far_v_ref[block].astype(f32)
        both = jnp.concatenate([dq_ref[block], dk], 1)
        swapped = jnp.where(even, pltpu.roll(both, lanes - 1, 1), pltpu.roll(both, 1, 1))
        both = both * widen(cos_ref[block], lanes) - swapped * widen(sin_ref[block], lanes)
        low = jnp.concatenate([both, dv], 1).astype(bf16)
        column = info_ref[2] - block
        column = jnp.where(column < 0, column + columns, column)
        part_ref[column] = contract(low, w_ref[...], (1, 1)).astype(bf16)
        piece = jnp.dot(xt_ref[block], low, preferred_element_type=f32)
        if block == 0:
            total[...] = piece
        else:
            total[...] += piece
    grad_ref[...] = total[...].astype(bf16)


def unproject(info, dq, dk, far_k, dv, far_v, tokens_t, weight, cosine, sine):
    columns, own, width = dq.shape
    feature = tokens_t.shape[1]
    return pl.pallas_call(
        unproject_kernel,
        in_specs=[pl.BlockSpec(memory_space=pltpu.SMEM)] + [pl.BlockSpec(memory_space=pltpu.VMEM)] * 9,
        out_shape=[jax.ShapeDtypeStruct((columns, own, feature), bf16), jax.ShapeDtypeStruct(weight.shape, bf16)],
        scratch_shapes=[pltpu.VMEM(weight.shape, f32)],
        compiler_params=pltpu.CompilerParams(vmem_limit_bytes=20 << 20),
        cost_estimate=cost(0.001),
        name="unproject",
    )(info, dq, dk, far_k, dv, far_v, weight, cosine, sine, tokens_t)


def mean_lanes(values):
    return jnp.sum(values, 1, keepdims=True) * (1.0 / values.shape[1])


def norm_forward(values, gain, shift):
    centred = values - mean_lanes(values)
    inverse = lax.rsqrt(mean_lanes(centred * centred) + EPSILON)
    normed = centred * inverse
    return normed * gain + shift, normed, inverse


def norm_backward(grad, normed, inverse, gain):
    scaled = grad * gain
    return inverse * (scaled - mean_lanes(scaled) - normed * mean_lanes(scaled * normed))


def unit(size):
    rows = lax.broadcasted_iota(jnp.int32, (size, size), 0)
    return (rows == lax.broadcasted_iota(jnp.int32, (size, size), 1)).astype(bf16)


def feed_kernel(info_ref, x_ref, cot_ref, w_ref, *refs):
    parts, _, columns, slab, _ = w_ref.shape
    att_refs, refs = refs[:columns], refs[columns:]
    result_ref, refs, grad_atts = refs[0], refs[1 + columns :], refs[1 : 1 + columns]
    grad_one_ref, hidden_ref, act_ref, gin_ref, gtwo_ref, gone_ref, sums_ref, w, slopes, outer, sems = refs
    rows, columns, quarter, _ = w.shape

    def turned(step):
        column = info_ref[2] + step
        return jnp.where(column >= columns, column - columns, column)

    hidden_cols = act_ref.shape[2]
    both = 2 * hidden_cols
    spans = ((0, hidden_cols), (hidden_cols, hidden_cols), (both, w.shape[3] - both))

    def copies(kind):
        lanes = pl.ds(*spans[kind])
        for part in range(parts):
            target = w.at[:, :, pl.ds(part * slab, slab), lanes]
            yield pltpu.make_async_copy(w_ref.at[part, :, :, :, lanes], target, sems.at[kind, part])

    def wait(kind):
        for each in copies(kind):
            each.wait()

    for kind in (2, 0, 1):
        for each in copies(kind):
            each.start()

    def block(kind, column):
        lanes = pl.ds(*spans[kind])
        return jnp.concatenate([w[row, column, :, lanes] for row in range(rows)], 0)

    wait(2)
    mix = pl.ds(both, quarter)
    attended = jnp.concatenate([ref[...] for ref in att_refs], 0)
    branch = []
    for row in range(rows):
        weight = jnp.concatenate([w[row, turned(step), :, mix] for step in range(columns)], 0)
        branch.append(contract(attended, weight, (0, 0)))
    branch = jnp.concatenate(branch, 1)
    eye = unit(quarter)
    small = [contract(w[row, 0, :, pl.ds(both + quarter, 12)], eye, (0, 0)) for row in range(rows)]
    small = jnp.concatenate(small, 1)
    vectors = small[0:4] + (small[4:8] + small[8:12])
    gain_one, shift_one, gain_two, shift_two = (vectors[i : i + 1] for i in range(4))

    hidden, normed_one, inverse_one = norm_forward(x_ref[...].astype(f32) + branch, gain_one, shift_one)
    low = hidden.astype(bf16)
    hidden_ref[...] = low.T
    outer[...] = jnp.zeros_like(outer)

    wait(0)

    def forward(column, carry):
        inner = jnp.dot(low, block(0, column), preferred_element_type=f32)
        cumulative = 0.5 * (1.0 + lax.erf(inner * (0.5**0.5)))
        slopes[column] = cumulative + inner * (jnp.exp(-0.5 * inner * inner) * 0.3989422804014327)
        act_ref[column] = (inner * cumulative).astype(bf16)
        return carry

    lax.fori_loop(0, columns, forward, 0)
    wait(1)

    def combine(column, carry):
        outer[...] += contract(act_ref[column], block(1, column), (1, 1))
        return carry

    lax.fori_loop(0, columns, combine, 0)
    result, normed_two, inverse_two = norm_forward(hidden + outer[...], gain_two, shift_two)
    result_ref[...] = result.astype(bf16)
    cot = jnp.concatenate([cot_ref[row] for row in range(rows)], 1).astype(f32)
    grad_two = norm_backward(cot, normed_two, inverse_two, gain_two)
    grad_two_low = grad_two.astype(bf16)
    gtwo_ref[...] = grad_two_low.T
    outer[...] = grad_two

    def backward(column, carry):
        grad = jnp.dot(grad_two_low, block(1, column), preferred_element_type=f32)
        gin_ref[column] = (grad * slopes[column]).astype(bf16)
        outer[...] += contract(gin_ref[column], block(0, column), (1, 1))
        return carry

    lax.fori_loop(0, columns, backward, 0)
    grad_hidden = outer[...]
    grad_one = norm_backward(grad_hidden, normed_one, inverse_one, gain_one)
    grad_one_ref[...] = grad_one
    gone_ref[...] = grad_one.astype(bf16)
    for step in range(columns):
        weight = jnp.concatenate([w[row, turned(step), :, mix] for row in range(rows)], 1)
        grad_atts[step][...] = contract(weight, gone_ref[...], (1, 1)).astype(bf16)
    sums_ref[0:1, :] = jnp.sum(grad_hidden * normed_one, 0, keepdims=True)
    sums_ref[1:2, :] = jnp.sum(grad_hidden, 0, keepdims=True)
    sums_ref[2:3, :] = jnp.sum(cot * normed_two, 0, keepdims=True)
    sums_ref[3:4, :] = jnp.sum(cot, 0, keepdims=True)


def feed(info, attended, tokens, cot, weights):
    own, feature = tokens.shape
    parts, rows, columns, slab, lanes = weights.shape
    quarter = parts * slab
    hidden_cols = feature
    vmem, smem = pl.BlockSpec(memory_space=pltpu.VMEM), pl.BlockSpec(memory_space=pltpu.SMEM)
    wide = jax.ShapeDtypeStruct((columns, own, hidden_cols), bf16)
    flat = lambda kind: jax.ShapeDtypeStruct((own, feature), kind)
    tall = jax.ShapeDtypeStruct((feature, own), bf16)
    return pl.pallas_call(
        feed_kernel,
        in_specs=[smem, vmem, vmem, pl.BlockSpec(memory_space=pl.ANY)] + [vmem] * columns,
        out_specs=[vmem] * (8 + columns),
        out_shape=[flat(bf16)]
        + [jax.ShapeDtypeStruct((quarter, own), bf16)] * columns
        + [flat(f32), tall, wide, wide, tall, flat(bf16), jax.ShapeDtypeStruct((4, feature), f32)],
        scratch_shapes=[
            pltpu.VMEM((rows, columns, quarter, lanes), bf16),
            pltpu.VMEM((columns, own, hidden_cols), f32),
            pltpu.VMEM((own, feature), f32),
            pltpu.SemaphoreType.DMA((3, parts)),
        ],
        compiler_params=pltpu.CompilerParams(vmem_limit_bytes=34 << 20),
        cost_estimate=cost(0.001),
        name="feed",
    )(info, tokens, cot, weights, *attended)


def weigh_kernel(info_ref, hidden_ref, act_ref, gin_ref, gtwo_ref, gone_ref, sums_ref, *refs):
    att_refs, (kept_ref, sent_ref, across_ref) = refs[:-3], refs[-3:]
    _, slabs, _, slab, lanes = kept_ref.shape
    quarter = slabs * slab
    hidden_cols = act_ref.shape[2]
    columns = len(att_refs)
    step = pl.program_id(0) - info_ref[2]
    step = jnp.where(step < 0, step + columns, step)
    attended = att_refs[0][...]
    for index in range(1, columns):
        attended = jnp.where(step == index, att_refs[index][...], attended)
    inner = jnp.dot(hidden_ref[...], gin_ref[0], preferred_element_type=f32).astype(bf16)
    outer = jnp.dot(gtwo_ref[...], act_ref[0], preferred_element_type=f32).astype(bf16)
    mixed = jnp.dot(attended, gone_ref[...], preferred_element_type=f32).astype(bf16)
    eye = unit(quarter)
    away = lambda index, mine: jnp.where(index == mine, 0, 1)
    for row in range(4):
        mine = slice(row * quarter, (row + 1) * quarter)
        vector = contract(eye, sums_ref[:, mine].astype(bf16), (1, 1)).astype(bf16)
        rest = jnp.zeros((quarter, lanes - 2 * hidden_cols - quarter - 4), bf16)
        tail = jnp.concatenate([mixed[:, mine], vector, rest], 1)
        far = away(row // 2, info_ref[3])

        def write(ref, where, rows):
            ref[where + (0, slice(None), slice(0, hidden_cols))] = inner[mine][rows]
            ref[where + (0, slice(None), slice(hidden_cols, 2 * hidden_cols))] = outer[mine][rows]
            ref[where + (0, slice(None), slice(2 * hidden_cols, lanes))] = tail[rows]

        for part in range(slabs):
            place = away(part, info_ref[4]) if slabs > 1 else 0
            rows = slice(part * slab, (part + 1) * slab)
            kept = info_ref[1] == row % 2
            beyond = (far == 1) & (place == slabs - 1)

            @pl.when(kept)
            def _():
                write(kept_ref, (far, place), rows)

            @pl.when(jnp.logical_not(kept) & beyond)
            def _():
                write(across_ref, (), rows)

            @pl.when(jnp.logical_not(kept | beyond))
            def _():
                write(sent_ref, (far * slabs + place,), rows)


def weigh(info, attended, hidden, act, gin, gtwo, gone, sums, lanes, slabs):
    feature = hidden.shape[0]
    columns = act.shape[0]
    quarter = attended[0].shape[0]
    whole = lambda a: pl.BlockSpec(a.shape, lambda i, s: (0, 0))
    piece = pl.BlockSpec((1,) + act.shape[1:], lambda i, s: (i, 0, 0))
    tail = (columns, quarter // slabs, lanes)
    block = (1,) + tail[1:]
    return pl.pallas_call(
        weigh_kernel,
        grid_spec=pltpu.PrefetchScalarGridSpec(
            num_scalar_prefetch=1,
            grid=(columns,),
            in_specs=[whole(hidden), piece, piece, whole(gtwo), whole(gone), whole(sums)] + [whole(a) for a in attended],
            out_specs=[
                pl.BlockSpec((2, slabs) + block, lambda i, s: (0, 0, i, 0, 0)),
                pl.BlockSpec((2 * slabs - 1,) + block, lambda i, s: (0, i, 0, 0)),
                pl.BlockSpec(block, lambda i, s: (i, 0, 0)),
            ],
        ),
        out_shape=[jax.ShapeDtypeStruct(dims + tail, bf16) for dims in ((2, slabs), (2 * slabs - 1,), ())],
        compiler_params=pltpu.CompilerParams(vmem_limit_bytes=24 << 20),
        cost_estimate=cost(0.001),
        name="weigh",
    )(info, hidden, act, gin, gtwo, gone, sums, *attended)


def parcel_kernel(info_ref, inner_ref, outer_ref, output_ref, *refs):
    small_refs, out_ref = refs[:-1], refs[-1]
    columns = inner_ref.shape[1]
    quarter = output_ref.shape[1]
    slab = out_ref.shape[0]
    offset = info_ref[4] * slab if slab < quarter else 0
    rows = pl.ds(pl.multiple_of(offset, slab), slab)
    values = jnp.concatenate([ref[...] for ref in small_refs], 0)
    high = values.astype(bf16)
    rest = values - high.astype(f32)
    middle = rest.astype(bf16)
    last = (rest - middle.astype(f32)).astype(bf16)
    pick = lax.broadcasted_iota(jnp.int32, (slab, quarter), 0) + offset
    pick = (pick == lax.broadcasted_iota(jnp.int32, (slab, quarter), 1)).astype(bf16)
    small = jnp.concatenate([contract(pick, part, (1, 1)) for part in (high, middle, last)], 1).astype(bf16)
    fill = jnp.zeros((slab, out_ref.shape[1] - 2 * columns - quarter - 12), bf16)
    out_ref[:, 0:columns] = inner_ref[rows, :]
    out_ref[:, columns : 2 * columns] = outer_ref[rows, :]
    out_ref[:, 2 * columns :] = jnp.concatenate([output_ref[rows, :], small, fill], 1)


def parcel(info, inner, outer, output, vectors, lanes, slabs):
    vmem, smem = pl.BlockSpec(memory_space=pltpu.VMEM), pl.BlockSpec(memory_space=pltpu.SMEM)
    return pl.pallas_call(
        parcel_kernel,
        in_specs=[smem] + [vmem] * 7,
        out_shape=jax.ShapeDtypeStruct((inner.shape[0] // slabs, lanes), bf16),
        cost_estimate=cost(0.001),
        name="parcel",
    )(info, inner, outer, output, *(v.reshape(1, -1) for v in vectors))


def keep(values, index, axis=0):
    first, second = lax.index_in_dim(values, 0, axis, False), lax.index_in_dim(values, 1, axis, False)
    chosen = index == 0
    return jnp.where(chosen, first, second), jnp.where(chosen, second, first)


def tie(*values):
    return lax.optimization_barrier(values)


def shift(values, step):
    columns = lax.axis_size("col")
    if step % columns == 0:
        return values
    return lax.ppermute(values, "col", [(i, (i + step) % columns) for i in range(columns)])


def add_kernel(low_only, *refs):
    total = sum(ref[...].reshape(refs[-1].shape).astype(f32) for ref in refs[:-2])
    if low_only is None:
        refs[-1][...] = (total + refs[-2][...].astype(f32)).astype(bf16)
        return
    middle = pl.num_programs(0) // 2
    inside = (pl.program_id(0) < middle) == low_only

    @pl.when(inside)
    def _():
        refs[-1][...] = (total + refs[-2][...].astype(f32)).astype(bf16)

    @pl.when(jnp.logical_not(inside))
    def _():
        refs[-1][...] = total.astype(bf16)


def add_blocks(kept, place, *others, low_only=None):
    columns = kept.shape[2]
    block = (1,) + kept.shape[3:]
    spec = lambda lead: pl.BlockSpec((1,) * len(lead) + block, lambda i: lead + (i, 0, 0))
    arrays, specs = [kept], [spec(place)]
    for array, lead in others:
        arrays.append(array)
        specs.append(spec(lead))
    if low_only is not None:
        middle = columns // 2
        held = (lambda i: jnp.minimum(i, middle - 1)) if low_only else (lambda i: jnp.maximum(i - middle, 0))
        specs[-1] = pl.BlockSpec(block, lambda i: (held(i), 0, 0))
    return pl.pallas_call(
        lambda *refs: add_kernel(low_only, *refs),
        grid=(columns,),
        in_specs=specs,
        out_specs=spec(()),
        out_shape=jax.ShapeDtypeStruct(kept.shape[2:], bf16),
        compiler_params=pltpu.CompilerParams(vmem_limit_bytes=16 << 20),
        cost_estimate=cost(0.001),
        name="add_blocks",
    )(*arrays)


def sum_shards(kept, sent, across, mark):
    middle = kept.shape[2] // 2
    across, twin = swap(across, "yb"), swap(sent, "yb")
    half = lambda span: (kept[1, 1, span].astype(f32) + across[span].astype(f32)).astype(bf16)
    low, high = half(slice(0, middle)), half(slice(middle, None))
    mark, low, high = tie(mark, low, high)
    by_dp, by_ya = swap(low, "dp"), swap(high, "ya")

    def sides(mark):
        low, high, mark = tie(by_dp, by_ya, mark)
        far_ya = add_blocks(kept, (1, 0), (twin, (2,)), (low, ()), low_only=True)
        far_dp = add_blocks(kept, (0, 1), (twin, (1,)), (high, ()), low_only=False)
        mark, far_ya, far_dp = tie(mark, far_ya, far_dp)
        far_ya, far_dp = swap(far_ya, "ya"), swap(far_dp, "dp")

        def finish(mark):
            *parts, mark = tie(far_ya, far_dp, mark)
            own = add_blocks(kept, (0, 0), (twin, (0,)), *((part, ()) for part in parts))
            mine = lax.psum_scatter(own, "col", scatter_dimension=0, tiled=False)
            other = swap(mine, "dp")
            first = lax.axis_index("dp") == 0
            return jnp.concatenate([jnp.where(first, mine, other), jnp.where(first, other, mine)], 0).astype(f32), mark

        return mark, finish

    return mark, sides


def body(
    inputs, cotangent, lengths, source, query_weight, key_weight, value_weight, output_weight, inner_weight, outer_weight,
    first_gain, first_shift, second_gain, second_shift,
):
    micro, quarter, share = inputs.shape
    dp_count, columns = lax.axis_size("dp"), lax.axis_size("col")
    pack, own = share * columns, share // 2
    feature, count = 4 * quarter, share * micro
    width, hidden_cols = query_weight.shape[1], inner_weight.shape[1]
    lanes = -(-(2 * hidden_cols + quarter + 12) // 128) * 128
    me, m, half, z = (lax.axis_index(a) for a in ("dp", "ya", "yb", "col"))

    boundary = jnp.where(m == 0, lengths[0, 0], lengths[0, 1])
    info = jnp.stack([boundary, half, z, m, me]).astype(jnp.int32)
    slabs = 2 if dp_count == 2 else 1

    vectors = (first_gain, first_shift, second_gain, second_shift)
    anchors = spread_dp(source)
    packed = parcel(info, inner_weight, outer_weight, output_weight, vectors, lanes, slabs)
    axes = ("dp",) + SHARDS if slabs == 2 else SHARDS
    everywhere = lax.all_gather(packed, axes, axis=0).reshape(slabs, 4, columns, quarter // slabs, lanes)
    anchor = source.reshape(count)
    place = anchor // (dp_count * pack) * share + anchor % share
    holder = anchor % (dp_count * pack) // pack
    wide_in, wide_cot = spread_dp(inputs), spread_dp(cotangent)
    if dp_count == 2:
        pick = (holder * count + place)[:, None] == jnp.arange(dp_count * count, dtype=jnp.int32)[None, :]
        pick = pick.astype(bf16).reshape(count, dp_count, micro, share)
        deal = lambda wide: jnp.einsum("tsmj,smfj->tf", pick, wide, preferred_element_type=f32).astype(bf16)
    else:
        deal = lambda wide: wide.transpose(0, 1, 3, 2).reshape(-1, quarter)[holder * count + place]

    def to_tokens(dealt):
        return lax.all_to_all(dealt.reshape(4, own, quarter), ROWS, split_axis=0, concat_axis=0, tiled=True)

    dealt = deal(wide_in)
    query_weight, dealt = tie(query_weight, dealt)
    tokens = to_tokens(dealt).transpose(1, 0, 2).reshape(own, feature)
    wide_cot, tokens = tie(wide_cot, tokens)
    cot = to_tokens(deal(wide_cot))
    qkv_weight = jnp.concatenate([query_weight, key_weight, value_weight], 1)
    qkv_weight = gather_rows(qkv_weight).reshape(feature, -1)

    steps = jnp.arange(columns, dtype=jnp.int32)
    spots = ((z - steps) % columns * share + half * own)[:, None] + jnp.arange(own, dtype=jnp.int32)[None, :]
    frequency = 10000.0 ** (-2.0 * jnp.arange(DH // 2, dtype=f32) / DH)
    angles = (spots - jnp.where(spots >= boundary, boundary, 0)).astype(f32)[..., None] * jnp.tile(jnp.repeat(frequency, 2), 2)
    signs = jnp.where(jnp.arange(2 * DH) % 2 == 0, -1.0, 1.0)
    cosine, sine = jnp.cos(angles), jnp.sin(angles) * signs

    blocks = [shift(tokens, step) for step in range(columns)]
    blocks[-1], cot = tie(blocks[-1], cot)
    q, kv, turned, tokens_t = project(blocks, qkv_weight, cosine, sine)
    kv_twin, turned_twin = swap(kv, "yb"), swap(turned, "yb")
    mixed, lses = attend_forward(1, columns - 1, info, q, kv, kv_twin, turned, turned_twin, share)
    q, mixed, cot = tie(q, mixed, cot)
    last = attend_forward(0, 1, info, q, kv, kv_twin, turned, turned_twin, share)
    mixed, lses = last[0] + mixed, last[1] + lses
    attended = [shift(mixed[step], -step) for step in range(columns)]

    result, *grad_att, grad_one, hidden, act, gin, gtwo, gone, sums = feed(info, attended, tokens, cot, everywhere)
    grad_att = [shift(grad_att[step], step) for step in range(columns)]
    def to_loader(*rows):
        cut = jnp.concatenate([a.astype(bf16).reshape(own, 4, quarter).transpose(1, 0, 2) for a in rows], 2)
        cut = jnp.broadcast_to(cut[None], (dp_count,) + cut.shape).reshape(dp_count * 4, own, -1)
        moved = lax.all_to_all(cut, ("dp",) + ROWS, split_axis=0, concat_axis=0, tiled=True)
        return moved.reshape(-1, len(rows) * quarter)

    spot = jnp.arange(count, dtype=jnp.int32)
    wanted = spot // share * (dp_count * pack) + me * pack + z * share + spot % share
    if dp_count == 2:
        put = (anchors.reshape(-1)[:, None] == wanted[None, :]).astype(bf16)
        settle = lambda wide: contract(wide, put, (0, 0)).astype(bf16)
    else:
        order = jnp.argsort(anchors.reshape(-1))
        spots_in = jnp.searchsorted(anchors.reshape(-1)[order], wanted)
        settle = lambda wide: wide[order[spots_in]].T
    kept, sent, across = weigh(info, attended, hidden, act, gin, gtwo, gone, sums, lanes, slabs)
    if slabs == 2:
        grad_att, sides = sum_shards(kept, sent, across, grad_att)
    else:
        flip = lambda a, index, axis: jnp.where(index == 0, a, jnp.flip(a, axis))
        sent = jnp.stack([sent[0], across])[:, None]
        cut = flip(flip(jnp.stack([kept, sent], 1), m, 0), half, 1).reshape(4 * columns, quarter, lanes)
        summed = lax.psum_scatter(cut, SHARDS, scatter_dimension=0, tiled=False)
        summed = lax.psum(summed, "dp").astype(f32)

    dq, dk, dv, far_k, far_v = attend_backward(info, q, kv, kv_twin, turned, turned_twin, grad_att, mixed, lses, share)
    far_k, far_v = swap(far_k, "yb"), swap(far_v, "yb")
    if slabs == 2:
        dq, finish = sides(dq)
    partial, grad_qkv = unproject(info, dq, dk, far_k, dv, far_v, tokens_t, qkv_weight, cosine, sine)
    partial = lax.all_to_all(partial, "col", split_axis=0, concat_axis=0, tiled=True)
    grad_tokens = grad_one + jnp.sum(partial.astype(f32), 0)

    grad_qkv = grad_qkv.reshape(2, 2, quarter, 3 * width)
    for axis, index, place_axis in (("yb", half, 1), ("ya", m, 0)):
        kept, sent = keep(grad_qkv, index, place_axis)
        grad_qkv = (kept.astype(f32) + swap(sent, axis).astype(f32)).astype(bf16)
        if slabs == 2 and axis == "yb":
            summed, grad_qkv = finish(grad_qkv)

    def over_dp(values):
        if dp_count == 2:
            return values.astype(f32) + swap(values, "dp").astype(f32)
        return lax.psum(values, "dp").astype(f32)

    grad_qkv = over_dp(grad_qkv)
    sum_inner, sum_outer = summed[:, :hidden_cols], summed[:, hidden_cols : 2 * hidden_cols]
    sum_output = summed[:, 2 * hidden_cols : 2 * hidden_cols + quarter]
    sum_vectors = summed[:, 2 * hidden_cols + quarter : 2 * hidden_cols + quarter + 4].T

    shape = lambda a: a.reshape(quarter, micro, share).transpose(1, 0, 2)
    settled = settle(to_loader(result, grad_tokens))
    final_out, final_grad = shape(settled[:quarter]), shape(settled[quarter:])
    return (
        final_out, final_grad, grad_qkv[:, :width], grad_qkv[:, width : 2 * width], grad_qkv[:, 2 * width :],
        sum_output, sum_inner, sum_outer, sum_vectors[0], sum_vectors[1], sum_vectors[2], sum_vectors[3],
    )


def solution(mesh):
    dp, row, col = (mesh.shape[a] for a in ("dp", "row", "col"))
    fine = Mesh(mesh.devices.reshape(dp, 2, row // 2, col), ("dp", "ya", "yb", "col"))
    tokens, matrix = P(None, ROWS, ("dp", "col")), P(ROWS, "col")
    weights = (matrix, matrix, matrix, P("col", ROWS), matrix, matrix, P(ROWS), P(ROWS), P(ROWS), P(ROWS))
    return jax.shard_map(
        body,
        mesh=fine,
        in_specs=(tokens, tokens, P("dp", None), P(None, ("dp", "col"))) + weights,
        out_specs=(tokens, tokens) + weights,
        check_vma=False,
    )
```

time: 352 us -> 324 us (0.920); the launches traced: 350 us -> 318 us
  blocking collectives: 51 us -> 0 us
  waiting for transfers between devices: 106 us -> 121 us
  starting transfers between devices: 44.9 us -> 56.6 us
  Pallas kernels: 78 us -> 69.7 us
  local copies, waits for them, and re-layouts: 32.8 us -> 36.8 us
    all_to_all x5 -> x2, waiting for transfers between devices: 71.3 us -> 0.01 us  [the longest x1 0.01 us: to_loader(): lax.all_to_all(cut, ('dp',) + ROWS, split_axis=0, concat_axis=0, tiled=True)]
    all_gather x2 -> x0, blocking collectives: 51 us -> none  [body(): lax.all_gather(tokens[i * own // 2:(i + 1) * own // 2], 'col', axis=0)]
    ppermute x17 -> x19, waiting for transfers between devices: 29.7 us -> 77.4 us  [swap(): return lax.ppermute(values, axis, SWAP)]
    ppermute x0 -> x9, waiting for transfers between devices: none -> 33.3 us  [shift(): lax.ppermute(values, 'col', [(i, (i + step) % columns) for i in range(col...]
    ppermute x0 -> x9, starting transfers between devices: none -> 14.3 us  [shift(): lax.ppermute(values, 'col', [(i, (i + step) % columns) for i in range(col...]
    all_to_all x5 -> x2, starting transfers between devices: 19.1 us -> 9.82 us  [the longest x1 5.62 us: body(): lax.all_to_all(partial, 'col', split_axis=0, concat_axis=0, tiled=True)]
    unnamed x70 -> x74, local copies, waits for them, and re-layouts: 14.2 us -> 22.9 us
    pallas_call x7 -> x11, Pallas kernels: 78 us -> 69.7 us  [the longest x2 16.1 us: attend_forward(): pl.pallas_call(lambda *refs: forward_kernel(first, share, *refs), grid_sp...]
  transfers between devices with their start and end apart: 26 -> 34, of which waited for: 15 -> 17; matrix products, arithmetic and copies ran while one was open for 10% -> 9% of each run, Pallas kernels for 15% -> 12%
where the time goes in v3:
time: 324 us; the launch traced here: 318 us
  waiting for transfers between devices  121 us (37%)
  Pallas kernels  69.7 us (22%)
  starting transfers between devices  56.6 us (17%)
  local copies, waits for them, and re-layouts  36.8 us (11%)
  between operations  16.2 us (5%)
  other arithmetic  10.9 us (3%)
  matrix products  6.65 us (2%)
    ppermute x19, waiting for transfers between devices, swap(): return lax.ppermute(values, axis, SWAP)  77.4 us
    ppermute x9, waiting for transfers between devices, shift(): lax.ppermute(values, 'col', [(i, (i + step) % columns) for i in range(col...  33.3 us
    ppermute x19, starting transfers between devices, swap(): return lax.ppermute(values, axis, SWAP)  24.2 us
    unnamed x74, local copies, waits for them, and re-layouts  22.9 us
    pallas_call x2, Pallas kernels, attend_forward(): pl.pallas_call(lambda *refs: forward_kernel(first, share, *refs), grid_sp...  16.1 us
    pallas_call x1, Pallas kernels, attend_backward(): pl.pallas_call(lambda *refs: backward_kernel(columns, share, *refs), in_s...  15.5 us
    ppermute x9, starting transfers between devices, shift(): lax.ppermute(values, 'col', [(i, (i + step) % columns) for i in range(col...  14.3 us
    pallas_call x1, Pallas kernels, feed(): pl.pallas_call(feed_kernel, in_specs=[smem, vmem, vmem, pl.BlockSpec(memo...  12.8 us
  transfers between devices with their start and end apart: 34, of which 17 were waited for; matrix products, arithmetic and copies ran while one was open for 9% of the time, Pallas kernels for 12%

profile of v3, /device:TPU:0, one launch (start us, length us, event | category | flops | bytes accessed | tf_op | source)
XLA Modules:
  0.0 317.5 jit_solution(16553494136097962290)
XLA Ops:
  10.5 2.2 parcel.1
  12.7 3.0 collective-permute-start.1
  16.9 9.3 %collective-permute-done.1 = bf16[2,192,512]{2,1,0:T(8,128)(2,1)S(1)} collective-permute-done((bf16[2,192,512]{2,1,0:T(8,128)(2,1)}, bf16[2,192,512]{2,1,0:T(8,128)(2,1)S(1)}, u32[]{:S(2)}, u32[]{:S(2)}) %collective-permute-start.1) | collective-permute-done | bytes 393248 | tf_op jit(solution)/shard_map/ppermute | solution.py:28
  26.3 1.8 fusion.26
  28.2 1.8 collective-permute-start.5
  30.0 1.9 fusion.34
  32.8 3.6 %all-to-all-start = ((bf16[4,256,192]{1,2,0:T(8,128)(2,1)}), bf16[4,256,192]{1,2,0:T(8,128)(2,1)S(1)}, u32[]{:S(2)}, u32[]{:S(2)}) async-start(bf16[4,256,192]{1,2,0:T(8,128)(2,1)} %bitcast.115), calls=%async_computation | async-start | bytes 786432 | tf_op jit(solution)/shard_map/all_to_all | solution.py:691
  39.9 3.9 %all-to-all-done = bf16[4,256,192]{1,2,0:T(8,128)(2,1)S(1)} async-done(((bf16[4,256,192]{1,2,0:T(8,128)(2,1)}), bf16[4,256,192]{1,2,0:T(8,128)(2,1)S(1)}, u32[]{:S(2)}, u32[]{:S(2)}) %all-to-all-start) | async-done | bytes 393248 | tf_op jit(solution)/shard_map/all_to_all | solution.py:691
  44.0 3.6 %collective-permute-start.4 = (bf16[256,768]{1,0:T(8,128)(2,1)S(1)}, bf16[256,768]{1,0:T(8,128)(2,1)S(1)}, u32[]{:S(2)}, u32[]{:S(2)}) collective-permute-start(bf16[256,768]{1,0:T(8,128)(2,1)S(1)} %copy.65.refs_0_.x_ref), channel_id=1, source_target_pairs={{0,3},{1,0},{2,1},{3,2},{4,7},{5,4},{6,5},{7,6},{8,11},{9,8},{10,9... | collective-permute-start | bytes 1179656 | tf_op jit(solution)/shard_map/ppermute | solution.py:586
  48.7 2.9 fusion.23
  52.3 4.6 %all-to-all-start.1 = ((bf16[4,256,192]{1,2,0:T(8,128)(2,1)}), bf16[4,256,192]{1,2,0:T(8,128)(2,1)}, u32[]{:S(2)}, u32[]{:S(2)}) async-start(bf16[4,256,192]{1,2,0:T(8,128)(2,1)} %bitcast.114), calls=%async_computation.1 | async-start | bytes 786432 | tf_op jit(solution)/shard_map/all_to_all | solution.py:691
  58.4 6.1 %all-to-all-done.1 = bf16[4,256,192]{1,2,0:T(8,128)(2,1)} async-done(((bf16[4,256,192]{1,2,0:T(8,128)(2,1)}), bf16[4,256,192]{1,2,0:T(8,128)(2,1)}, u32[]{:S(2)}, u32[]{:S(2)}) %all-to-all-start.1) | async-done | bytes 393248 | tf_op jit(solution)/shard_map/all_to_all | solution.py:691
  64.5 9.8 %collective-permute-done.4.refs_3_ = bf16[256,768]{1,0:T(8,128)(2,1)S(1)} collective-permute-done((bf16[256,768]{1,0:T(8,128)(2,1)S(1)}, bf16[256,768]{1,0:T(8,128)(2,1)S(1)}, u32[]{:S(2)}, u32[]{:S(2)}) %collective-permute-start.4) | collective-permute-done | bytes 393248 | tf_op jit(solution)/shard_map/ppermute | solution.py:586
  75.1 5.3 %collective-permute-done.2.refs_1_ = bf16[256,768]{1,0:T(8,128)(2,1)S(1)} collective-permute-done((bf16[256,768]{1,0:T(8,128)(2,1)S(1)}, bf16[256,768]{1,0:T(8,128)(2,1)S(1)}, u32[]{:S(2)}, u32[]{:S(2)}) %collective-permute-start.2) | collective-permute-done | bytes 393248 | tf_op jit(solution)/shard_map/ppermute | solution.py:586
  81.1 15.3 %collective-permute-done.3.refs_2_ = bf16[256,768]{1,0:T(8,128)(2,1)} collective-permute-done((bf16[256,768]{1,0:T(8,128)(2,1)S(1)}, bf16[256,768]{1,0:T(8,128)(2,1)}, u32[]{:S(2)}, u32[]{:S(2)}) %collective-permute-start.3) | collective-permute-done | bytes 393248 | tf_op jit(solution)/shard_map/ppermute | solution.py:586
  98.5 4.4 %project.1 = (bf16[4,256,192]{2,1,0:T(8,128)(2,1)S(1)}, bf16[8,256,192]{2,1,0:T(8,128)(2,1)S(1)}, bf16[8,192,256]{2,1,0:T(8,128)(2,1)}, bf16[4,768,256]{2,1,0:T(8,128)(2,1)S(1)}) custom-call(bf16[256,768]{1,0:T(8,128)(2,1)S(1)} %copy.65.refs_0_.x_ref, bf16[256,768]{1,0:T(8,128)(2,1)S(1)} %copy-done.24, bf16[256,768]{1,0:T(8,128)(2,1)} %collective-permute-done.3.refs_2_, ...), custom_call_target="tpu_custom_call" | custom-call | flops 1000000 | bytes 3000 | tf_op jit(solution)/shard_map/project/pallas_call | solution.py:75
  105.9 2.2 collective-permute-done.7
  110.6 13.1 %attend_forward.2 = (bf16[192,256]{1,0:T(8,128)(2,1)}, bf16[192,256]{1,0:T(8,128)(2,1)}, bf16[192,256]{1,0:T(8,128)(2,1)}, f32[3,256]{1,0:T(4,128)S(1)}, f32[3,256]{1,0:T(4,128)S(1)}, /*index=5*/f32[3,256]{1,0:T(4,128)S(1)}) custom-call(s32[5]{0:T(128)S(1)} %copy-done.27, bf16[4,256,192]{2,1,0:T(8,128)(2,1)S(1)} %copy-done.6, ...), custom_call_target="tpu_custom_call" | custom-call | flops 1000000 | bytes 3000 | tf_op jit(solution)/shard_map/attend_forward/pallas_call | solution.py:179
  123.7 3.0 collective-permute-start.11
  127.7 2.0 copy.66.cot_ref
  130.7 3.0 attend_forward.3
  135.2 4.1 %copy-done.4 = bf16[3072,1792]{1,0:T(8,128)(2,1)S(1)} copy-done((bf16[3072,1792]{1,0:T(8,128)(2,1)S(1)}, bf16[3072,1792]{1,0:T(8,128)(2,1)}, u32[]{:S(2)}) %copy-start.4) | copy-done | bytes 11010072
  141.3 12.8 %feed.1 = (bf16[256,768]{1,0:T(8,128)(2,1)S(1)}, bf16[192,256]{1,0:T(8,128)(2,1)S(1)}, bf16[192,256]{1,0:T(8,128)(2,1)S(1)}, bf16[192,256]{1,0:T(8,128)(2,1)S(1)...) custom-call(s32[5]{0:T(128)S(1)} %copy-done.27, ...), custom_call_target="tpu_custom_call" | custom-call | flops 1000000 | bytes 3000 | tf_op jit(solution)/shard_map/feed/pallas_call | solution.py:447
  154.1 10.8 %weigh.1 = (bf16[2,2,4,96,1792]{4,3,2,1,0:T(8,128)(2,1)S(1)}, bf16[3,4,96,1792]{3,2,1,0:T(8,128)(2,1)S(1)}, bf16[4,96,1792]{2,1,0:T(8,128)(2,1)S(1)}) custom-call(s32[5]{0:T(128)S(1)} %copy-done.27, bf16[768,256]{1,0:T(8,128)(2,1)S(1)} %get-tuple-element.96.hidden_ref, bf16[4,256,768]{2,1,0:T(8,128)(2,1)S(1)} %get-tuple-element.97.act_ref, ...), custom_call_target="tpu_custom_call" | custom-call | flops 1000000 | bytes 3000 | tf_op jit(solution)/shard_map/weigh/pallas_call | solution.py:521
  165.5 2.6 collective-permute-start.12
  168.1 3.0 collective-permute-start.14
  171.2 2.8 collective-permute-done.15
  174.3 2.0 collective-permute-done.13.refs_8_
  176.4 6.4 %collective-permute-start.16 = (bf16[2,96,1792]{2,1,0:T(8,128)(2,1)S(1)}, bf16[2,96,1792]{2,1,0:T(8,128)(2,1)S(1)}, u32[]{:S(2)}, u32[]{:S(2)}) collective-permute-start(bf16[2,96,1792]{2,1,0:T(8,128)(2,1)S(1)} %get-tuple-element.104), channel_id=1, source_target_pairs={{0,16},{16,0},{1,17},{17,1},{2,18},{18,2},{3,19},{19,3},{4,20},{20... | collective-permute-start | bytes 2064392 | tf_op jit(solution)/shard_map/ppermute | solution.py:28
  183.5 15.5 %attend_backward.1 = (f32[4,256,192]{2,1,0:T(8,128)S(1)}, f32[4,256,192]{2,1,0:T(8,128)S(1)}, f32[4,256,192]{2,1,0:T(8,128)S(1)}, bf16[4,256,192]{2,1,0:T(8,128)(2,1)S(1)}, bf16[4,256,192]{2,1,0:T(8,128)(2,1)S(1)}) custom-call(s32[5]{0:T(128)S(1)} %copy-done.27, bf16[4,256,192]{2,1,0:T(8,128)(2,1)S(1)} %copy-done.8, ...), custom_call_target="tpu_custom_call" | custom-call | flops 1000000 | bytes 3000 | tf_op jit(solution)/shard_map/attend_backward/pallas_call | solution.py:261
  203.6 4.4 %unproject.1 = (bf16[4,256,768]{2,1,0:T(8,128)(2,1)}, bf16[768,576]{1,0:T(8,128)(2,1)S(1)}) custom-call(s32[5]{0:T(128)S(1)} %copy-done.27, f32[4,256,192]{2,1,0:T(8,128)S(1)} %get-tuple-element.119.dq_ref, f32[4,256,192]{2,1,0:T(8,128)S(1)} %get-tuple-element.120.dk_ref, bf16[4,256,192]{2,1,0:T(8,128)(2,1)S(1)} %collective-permute-done.19.far_k_ref, ...), custom_call_target="tpu_custom_call" | custom-call | flops 1000000 | bytes 3000 | tf_op jit(solution)/shard_map/unproject/pallas_call | solution.py:309
  207.9 5.6 %all-to-all-start.2 = ((bf16[4,256,768]{2,1,0:T(8,128)(2,1)}), bf16[4,256,768]{2,1,0:T(8,128)(2,1)}, u32[]{:S(2)}, u32[]{:S(2)}) async-start(bf16[4,256,768]{2,1,0:T(8,128)(2,1)} %get-tuple-element.125), calls=%async_computation.2 | async-start | bytes 3145728 | tf_op jit(solution)/shard_map/all_to_all | solution.py:750
  214.2 2.6 collective-permute-start.23
  217.0 1.9 collective-permute-done.24
  219.8 25.9 %collective-permute-done.22.refs_2_ = bf16[4,96,1792]{2,1,0:T(8,128)(2,1)S(1)} collective-permute-done((bf16[4,96,1792]{2,1,0:T(8,128)(2,1)}, bf16[4,96,1792]{2,1,0:T(8,128)(2,1)S(1)}, u32[]{:S(2)}, u32[]{:S(2)}) %collective-permute-start.22) | collective-permute-done | bytes 1376288 | tf_op jit(solution)/shard_map/ppermute | solution.py:28
  246.7 2.6 copy-done.1
  249.3 2.2 copy-done.3
  251.4 2.0 add_blocks.5
  254.6 1.7 convert_reduce_fusion
  258.4 4.2 %all-to-all-start.3 = ((bf16[8,256,384]{2,1,0:T(8,128)(2,1)}), bf16[8,256,384]{2,1,0:T(8,128)(2,1)S(1)}, u32[]{:S(2)}, u32[]{:S(2)}) async-start(bf16[8,256,384]{2,1,0:T(8,128)(2,1)} %bitcast.34), calls=%async_computation.3 | async-start | bytes 3145728 | tf_op jit(solution)/shard_map/all_to_all | solution.py:723
  262.6 2.1 collective-permute-start.25
  264.7 1.5 collective-permute-start.21
  266.2 21.7 %collective-permute-done.25 = bf16[192,576]{1,0:T(8,128)(2,1)S(1)} collective-permute-done((bf16[192,576]{1,0:T(8,128)(2,1)S(1)}, bf16[192,576]{1,0:T(8,128)(2,1)S(1)}, u32[]{:S(2)}, u32[]{:S(2)}) %collective-permute-start.25) | collective-permute-done | bytes 221216 | tf_op jit(solution)/shard_map/ppermute | solution.py:28
  288.0 1.5 collective-permute-start.26
  289.6 6.0 %collective-permute-done.26 = bf16[192,576]{1,0:T(8,128)(2,1)S(1)} collective-permute-done((bf16[192,576]{1,0:T(8,128)(2,1)S(1)}, bf16[192,576]{1,0:T(8,128)(2,1)S(1)}, u32[]{:S(2)}, u32[]{:S(2)}) %collective-permute-start.26) | collective-permute-done | bytes 221216 | tf_op jit(solution)/shard_map/ppermute | solution.py:28
  296.5 1.9 fusion.12
  298.5 1.5 collective-permute-start.27
  301.0 6.5 %collective-permute-done.27 = bf16[96,1792]{1,0:T(8,128)(2,1)S(1)} collective-permute-done((bf16[96,1792]{1,0:T(8,128)(2,1)}, bf16[96,1792]{1,0:T(8,128)(2,1)S(1)}, u32[]{:S(2)}, u32[]{:S(2)}) %collective-permute-start.27) | collective-permute-done | bytes 344096 | tf_op jit(solution)/shard_map/ppermute | solution.py:28
  (163 shorter events, 42.5 us)
Async XLA Ops:
  7.2 19.0 %copy-start.29 = (bf16[2,192,512]{2,1,0:T(8,128)(2,1)S(1)}, bf16[2,192,512]{2,1,0:T(8,128)(2,1)}, u32[]{:S(2)}) copy-start(bf16[2,192,512]{2,1,0:T(8,128)(2,1)} %param.14) | copy-start | bytes 1179652
  7.2 128.0 %all-gather.3.cloned.1.call-start = ((), (), s32[]{:S(2)}) async-start(), calls=%async_computation.6 | async-start | bytes 11354112 | tf_op jit(solution)/shard_map/all_gather | solution.py:678
  12.7 13.5 %collective-permute-start.1 = (bf16[2,192,512]{2,1,0:T(8,128)(2,1)}, bf16[2,192,512]{2,1,0:T(8,128)(2,1)S(1)}, u32[]{:S(2)}, u32[]{:S(2)}) collective-permute-start(bf16[2,192,512]{2,1,0:T(8,128)(2,1)} %param.14), channel_id=1, source_target_pairs={{0,16},{16,0},{1,17},{17,1},{2,18},{18,2},{3,19},{19,3},{4,20},{20... | collective-permute-start | bytes 1179656 | tf_op jit(solution)/shard_map/ppermute | solution.py:28
  15.7 22.2 %collective-permute-start = (bf16[2,192,512]{2,1,0:T(8,128)(2,1)}, bf16[2,192,512]{2,1,0:T(8,128)(2,1)}, u32[]{:S(2)}, u32[]{:S(2)}) collective-permute-start(bf16[2,192,512]{2,1,0:T(8,128)(2,1)} %param.15), channel_id=1, source_target_pairs={{0,16},{16,0},{1,17},{17,1},{2,18},{18,2},{3,19},{19,3},{4,20},{20... | collective-permute-start | bytes 1179656 | tf_op jit(solution)/shard_map/ppermute | solution.py:28
  28.2 8.2 %collective-permute-start.5 = (bf16[192,576]{1,0:T(8,128)(2,1)S(1)}, bf16[192,576]{1,0:T(8,128)(2,1)S(1)}, u32[]{:S(2)}, u32[]{:S(2)}) collective-permute-start(bf16[192,576]{1,0:T(8,128)(2,1)S(1)} %pad_maximum_fusion.4), channel_id=1, source_target_pairs={{0,8},{8,0},{1,9},{9,1},{2,10},{10,2},{3,11},{11,3},{4,12},{12,4},... | collective-permute-start | bytes 663560 | tf_op jit(solution)/shard_map/ppermute | solution.py:28
  31.9 64.5 %copy-start.9 = (f32[4,256,128]{2,1,0:T(8,128)}, f32[4,256,128]{2,1,0:T(8,128)S(1)}, u32[]{:S(2)}) copy-start(f32[4,256,128]{2,1,0:T(8,128)S(1)} %get-tuple-element.157.refs_6_.sin_ref) | copy-start | bytes 1572868
  31.9 64.5 %copy-start.11 = (f32[4,256,128]{2,1,0:T(8,128)}, f32[4,256,128]{2,1,0:T(8,128)S(1)}, u32[]{:S(2)}) copy-start(f32[4,256,128]{2,1,0:T(8,128)S(1)} %get-tuple-element.158.refs_5_.cos_ref) | copy-start | bytes 1572868
  32.8 5.1 %copy-start.30 = (bf16[2,192,512]{2,1,0:T(8,128)(2,1)S(1)}, bf16[2,192,512]{2,1,0:T(8,128)(2,1)}, u32[]{:S(2)}) copy-start(bf16[2,192,512]{2,1,0:T(8,128)(2,1)} %param.15) | copy-start | bytes 1179652
  32.8 11.0 %all-to-all-start = ((bf16[4,256,192]{1,2,0:T(8,128)(2,1)}), bf16[4,256,192]{1,2,0:T(8,128)(2,1)S(1)}, u32[]{:S(2)}, u32[]{:S(2)}) async-start(bf16[4,256,192]{1,2,0:T(8,128)(2,1)} %bitcast.115), calls=%async_computation | async-start | bytes 786432 | tf_op jit(solution)/shard_map/all_to_all | solution.py:691
  37.4 19.6 %collective-permute-start.6 = (bf16[2,192,576]{2,1,0:T(8,128)(2,1)}, bf16[2,192,576]{2,1,0:T(8,128)(2,1)}, u32[]{:S(2)}, u32[]{:S(2)}) collective-permute-start(bf16[2,192,576]{2,1,0:T(8,128)(2,1)} %pad_maximum_fusion.3), channel_id=1, source_target_pairs={{0,4},{4,0},{1,5},{5,1},{2,6},{6,2},{3,7},{7,3},{8,12},{12,8},{9,1... | collective-permute-start | bytes 1327112 | tf_op jit(solution)/shard_map/ppermute | solution.py:28
  44.0 30.3 %collective-permute-start.4 = (bf16[256,768]{1,0:T(8,128)(2,1)S(1)}, bf16[256,768]{1,0:T(8,128)(2,1)S(1)}, u32[]{:S(2)}, u32[]{:S(2)}) collective-permute-start(bf16[256,768]{1,0:T(8,128)(2,1)S(1)} %copy.65.refs_0_.x_ref), channel_id=1, source_target_pairs={{0,3},{1,0},{2,1},{3,2},{4,7},{5,4},{6,5},{7,6},{8,11},{9,8},{10,9... | collective-permute-start | bytes 1179656 | tf_op jit(solution)/shard_map/ppermute | solution.py:586
  47.6 32.8 %collective-permute-start.2 = (bf16[256,768]{1,0:T(8,128)(2,1)S(1)}, bf16[256,768]{1,0:T(8,128)(2,1)S(1)}, u32[]{:S(2)}, u32[]{:S(2)}) collective-permute-start(bf16[256,768]{1,0:T(8,128)(2,1)S(1)} %copy.65.refs_0_.x_ref), channel_id=1, source_target_pairs={{0,1},{1,2},{2,3},{3,0},{4,5},{5,6},{6,7},{7,4},{8,9},{9,10},{10,1... | collective-permute-start | bytes 1179656 | tf_op jit(solution)/shard_map/ppermute | solution.py:586
  47.6 48.8 %collective-permute-start.3 = (bf16[256,768]{1,0:T(8,128)(2,1)S(1)}, bf16[256,768]{1,0:T(8,128)(2,1)}, u32[]{:S(2)}, u32[]{:S(2)}) collective-permute-start(bf16[256,768]{1,0:T(8,128)(2,1)S(1)} %copy.65.refs_0_.x_ref), channel_id=1, source_target_pairs={{0,2},{1,3},{2,0},{3,1},{4,6},{5,7},{6,4},{7,5},{8,10},{9,11},{10,... | collective-permute-start | bytes 1179656 | tf_op jit(solution)/shard_map/ppermute | solution.py:586
  52.3 12.1 %all-to-all-start.1 = ((bf16[4,256,192]{1,2,0:T(8,128)(2,1)}), bf16[4,256,192]{1,2,0:T(8,128)(2,1)}, u32[]{:S(2)}, u32[]{:S(2)}) async-start(bf16[4,256,192]{1,2,0:T(8,128)(2,1)} %bitcast.114), calls=%async_computation.1 | async-start | bytes 786432 | tf_op jit(solution)/shard_map/all_to_all | solution.py:691
  104.8 4.8 %copy-start.27 = (s32[5]{0:T(128)S(1)}, s32[5]{0:T(128)}, u32[]{:S(2)}) copy-start(s32[5]{0:T(128)} %stack.68.refs_0_.info_ref) | copy-start | bytes 64
  105.3 2.8 collective-permute-start.7
  105.4 4.2 %collective-permute-start.8 = (bf16[8,192,256]{2,1,0:T(8,128)(2,1)}, bf16[8,192,256]{2,1,0:T(8,128)(2,1)}, u32[]{:S(2)}, u32[]{:S(2)}) collective-permute-start(bf16[8,192,256]{2,1,0:T(8,128)(2,1)} %get-tuple-element.79.refs_4_), channel_id=1, source_target_pairs={{0,4},{4,0},{1,5},{5,1},{2,6},{6,2},{3,7},{7,3},{8,12},{12,8},{9,1... | collective-permute-start | bytes 2359304 | tf_op jit(solution)/shard_map/ppermute | solution.py:28
  123.7 10.7 %collective-permute-start.10 = (bf16[192,256]{1,0:T(8,128)(2,1)}, bf16[192,256]{1,0:T(8,128)(2,1)}, u32[]{:S(2)}, u32[]{:S(2)}) collective-permute-start(bf16[192,256]{1,0:T(8,128)(2,1)} %get-tuple-element.88.refs_12_), channel_id=1, source_target_pairs={{0,2},{1,3},{2,0},{3,1},{4,6},{5,7},{6,4},{7,5},{8,10},{9,11},{10,... | collective-permute-start | bytes 294920 | tf_op jit(solution)/shard_map/ppermute | solution.py:586
  123.7 10.7 %collective-permute-start.11 = (bf16[192,256]{1,0:T(8,128)(2,1)}, bf16[192,256]{1,0:T(8,128)(2,1)}, u32[]{:S(2)}, u32[]{:S(2)}) collective-permute-start(bf16[192,256]{1,0:T(8,128)(2,1)} %get-tuple-element.89.refs_13_), channel_id=1, source_target_pairs={{0,1},{1,2},{2,3},{3,0},{4,5},{5,6},{6,7},{7,4},{8,9},{9,10},{10,1... | collective-permute-start | bytes 294920 | tf_op jit(solution)/shard_map/ppermute | solution.py:586
  126.7 8.5 %collective-permute-start.9 = (bf16[192,256]{1,0:T(8,128)(2,1)}, bf16[192,256]{1,0:T(8,128)(2,1)}, u32[]{:S(2)}, u32[]{:S(2)}) collective-permute-start(bf16[192,256]{1,0:T(8,128)(2,1)} %get-tuple-element.87.refs_11_), channel_id=1, source_target_pairs={{0,3},{1,0},{2,1},{3,2},{4,7},{5,4},{6,5},{7,6},{8,11},{9,8},{10,9... | collective-permute-start | bytes 294920 | tf_op jit(solution)/shard_map/ppermute | solution.py:586
  135.2 4.1 %copy-start.4 = (bf16[3072,1792]{1,0:T(8,128)(2,1)S(1)}, bf16[3072,1792]{1,0:T(8,128)(2,1)}, u32[]{:S(2)}) copy-start(bf16[3072,1792]{1,0:T(8,128)(2,1)} %all-gather.3.cloned.1.call-done) | copy-start | bytes 33030148
  154.1 10.8 %copy-start.19 = (f32[256,768]{1,0:T(8,128)}, f32[256,768]{1,0:T(8,128)S(1)}, u32[]{:S(2)}) copy-start(f32[256,768]{1,0:T(8,128)S(1)} %get-tuple-element.91) | copy-start | bytes 2359300
  154.1 10.8 %copy-start.25 = (bf16[256,768]{1,0:T(8,128)(2,1)}, bf16[256,768]{1,0:T(8,128)(2,1)S(1)}, u32[]{:S(2)}) copy-start(bf16[256,768]{1,0:T(8,128)(2,1)S(1)} %get-tuple-element.90) | copy-start | bytes 1179652
  164.9 35.6 %copy-start = (bf16[2,2,4,96,1792]{4,3,2,1,0:T(8,128)(2,1)}, bf16[2,2,4,96,1792]{4,3,2,1,0:T(8,128)(2,1)S(1)}, u32[]{:S(2)}) copy-start(bf16[2,2,4,96,1792]{4,3,2,1,0:T(8,128)(2,1)S(1)} %get-tuple-element.102.refs_0_) | copy-start | bytes 16515076
  164.9 34.8 %collective-permute-start.18 = (bf16[3,4,96,1792]{3,2,1,0:T(8,128)(2,1)S(1)}, bf16[3,4,96,1792]{3,2,1,0:T(8,128)(2,1)S(1)}, u32[]{:S(2)}, u32[]{:S(2)}) collective-permute-start(bf16[3,4,96,1792]{3,2,1,0:T(8,128)(2,1)S(1)} %get-tuple-element.116), channel_id=1, source_target_pairs={{0,4},{4,0},{1,5},{5,1},{2,6},{6,2},{3,7},{7,3},{8,12},{12,8},{9,1... | collective-permute-start | bytes 12386312 | tf_op jit(solution)/shard_map/ppermute | solution.py:28
  165.0 9.0 %collective-permute-start.15 = (bf16[4,96,1792]{2,1,0:T(8,128)(2,1)S(1)}, bf16[4,96,1792]{2,1,0:T(8,128)(2,1)S(1)}, u32[]{:S(2)}, u32[]{:S(2)}) collective-permute-start(bf16[4,96,1792]{2,1,0:T(8,128)(2,1)S(1)} %get-tuple-element.103), channel_id=1, source_target_pairs={{0,4},{4,0},{1,5},{5,1},{2,6},{6,2},{3,7},{7,3},{8,12},{12,8},{9,1... | collective-permute-start | bytes 4128776 | tf_op jit(solution)/shard_map/ppermute | solution.py:28
  165.5 8.8 %collective-permute-start.12 = (bf16[192,256]{1,0:T(8,128)(2,1)S(1)}, bf16[192,256]{1,0:T(8,128)(2,1)S(1)}, u32[]{:S(2)}, u32[]{:S(2)}) collective-permute-start(bf16[192,256]{1,0:T(8,128)(2,1)S(1)} %get-tuple-element.93), channel_id=1, source_target_pairs={{0,1},{1,2},{2,3},{3,0},{4,5},{5,6},{6,7},{7,4},{8,9},{9,10},{10,1... | collective-permute-start | bytes 294920 | tf_op jit(solution)/shard_map/ppermute | solution.py:586
  168.1 8.3 %collective-permute-start.13 = (bf16[192,256]{1,0:T(8,128)(2,1)S(1)}, bf16[192,256]{1,0:T(8,128)(2,1)S(1)}, u32[]{:S(2)}, u32[]{:S(2)}) collective-permute-start(bf16[192,256]{1,0:T(8,128)(2,1)S(1)} %get-tuple-element.94), channel_id=1, source_target_pairs={{0,2},{1,3},{2,0},{3,1},{4,6},{5,7},{6,4},{7,5},{8,10},{9,11},{10,... | collective-permute-start | bytes 294920 | tf_op jit(solution)/shard_map/ppermute | solution.py:586
  168.1 8.2 %collective-permute-start.14 = (bf16[192,256]{1,0:T(8,128)(2,1)S(1)}, bf16[192,256]{1,0:T(8,128)(2,1)S(1)}, u32[]{:S(2)}, u32[]{:S(2)}) collective-permute-start(bf16[192,256]{1,0:T(8,128)(2,1)S(1)} %get-tuple-element.95), channel_id=1, source_target_pairs={{0,3},{1,0},{2,1},{3,2},{4,7},{5,4},{6,5},{7,6},{8,11},{9,8},{10,9... | collective-permute-start | bytes 294920 | tf_op jit(solution)/shard_map/ppermute | solution.py:586
  174.0 9.5 %copy-start.8 = (bf16[4,256,192]{2,1,0:T(8,128)(2,1)S(1)}, bf16[4,256,192]{2,1,0:T(8,128)(2,1)}, u32[]{:S(2)}) copy-start(bf16[4,256,192]{2,1,0:T(8,128)(2,1)} %copy-done.5) | copy-start | bytes 1179652
  176.4 23.3 %collective-permute-start.16 = (bf16[2,96,1792]{2,1,0:T(8,128)(2,1)S(1)}, bf16[2,96,1792]{2,1,0:T(8,128)(2,1)S(1)}, u32[]{:S(2)}, u32[]{:S(2)}) collective-permute-start(bf16[2,96,1792]{2,1,0:T(8,128)(2,1)S(1)} %get-tuple-element.104), channel_id=1, source_target_pairs={{0,16},{16,0},{1,17},{17,1},{2,18},{18,2},{3,19},{19,3},{4,20},{20... | collective-permute-start | bytes 2064392 | tf_op jit(solution)/shard_map/ppermute | solution.py:28
  182.7 17.0 %collective-permute-start.17 = (bf16[2,96,1792]{2,1,0:T(8,128)(2,1)S(1)}, bf16[2,96,1792]{2,1,0:T(8,128)(2,1)S(1)}, u32[]{:S(2)}, u32[]{:S(2)}) collective-permute-start(bf16[2,96,1792]{2,1,0:T(8,128)(2,1)S(1)} %get-tuple-element.105), channel_id=1, source_target_pairs={{0,8},{8,0},{1,9},{9,1},{2,10},{10,2},{3,11},{11,3},{4,12},{12,4},... | collective-permute-start | bytes 2064392 | tf_op jit(solution)/shard_map/ppermute | solution.py:28
  199.1 4.4 %collective-permute-start.19 = (bf16[4,256,192]{2,1,0:T(8,128)(2,1)S(1)}, bf16[4,256,192]{2,1,0:T(8,128)(2,1)S(1)}, u32[]{:S(2)}, u32[]{:S(2)}) collective-permute-start(bf16[4,256,192]{2,1,0:T(8,128)(2,1)S(1)} %get-tuple-element.121), channel_id=1, source_target_pairs={{0,4},{4,0},{1,5},{5,1},{2,6},{6,2},{3,7},{7,3},{8,12},{12,8},{9,1... | collective-permute-start | bytes 1179656 | tf_op jit(solution)/shard_map/ppermute | solution.py:28
  199.2 4.4 %collective-permute-start.20 = (bf16[4,256,192]{2,1,0:T(8,128)(2,1)S(1)}, bf16[4,256,192]{2,1,0:T(8,128)(2,1)S(1)}, u32[]{:S(2)}, u32[]{:S(2)}) collective-permute-start(bf16[4,256,192]{2,1,0:T(8,128)(2,1)S(1)} %get-tuple-element.123), channel_id=1, source_target_pairs={{0,4},{4,0},{1,5},{5,1},{2,6},{6,2},{3,7},{7,3},{8,12},{12,8},{9,1... | collective-permute-start | bytes 1179656 | tf_op jit(solution)/shard_map/ppermute | solution.py:28
  207.9 46.7 %all-to-all-start.2 = ((bf16[4,256,768]{2,1,0:T(8,128)(2,1)}), bf16[4,256,768]{2,1,0:T(8,128)(2,1)}, u32[]{:S(2)}, u32[]{:S(2)}) async-start(bf16[4,256,768]{2,1,0:T(8,128)(2,1)} %get-tuple-element.125), calls=%async_computation.2 | async-start | bytes 3145728 | tf_op jit(solution)/shard_map/all_to_all | solution.py:750
  213.6 84.9 %reduce-scatter.2.cloned.1.call-start = ((), (), s32[]{:S(2)}) async-start(), calls=%async_computation.5 | async-start | bytes 1720320 | tf_op jit(solution)/shard_map/reduce_scatter | solution.py:648
  213.6 32.1 %collective-permute-start.22 = (bf16[4,96,1792]{2,1,0:T(8,128)(2,1)}, bf16[4,96,1792]{2,1,0:T(8,128)(2,1)S(1)}, u32[]{:S(2)}, u32[]{:S(2)}) collective-permute-start(bf16[4,96,1792]{2,1,0:T(8,128)(2,1)} %copy-done.16), channel_id=1, source_target_pairs={{0,8},{8,0},{1,9},{9,1},{2,10},{10,2},{3,11},{11,3},{4,12},{12,4},... | collective-permute-start | bytes 4128776 | tf_op jit(solution)/shard_map/ppermute | solution.py:28
  214.2 32.5 %collective-permute-start.23 = (bf16[4,96,1792]{2,1,0:T(8,128)(2,1)S(1)}, bf16[4,96,1792]{2,1,0:T(8,128)(2,1)S(1)}, u32[]{:S(2)}, u32[]{:S(2)}) collective-permute-start(bf16[4,96,1792]{2,1,0:T(8,128)(2,1)S(1)} %add_blocks.4), channel_id=1, source_target_pairs={{0,16},{16,0},{1,17},{17,1},{2,18},{18,2},{3,19},{19,3},{4,20},{20... | collective-permute-start | bytes 4128776 | tf_op jit(solution)/shard_map/ppermute | solution.py:28
  216.9 1.9 collective-permute-start.24
  246.7 2.6 copy-start.1
  258.4 4.2 %copy-start.28 = (bf16[2,192,576]{2,1,0:T(8,128)(2,1)S(1)}, bf16[2,192,576]{2,1,0:T(8,128)(2,1)}, u32[]{:S(2)}) copy-start(bf16[2,192,576]{2,1,0:T(8,128)(2,1)} %fusion.29) | copy-start | bytes 1327108
  258.4 6.3 %copy-start.35 = (s32[2,512]{1,0:T(2,128)S(1)}, s32[2,512]{1,0:T(2,128)}, u32[]{:S(2)}) copy-start(s32[2,512]{1,0:T(2,128)} %param.17) | copy-start | bytes 12292
  258.4 38.1 %all-to-all-start.3 = ((bf16[8,256,384]{2,1,0:T(8,128)(2,1)}), bf16[8,256,384]{2,1,0:T(8,128)(2,1)S(1)}, u32[]{:S(2)}, u32[]{:S(2)}) async-start(bf16[8,256,384]{2,1,0:T(8,128)(2,1)} %bitcast.34), calls=%async_computation.3 | async-start | bytes 3145728 | tf_op jit(solution)/shard_map/all_to_all | solution.py:723
  262.6 25.3 %collective-permute-start.25 = (bf16[192,576]{1,0:T(8,128)(2,1)S(1)}, bf16[192,576]{1,0:T(8,128)(2,1)S(1)}, u32[]{:S(2)}, u32[]{:S(2)}) collective-permute-start(bf16[192,576]{1,0:T(8,128)(2,1)S(1)} %select_bitcast_fusion.7), channel_id=1, source_target_pairs={{0,8},{8,0},{1,9},{9,1},{2,10},{10,2},{3,11},{11,3},{4,12},{12,4},... | collective-permute-start | bytes 663560 | tf_op jit(solution)/shard_map/ppermute | solution.py:28
  264.7 24.8 %collective-permute-start.21 = (s32[2,512]{1,0:T(2,128)S(1)}, s32[2,512]{1,0:T(2,128)S(1)}, u32[]{:S(2)}, u32[]{:S(2)}) collective-permute-start(s32[2,512]{1,0:T(2,128)S(1)} %copy-done.35), channel_id=1, source_target_pairs={{0,16},{16,0},{1,17},{17,1},{2,18},{18,2},{3,19},{19,3},{4,20},{20... | collective-permute-start | bytes 12296 | tf_op jit(solution)/shard_map/ppermute | solution.py:28
  288.0 7.6 %collective-permute-start.26 = (bf16[192,576]{1,0:T(8,128)(2,1)S(1)}, bf16[192,576]{1,0:T(8,128)(2,1)S(1)}, u32[]{:S(2)}, u32[]{:S(2)}) collective-permute-start(bf16[192,576]{1,0:T(8,128)(2,1)S(1)} %fusion.35), channel_id=1, source_target_pairs={{0,16},{16,0},{1,17},{17,1},{2,18},{18,2},{3,19},{19,3},{4,20},{20... | collective-permute-start | bytes 663560 | tf_op jit(solution)/shard_map/ppermute | solution.py:28
  298.5 9.0 %copy-start.34 = (bf16[1,96,1792]{2,1,0:T(8,128)(2,1)S(1)}, bf16[1,96,1792]{2,1,0:T(8,128)(2,1)}, u32[]{:S(2)}) copy-start(bf16[1,96,1792]{2,1,0:T(8,128)(2,1)} %reduce-scatter.2.cloned.1.call-done) | copy-start | bytes 1032196
  298.5 9.0 %collective-permute-start.27 = (bf16[96,1792]{1,0:T(8,128)(2,1)}, bf16[96,1792]{1,0:T(8,128)(2,1)S(1)}, u32[]{:S(2)}, u32[]{:S(2)}) collective-permute-start(bf16[96,1792]{1,0:T(8,128)(2,1)} %bitcast.129), channel_id=1, source_target_pairs={{0,16},{16,0},{1,17},{17,1},{2,18},{18,2},{3,19},{19,3},{4,20},{20... | collective-permute-start | bytes 1032200 | tf_op jit(solution)/shard_map/ppermute | solution.py:28
  (22 other events, 29.3 us)
Sparse Core Ops, SparseCore 0:
  12.8 116.7 all-gather.2
  253.6 33.4 reduce-scatter.1

commit v4 on v3

--- a/solution.py
+++ b/solution.py
@@ -58,29 +58,29 @@
 
 def project_kernel(blocks, *refs):
     x_refs, (w_ref, cos_ref, sin_ref) = refs[:blocks], refs[blocks : blocks + 3]
-    q_ref, kv_ref, turned_ref, xt_ref = refs[-4:]
-    width = q_ref.shape[2]
+    q_ref, kv_ref, turned_ref = refs[-3:]
+    width = turned_ref.shape[1]
     for index, x_ref in enumerate(x_refs):
         wide = jnp.dot(x_ref[...], w_ref[...], preferred_element_type=f32)
-        xt_ref[index] = x_ref[...].T
         turned = turn(wide[:, : 2 * width], cos_ref[index], sin_ref[index])
-        q_ref[index] = turned[:, :width].astype(bf16)
-        for place, part in ((index, turned[:, width:]), (blocks + index, wide[:, 2 * width :])):
-            kv_ref[place] = part.astype(bf16)
-            turned_ref[place] = part.T.astype(bf16)
+        parts = turned[:, :width], turned[:, width:], wide[:, 2 * width :]
+        for ref, place, part in ((q_ref, index, parts[0]), (kv_ref, index, parts[1]), (kv_ref, blocks + index, parts[2])):
+            ref[place] = jnp.concatenate([part, jnp.zeros((part.shape[0], ref.shape[2] - width), f32)], 1).astype(bf16)
+        turned_ref[index] = parts[1].T.astype(bf16)
+        turned_ref[blocks + index] = parts[2].T.astype(bf16)
 
 
 def project(blocks, weight, cosine, sine):
     own, width, count = blocks[0].shape[0], weight.shape[1] // 3, len(blocks)
+    padded = -(-width // 128) * 128
     return pl.pallas_call(
         lambda *refs: project_kernel(count, *refs),
         out_shape=[
-            jax.ShapeDtypeStruct((count, own, width), bf16),
-            jax.ShapeDtypeStruct((2 * count, own, width), bf16),
+            jax.ShapeDtypeStruct((count, own, padded), bf16),
+            jax.ShapeDtypeStruct((2 * count, own, padded), bf16),
             jax.ShapeDtypeStruct((2 * count, width, own), bf16),
-            jax.ShapeDtypeStruct((count, blocks[0].shape[1], own), bf16),
         ],
-        compiler_params=pltpu.CompilerParams(vmem_limit_bytes=16 << 20),
+        compiler_params=pltpu.CompilerParams(vmem_limit_bytes=60 << 20),
         cost_estimate=cost(0.001),
         name="project",
     )(*blocks, weight, cosine, sine)
@@ -130,7 +130,8 @@
 
 
 def forward_kernel(first, share, info_ref, q_ref, k0_ref, k1_ref, vt0_ref, vt1_ref, *refs):
-    columns, own, width = k0_ref.shape
+    columns, own, _ = k0_ref.shape
+    width = vt0_ref.shape[1]
     heads = width // DH
     count = (len(refs) - 4) // 2
     outs, lses, (parts, top, total, sums) = refs[:count], refs[count : 2 * count], refs[2 * count :]
@@ -171,9 +172,10 @@
 
 
 def attend_forward(first, count, info, q, kv, kv_twin, turned, turned_twin, share):
-    columns, own, width = q.shape
+    columns, own, padded = q.shape
+    width = turned.shape[1]
     heads = width // DH
-    keys = pl.BlockSpec((columns, own, width), lambda i, s: (0, 0, 0))
+    keys = pl.BlockSpec((columns, own, padded), lambda i, s: (0, 0, 0))
     values = pl.BlockSpec((columns, width, own), lambda i, s: (1, 0, 0))
     flat = lambda rows: pl.BlockSpec((rows, own), lambda i, s: (0, 0))
     outs = pl.pallas_call(
@@ -184,14 +186,14 @@
             in_specs=[keys, keys, keys, values, values],
             out_specs=[flat(width)] * count + [flat(heads)] * count,
             scratch_shapes=[
-                pltpu.VMEM((heads, own, width), bf16),
+                pltpu.VMEM((heads, own, padded), bf16),
                 pltpu.VMEM((heads, own), f32),
                 pltpu.VMEM((heads, own), f32),
                 pltpu.VMEM((width, own), f32),
             ],
         ),
         out_shape=[jax.ShapeDtypeStruct((width, own), bf16)] * count + [jax.ShapeDtypeStruct((heads, own), f32)] * count,
-        compiler_params=pltpu.CompilerParams(vmem_limit_bytes=16 << 20),
+        compiler_params=pltpu.CompilerParams(vmem_limit_bytes=60 << 20),
         cost_estimate=cost(0.001),
         name="attend_forward",
     )(info, q, kv, kv_twin, turned, turned_twin)
@@ -199,20 +201,22 @@
 
 
 def backward_kernel(columns, share, info_ref, q_ref, kv0_ref, kv1_ref, kt0_ref, kt1_ref, *refs):
-    grads, outs, lses, refs = refs[:columns], refs[columns : 2 * columns], refs[2 * columns : 3 * columns], refs[3 * columns :]
-    dq_ref, dk_ref, dv_ref, far_k_ref, far_v_ref, part_q, part_g, delta, lse, sum_q, sum_k, sum_v = refs
-    _, own, width = q_ref.shape
+    grads, outs, lses, refs = refs[0], refs[1 : columns + 1], refs[columns + 1 : 2 * columns + 1], refs[2 * columns + 1 :]
+    dq_ref, near_ref, far_ref, part_q, part_g, delta, lse, sum_q, sum_k, sum_v = refs
+    own, width = q_ref.shape[1], kt0_ref.shape[1]
     heads = width // DH
     scaling = DH ** (-0.5)
     sum_k[...] = jnp.zeros_like(sum_k)
     sum_v[...] = jnp.zeros_like(sum_v)
     for block in range(columns):
         lse[block] = lses[block][...]
-        grad = grads[block][...]
+        column = info_ref[2] - block
+        grad = grads[jnp.where(column < 0, column + columns, column)]
+        spare = jnp.zeros((part_g.shape[1] - width, own), bf16)
         product = grad.astype(f32) * outs[block][...].astype(f32)
         for head in range(heads):
             part_q[block, pl.ds(head * own, own), :] = head_lanes(q_ref[block], head)
-            part_g[block, :, pl.ds(head * own, own)] = head_rows(grad, head)
+            part_g[block, :, pl.ds(head * own, own)] = jnp.concatenate([head_rows(grad, head), spare], 0)
             delta[block, pl.ds(head, 1), :] = jnp.sum(product[head * DH : (head + 1) * DH], 0, keepdims=True)
 
     def query_step(block, carry):
@@ -246,75 +250,86 @@
 
     lax.fori_loop(0, columns, query_step, 0)
     for block in range(columns):
-        dk_ref[block] = sum_k[block, :own]
-        dv_ref[block] = sum_v[block, :own]
-        far_k_ref[block] = sum_k[block, own:].astype(bf16)
-        far_v_ref[block] = sum_v[block, own:].astype(bf16)
+        for place, sums in ((block, sum_k), (columns + block, sum_v)):
+            near_ref[place] = sums[block, :own].astype(bf16)
+            far_ref[place] = sums[block, own:].astype(bf16)
 
 
 def attend_backward(info, q, kv, kv_twin, turned, turned_twin, grads, outs, lses, share):
-    columns, own, width = q.shape
+    columns, own, padded = q.shape
+    width = turned.shape[1]
     heads = width // DH
     vmem = pl.BlockSpec(memory_space=pltpu.VMEM)
-    shape = lambda kind: jax.ShapeDtypeStruct((columns, own, width), kind)
-    operands = [q, kv, kv_twin, turned, turned_twin, *grads, *outs, *lses]
+    operands = [q, kv, kv_twin, turned, turned_twin, grads, *outs, *lses]
     return pl.pallas_call(
         lambda *refs: backward_kernel(columns, share, *refs),
         in_specs=[pl.BlockSpec(memory_space=pltpu.SMEM)] + [vmem] * len(operands),
-        out_specs=[vmem] * 5,
-        out_shape=[shape(f32), shape(f32), shape(f32), shape(bf16), shape(bf16)],
+        out_specs=[vmem] * 3,
+        out_shape=[jax.ShapeDtypeStruct((columns, own, width), f32)]
+        + [jax.ShapeDtypeStruct((2 * columns, own, padded), bf16)] * 2,
         scratch_shapes=[
-            pltpu.VMEM((columns, heads * own, width), bf16),
-            pltpu.VMEM((columns, width, heads * own), bf16),
+            pltpu.VMEM((columns, heads * own, padded), bf16),
+            pltpu.VMEM((columns, padded, heads * own), bf16),
             pltpu.VMEM((columns, heads, own), f32),
             pltpu.VMEM((columns, heads, own), f32),
             pltpu.VMEM((width, own), f32),
-            pltpu.VMEM((columns, share, width), f32),
-            pltpu.VMEM((columns, share, width), f32),
+            pltpu.VMEM((columns, share, padded), f32),
+            pltpu.VMEM((columns, share, padded), f32),
         ],
-        compiler_params=pltpu.CompilerParams(vmem_limit_bytes=28 << 20),
+        compiler_params=pltpu.CompilerParams(vmem_limit_bytes=60 << 20),
         cost_estimate=cost(0.001),
         name="attend_backward",
     )(info, *operands)
 
 
 def unproject_kernel(
-    info_ref, dq_ref, dk_ref, far_k_ref, dv_ref, far_v_ref, w_ref, cos_ref, sin_ref, xt_ref, part_ref, grad_ref, total
+    info_ref, dq_ref, near_k_ref, far_k_ref, near_v_ref, far_v_ref, w_ref, cos_ref, sin_ref, *refs
 ):
-    columns = dq_ref.shape[0]
+    x_refs, (part_ref, grad_ref, total) = refs[:-3], refs[-3:]
+    step = pl.program_id(0)
     width = dq_ref.shape[2]
     lanes = 2 * width
     even = lax.broadcasted_iota(jnp.int32, (dq_ref.shape[1], lanes), 1) % 2 == 0
-    for block in range(columns):
-        dk = (dk_ref[block] + far_k_ref[block].astype(f32)) * DH ** (-0.5)
-        dv = dv_ref[block] + far_v_ref[block].astype(f32)
-        both = jnp.concatenate([dq_ref[block], dk], 1)
-        swapped = jnp.where(even, pltpu.roll(both, lanes - 1, 1), pltpu.roll(both, 1, 1))
-        both = both * widen(cos_ref[block], lanes) - swapped * widen(sin_ref[block], lanes)
-        low = jnp.concatenate([both, dv], 1).astype(bf16)
-        column = info_ref[2] - block
-        column = jnp.where(column < 0, column + columns, column)
-        part_ref[column] = contract(low, w_ref[...], (1, 1)).astype(bf16)
-        piece = jnp.dot(xt_ref[block], low, preferred_element_type=f32)
-        if block == 0:
-            total[...] = piece
-        else:
-            total[...] += piece
-    grad_ref[...] = total[...].astype(bf16)
-
-
-def unproject(info, dq, dk, far_k, dv, far_v, tokens_t, weight, cosine, sine):
+    dk = (near_k_ref[0, :, :width].astype(f32) + far_k_ref[0, :, :width].astype(f32)) * DH ** (-0.5)
+    dv = near_v_ref[0, :, :width].astype(f32) + far_v_ref[0, :, :width].astype(f32)
+    both = jnp.concatenate([dq_ref[0], dk], 1)
+    swapped = jnp.where(even, pltpu.roll(both, lanes - 1, 1), pltpu.roll(both, 1, 1))
+    both = both * widen(cos_ref[0], lanes) - swapped * widen(sin_ref[0], lanes)
+    low = jnp.concatenate([both, dv], 1).astype(bf16)
+    part_ref[0] = contract(low, w_ref[...], (1, 1)).astype(bf16)
+    for block, x_ref in enumerate(x_refs):
+
+        @pl.when(step == block)
+        def _():
+            piece = contract(x_ref[...], low, (0, 0))
+            total[...] = piece if block == 0 else total[...] + piece
+
+    @pl.when(step == len(x_refs) - 1)
+    def _():
+        grad_ref[...] = total[...].astype(bf16)
+
+
+def unproject(info, dq, near, far, blocks, weight, cosine, sine):
     columns, own, width = dq.shape
-    feature = tokens_t.shape[1]
+    feature = blocks[0].shape[1]
+    block = lambda a, first: pl.BlockSpec((1,) + a.shape[1:], lambda i, s: (first + i, 0, 0))
+    whole = lambda a: pl.BlockSpec(a.shape, lambda i, s: (0, 0))
+    place = lambda i, s: (jnp.where(s[2] >= i, s[2] - i, s[2] - i + columns), 0, 0)
     return pl.pallas_call(
         unproject_kernel,
-        in_specs=[pl.BlockSpec(memory_space=pltpu.SMEM)] + [pl.BlockSpec(memory_space=pltpu.VMEM)] * 9,
+        grid_spec=pltpu.PrefetchScalarGridSpec(
+            num_scalar_prefetch=1,
+            grid=(columns,),
+            in_specs=[block(dq, 0), block(near, 0), block(far, 0), block(near, columns), block(far, columns), whole(weight)]
+            + [block(cosine, 0), block(sine, 0)] + [whole(a) for a in blocks],
+            out_specs=[pl.BlockSpec((1, own, feature), place), whole(weight)],
+            scratch_shapes=[pltpu.VMEM(weight.shape, f32)],
+        ),
         out_shape=[jax.ShapeDtypeStruct((columns, own, feature), bf16), jax.ShapeDtypeStruct(weight.shape, bf16)],
-        scratch_shapes=[pltpu.VMEM(weight.shape, f32)],
-        compiler_params=pltpu.CompilerParams(vmem_limit_bytes=20 << 20),
+        compiler_params=pltpu.CompilerParams(vmem_limit_bytes=60 << 20),
         cost_estimate=cost(0.001),
         name="unproject",
-    )(info, dq, dk, far_k, dv, far_v, weight, cosine, sine, tokens_t)
+    )(info, dq, near, far, near, far, weight, cosine, sine, *blocks)
 
 
 def mean_lanes(values):
@@ -341,7 +356,7 @@
 def feed_kernel(info_ref, x_ref, cot_ref, w_ref, *refs):
     parts, _, columns, slab, _ = w_ref.shape
     att_refs, refs = refs[:columns], refs[columns:]
-    result_ref, refs, grad_atts = refs[0], refs[1 + columns :], refs[1 : 1 + columns]
+    result_ref, grad_att_ref, *refs = refs
     grad_one_ref, hidden_ref, act_ref, gin_ref, gtwo_ref, gone_ref, sums_ref, w, slopes, outer, sems = refs
     rows, columns, quarter, _ = w.shape
 
@@ -409,7 +424,7 @@
     lax.fori_loop(0, columns, combine, 0)
     result, normed_two, inverse_two = norm_forward(hidden + outer[...], gain_two, shift_two)
     result_ref[...] = result.astype(bf16)
-    cot = jnp.concatenate([cot_ref[row] for row in range(rows)], 1).astype(f32)
+    cot = cot_ref[...].astype(f32)
     grad_two = norm_backward(cot, normed_two, inverse_two, gain_two)
     grad_two_low = grad_two.astype(bf16)
     gtwo_ref[...] = grad_two_low.T
@@ -425,14 +440,16 @@
     grad_hidden = outer[...]
     grad_one = norm_backward(grad_hidden, normed_one, inverse_one, gain_one)
     grad_one_ref[...] = grad_one
-    gone_ref[...] = grad_one.astype(bf16)
+    grad_one_low = grad_one.astype(bf16)
     for step in range(columns):
         weight = jnp.concatenate([w[row, turned(step), :, mix] for row in range(rows)], 1)
-        grad_atts[step][...] = contract(weight, gone_ref[...], (1, 1)).astype(bf16)
-    sums_ref[0:1, :] = jnp.sum(grad_hidden * normed_one, 0, keepdims=True)
-    sums_ref[1:2, :] = jnp.sum(grad_hidden, 0, keepdims=True)
-    sums_ref[2:3, :] = jnp.sum(cot * normed_two, 0, keepdims=True)
-    sums_ref[3:4, :] = jnp.sum(cot, 0, keepdims=True)
+        grad_att_ref[turned(step)] = contract(weight, grad_one_low, (1, 1)).astype(bf16)
+    sums = [jnp.sum(a, 0, keepdims=True) for a in (grad_hidden * normed_one, grad_hidden, cot * normed_two, cot)]
+    sums = jnp.concatenate(sums, 0)
+    for row in range(rows):
+        mine = slice(row * quarter, (row + 1) * quarter)
+        gone_ref[row] = grad_one_low[:, mine]
+        sums_ref[row] = sums[:, mine].astype(bf16)
 
 
 def feed(info, attended, tokens, cot, weights):
@@ -446,26 +463,27 @@
     tall = jax.ShapeDtypeStruct((feature, own), bf16)
     return pl.pallas_call(
         feed_kernel,
-        in_specs=[smem, vmem, vmem, pl.BlockSpec(memory_space=pl.ANY)] + [vmem] * columns,
-        out_specs=[vmem] * (8 + columns),
-        out_shape=[flat(bf16)]
-        + [jax.ShapeDtypeStruct((quarter, own), bf16)] * columns
-        + [flat(f32), tall, wide, wide, tall, flat(bf16), jax.ShapeDtypeStruct((4, feature), f32)],
+        in_specs=[smem, vmem, vmem, pl.BlockSpec(memory_space=pltpu.HBM)] + [vmem] * columns,
+        out_specs=[vmem] * 9,
+        out_shape=[
+            flat(bf16), jax.ShapeDtypeStruct((columns, quarter, own), bf16), flat(f32), tall, wide, wide, tall,
+            jax.ShapeDtypeStruct((rows, own, quarter), bf16), jax.ShapeDtypeStruct((rows, 4, quarter), bf16),
+        ],
         scratch_shapes=[
             pltpu.VMEM((rows, columns, quarter, lanes), bf16),
             pltpu.VMEM((columns, own, hidden_cols), f32),
             pltpu.VMEM((own, feature), f32),
             pltpu.SemaphoreType.DMA((3, parts)),
         ],
-        compiler_params=pltpu.CompilerParams(vmem_limit_bytes=34 << 20),
+        compiler_params=pltpu.CompilerParams(vmem_limit_bytes=60 << 20),
         cost_estimate=cost(0.001),
         name="feed",
     )(info, tokens, cot, weights, *attended)
 
 
-def weigh_kernel(info_ref, hidden_ref, act_ref, gin_ref, gtwo_ref, gone_ref, sums_ref, *refs):
-    att_refs, (kept_ref, sent_ref, across_ref) = refs[:-3], refs[-3:]
-    _, slabs, _, slab, lanes = kept_ref.shape
+def weigh_kernel(twin, info_ref, hidden_ref, act_ref, gin_ref, gtwo_ref, gone_ref, sums_ref, *refs):
+    att_refs, out_ref = refs[:-1], refs[-1]
+    _, slabs, _, slab, lanes = out_ref.shape
     quarter = slabs * slab
     hidden_cols = act_ref.shape[2]
     columns = len(att_refs)
@@ -474,64 +492,43 @@
     attended = att_refs[0][...]
     for index in range(1, columns):
         attended = jnp.where(step == index, att_refs[index][...], attended)
-    inner = jnp.dot(hidden_ref[...], gin_ref[0], preferred_element_type=f32).astype(bf16)
-    outer = jnp.dot(gtwo_ref[...], act_ref[0], preferred_element_type=f32).astype(bf16)
-    mixed = jnp.dot(attended, gone_ref[...], preferred_element_type=f32).astype(bf16)
+    core = 1 - info_ref[1] if twin else info_ref[1]
     eye = unit(quarter)
     away = lambda index, mine: jnp.where(index == mine, 0, 1)
-    for row in range(4):
-        mine = slice(row * quarter, (row + 1) * quarter)
-        vector = contract(eye, sums_ref[:, mine].astype(bf16), (1, 1)).astype(bf16)
+    for pair in range(2):
+        row = 2 * pair + core
+        mine = pl.ds(pl.multiple_of(row * quarter, quarter), quarter)
+        inner = jnp.dot(hidden_ref[mine, :], gin_ref[0], preferred_element_type=f32).astype(bf16)
+        outer = jnp.dot(gtwo_ref[mine, :], act_ref[0], preferred_element_type=f32).astype(bf16)
+        mixed = jnp.dot(attended, gone_ref[row], preferred_element_type=f32).astype(bf16)
+        vector = contract(eye, sums_ref[row], (1, 1)).astype(bf16)
         rest = jnp.zeros((quarter, lanes - 2 * hidden_cols - quarter - 4), bf16)
-        tail = jnp.concatenate([mixed[:, mine], vector, rest], 1)
-        far = away(row // 2, info_ref[3])
-
-        def write(ref, where, rows):
-            ref[where + (0, slice(None), slice(0, hidden_cols))] = inner[mine][rows]
-            ref[where + (0, slice(None), slice(hidden_cols, 2 * hidden_cols))] = outer[mine][rows]
-            ref[where + (0, slice(None), slice(2 * hidden_cols, lanes))] = tail[rows]
-
+        tail = jnp.concatenate([mixed, vector, rest], 1)
+        far = away(pair, info_ref[3])
         for part in range(slabs):
             place = away(part, info_ref[4]) if slabs > 1 else 0
             rows = slice(part * slab, (part + 1) * slab)
-            kept = info_ref[1] == row % 2
-            beyond = (far == 1) & (place == slabs - 1)
-
-            @pl.when(kept)
-            def _():
-                write(kept_ref, (far, place), rows)
-
-            @pl.when(jnp.logical_not(kept) & beyond)
-            def _():
-                write(across_ref, (), rows)
-
-            @pl.when(jnp.logical_not(kept | beyond))
-            def _():
-                write(sent_ref, (far * slabs + place,), rows)
-
-
-def weigh(info, attended, hidden, act, gin, gtwo, gone, sums, lanes, slabs):
-    feature = hidden.shape[0]
+            out_ref[far, place, 0, :, 0:hidden_cols] = inner[rows]
+            out_ref[far, place, 0, :, hidden_cols : 2 * hidden_cols] = outer[rows]
+            out_ref[far, place, 0, :, 2 * hidden_cols :] = tail[rows]
+
+
+def weigh(twin, info, attended, hidden, act, gin, gtwo, gone, sums, lanes, slabs):
     columns = act.shape[0]
     quarter = attended[0].shape[0]
-    whole = lambda a: pl.BlockSpec(a.shape, lambda i, s: (0, 0))
+    whole = lambda a: pl.BlockSpec(a.shape, lambda i, s: (0,) * a.ndim)
     piece = pl.BlockSpec((1,) + act.shape[1:], lambda i, s: (i, 0, 0))
-    tail = (columns, quarter // slabs, lanes)
-    block = (1,) + tail[1:]
+    slab = quarter // slabs
     return pl.pallas_call(
-        weigh_kernel,
+        lambda *refs: weigh_kernel(twin, *refs),
         grid_spec=pltpu.PrefetchScalarGridSpec(
             num_scalar_prefetch=1,
             grid=(columns,),
             in_specs=[whole(hidden), piece, piece, whole(gtwo), whole(gone), whole(sums)] + [whole(a) for a in attended],
-            out_specs=[
-                pl.BlockSpec((2, slabs) + block, lambda i, s: (0, 0, i, 0, 0)),
-                pl.BlockSpec((2 * slabs - 1,) + block, lambda i, s: (0, i, 0, 0)),
-                pl.BlockSpec(block, lambda i, s: (i, 0, 0)),
-            ],
+            out_specs=pl.BlockSpec((2, slabs, 1, slab, lanes), lambda i, s: (0, 0, i, 0, 0)),
         ),
-        out_shape=[jax.ShapeDtypeStruct(dims + tail, bf16) for dims in ((2, slabs), (2 * slabs - 1,), ())],
-        compiler_params=pltpu.CompilerParams(vmem_limit_bytes=24 << 20),
+        out_shape=jax.ShapeDtypeStruct((2, slabs, columns, slab, lanes), bf16),
+        compiler_params=pltpu.CompilerParams(vmem_limit_bytes=60 << 20),
         cost_estimate=cost(0.001),
         name="weigh",
     )(info, hidden, act, gin, gtwo, gone, sums, *attended)
@@ -542,7 +539,7 @@
     columns = inner_ref.shape[1]
     quarter = output_ref.shape[1]
     slab = out_ref.shape[0]
-    offset = info_ref[4] * slab if slab < quarter else 0
+    offset = info_ref[0] * slab if slab < quarter else 0
     rows = pl.ds(pl.multiple_of(offset, slab), slab)
     values = jnp.concatenate([ref[...] for ref in small_refs], 0)
     high = values.astype(bf16)
@@ -558,7 +555,7 @@
     out_ref[:, 2 * columns :] = jnp.concatenate([output_ref[rows, :], small, fill], 1)
 
 
-def parcel(info, inner, outer, output, vectors, lanes, slabs):
+def parcel(part, inner, outer, output, vectors, lanes, slabs):
     vmem, smem = pl.BlockSpec(memory_space=pltpu.VMEM), pl.BlockSpec(memory_space=pltpu.SMEM)
     return pl.pallas_call(
         parcel_kernel,
@@ -566,7 +563,7 @@
         out_shape=jax.ShapeDtypeStruct((inner.shape[0] // slabs, lanes), bf16),
         cost_estimate=cost(0.001),
         name="parcel",
-    )(info, inner, outer, output, *(v.reshape(1, -1) for v in vectors))
+    )(part, inner, outer, output, *(v.reshape(1, -1) for v in vectors))
 
 
 def keep(values, index, axis=0):
@@ -586,65 +583,71 @@
     return lax.ppermute(values, "col", [(i, (i + step) % columns) for i in range(columns)])
 
 
-def add_kernel(low_only, *refs):
-    total = sum(ref[...].reshape(refs[-1].shape).astype(f32) for ref in refs[:-2])
-    if low_only is None:
-        refs[-1][...] = (total + refs[-2][...].astype(f32)).astype(bf16)
-        return
-    middle = pl.num_programs(0) // 2
-    inside = (pl.program_id(0) < middle) == low_only
-
-    @pl.when(inside)
-    def _():
-        refs[-1][...] = (total + refs[-2][...].astype(f32)).astype(bf16)
-
-    @pl.when(jnp.logical_not(inside))
-    def _():
-        refs[-1][...] = total.astype(bf16)
-
-
-def add_blocks(kept, place, *others, low_only=None):
-    columns = kept.shape[2]
-    block = (1,) + kept.shape[3:]
-    spec = lambda lead: pl.BlockSpec((1,) * len(lead) + block, lambda i: lead + (i, 0, 0))
-    arrays, specs = [kept], [spec(place)]
-    for array, lead in others:
-        arrays.append(array)
-        specs.append(spec(lead))
-    if low_only is not None:
-        middle = columns // 2
-        held = (lambda i: jnp.minimum(i, middle - 1)) if low_only else (lambda i: jnp.maximum(i - middle, 0))
-        specs[-1] = pl.BlockSpec(block, lambda i: (held(i), 0, 0))
+def add_kernel(sums, *refs):
+    count = max(index for index, *_ in sums[-1:]) + 1
+    results, refs = refs[-count - 2 : -2], refs[: -count - 2] + refs[-2:]
+    *sources, buffer, sems = refs
+    copies, rows, first = [], [], 0
+    for number, (index, start, parts) in enumerate(sums):
+        row = []
+        for which, lead, low, high in parts:
+            target = buffer.at[pl.ds(first, high - low)]
+            source = sources[which].at[lead + (pl.ds(low, high - low),)]
+            copies.append(pltpu.make_async_copy(source, target, sems.at[len(copies)]))
+            copies[-1].start()
+            row.append((first, high - low))
+            first += high - low
+        rows.append((index, start, row))
+    for copy in copies:
+        copy.wait()
+    for index, start, row in rows:
+        size = row[0][1]
+        total = sum(buffer[first : first + size].astype(f32) for first, _ in row)
+        results[index][start : start + size] = total.astype(bf16)
+
+
+def add_blocks(arrays, lengths, sums):
+    hbm, vmem = pl.BlockSpec(memory_space=pltpu.HBM), pl.BlockSpec(memory_space=pltpu.VMEM)
+    tail = arrays[0].shape[-2:]
+    parts = [part for *_, each in sums for part in each]
     return pl.pallas_call(
-        lambda *refs: add_kernel(low_only, *refs),
-        grid=(columns,),
-        in_specs=specs,
-        out_specs=spec(()),
-        out_shape=jax.ShapeDtypeStruct(kept.shape[2:], bf16),
-        compiler_params=pltpu.CompilerParams(vmem_limit_bytes=16 << 20),
+        lambda *refs: add_kernel(sums, *refs),
+        in_specs=[hbm] * len(arrays),
+        out_specs=[vmem] * len(lengths),
+        out_shape=[jax.ShapeDtypeStruct((length,) + tail, bf16) for length in lengths],
+        scratch_shapes=[
+            pltpu.VMEM((sum(high - low for *_, low, high in parts),) + tail, bf16),
+            pltpu.SemaphoreType.DMA((len(parts),)),
+        ],
+        compiler_params=pltpu.CompilerParams(vmem_limit_bytes=60 << 20),
         cost_estimate=cost(0.001),
         name="add_blocks",
     )(*arrays)
 
 
-def sum_shards(kept, sent, across, mark):
-    middle = kept.shape[2] // 2
-    across, twin = swap(across, "yb"), swap(sent, "yb")
-    half = lambda span: (kept[1, 1, span].astype(f32) + across[span].astype(f32)).astype(bf16)
-    low, high = half(slice(0, middle)), half(slice(middle, None))
-    mark, low, high = tie(mark, low, high)
-    by_dp, by_ya = swap(low, "dp"), swap(high, "ya")
+def sum_shards(kept, sent, mark):
+    columns = kept.shape[2]
+    middle = columns // 2
+    pair = kept, swap(sent, "yb")
+    both = lambda lead, low, high: [(0, lead, low, high), (1, lead, low, high)]
+    to_dp = [(0, 0, both((1, 1), 0, middle)), (0, middle, both((0, 1), 0, middle))]
+    to_ya = [(1, 0, both((1, 1), middle, columns)), (1, middle, both((1, 0), middle, columns))]
+    to_dp, to_ya = add_blocks(pair, (columns, columns), to_dp + to_ya)
+    mark, to_dp, to_ya = tie(mark, to_dp, to_ya)
+    by_dp, by_ya = swap(to_dp, "dp"), swap(to_ya, "ya")
 
     def sides(mark):
-        low, high, mark = tie(by_dp, by_ya, mark)
-        far_ya = add_blocks(kept, (1, 0), (twin, (2,)), (low, ()), low_only=True)
-        far_dp = add_blocks(kept, (0, 1), (twin, (1,)), (high, ()), low_only=False)
-        mark, far_ya, far_dp = tie(mark, far_ya, far_dp)
-        far_ya, far_dp = swap(far_ya, "ya"), swap(far_dp, "dp")
+        dp, ya, mark = tie(by_dp, by_ya, mark)
+        rest_ya = (0, 0, both((1, 0), 0, middle) + [(2, (), 0, middle)])
+        rest_dp = (1, 0, both((0, 1), middle, columns) + [(3, (), 0, middle)])
+        rest_ya, rest_dp = add_blocks(pair + (dp, ya), (middle, columns - middle), [rest_ya, rest_dp])
+        rest_ya, rest_dp = swap(rest_ya, "ya"), swap(rest_dp, "dp")
 
         def finish(mark):
-            *parts, mark = tie(far_ya, far_dp, mark)
-            own = add_blocks(kept, (0, 0), (twin, (0,)), *((part, ()) for part in parts))
+            low_ya, high_dp, mark = tie(rest_ya, rest_dp, mark)
+            low = both((0, 0), 0, middle) + [(2, (), middle, columns), (4, (), 0, middle)]
+            high = both((0, 0), middle, columns) + [(3, (), middle, columns), (5, (), 0, columns - middle)]
+            (own,) = add_blocks(pair + (dp, ya, low_ya, high_dp), (columns,), [(0, 0, low), (0, middle, high)])
             mine = lax.psum_scatter(own, "col", scatter_dimension=0, tiled=False)
             other = swap(mine, "dp")
             first = lax.axis_index("dp") == 0
@@ -673,13 +676,22 @@
 
     vectors = (first_gain, first_shift, second_gain, second_shift)
     anchors = spread_dp(source)
-    packed = parcel(info, inner_weight, outer_weight, output_weight, vectors, lanes, slabs)
+    packed = parcel(jnp.reshape(me, (1,)).astype(jnp.int32), inner_weight, outer_weight, output_weight, vectors, lanes, slabs)
     axes = ("dp",) + SHARDS if slabs == 2 else SHARDS
     everywhere = lax.all_gather(packed, axes, axis=0).reshape(slabs, 4, columns, quarter // slabs, lanes)
     anchor = source.reshape(count)
     place = anchor // (dp_count * pack) * share + anchor % share
     holder = anchor % (dp_count * pack) // pack
-    wide_in, wide_cot = spread_dp(inputs), spread_dp(cotangent)
+    wide_in = spread_dp(inputs)
+
+    steps = jnp.arange(columns, dtype=jnp.int32)
+    spots = ((z - steps) % columns * share + half * own)[:, None] + jnp.arange(own, dtype=jnp.int32)[None, :]
+    frequency = 10000.0 ** (-2.0 * jnp.arange(DH // 2, dtype=f32) / DH)
+    angles = (spots - jnp.where(spots >= boundary, boundary, 0)).astype(f32)[..., None] * jnp.tile(jnp.repeat(frequency, 2), 2)
+    signs = jnp.where(jnp.arange(2 * DH) % 2 == 0, -1.0, 1.0)
+    cosine, sine = jnp.cos(angles), jnp.sin(angles) * signs
+    wide_in, cosine, sine = tie(wide_in, cosine, sine)
+
     if dp_count == 2:
         pick = (holder * count + place)[:, None] == jnp.arange(dp_count * count, dtype=jnp.int32)[None, :]
         pick = pick.astype(bf16).reshape(count, dp_count, micro, share)
@@ -691,32 +703,25 @@
         return lax.all_to_all(dealt.reshape(4, own, quarter), ROWS, split_axis=0, concat_axis=0, tiled=True)
 
     dealt = deal(wide_in)
-    query_weight, dealt = tie(query_weight, dealt)
     tokens = to_tokens(dealt).transpose(1, 0, 2).reshape(own, feature)
-    wide_cot, tokens = tie(wide_cot, tokens)
-    cot = to_tokens(deal(wide_cot))
+    cotangent, query_weight, tokens = tie(cotangent, query_weight, tokens)
+    wide_cot, tokens = tie(spread_dp(cotangent), tokens)
+    blocks = [shift(tokens, step) for step in range(columns)]
+    cot = to_tokens(deal(wide_cot)).transpose(1, 0, 2).reshape(own, feature)
     qkv_weight = jnp.concatenate([query_weight, key_weight, value_weight], 1)
     qkv_weight = gather_rows(qkv_weight).reshape(feature, -1)
 
-    steps = jnp.arange(columns, dtype=jnp.int32)
-    spots = ((z - steps) % columns * share + half * own)[:, None] + jnp.arange(own, dtype=jnp.int32)[None, :]
-    frequency = 10000.0 ** (-2.0 * jnp.arange(DH // 2, dtype=f32) / DH)
-    angles = (spots - jnp.where(spots >= boundary, boundary, 0)).astype(f32)[..., None] * jnp.tile(jnp.repeat(frequency, 2), 2)
-    signs = jnp.where(jnp.arange(2 * DH) % 2 == 0, -1.0, 1.0)
-    cosine, sine = jnp.cos(angles), jnp.sin(angles) * signs
-
-    blocks = [shift(tokens, step) for step in range(columns)]
-    blocks[-1], cot = tie(blocks[-1], cot)
-    q, kv, turned, tokens_t = project(blocks, qkv_weight, cosine, sine)
+    blocks[-1], cot, anchors = tie(blocks[-1], cot, anchors)
+    q, kv, turned = project(blocks, qkv_weight, cosine, sine)
     kv_twin, turned_twin = swap(kv, "yb"), swap(turned, "yb")
     mixed, lses = attend_forward(1, columns - 1, info, q, kv, kv_twin, turned, turned_twin, share)
-    q, mixed, cot = tie(q, mixed, cot)
+    q, mixed = tie(q, mixed)
     last = attend_forward(0, 1, info, q, kv, kv_twin, turned, turned_twin, share)
     mixed, lses = last[0] + mixed, last[1] + lses
     attended = [shift(mixed[step], -step) for step in range(columns)]
 
-    result, *grad_att, grad_one, hidden, act, gin, gtwo, gone, sums = feed(info, attended, tokens, cot, everywhere)
-    grad_att = [shift(grad_att[step], step) for step in range(columns)]
+    result, grad_att, grad_one, hidden, act, gin, gtwo, gone, sums = feed(info, attended, tokens, cot, everywhere)
+    grad_att = lax.all_to_all(grad_att, "col", split_axis=0, concat_axis=0, tiled=True)
     def to_loader(*rows):
         cut = jnp.concatenate([a.astype(bf16).reshape(own, 4, quarter).transpose(1, 0, 2) for a in rows], 2)
         cut = jnp.broadcast_to(cut[None], (dp_count,) + cut.shape).reshape(dp_count * 4, own, -1)
@@ -732,37 +737,40 @@
         order = jnp.argsort(anchors.reshape(-1))
         spots_in = jnp.searchsorted(anchors.reshape(-1)[order], wanted)
         settle = lambda wide: wide[order[spots_in]].T
-    kept, sent, across = weigh(info, attended, hidden, act, gin, gtwo, gone, sums, lanes, slabs)
+    pieces = (hidden, act, gin, gtwo, gone, sums)
+    sent = weigh(True, info, attended, *pieces, lanes, slabs)
+    act, sent = tie(act, sent)
+    kept = weigh(False, info, attended, hidden, act, *pieces[2:], lanes, slabs)
     if slabs == 2:
-        grad_att, sides = sum_shards(kept, sent, across, grad_att)
+        grad_att, sides = sum_shards(kept, sent, grad_att)
     else:
         flip = lambda a, index, axis: jnp.where(index == 0, a, jnp.flip(a, axis))
-        sent = jnp.stack([sent[0], across])[:, None]
         cut = flip(flip(jnp.stack([kept, sent], 1), m, 0), half, 1).reshape(4 * columns, quarter, lanes)
         summed = lax.psum_scatter(cut, SHARDS, scatter_dimension=0, tiled=False)
         summed = lax.psum(summed, "dp").astype(f32)
 
-    dq, dk, dv, far_k, far_v = attend_backward(info, q, kv, kv_twin, turned, turned_twin, grad_att, mixed, lses, share)
-    far_k, far_v = swap(far_k, "yb"), swap(far_v, "yb")
+    dq, near, far = attend_backward(info, q, kv, kv_twin, turned, turned_twin, grad_att, mixed, lses, share)
+    far = swap(far, "yb")
+    partial, grad_qkv = unproject(info, dq, near, far, blocks, qkv_weight, cosine, sine)
     if slabs == 2:
-        dq, finish = sides(dq)
-    partial, grad_qkv = unproject(info, dq, dk, far_k, dv, far_v, tokens_t, qkv_weight, cosine, sine)
+        grad_qkv, finish = sides(grad_qkv)
     partial = lax.all_to_all(partial, "col", split_axis=0, concat_axis=0, tiled=True)
     grad_tokens = grad_one + jnp.sum(partial.astype(f32), 0)
-
-    grad_qkv = grad_qkv.reshape(2, 2, quarter, 3 * width)
-    for axis, index, place_axis in (("yb", half, 1), ("ya", m, 0)):
-        kept, sent = keep(grad_qkv, index, place_axis)
-        grad_qkv = (kept.astype(f32) + swap(sent, axis).astype(f32)).astype(bf16)
-        if slabs == 2 and axis == "yb":
-            summed, grad_qkv = finish(grad_qkv)
 
     def over_dp(values):
         if dp_count == 2:
             return values.astype(f32) + swap(values, "dp").astype(f32)
         return lax.psum(values, "dp").astype(f32)
 
-    grad_qkv = over_dp(grad_qkv)
+    def halve(grad, axis, index, place_axis):
+        kept, sent = keep(grad, index, place_axis)
+        return (kept.astype(f32) + swap(sent, axis).astype(f32)).astype(bf16)
+
+    grad_qkv = halve(grad_qkv.reshape(2, 2, quarter, 3 * width), "yb", half, 1)
+    if slabs == 2:
+        summed, grad_qkv = finish(grad_qkv)
+    grad_qkv = over_dp(halve(grad_qkv, "ya", m, 0))
+    grad_tokens, grad_qkv = tie(grad_tokens, grad_qkv)
     sum_inner, sum_outer = summed[:, :hidden_cols], summed[:, hidden_cols : 2 * hidden_cols]
     sum_output = summed[:, 2 * hidden_cols : 2 * hidden_cols + quarter]
     sum_vectors = summed[:, 2 * hidden_cols + quarter : 2 * hidden_cols + quarter + 4].T

time: 324 us -> 327 us (level); the launches traced: 318 us -> 325 us
  Pallas kernels: 69.7 us -> 95.4 us
  local copies, waits for them, and re-layouts: 36.8 us -> 16.2 us
  waiting for transfers between devices: 121 us -> 133 us
  starting transfers between devices: 56.6 us -> 46.8 us
    ppermute x19 -> x17, waiting for transfers between devices: 77.4 us -> 52 us  [swap(): return lax.ppermute(values, axis, SWAP)]
    all_to_all x1, waiting for transfers between devices: 0.01 us -> 18.8 us  [to_loader(): lax.all_to_all(cut, ('dp',) + ROWS, split_axis=0, concat_axis=0, tiled=True)]
    unnamed x74 -> x48, local copies, waits for them, and re-layouts: 22.9 us -> 4.47 us
    pallas_call x5 -> x6, Pallas kernels: 18.7 us -> 35.9 us  [the longest x2 14.3 us: weigh(): pl.pallas_call(lambda *refs: weigh_kernel(twin, *refs), grid_spec=pltpu.P...]
    ppermute x9 -> x6, waiting for transfers between devices: 33.3 us -> 49.7 us  [shift(): lax.ppermute(values, 'col', [(i, (i + step) % columns) for i in range(col...]
    ppermute x9 -> x6, starting transfers between devices: 14.3 us -> 6.67 us  [shift(): lax.ppermute(values, 'col', [(i, (i + step) % columns) for i in range(col...]
    ppermute x19 -> x17, starting transfers between devices: 24.2 us -> 20.4 us  [swap(): return lax.ppermute(values, axis, SWAP)]
    all_to_all x0 -> x1, starting transfers between devices: none -> 3.73 us  [body(): lax.all_to_all(grad_att, 'col', split_axis=0, concat_axis=0, tiled=True)]
  transfers between devices with their start and end apart: 34 -> 30, of which waited for: 17 -> 18; matrix products, arithmetic and copies ran while one was open for 9% -> 9% of each run, Pallas kernels for 12% -> 22%
where the time goes in v4:
time: 327 us; the launch traced here: 325 us
  waiting for transfers between devices  133 us (41%)
  Pallas kernels  95.4 us (29%)
  starting transfers between devices  46.8 us (14%)
  local copies, waits for them, and re-layouts  16.2 us (5%)
  between operations  15.8 us (5%)
  other arithmetic  12.9 us (4%)
  matrix products  5.5 us (2%)
    ppermute x17, waiting for transfers between devices, swap(): return lax.ppermute(values, axis, SWAP)  52 us
    ppermute x6, waiting for transfers between devices, shift(): lax.ppermute(values, 'col', [(i, (i + step) % columns) for i in range(col...  49.7 us
    ppermute x17, starting transfers between devices, swap(): return lax.ppermute(values, axis, SWAP)  20.4 us
    all_to_all x1, waiting for transfers between devices, to_loader(): lax.all_to_all(cut, ('dp',) + ROWS, split_axis=0, concat_axis=0, tiled=True)  18.8 us
    pallas_call x1, Pallas kernels, attend_backward(): pl.pallas_call(lambda *refs: backward_kernel(columns, share, *refs), in_s...  18 us
    pallas_call x2, Pallas kernels, attend_forward(): pl.pallas_call(lambda *refs: forward_kernel(first, share, *refs), grid_sp...  17.9 us
    pallas_call x1, Pallas kernels, feed(): pl.pallas_call(feed_kernel, in_specs=[smem, vmem, vmem, pl.BlockSpec(memo...  15.8 us
    pallas_call x2, Pallas kernels, weigh(): pl.pallas_call(lambda *refs: weigh_kernel(twin, *refs), grid_spec=pltpu.P...  14.3 us
  transfers between devices with their start and end apart: 30, of which 18 were waited for; matrix products, arithmetic and copies ran while one was open for 9% of the time, Pallas kernels for 22%

profile of v4, /device:TPU:0, one launch (start us, length us, event | category | flops | bytes accessed | tf_op | source)
XLA Modules:
  0.0 325.3 jit_solution(17246556383989197378)
XLA Ops:
  7.2 2.2 parcel.1
  9.5 3.0 collective-permute-start
  16.2 3.0 fusion.30
  19.3 2.5 collective-permute-done
  22.0 1.8 fusion.24
  24.6 3.5 %all-to-all-start = ((bf16[4,256,192]{1,2,0:T(8,128)(2,1)}), bf16[4,256,192]{1,2,0:T(8,128)(2,1)S(1)}, u32[]{:S(2)}, u32[]{:S(2)}) async-start(bf16[4,256,192]{1,2,0:T(8,128)(2,1)} %bitcast.109), calls=%async_computation | async-start | bytes 786432 | tf_op jit(solution)/shard_map/all_to_all | solution.py:703
  28.0 1.8 collective-permute-start.3
  29.9 5.6 %all-to-all-done = bf16[4,256,192]{1,2,0:T(8,128)(2,1)S(1)} async-done(((bf16[4,256,192]{1,2,0:T(8,128)(2,1)}), bf16[4,256,192]{1,2,0:T(8,128)(2,1)S(1)}, u32[]{:S(2)}, u32[]{:S(2)}) %all-to-all-start) | async-done | bytes 393248 | tf_op jit(solution)/shard_map/all_to_all | solution.py:703
  36.0 1.8 collective-permute-start.1
  37.8 6.0 %collective-permute-done.6 = bf16[192,576]{1,0:T(8,128)(2,1)S(1)} collective-permute-done((bf16[192,576]{1,0:T(8,128)(2,1)S(1)}, bf16[192,576]{1,0:T(8,128)(2,1)S(1)}, u32[]{:S(2)}, u32[]{:S(2)}) %collective-permute-start.6) | collective-permute-done | bytes 221216 | tf_op jit(solution)/shard_map/ppermute | solution.py:28
  44.9 7.7 %collective-permute-done.1 = bf16[2,192,512]{2,1,0:T(8,128)(2,1)S(1)} collective-permute-done((bf16[2,192,512]{2,1,0:T(8,128)(2,1)S(1)}, bf16[2,192,512]{2,1,0:T(8,128)(2,1)S(1)}, u32[]{:S(2)}, u32[]{:S(2)}) %collective-permute-start.1) | collective-permute-done | bytes 393248 | tf_op jit(solution)/shard_map/ppermute | solution.py:28
  52.9 3.7 %collective-permute-start.2 = (bf16[256,768]{1,0:T(8,128)(2,1)S(1)}, bf16[256,768]{1,0:T(8,128)(2,1)S(1)}, u32[]{:S(2)}, u32[]{:S(2)}) collective-permute-start(bf16[256,768]{1,0:T(8,128)(2,1)S(1)} %copy.45.refs_0_.x_ref), channel_id=1, source_target_pairs={{0,3},{1,0},{2,1},{3,2},{4,7},{5,4},{6,5},{7,6},{8,11},{9,8},{10,9... | collective-permute-start | bytes 1179656 | tf_op jit(solution)/shard_map/ppermute | solution.py:583
  57.6 1.8 fusion.21
  60.1 3.6 %all-to-all-start.1 = ((bf16[4,256,192]{1,2,0:T(8,128)(2,1)}), bf16[4,256,192]{1,2,0:T(8,128)(2,1)S(1)}, u32[]{:S(2)}, u32[]{:S(2)}) async-start(bf16[4,256,192]{1,2,0:T(8,128)(2,1)} %bitcast.108), calls=%async_computation.1 | async-start | bytes 786432 | tf_op jit(solution)/shard_map/all_to_all | solution.py:703
  65.1 5.9 %all-to-all-done.1 = bf16[4,256,192]{1,2,0:T(8,128)(2,1)S(1)} async-done(((bf16[4,256,192]{1,2,0:T(8,128)(2,1)}), bf16[4,256,192]{1,2,0:T(8,128)(2,1)S(1)}, u32[]{:S(2)}, u32[]{:S(2)}) %all-to-all-start.1) | async-done | bytes 393248 | tf_op jit(solution)/shard_map/all_to_all | solution.py:703
  71.0 4.6 %collective-permute-done.2.refs_3_ = bf16[256,768]{1,0:T(8,128)(2,1)S(1)} collective-permute-done((bf16[256,768]{1,0:T(8,128)(2,1)S(1)}, bf16[256,768]{1,0:T(8,128)(2,1)S(1)}, u32[]{:S(2)}, u32[]{:S(2)}) %collective-permute-start.2) | collective-permute-done | bytes 393248 | tf_op jit(solution)/shard_map/ppermute | solution.py:583
  75.6 5.9 %collective-permute-done.4.refs_1_ = bf16[256,768]{1,0:T(8,128)(2,1)S(1)} collective-permute-done((bf16[256,768]{1,0:T(8,128)(2,1)S(1)}, bf16[256,768]{1,0:T(8,128)(2,1)S(1)}, u32[]{:S(2)}, u32[]{:S(2)}) %collective-permute-start.4) | collective-permute-done | bytes 393248 | tf_op jit(solution)/shard_map/ppermute | solution.py:583
  81.5 36.2 %collective-permute-done.5.refs_2_ = bf16[256,768]{1,0:T(8,128)(2,1)S(1)} collective-permute-done((bf16[256,768]{1,0:T(8,128)(2,1)S(1)}, bf16[256,768]{1,0:T(8,128)(2,1)S(1)}, u32[]{:S(2)}, u32[]{:S(2)}) %collective-permute-start.5) | collective-permute-done | bytes 393248 | tf_op jit(solution)/shard_map/ppermute | solution.py:583
  118.5 5.5 %project.1 = (bf16[4,256,256]{2,1,0:T(8,128)(2,1)}, bf16[8,256,256]{2,1,0:T(8,128)(2,1)}, bf16[8,192,256]{2,1,0:T(8,128)(2,1)}) custom-call(bf16[256,768]{1,0:T(8,128)(2,1)} %copy-done.2, bf16[256,768]{1,0:T(8,128)(2,1)} %copy-done.6, bf16[256,768]{1,0:T(8,128)(2,1)} %copy-done.7, bf16[256,768]{1,0:T(8,128)(2,1)} %copy-done.5, bf16[768,576]{1,0:T(8,128)(2,1)} %bitcast.111, ...), custom_call_target="tpu_custom_call" | custom-call | flops 1000000 | bytes 3000 | tf_op jit(solution)/shard_map/project/pallas_call | solution.py:76
  125.1 3.6 %collective-permute-done.9.refs_5_ = bf16[8,192,256]{2,1,0:T(8,128)(2,1)S(1)} collective-permute-done((bf16[8,192,256]{2,1,0:T(8,128)(2,1)}, bf16[8,192,256]{2,1,0:T(8,128)(2,1)S(1)}, u32[]{:S(2)}, u32[]{:S(2)}) %collective-permute-start.9) | collective-permute-done | bytes 786464 | tf_op jit(solution)/shard_map/ppermute | solution.py:28
  130.0 13.6 %attend_forward.2 = (bf16[192,256]{1,0:T(8,128)(2,1)}, bf16[192,256]{1,0:T(8,128)(2,1)}, bf16[192,256]{1,0:T(8,128)(2,1)}, f32[3,256]{1,0:T(4,128)}, f32[3,256]{1,0:T(4,128)}, /*index=5*/f32[3,256]{1,0:T(4,128)}) custom-call(s32[5]{0:T(128)} %stack.68.refs_0_.info_ref, bf16[4,256,256]{2,1,0:T(8,128)(2,1)} %get-tuple-element.85.refs_1_, ...), custom_call_target="tpu_custom_call" | custom-call | flops 1000000 | bytes 3000 | tf_op jit(solution)/shard_map/attend_forward/pallas_call | solution.py:181
  143.8 1.9 collective-permute-start.12
  146.6 4.3 %attend_forward.3 = (bf16[192,256]{1,0:T(8,128)(2,1)}, f32[3,256]{1,0:T(4,128)}) custom-call(s32[5]{0:T(128)} %stack.68.refs_0_.info_ref, bf16[4,256,256]{2,1,0:T(8,128)(2,1)} %get-tuple-element.85.refs_1_, bf16[8,256,256]{2,1,0:T(8,128)(2,1)} %get-tuple-element.80.refs_2_, bf16[8,256,256]{2,1,0:T(8,128)(2,1)} %copy-done, ...), custom_call_target="tpu_custom_call" | custom-call | flops 1000000 | bytes 3000 | tf_op jit(solution)/shard_map/attend_forward/pallas_call | solution.py:181
  150.9 3.0 collective-permute-done.11.refs_2_.refs_9_
  154.6 15.8 %feed.1 = (bf16[256,768]{1,0:T(8,128)(2,1)}, bf16[4,192,256]{2,1,0:T(8,128)(2,1)}, f32[256,768]{1,0:T(8,128)}, bf16[768,256]{1,0:T(8,128)(2,1)}, bf16[4,256,768]...) custom-call(s32[5]{0:T(128)} %stack.68.refs_0_.info_ref, ...), custom_call_target="tpu_custom_call" | custom-call | flops 1000000 | bytes 3000 | tf_op jit(solution)/shard_map/feed/pallas_call | solution.py:464
  170.5 7.1 %weigh.2 = bf16[2,2,4,96,1792]{4,3,2,1,0:T(8,128)(2,1)} custom-call(s32[5]{0:T(128)} %stack.68.refs_0_.info_ref, bf16[768,256]{1,0:T(8,128)(2,1)} %get-tuple-element.93.refs_1_, bf16[4,256,768]{2,1,0:T(8,128)(2,1)} %get-tuple-element.99.refs_2_, bf16[4,256,768]{2,1,0:T(8,128)(2,1)} %get-tuple-element.95.refs_3_, bf16[768,256]{1,0:T(8,128)(2,1)} %get-tuple-element.96.refs_4_, ...), custom_call_target="tpu_custom_call" | custom-call | flops 1000000 | bytes 3000 | tf_op jit(solution)/shard_map/weigh/pallas_call | solution.py:522
  177.6 3.7 %all-to-all-start.2 = ((bf16[4,192,256]{2,1,0:T(8,128)(2,1)}), bf16[4,192,256]{2,1,0:T(8,128)(2,1)S(1)}, u32[]{:S(2)}, u32[]{:S(2)}) async-start(bf16[4,192,256]{2,1,0:T(8,128)(2,1)} %get-tuple-element.92), calls=%async_computation.2 | async-start | bytes 786432 | tf_op jit(solution)/shard_map/all_to_all | solution.py:724
  181.3 7.2 %weigh.3.refs_0_ = bf16[2,2,4,96,1792]{4,3,2,1,0:T(8,128)(2,1)} custom-call(s32[5]{0:T(128)} %stack.68.refs_0_.info_ref, bf16[768,256]{1,0:T(8,128)(2,1)} %get-tuple-element.93.refs_1_, bf16[4,256,768]{2,1,0:T(8,128)(2,1)} %get-tuple-element.99.refs_2_, bf16[4,256,768]{2,1,0:T(8,128)(2,1)} %get-tuple-element.95.refs_3_, ...), custom_call_target="tpu_custom_call" | custom-call | flops 1000000 | bytes 3000 | tf_op jit(solution)/shard_map/weigh/pallas_call | solution.py:522
  188.5 4.5 %add_blocks.3 = (bf16[4,96,1792]{2,1,0:T(8,128)(2,1)}, bf16[4,96,1792]{2,1,0:T(8,128)(2,1)}) custom-call(bf16[2,2,4,96,1792]{4,3,2,1,0:T(8,128)(2,1)} %weigh.3.refs_0_, bf16[2,2,4,96,1792]{4,3,2,1,0:T(8,128)(2,1)} %collective-permute-done.13.refs_1_), custom_call_target="tpu_custom_call" | custom-call | flops 1000000 | bytes 3000 | tf_op jit(solution)/shard_map/add_blocks/pallas_call | solution.py:613
  193.7 4.1 %collective-permute-start.15 = (bf16[4,96,1792]{2,1,0:T(8,128)(2,1)}, bf16[4,96,1792]{2,1,0:T(8,128)(2,1)S(1)}, u32[]{:S(2)}, u32[]{:S(2)}) collective-permute-start(bf16[4,96,1792]{2,1,0:T(8,128)(2,1)} %get-tuple-element.112), channel_id=1, source_target_pairs={{0,16},{16,0},{1,17},{17,1},{2,18},{18,2},{3,19},{19,3},{4,20},{20... | collective-permute-start | bytes 4128776 | tf_op jit(solution)/shard_map/ppermute | solution.py:28
  197.8 2.0 collective-permute-start.16
  199.8 18.0 %attend_backward.1 = (f32[4,256,192]{2,1,0:T(8,128)}, bf16[8,256,256]{2,1,0:T(8,128)(2,1)}, bf16[8,256,256]{2,1,0:T(8,128)(2,1)}) custom-call(s32[5]{0:T(128)} %stack.68.refs_0_.info_ref, bf16[4,256,256]{2,1,0:T(8,128)(2,1)} %get-tuple-element.85.refs_1_, bf16[8,256,256]{2,1,0:T(8,128)(2,1)} %get-tuple-element.80.refs_2_, bf16[8,256,256]{2,1,0:T(8,128)(2,1)} %copy-done, ...), custom_call_target="tpu_custom_call" | custom-call | flops 1000000 | bytes 3000 | tf_op jit(solution)/shard_map/attend_backward/pallas_call | solution.py:264
  217.8 2.9 collective-permute-done.14.far_k_ref.far_v_ref
  221.6 9.2 %unproject.1 = (bf16[4,256,768]{2,1,0:T(8,128)(2,1)}, bf16[768,576]{1,0:T(8,128)(2,1)}) custom-call(s32[5]{0:T(128)} %stack.68.refs_0_.info_ref, f32[4,256,192]{2,1,0:T(8,128)} %get-tuple-element.108.dq_ref, bf16[8,256,256]{2,1,0:T(8,128)(2,1)} %get-tuple-element.109.near_k_ref.near_v_ref, bf16[8,256,256]{2,1,0:T(8,128)(2,1)} %copy-done.4, ...), custom_call_target="tpu_custom_call" | custom-call | flops 1000000 | bytes 3000 | tf_op jit(solution)/shard_map/unproject/pallas_call | solution.py:318
  230.8 4.9 %all-to-all-start.3 = ((bf16[4,256,768]{2,1,0:T(8,128)(2,1)}), bf16[4,256,768]{2,1,0:T(8,128)(2,1)S(1)}, u32[]{:S(2)}, u32[]{:S(2)}) async-start(bf16[4,256,768]{2,1,0:T(8,128)(2,1)} %get-tuple-element.111), calls=%async_computation.3 | async-start | bytes 3145728 | tf_op jit(solution)/shard_map/all_to_all | solution.py:757
  235.8 2.5 select_bitcast_fusion
  238.3 3.5 %add_blocks.4 = (bf16[2,96,1792]{2,1,0:T(8,128)(2,1)}, bf16[2,96,1792]{2,1,0:T(8,128)(2,1)}) custom-call(bf16[2,2,4,96,1792]{4,3,2,1,0:T(8,128)(2,1)} %weigh.3.refs_0_, bf16[2,2,4,96,1792]{4,3,2,1,0:T(8,128)(2,1)} %collective-permute-done.13.refs_1_, bf16[4,96,1792]{2,1,0:T(8,128)(2,1)} %copy-done.3, bf16[4,96,1792]{2,1,0:T(8,128)(2,1)} %collective-permute-done.16.refs_3_), custom_call_target="tpu_custom_call" | custom-call | flops 1000000 | bytes 3000 | tf_op jit(solution)/shard_map/add_blocks/pallas_call | solution.py:613
  242.0 2.2 collective-permute-start.18
  245.6 14.4 %collective-permute-done.17.refs_4_ = bf16[2,96,1792]{2,1,0:T(8,128)(2,1)S(1)} collective-permute-done((bf16[2,96,1792]{2,1,0:T(8,128)(2,1)}, bf16[2,96,1792]{2,1,0:T(8,128)(2,1)S(1)}, u32[]{:S(2)}, u32[]{:S(2)}) %collective-permute-start.17) | collective-permute-done | bytes 688160 | tf_op jit(solution)/shard_map/ppermute | solution.py:28
  261.0 1.5 collective-permute-start.20
  262.5 4.4 %add_blocks.5 = bf16[4,96,1792]{2,1,0:T(8,128)(2,1)} custom-call(bf16[2,2,4,96,1792]{4,3,2,1,0:T(8,128)(2,1)} %weigh.3.refs_0_, bf16[2,2,4,96,1792]{4,3,2,1,0:T(8,128)(2,1)} %collective-permute-done.13.refs_1_, bf16[4,96,1792]{2,1,0:T(8,128)(2,1)} %copy-done.3, bf16[4,96,1792]{2,1,0:T(8,128)(2,1)} %collective-permute-done.16.refs_3_, ...), custom_call_target="tpu_custom_call" | custom-call | flops 1000000 | bytes 3000 | tf_op jit(solution)/shard_map/add_blocks/pallas_call | solution.py:613
  266.9 2.0 collective-permute-done.20
  271.5 5.3 %collective-permute-done.21 = bf16[192,576]{1,0:T(8,128)(2,1)} collective-permute-done((bf16[192,576]{1,0:T(8,128)(2,1)S(1)}, bf16[192,576]{1,0:T(8,128)(2,1)}, u32[]{:S(2)}, u32[]{:S(2)}) %collective-permute-start.21) | collective-permute-done | bytes 221216 | tf_op jit(solution)/shard_map/ppermute | solution.py:28
  280.1 3.9 %all-to-all-start.4 = ((bf16[8,256,384]{2,1,0:T(8,128)(2,1)}), bf16[8,256,384]{2,1,0:T(8,128)(2,1)S(1)}, u32[]{:S(2)}, u32[]{:S(2)}) async-start(bf16[8,256,384]{2,1,0:T(8,128)(2,1)} %bitcast.40), calls=%async_computation.4 | async-start | bytes 3145728 | tf_op jit(solution)/shard_map/all_to_all | solution.py:728
  284.9 18.8 %all-to-all-done.4 = bf16[8,256,384]{2,1,0:T(8,128)(2,1)S(1)} async-done(((bf16[8,256,384]{2,1,0:T(8,128)(2,1)}), bf16[8,256,384]{2,1,0:T(8,128)(2,1)S(1)}, u32[]{:S(2)}, u32[]{:S(2)}) %all-to-all-start.4) | async-done | bytes 1572896 | tf_op jit(solution)/shard_map/all_to_all | solution.py:728
  303.7 2.0 fusion.12
  305.7 1.5 collective-permute-start.22
  308.2 7.3 %collective-permute-done.22 = bf16[96,1792]{1,0:T(8,128)(2,1)S(1)} collective-permute-done((bf16[96,1792]{1,0:T(8,128)(2,1)}, bf16[96,1792]{1,0:T(8,128)(2,1)S(1)}, u32[]{:S(2)}, u32[]{:S(2)}) %collective-permute-start.22) | collective-permute-done | bytes 344096 | tf_op jit(solution)/shard_map/ppermute | solution.py:28
  (128 shorter events, 28.1 us)
Async XLA Ops:
  7.2 14.6 %copy-start.16 = (bf16[2,192,512]{2,1,0:T(8,128)(2,1)S(1)}, bf16[2,192,512]{2,1,0:T(8,128)(2,1)}, u32[]{:S(2)}) copy-start(bf16[2,192,512]{2,1,0:T(8,128)(2,1)} %param.14) | copy-start | bytes 1179652
  7.2 146.8 %all-gather.3.cloned.1.call-start = ((), (), s32[]{:S(2)}) async-start(), calls=%async_computation.7 | async-start | bytes 11354112 | tf_op jit(solution)/shard_map/all_gather | solution.py:681
  9.5 12.3 %collective-permute-start = (bf16[2,192,512]{2,1,0:T(8,128)(2,1)}, bf16[2,192,512]{2,1,0:T(8,128)(2,1)S(1)}, u32[]{:S(2)}, u32[]{:S(2)}) collective-permute-start(bf16[2,192,512]{2,1,0:T(8,128)(2,1)} %param.14), channel_id=1, source_target_pairs={{0,16},{16,0},{1,17},{17,1},{2,18},{18,2},{3,19},{19,3},{4,20},{20... | collective-permute-start | bytes 1179656 | tf_op jit(solution)/shard_map/ppermute | solution.py:28
  23.7 4.3 %copy-start.22 = (s32[2,512]{1,0:T(2,128)S(1)}, s32[2,512]{1,0:T(2,128)}, u32[]{:S(2)}) copy-start(s32[2,512]{1,0:T(2,128)} %param.17) | copy-start | bytes 12292
  23.7 11.7 %copy-start.18 = (bf16[192,192]{1,0:T(8,128)(2,1)S(1)}, bf16[192,192]{1,0:T(8,128)(2,1)}, u32[]{:S(2)}) copy-start(bf16[192,192]{1,0:T(8,128)(2,1)} %param.20) | copy-start | bytes 221188
  23.8 11.7 %copy-start.19 = (bf16[192,192]{1,0:T(8,128)(2,1)S(1)}, bf16[192,192]{1,0:T(8,128)(2,1)}, u32[]{:S(2)}) copy-start(bf16[192,192]{1,0:T(8,128)(2,1)} %param.19) | copy-start | bytes 221188
  23.8 11.7 %copy-start.20 = (bf16[192,192]{1,0:T(8,128)(2,1)S(1)}, bf16[192,192]{1,0:T(8,128)(2,1)}, u32[]{:S(2)}) copy-start(bf16[192,192]{1,0:T(8,128)(2,1)} %param.18) | copy-start | bytes 221188
  23.8 12.2 %copy-start.17 = (bf16[2,192,512]{2,1,0:T(8,128)(2,1)S(1)}, bf16[2,192,512]{2,1,0:T(8,128)(2,1)}, u32[]{:S(2)}) copy-start(bf16[2,192,512]{2,1,0:T(8,128)(2,1)} %param.15) | copy-start | bytes 1179652
  24.6 10.9 %all-to-all-start = ((bf16[4,256,192]{1,2,0:T(8,128)(2,1)}), bf16[4,256,192]{1,2,0:T(8,128)(2,1)S(1)}, u32[]{:S(2)}, u32[]{:S(2)}) async-start(bf16[4,256,192]{1,2,0:T(8,128)(2,1)} %bitcast.109), calls=%async_computation | async-start | bytes 786432 | tf_op jit(solution)/shard_map/all_to_all | solution.py:703
  28.0 8.0 %collective-permute-start.3 = (s32[2,512]{1,0:T(2,128)S(1)}, s32[2,512]{1,0:T(2,128)S(1)}, u32[]{:S(2)}, u32[]{:S(2)}) collective-permute-start(s32[2,512]{1,0:T(2,128)S(1)} %copy-done.22), channel_id=1, source_target_pairs={{0,16},{16,0},{1,17},{17,1},{2,18},{18,2},{3,19},{19,3},{4,20},{20... | collective-permute-start | bytes 12296 | tf_op jit(solution)/shard_map/ppermute | solution.py:28
  35.6 8.2 %collective-permute-start.6 = (bf16[192,576]{1,0:T(8,128)(2,1)S(1)}, bf16[192,576]{1,0:T(8,128)(2,1)S(1)}, u32[]{:S(2)}, u32[]{:S(2)}) collective-permute-start(bf16[192,576]{1,0:T(8,128)(2,1)S(1)} %pad_maximum_fusion.5), channel_id=1, source_target_pairs={{0,8},{8,0},{1,9},{9,1},{2,10},{10,2},{3,11},{11,3},{4,12},{12,4},... | collective-permute-start | bytes 663560 | tf_op jit(solution)/shard_map/ppermute | solution.py:28
  36.0 16.6 %collective-permute-start.1 = (bf16[2,192,512]{2,1,0:T(8,128)(2,1)S(1)}, bf16[2,192,512]{2,1,0:T(8,128)(2,1)S(1)}, u32[]{:S(2)}, u32[]{:S(2)}) collective-permute-start(bf16[2,192,512]{2,1,0:T(8,128)(2,1)S(1)} %copy-done.17), channel_id=1, source_target_pairs={{0,16},{16,0},{1,17},{17,1},{2,18},{18,2},{3,19},{19,3},{4,20},{20... | collective-permute-start | bytes 1179656 | tf_op jit(solution)/shard_map/ppermute | solution.py:28
  44.9 18.9 %collective-permute-start.7 = (bf16[2,192,576]{2,1,0:T(8,128)(2,1)}, bf16[2,192,576]{2,1,0:T(8,128)(2,1)S(1)}, u32[]{:S(2)}, u32[]{:S(2)}) collective-permute-start(bf16[2,192,576]{2,1,0:T(8,128)(2,1)} %pad_maximum_fusion.4), channel_id=1, source_target_pairs={{0,4},{4,0},{1,5},{5,1},{2,6},{6,2},{3,7},{7,3},{8,12},{12,8},{9,1... | collective-permute-start | bytes 1327112 | tf_op jit(solution)/shard_map/ppermute | solution.py:28
  52.9 6.5 %copy-start.2 = (bf16[256,768]{1,0:T(8,128)(2,1)}, bf16[256,768]{1,0:T(8,128)(2,1)S(1)}, u32[]{:S(2)}) copy-start(bf16[256,768]{1,0:T(8,128)(2,1)S(1)} %copy.45.refs_0_.x_ref) | copy-start | bytes 1179652
  52.9 22.7 %collective-permute-start.2 = (bf16[256,768]{1,0:T(8,128)(2,1)S(1)}, bf16[256,768]{1,0:T(8,128)(2,1)S(1)}, u32[]{:S(2)}, u32[]{:S(2)}) collective-permute-start(bf16[256,768]{1,0:T(8,128)(2,1)S(1)} %copy.45.refs_0_.x_ref), channel_id=1, source_target_pairs={{0,3},{1,0},{2,1},{3,2},{4,7},{5,4},{6,5},{7,6},{8,11},{9,8},{10,9... | collective-permute-start | bytes 1179656 | tf_op jit(solution)/shard_map/ppermute | solution.py:583
  56.7 24.9 %collective-permute-start.4 = (bf16[256,768]{1,0:T(8,128)(2,1)S(1)}, bf16[256,768]{1,0:T(8,128)(2,1)S(1)}, u32[]{:S(2)}, u32[]{:S(2)}) collective-permute-start(bf16[256,768]{1,0:T(8,128)(2,1)S(1)} %copy.45.refs_0_.x_ref), channel_id=1, source_target_pairs={{0,1},{1,2},{2,3},{3,0},{4,5},{5,6},{6,7},{7,4},{8,9},{9,10},{10,1... | collective-permute-start | bytes 1179656 | tf_op jit(solution)/shard_map/ppermute | solution.py:583
  56.7 61.1 %collective-permute-start.5 = (bf16[256,768]{1,0:T(8,128)(2,1)S(1)}, bf16[256,768]{1,0:T(8,128)(2,1)S(1)}, u32[]{:S(2)}, u32[]{:S(2)}) collective-permute-start(bf16[256,768]{1,0:T(8,128)(2,1)S(1)} %copy.45.refs_0_.x_ref), channel_id=1, source_target_pairs={{0,2},{1,3},{2,0},{3,1},{4,6},{5,7},{6,4},{7,5},{8,10},{9,11},{10,... | collective-permute-start | bytes 1179656 | tf_op jit(solution)/shard_map/ppermute | solution.py:583
  60.1 10.9 %all-to-all-start.1 = ((bf16[4,256,192]{1,2,0:T(8,128)(2,1)}), bf16[4,256,192]{1,2,0:T(8,128)(2,1)S(1)}, u32[]{:S(2)}, u32[]{:S(2)}) async-start(bf16[4,256,192]{1,2,0:T(8,128)(2,1)} %bitcast.108), calls=%async_computation.1 | async-start | bytes 786432 | tf_op jit(solution)/shard_map/all_to_all | solution.py:703
  75.6 42.1 %copy-start.5 = (bf16[256,768]{1,0:T(8,128)(2,1)}, bf16[256,768]{1,0:T(8,128)(2,1)S(1)}, u32[]{:S(2)}) copy-start(bf16[256,768]{1,0:T(8,128)(2,1)S(1)} %collective-permute-done.2.refs_3_) | copy-start | bytes 1179652
  81.5 36.2 %copy-start.6 = (bf16[256,768]{1,0:T(8,128)(2,1)}, bf16[256,768]{1,0:T(8,128)(2,1)S(1)}, u32[]{:S(2)}) copy-start(bf16[256,768]{1,0:T(8,128)(2,1)S(1)} %collective-permute-done.4.refs_1_) | copy-start | bytes 1179652
  124.0 4.7 %collective-permute-start.8 = (bf16[8,256,256]{2,1,0:T(8,128)(2,1)}, bf16[8,256,256]{2,1,0:T(8,128)(2,1)S(1)}, u32[]{:S(2)}, u32[]{:S(2)}) collective-permute-start(bf16[8,256,256]{2,1,0:T(8,128)(2,1)} %get-tuple-element.80.refs_2_), channel_id=1, source_target_pairs={{0,4},{4,0},{1,5},{5,1},{2,6},{6,2},{3,7},{7,3},{8,12},{12,8},{9,1... | collective-permute-start | bytes 3145736 | tf_op jit(solution)/shard_map/ppermute | solution.py:28
  124.0 4.7 %collective-permute-start.9 = (bf16[8,192,256]{2,1,0:T(8,128)(2,1)}, bf16[8,192,256]{2,1,0:T(8,128)(2,1)S(1)}, u32[]{:S(2)}, u32[]{:S(2)}) collective-permute-start(bf16[8,192,256]{2,1,0:T(8,128)(2,1)} %get-tuple-element.81.refs_4_), channel_id=1, source_target_pairs={{0,4},{4,0},{1,5},{5,1},{2,6},{6,2},{3,7},{7,3},{8,12},{12,8},{9,1... | collective-permute-start | bytes 2359304 | tf_op jit(solution)/shard_map/ppermute | solution.py:28
  128.7 1.3 copy-start
  143.7 7.2 %collective-permute-start.10 = (bf16[192,256]{1,0:T(8,128)(2,1)}, bf16[192,256]{1,0:T(8,128)(2,1)S(1)}, u32[]{:S(2)}, u32[]{:S(2)}) collective-permute-start(bf16[192,256]{1,0:T(8,128)(2,1)} %get-tuple-element.87.refs_8_), channel_id=1, source_target_pairs={{0,3},{1,0},{2,1},{3,2},{4,7},{5,4},{6,5},{7,6},{8,11},{9,8},{10,9... | collective-permute-start | bytes 294920 | tf_op jit(solution)/shard_map/ppermute | solution.py:583
  143.7 10.3 %collective-permute-start.11 = (bf16[192,256]{1,0:T(8,128)(2,1)}, bf16[192,256]{1,0:T(8,128)(2,1)S(1)}, u32[]{:S(2)}, u32[]{:S(2)}) collective-permute-start(bf16[192,256]{1,0:T(8,128)(2,1)} %get-tuple-element.88.refs_9_), channel_id=1, source_target_pairs={{0,2},{1,3},{2,0},{3,1},{4,6},{5,7},{6,4},{7,5},{8,10},{9,11},{10,... | collective-permute-start | bytes 294920 | tf_op jit(solution)/shard_map/ppermute | solution.py:583
  143.8 10.2 %collective-permute-start.12 = (bf16[192,256]{1,0:T(8,128)(2,1)}, bf16[192,256]{1,0:T(8,128)(2,1)S(1)}, u32[]{:S(2)}, u32[]{:S(2)}) collective-permute-start(bf16[192,256]{1,0:T(8,128)(2,1)} %get-tuple-element.89.refs_10_), channel_id=1, source_target_pairs={{0,1},{1,2},{2,3},{3,0},{4,5},{5,6},{6,7},{7,4},{8,9},{9,10},{10,1... | collective-permute-start | bytes 294920 | tf_op jit(solution)/shard_map/ppermute | solution.py:583
  150.9 3.1 copy-start.9
  177.6 11.0 %collective-permute-start.13 = (bf16[2,2,4,96,1792]{4,3,2,1,0:T(8,128)(2,1)}, bf16[2,2,4,96,1792]{4,3,2,1,0:T(8,128)(2,1)}, u32[]{:S(2)}, u32[]{:S(2)}) collective-permute-start(bf16[2,2,4,96,1792]{4,3,2,1,0:T(8,128)(2,1)} %weigh.2), channel_id=1, source_target_pairs={{0,4},{4,0},{1,5},{5,1},{2,6},{6,2},{3,7},{7,3},{8,12},{12,8},{9,1... | collective-permute-start | bytes 16515080 | tf_op jit(solution)/shard_map/ppermute | solution.py:28
  177.6 16.1 %all-to-all-start.2 = ((bf16[4,192,256]{2,1,0:T(8,128)(2,1)}), bf16[4,192,256]{2,1,0:T(8,128)(2,1)S(1)}, u32[]{:S(2)}, u32[]{:S(2)}) async-start(bf16[4,192,256]{2,1,0:T(8,128)(2,1)} %get-tuple-element.92), calls=%async_computation.2 | async-start | bytes 786432 | tf_op jit(solution)/shard_map/all_to_all | solution.py:724
  193.7 6.1 %copy-start.8 = (bf16[4,192,256]{2,1,0:T(8,128)(2,1)}, bf16[4,192,256]{2,1,0:T(8,128)(2,1)S(1)}, u32[]{:S(2)}) copy-start(bf16[4,192,256]{2,1,0:T(8,128)(2,1)S(1)} %all-to-all-done.2.refs_6_) | copy-start | bytes 1179652
  193.7 42.1 %collective-permute-start.15 = (bf16[4,96,1792]{2,1,0:T(8,128)(2,1)}, bf16[4,96,1792]{2,1,0:T(8,128)(2,1)S(1)}, u32[]{:S(2)}, u32[]{:S(2)}) collective-permute-start(bf16[4,96,1792]{2,1,0:T(8,128)(2,1)} %get-tuple-element.112), channel_id=1, source_target_pairs={{0,16},{16,0},{1,17},{17,1},{2,18},{18,2},{3,19},{19,3},{4,20},{20... | collective-permute-start | bytes 4128776 | tf_op jit(solution)/shard_map/ppermute | solution.py:28
  197.8 37.9 %collective-permute-start.16 = (bf16[4,96,1792]{2,1,0:T(8,128)(2,1)}, bf16[4,96,1792]{2,1,0:T(8,128)(2,1)}, u32[]{:S(2)}, u32[]{:S(2)}) collective-permute-start(bf16[4,96,1792]{2,1,0:T(8,128)(2,1)} %get-tuple-element.113), channel_id=1, source_target_pairs={{0,8},{8,0},{1,9},{9,1},{2,10},{10,2},{3,11},{11,3},{4,12},{12,4},... | collective-permute-start | bytes 4128776 | tf_op jit(solution)/shard_map/ppermute | solution.py:28
  217.8 2.9 collective-permute-start.14
  230.8 47.0 %all-to-all-start.3 = ((bf16[4,256,768]{2,1,0:T(8,128)(2,1)}), bf16[4,256,768]{2,1,0:T(8,128)(2,1)S(1)}, u32[]{:S(2)}, u32[]{:S(2)}) async-start(bf16[4,256,768]{2,1,0:T(8,128)(2,1)} %get-tuple-element.111), calls=%async_computation.3 | async-start | bytes 3145728 | tf_op jit(solution)/shard_map/all_to_all | solution.py:757
  235.7 69.9 %reduce-scatter.2.cloned.1.call-start = ((), (), s32[]{:S(2)}) async-start(), calls=%async_computation.6 | async-start | bytes 1720320 | tf_op jit(solution)/shard_map/reduce_scatter | solution.py:651
  235.8 2.5 copy-start.3
  238.3 5.9 %collective-permute-start.19 = (bf16[2,192,576]{2,1,0:T(8,128)(2,1)}, bf16[2,192,576]{2,1,0:T(8,128)(2,1)S(1)}, u32[]{:S(2)}, u32[]{:S(2)}) collective-permute-start(bf16[2,192,576]{2,1,0:T(8,128)(2,1)} %select_bitcast_fusion), channel_id=1, source_target_pairs={{0,4},{4,0},{1,5},{5,1},{2,6},{6,2},{3,7},{7,3},{8,12},{12,8},{9,1... | collective-permute-start | bytes 1327112 | tf_op jit(solution)/shard_map/ppermute | solution.py:28
  241.8 18.1 %collective-permute-start.17 = (bf16[2,96,1792]{2,1,0:T(8,128)(2,1)}, bf16[2,96,1792]{2,1,0:T(8,128)(2,1)S(1)}, u32[]{:S(2)}, u32[]{:S(2)}) collective-permute-start(bf16[2,96,1792]{2,1,0:T(8,128)(2,1)} %get-tuple-element.117), channel_id=1, source_target_pairs={{0,8},{8,0},{1,9},{9,1},{2,10},{10,2},{3,11},{11,3},{4,12},{12,4},... | collective-permute-start | bytes 2064392 | tf_op jit(solution)/shard_map/ppermute | solution.py:28
  242.0 18.1 %collective-permute-start.18 = (bf16[2,96,1792]{2,1,0:T(8,128)(2,1)}, bf16[2,96,1792]{2,1,0:T(8,128)(2,1)S(1)}, u32[]{:S(2)}, u32[]{:S(2)}) collective-permute-start(bf16[2,96,1792]{2,1,0:T(8,128)(2,1)} %get-tuple-element.118), channel_id=1, source_target_pairs={{0,16},{16,0},{1,17},{17,1},{2,18},{18,2},{3,19},{19,3},{4,20},{20... | collective-permute-start | bytes 2064392 | tf_op jit(solution)/shard_map/ppermute | solution.py:28
  260.0 2.5 copy-start.13
  260.2 2.3 copy-start.14
  261.0 7.9 %collective-permute-start.20 = (bf16[192,576]{1,0:T(8,128)(2,1)}, bf16[192,576]{1,0:T(8,128)(2,1)}, u32[]{:S(2)}, u32[]{:S(2)}) collective-permute-start(bf16[192,576]{1,0:T(8,128)(2,1)} %select_bitcast_fusion.7), channel_id=1, source_target_pairs={{0,8},{8,0},{1,9},{9,1},{2,10},{10,2},{3,11},{11,3},{4,12},{12,4},... | collective-permute-start | bytes 663560 | tf_op jit(solution)/shard_map/ppermute | solution.py:28
  266.9 4.4 %copy-start.15 = (bf16[256,768]{1,0:T(8,128)(2,1)S(1)}, bf16[256,768]{1,0:T(8,128)(2,1)}, u32[]{:S(2)}) copy-start(bf16[256,768]{1,0:T(8,128)(2,1)} %get-tuple-element.90) | copy-start | bytes 1179652
  269.9 6.9 %collective-permute-start.21 = (bf16[192,576]{1,0:T(8,128)(2,1)S(1)}, bf16[192,576]{1,0:T(8,128)(2,1)}, u32[]{:S(2)}, u32[]{:S(2)}) collective-permute-start(bf16[192,576]{1,0:T(8,128)(2,1)S(1)} %fusion.31), channel_id=1, source_target_pairs={{0,16},{16,0},{1,17},{17,1},{2,18},{18,2},{3,19},{19,3},{4,20},{20... | collective-permute-start | bytes 663560 | tf_op jit(solution)/shard_map/ppermute | solution.py:28
  271.5 6.5 %copy-start.12 = (f32[256,768]{1,0:T(8,128)S(1)}, f32[256,768]{1,0:T(8,128)}, u32[]{:S(2)}) copy-start(f32[256,768]{1,0:T(8,128)} %get-tuple-element.91) | copy-start | bytes 2359300
  280.1 23.6 %all-to-all-start.4 = ((bf16[8,256,384]{2,1,0:T(8,128)(2,1)}), bf16[8,256,384]{2,1,0:T(8,128)(2,1)S(1)}, u32[]{:S(2)}, u32[]{:S(2)}) async-start(bf16[8,256,384]{2,1,0:T(8,128)(2,1)} %bitcast.40), calls=%async_computation.4 | async-start | bytes 3145728 | tf_op jit(solution)/shard_map/all_to_all | solution.py:728
  305.7 9.9 %copy-start.21 = (bf16[1,96,1792]{2,1,0:T(8,128)(2,1)S(1)}, bf16[1,96,1792]{2,1,0:T(8,128)(2,1)}, u32[]{:S(2)}) copy-start(bf16[1,96,1792]{2,1,0:T(8,128)(2,1)} %reduce-scatter.2.cloned.1.call-done) | copy-start | bytes 1032196
  305.7 9.9 %collective-permute-start.22 = (bf16[96,1792]{1,0:T(8,128)(2,1)}, bf16[96,1792]{1,0:T(8,128)(2,1)S(1)}, u32[]{:S(2)}, u32[]{:S(2)}) collective-permute-start(bf16[96,1792]{1,0:T(8,128)(2,1)} %bitcast.124), channel_id=1, source_target_pairs={{0,16},{16,0},{1,17},{17,1},{2,18},{18,2},{3,19},{19,3},{4,20},{20... | collective-permute-start | bytes 1032200 | tf_op jit(solution)/shard_map/ppermute | solution.py:28
  (5 other events, 4.0 us)
Sparse Core Ops, SparseCore 0:
  10.9 117.1 all-gather.2
  267.0 32.8 reduce-scatter.1

commit v5 on v4

--- a/solution.py
+++ b/solution.py
@@ -202,7 +202,7 @@
 
 def backward_kernel(columns, share, info_ref, q_ref, kv0_ref, kv1_ref, kt0_ref, kt1_ref, *refs):
     grads, outs, lses, refs = refs[0], refs[1 : columns + 1], refs[columns + 1 : 2 * columns + 1], refs[2 * columns + 1 :]
-    dq_ref, near_ref, far_ref, part_q, part_g, delta, lse, sum_q, sum_k, sum_v = refs
+    dq_ref, near_ref, *fars, part_q, part_g, delta, lse, sum_q, sum_k, sum_v = refs
     own, width = q_ref.shape[1], kt0_ref.shape[1]
     heads = width // DH
     scaling = DH ** (-0.5)
@@ -250,9 +250,9 @@
 
     lax.fori_loop(0, columns, query_step, 0)
     for block in range(columns):
-        for place, sums in ((block, sum_k), (columns + block, sum_v)):
+        for place, sums, far_ref in ((block, sum_k, fars[0]), (columns + block, sum_v, fars[1])):
             near_ref[place] = sums[block, :own].astype(bf16)
-            far_ref[place] = sums[block, own:].astype(bf16)
+            far_ref[block] = sums[block, own:].astype(bf16)
 
 
 def attend_backward(info, q, kv, kv_twin, turned, turned_twin, grads, outs, lses, share):
@@ -264,9 +264,9 @@
     return pl.pallas_call(
         lambda *refs: backward_kernel(columns, share, *refs),
         in_specs=[pl.BlockSpec(memory_space=pltpu.SMEM)] + [vmem] * len(operands),
-        out_specs=[vmem] * 3,
+        out_specs=[vmem] * 4,
         out_shape=[jax.ShapeDtypeStruct((columns, own, width), f32)]
-        + [jax.ShapeDtypeStruct((2 * columns, own, padded), bf16)] * 2,
+        + [jax.ShapeDtypeStruct((many, own, padded), bf16) for many in (2 * columns, columns, columns)],
         scratch_shapes=[
             pltpu.VMEM((columns, heads * own, padded), bf16),
             pltpu.VMEM((columns, padded, heads * own), bf16),
@@ -282,11 +282,7 @@
     )(info, *operands)
 
 
-def unproject_kernel(
-    info_ref, dq_ref, near_k_ref, far_k_ref, near_v_ref, far_v_ref, w_ref, cos_ref, sin_ref, *refs
-):
-    x_refs, (part_ref, grad_ref, total) = refs[:-3], refs[-3:]
-    step = pl.program_id(0)
+def unproject_kernel(info_ref, dq_ref, near_k_ref, far_k_ref, near_v_ref, far_v_ref, w_ref, cos_ref, sin_ref, part_ref, low_ref):
     width = dq_ref.shape[2]
     lanes = 2 * width
     even = lax.broadcasted_iota(jnp.int32, (dq_ref.shape[1], lanes), 1) % 2 == 0
@@ -296,40 +292,50 @@
     swapped = jnp.where(even, pltpu.roll(both, lanes - 1, 1), pltpu.roll(both, 1, 1))
     both = both * widen(cos_ref[0], lanes) - swapped * widen(sin_ref[0], lanes)
     low = jnp.concatenate([both, dv], 1).astype(bf16)
+    low_ref[0] = low
     part_ref[0] = contract(low, w_ref[...], (1, 1)).astype(bf16)
-    for block, x_ref in enumerate(x_refs):
-
-        @pl.when(step == block)
-        def _():
-            piece = contract(x_ref[...], low, (0, 0))
-            total[...] = piece if block == 0 else total[...] + piece
-
-    @pl.when(step == len(x_refs) - 1)
-    def _():
-        grad_ref[...] = total[...].astype(bf16)
-
-
-def unproject(info, dq, near, far, blocks, weight, cosine, sine):
+
+
+def unproject(info, dq, near, far_k, far_v, weight, cosine, sine):
     columns, own, width = dq.shape
-    feature = blocks[0].shape[1]
+    feature = weight.shape[0]
     block = lambda a, first: pl.BlockSpec((1,) + a.shape[1:], lambda i, s: (first + i, 0, 0))
     whole = lambda a: pl.BlockSpec(a.shape, lambda i, s: (0, 0))
     place = lambda i, s: (jnp.where(s[2] >= i, s[2] - i, s[2] - i + columns), 0, 0)
+    low = jax.ShapeDtypeStruct((columns, own, weight.shape[1]), bf16)
     return pl.pallas_call(
         unproject_kernel,
         grid_spec=pltpu.PrefetchScalarGridSpec(
             num_scalar_prefetch=1,
             grid=(columns,),
-            in_specs=[block(dq, 0), block(near, 0), block(far, 0), block(near, columns), block(far, columns), whole(weight)]
-            + [block(cosine, 0), block(sine, 0)] + [whole(a) for a in blocks],
-            out_specs=[pl.BlockSpec((1, own, feature), place), whole(weight)],
-            scratch_shapes=[pltpu.VMEM(weight.shape, f32)],
+            in_specs=[block(dq, 0), block(near, 0), block(far_k, 0), block(near, columns), block(far_v, 0), whole(weight)]
+            + [block(cosine, 0), block(sine, 0)],
+            out_specs=[pl.BlockSpec((1, own, feature), place), block(low, 0)],
         ),
-        out_shape=[jax.ShapeDtypeStruct((columns, own, feature), bf16), jax.ShapeDtypeStruct(weight.shape, bf16)],
+        out_shape=[jax.ShapeDtypeStruct((columns, own, feature), bf16), low],
         compiler_params=pltpu.CompilerParams(vmem_limit_bytes=60 << 20),
         cost_estimate=cost(0.001),
         name="unproject",
-    )(info, dq, near, far, near, far, weight, cosine, sine, *blocks)
+    )(info, dq, near, far_k, near, far_v, weight, cosine, sine)
+
+
+def project_grad_kernel(low_ref, *refs):
+    x_refs, (grad_ref,) = refs[:-1], refs[-1:]
+    total = None
+    for block, x_ref in enumerate(x_refs):
+        piece = contract(x_ref[...], low_ref[block], (0, 0))
+        total = piece if total is None else total + piece
+    grad_ref[...] = total.astype(bf16)
+
+
+def project_grad(low, blocks):
+    return pl.pallas_call(
+        project_grad_kernel,
+        out_shape=jax.ShapeDtypeStruct((blocks[0].shape[1], low.shape[2]), bf16),
+        compiler_params=pltpu.CompilerParams(vmem_limit_bytes=60 << 20),
+        cost_estimate=cost(0.001),
+        name="project_grad",
+    )(low, *blocks)
 
 
 def mean_lanes(values):
@@ -583,46 +589,86 @@
     return lax.ppermute(values, "col", [(i, (i + step) % columns) for i in range(columns)])
 
 
-def add_kernel(sums, *refs):
-    count = max(index for index, *_ in sums[-1:]) + 1
-    results, refs = refs[-count - 2 : -2], refs[: -count - 2] + refs[-2:]
-    *sources, buffer, sems = refs
-    copies, rows, first = [], [], 0
-    for number, (index, start, parts) in enumerate(sums):
+def add_kernel(count, sums, *refs):
+    results, (*sources, buffer, held, sems, ends) = refs[-count - 4 : -4], refs[: -count - 4] + refs[-4:]
+    rows, first, number = [], 0, 0
+    for index, start, parts in sums:
         row = []
         for which, lead, low, high in parts:
-            target = buffer.at[pl.ds(first, high - low)]
             source = sources[which].at[lead + (pl.ds(low, high - low),)]
-            copies.append(pltpu.make_async_copy(source, target, sems.at[len(copies)]))
-            copies[-1].start()
-            row.append((first, high - low))
-            first += high - low
-        rows.append((index, start, row))
+            copy = pltpu.make_async_copy(source, buffer.at[pl.ds(first, high - low)], sems.at[number])
+            copy.start()
+            row.append((first, high - low, copy))
+            first, number = first + high - low, number + 1
+        rows.append(row)
+    copies, first = [], 0
+    for place, ((index, start, _), row) in enumerate(zip(sums, rows)):
+        size = row[0][1]
+        for *_, copy in row:
+            copy.wait()
+        total = sum(buffer[at : at + size].astype(f32) for at, *_ in row)
+        held[first : first + size] = total.astype(bf16)
+        target = results[index].at[pl.ds(start, size)]
+        copies.append(pltpu.make_async_copy(held.at[pl.ds(first, size)], target, ends.at[place]))
+        copies[-1].start()
+        first += size
     for copy in copies:
         copy.wait()
-    for index, start, row in rows:
-        size = row[0][1]
-        total = sum(buffer[first : first + size].astype(f32) for first, _ in row)
-        results[index][start : start + size] = total.astype(bf16)
 
 
 def add_blocks(arrays, lengths, sums):
-    hbm, vmem = pl.BlockSpec(memory_space=pltpu.HBM), pl.BlockSpec(memory_space=pltpu.VMEM)
+    hbm = pl.BlockSpec(memory_space=pltpu.HBM)
     tail = arrays[0].shape[-2:]
     parts = [part for *_, each in sums for part in each]
     return pl.pallas_call(
-        lambda *refs: add_kernel(sums, *refs),
+        lambda *refs: add_kernel(len(lengths), sums, *refs),
         in_specs=[hbm] * len(arrays),
-        out_specs=[vmem] * len(lengths),
+        out_specs=[hbm] * len(lengths),
         out_shape=[jax.ShapeDtypeStruct((length,) + tail, bf16) for length in lengths],
         scratch_shapes=[
             pltpu.VMEM((sum(high - low for *_, low, high in parts),) + tail, bf16),
+            pltpu.VMEM((sum(lengths),) + tail, bf16),
             pltpu.SemaphoreType.DMA((len(parts),)),
+            pltpu.SemaphoreType.DMA((len(sums),)),
         ],
         compiler_params=pltpu.CompilerParams(vmem_limit_bytes=60 << 20),
         cost_estimate=cost(0.001),
         name="add_blocks",
     )(*arrays)
+
+
+def open_kernel(swapped_ref, mine_ref, other_ref, *outs):
+    slab = mine_ref.shape[0]
+    hidden_cols, quarter = outs[0].shape[1], outs[2].shape[1]
+    spans = (0, hidden_cols), (hidden_cols, hidden_cols), (2 * hidden_cols, quarter)
+
+    def write(first, second):
+        for (start, size), out in zip(spans, outs):
+            out[0:slab, :] = first[:, start : start + size].astype(f32)
+            out[slab : 2 * slab, :] = second[:, start : start + size].astype(f32)
+        last = jnp.concatenate([first[:, 2 * hidden_cols + quarter :], second[:, 2 * hidden_cols + quarter :]], 0)
+        outs[3][...] = contract(last[:, 0:4], unit(2 * slab), (0, 0))
+
+    @pl.when(swapped_ref[0] == 0)
+    def _():
+        write(mine_ref[...], other_ref[...])
+
+    @pl.when(swapped_ref[0] != 0)
+    def _():
+        write(other_ref[...], mine_ref[...])
+
+
+def open_shards(part, mine, other, hidden_cols, quarter):
+    vmem, smem = pl.BlockSpec(memory_space=pltpu.VMEM), pl.BlockSpec(memory_space=pltpu.SMEM)
+    lanes = hidden_cols, hidden_cols, quarter
+    return pl.pallas_call(
+        open_kernel,
+        in_specs=[smem, vmem, vmem],
+        out_shape=[jax.ShapeDtypeStruct((quarter, a), f32) for a in lanes] + [jax.ShapeDtypeStruct((4, quarter), f32)],
+        compiler_params=pltpu.CompilerParams(vmem_limit_bytes=16 << 20),
+        cost_estimate=cost(0.001),
+        name="open_shards",
+    )(part, mine, other)
 
 
 def sum_shards(kept, sent, mark):
@@ -641,6 +687,7 @@
         rest_ya = (0, 0, both((1, 0), 0, middle) + [(2, (), 0, middle)])
         rest_dp = (1, 0, both((0, 1), middle, columns) + [(3, (), 0, middle)])
         rest_ya, rest_dp = add_blocks(pair + (dp, ya), (middle, columns - middle), [rest_ya, rest_dp])
+        mark, rest_ya, rest_dp = tie(mark, rest_ya, rest_dp)
         rest_ya, rest_dp = swap(rest_ya, "ya"), swap(rest_dp, "dp")
 
         def finish(mark):
@@ -648,10 +695,10 @@
             low = both((0, 0), 0, middle) + [(2, (), middle, columns), (4, (), 0, middle)]
             high = both((0, 0), middle, columns) + [(3, (), middle, columns), (5, (), 0, columns - middle)]
             (own,) = add_blocks(pair + (dp, ya, low_ya, high_dp), (columns,), [(0, 0, low), (0, middle, high)])
+            own, mark = tie(own, mark)
             mine = lax.psum_scatter(own, "col", scatter_dimension=0, tiled=False)
             other = swap(mine, "dp")
-            first = lax.axis_index("dp") == 0
-            return jnp.concatenate([jnp.where(first, mine, other), jnp.where(first, other, mine)], 0).astype(f32), mark
+            return (mine, other), mark
 
         return mark, finish
 
@@ -703,8 +750,8 @@
         return lax.all_to_all(dealt.reshape(4, own, quarter), ROWS, split_axis=0, concat_axis=0, tiled=True)
 
     dealt = deal(wide_in)
+    cotangent, query_weight, dealt = tie(cotangent, query_weight, dealt)
     tokens = to_tokens(dealt).transpose(1, 0, 2).reshape(own, feature)
-    cotangent, query_weight, tokens = tie(cotangent, query_weight, tokens)
     wide_cot, tokens = tie(spread_dp(cotangent), tokens)
     blocks = [shift(tokens, step) for step in range(columns)]
     cot = to_tokens(deal(wide_cot)).transpose(1, 0, 2).reshape(own, feature)
@@ -749,11 +796,11 @@
         summed = lax.psum_scatter(cut, SHARDS, scatter_dimension=0, tiled=False)
         summed = lax.psum(summed, "dp").astype(f32)
 
-    dq, near, far = attend_backward(info, q, kv, kv_twin, turned, turned_twin, grad_att, mixed, lses, share)
-    far = swap(far, "yb")
-    partial, grad_qkv = unproject(info, dq, near, far, blocks, qkv_weight, cosine, sine)
+    dq, near, *far = attend_backward(info, q, kv, kv_twin, turned, turned_twin, grad_att, mixed, lses, share)
+    partial, low = unproject(info, dq, near, *(swap(each, "yb") for each in far), qkv_weight, cosine, sine)
     if slabs == 2:
-        grad_qkv, finish = sides(grad_qkv)
+        low, finish = sides(low)
+    grad_qkv = project_grad(low, blocks)
     partial = lax.all_to_all(partial, "col", split_axis=0, concat_axis=0, tiled=True)
     grad_tokens = grad_one + jnp.sum(partial.astype(f32), 0)
 
@@ -766,17 +813,25 @@
         kept, sent = keep(grad, index, place_axis)
         return (kept.astype(f32) + swap(sent, axis).astype(f32)).astype(bf16)
 
-    grad_qkv = halve(grad_qkv.reshape(2, 2, quarter, 3 * width), "yb", half, 1)
     if slabs == 2:
         summed, grad_qkv = finish(grad_qkv)
-    grad_qkv = over_dp(halve(grad_qkv, "ya", m, 0))
+    grad_qkv = halve(grad_qkv.reshape(2, 2, quarter, 3 * width), "yb", half, 1)
+    grad_qkv = halve(grad_qkv, "ya", m, 0)
     grad_tokens, grad_qkv = tie(grad_tokens, grad_qkv)
-    sum_inner, sum_outer = summed[:, :hidden_cols], summed[:, hidden_cols : 2 * hidden_cols]
-    sum_output = summed[:, 2 * hidden_cols : 2 * hidden_cols + quarter]
-    sum_vectors = summed[:, 2 * hidden_cols + quarter : 2 * hidden_cols + quarter + 4].T
+    if slabs == 1:
+        grad_qkv = over_dp(grad_qkv)
+        sum_inner, sum_outer = summed[:, :hidden_cols], summed[:, hidden_cols : 2 * hidden_cols]
+        sum_output = summed[:, 2 * hidden_cols : 2 * hidden_cols + quarter]
+        sum_vectors = summed[:, 2 * hidden_cols + quarter : 2 * hidden_cols + quarter + 4].T
 
     shape = lambda a: a.reshape(quarter, micro, share).transpose(1, 0, 2)
-    settled = settle(to_loader(result, grad_tokens))
+    moved = to_loader(result, grad_tokens)
+    if slabs == 2:
+        (mine, other), (moved, mine, grad_qkv) = summed, tie(moved, summed[0], grad_qkv)
+        grad_qkv = over_dp(grad_qkv)
+        part = jnp.reshape(me, (1,)).astype(jnp.int32)
+        sum_inner, sum_outer, sum_output, sum_vectors = open_shards(part, mine, other, hidden_cols, quarter)
+    settled = settle(moved)
     final_out, final_grad = shape(settled[:quarter]), shape(settled[quarter:])
     return (
         final_out, final_grad, grad_qkv[:, :width], grad_qkv[:, width : 2 * width], grad_qkv[:, 2 * width :],

time: 327 us -> 298 us (0.911)
  waiting for transfers between devices: 133 us -> 104 us
  other arithmetic: 12.9 us -> 7.86 us
    reduce_scatter x1, waiting for transfers between devices: 0.02 us -> 14.4 us  [finish(): mine = lax.psum_scatter(own, 'col', scatter_dimension=0, tiled=False)]
    ppermute x17 -> x18, waiting for transfers between devices: 52 us -> 38 us  [swap(): return lax.ppermute(values, axis, SWAP)]
    all_to_all x1, waiting for transfers between devices: 18.8 us -> 4.87 us  [to_loader(): lax.all_to_all(cut, ('dp',) + ROWS, split_axis=0, concat_axis=0, tiled=True)]
    ppermute x6, waiting for transfers between devices: 49.7 us -> 37.6 us  [shift(): lax.ppermute(values, 'col', [(i, (i + step) % columns) for i in range(col...]
    ppermute x6, starting transfers between devices: 6.67 us -> 11.7 us  [shift(): lax.ppermute(values, 'col', [(i, (i + step) % columns) for i in range(col...]
    pallas_call x3 -> x5, Pallas kernels: 12.4 us -> 16.5 us  [the longest x3 11.1 us: add_blocks(): pl.pallas_call(lambda *refs: add_kernel(len(lengths), sums, *refs), in_sp...]
    all_to_all x2, waiting for transfers between devices: 11.5 us -> 7.89 us  [to_tokens(): lax.all_to_all(dealt.reshape(4, own, quarter), ROWS, split_axis=0, concat...]
    ppermute x17 -> x18, starting transfers between devices: 20.4 us -> 17.6 us  [swap(): return lax.ppermute(values, axis, SWAP)]
  transfers between devices with their start and end apart: 30 -> 31, of which waited for: 18 -> 20; matrix products, arithmetic and copies ran while one was open for 9% -> 8% of each run, Pallas kernels for 22% -> 24%
where the time goes in v5:
time: 298 us; the launch traced here: 297 us
  waiting for transfers between devices  104 us (35%)
  Pallas kernels  97.1 us (33%)
  starting transfers between devices  49.9 us (17%)
  local copies, waits for them, and re-layouts  16.6 us (6%)
  between operations  15.8 us (5%)
  other arithmetic  7.86 us (3%)
  matrix products  5.5 us (2%)
    ppermute x18, waiting for transfers between devices, swap(): return lax.ppermute(values, axis, SWAP)  38 us
    ppermute x6, waiting for transfers between devices, shift(): lax.ppermute(values, 'col', [(i, (i + step) % columns) for i in range(col...  37.6 us
    pallas_call x2, Pallas kernels, attend_forward(): pl.pallas_call(lambda *refs: forward_kernel(first, share, *refs), grid_sp...  18.1 us
    pallas_call x1, Pallas kernels, attend_backward(): pl.pallas_call(lambda *refs: backward_kernel(columns, share, *refs), in_s...  17.9 us
    ppermute x18, starting transfers between devices, swap(): return lax.ppermute(values, axis, SWAP)  17.6 us
    pallas_call x1, Pallas kernels, feed(): pl.pallas_call(feed_kernel, in_specs=[smem, vmem, vmem, pl.BlockSpec(memo...  15.7 us
    pallas_call x2, Pallas kernels, weigh(): pl.pallas_call(lambda *refs: weigh_kernel(twin, *refs), grid_spec=pltpu.P...  14.4 us
    reduce_scatter x1, waiting for transfers between devices, finish(): mine = lax.psum_scatter(own, 'col', scatter_dimension=0, tiled=False)  14.4 us
  transfers between devices with their start and end apart: 31, of which 20 were waited for; matrix products, arithmetic and copies ran while one was open for 8% of the time, Pallas kernels for 24%

profile of v5, /device:TPU:0, one launch (start us, length us, event | category | flops | bytes accessed | tf_op | source)
XLA Modules:
  0.0 296.7 jit_solution(13834691508879039629)
XLA Ops:
  7.2 2.2 parcel.1
  9.5 3.0 %collective-permute-start = (bf16[2,192,512]{2,1,0:T(8,128)(2,1)}, bf16[2,192,512]{2,1,0:T(8,128)(2,1)S(1)}, u32[]{:S(2)}, u32[]{:S(2)}) collective-permute-start(bf16[2,192,512]{2,1,0:T(8,128)(2,1)} %param.14), channel_id=1, source_target_pairs={{0,16},{16,0},{1,17},{17,1},{2,18},{18,2},{3,19},{19,3},{4,20},{20... | collective-permute-start | bytes 1179656 | tf_op jit(solution)/shard_map/ppermute | solution.py:28
  16.3 3.0 %fusion.30 = (f32[4,256,128]{2,1,0:T(8,128)}, f32[4,256,128]{2,1,0:T(8,128)}) fusion(f32[128]{0:T(128)S(1)} %compare_select_fusion.2, f32[128]{0:T(128)S(1)} %mul.76, f32[4,256]{1,0:T(4,128)S(1)} %subtract_convert_fusion), kind=kLoop, calls=%fused_computation.28 | loop fusion | flops 262144 | bytes 1053696 | tf_op jit(solution)/shard_map/mul | solution.py:739
  19.4 2.5 collective-permute-done
  22.0 1.8 fusion.24
  24.0 1.8 collective-permute-start.6
  25.8 1.6 collective-permute-start.1
  28.2 3.5 %all-to-all-start = ((bf16[4,256,192]{1,2,0:T(8,128)(2,1)}), bf16[4,256,192]{1,2,0:T(8,128)(2,1)S(1)}, u32[]{:S(2)}, u32[]{:S(2)}) async-start(bf16[4,256,192]{1,2,0:T(8,128)(2,1)} %bitcast.109), calls=%async_computation | async-start | bytes 786432 | tf_op jit(solution)/shard_map/all_to_all | solution.py:750
  33.8 2.1 collective-permute-done.1
  36.0 3.0 %all-to-all-done = bf16[4,256,192]{1,2,0:T(8,128)(2,1)S(1)} async-done(((bf16[4,256,192]{1,2,0:T(8,128)(2,1)}), bf16[4,256,192]{1,2,0:T(8,128)(2,1)S(1)}, u32[]{:S(2)}, u32[]{:S(2)}) %all-to-all-start) | async-done | bytes 393248 | tf_op jit(solution)/shard_map/all_to_all | solution.py:750
  39.2 3.7 %collective-permute-start.2 = (bf16[256,768]{1,0:T(8,128)(2,1)S(1)}, bf16[256,768]{1,0:T(8,128)(2,1)S(1)}, u32[]{:S(2)}, u32[]{:S(2)}) collective-permute-start(bf16[256,768]{1,0:T(8,128)(2,1)S(1)} %copy.45.refs_0_.x_ref), channel_id=1, source_target_pairs={{0,3},{1,0},{2,1},{3,2},{4,7},{5,4},{6,5},{7,6},{8,11},{9,8},{10,9... | collective-permute-start | bytes 1179656 | tf_op jit(solution)/shard_map/ppermute | solution.py:589
  43.9 1.8 fusion.21
  46.5 3.6 %all-to-all-start.1 = ((bf16[4,256,192]{1,2,0:T(8,128)(2,1)}), bf16[4,256,192]{1,2,0:T(8,128)(2,1)S(1)}, u32[]{:S(2)}, u32[]{:S(2)}) async-start(bf16[4,256,192]{1,2,0:T(8,128)(2,1)} %bitcast.108), calls=%async_computation.1 | async-start | bytes 786432 | tf_op jit(solution)/shard_map/all_to_all | solution.py:750
  52.5 4.9 %all-to-all-done.1 = bf16[4,256,192]{1,2,0:T(8,128)(2,1)S(1)} async-done(((bf16[4,256,192]{1,2,0:T(8,128)(2,1)}), bf16[4,256,192]{1,2,0:T(8,128)(2,1)S(1)}, u32[]{:S(2)}, u32[]{:S(2)}) %all-to-all-start.1) | async-done | bytes 393248 | tf_op jit(solution)/shard_map/all_to_all | solution.py:750
  57.3 14.7 %collective-permute-done.2.refs_3_ = bf16[256,768]{1,0:T(8,128)(2,1)S(1)} collective-permute-done((bf16[256,768]{1,0:T(8,128)(2,1)S(1)}, bf16[256,768]{1,0:T(8,128)(2,1)S(1)}, u32[]{:S(2)}, u32[]{:S(2)}) %collective-permute-start.2) | collective-permute-done | bytes 393248 | tf_op jit(solution)/shard_map/ppermute | solution.py:589
  72.1 4.4 %collective-permute-done.4.refs_1_ = bf16[256,768]{1,0:T(8,128)(2,1)S(1)} collective-permute-done((bf16[256,768]{1,0:T(8,128)(2,1)S(1)}, bf16[256,768]{1,0:T(8,128)(2,1)S(1)}, u32[]{:S(2)}, u32[]{:S(2)}) %collective-permute-start.4) | collective-permute-done | bytes 393248 | tf_op jit(solution)/shard_map/ppermute | solution.py:589
  76.5 14.6 %collective-permute-done.5.refs_2_ = bf16[256,768]{1,0:T(8,128)(2,1)S(1)} collective-permute-done((bf16[256,768]{1,0:T(8,128)(2,1)S(1)}, bf16[256,768]{1,0:T(8,128)(2,1)S(1)}, u32[]{:S(2)}, u32[]{:S(2)}) %collective-permute-start.5) | collective-permute-done | bytes 393248 | tf_op jit(solution)/shard_map/ppermute | solution.py:589
  91.8 5.3 %project.1 = (bf16[4,256,256]{2,1,0:T(8,128)(2,1)}, bf16[8,256,256]{2,1,0:T(8,128)(2,1)}, bf16[8,192,256]{2,1,0:T(8,128)(2,1)}) custom-call(bf16[256,768]{1,0:T(8,128)(2,1)} %copy-done.4, bf16[256,768]{1,0:T(8,128)(2,1)} %copy-done.7, bf16[256,768]{1,0:T(8,128)(2,1)} %copy-done.8, bf16[256,768]{1,0:T(8,128)(2,1)} %copy-done.6, bf16[768,576]{1,0:T(8,128)(2,1)} %bitcast.113, ...), custom_call_target="tpu_custom_call" | custom-call | flops 1000000 | bytes 3000 | tf_op jit(solution)/shard_map/project/pallas_call | solution.py:76
  98.3 2.9 collective-permute-done.9.refs_5_
  102.4 13.6 %attend_forward.2 = (bf16[192,256]{1,0:T(8,128)(2,1)}, bf16[192,256]{1,0:T(8,128)(2,1)}, bf16[192,256]{1,0:T(8,128)(2,1)}, f32[3,256]{1,0:T(4,128)}, f32[3,256]{1,0:T(4,128)}, /*index=5*/f32[3,256]{1,0:T(4,128)}) custom-call(s32[5]{0:T(128)} %stack.68.refs_0_.info_ref, bf16[4,256,256]{2,1,0:T(8,128)(2,1)} %get-tuple-element.98.refs_1_, ...), custom_call_target="tpu_custom_call" | custom-call | flops 1000000 | bytes 3000 | tf_op jit(solution)/shard_map/attend_forward/pallas_call | solution.py:181
  116.0 6.4 %collective-permute-start.10 = (bf16[192,256]{1,0:T(8,128)(2,1)}, bf16[192,256]{1,0:T(8,128)(2,1)S(1)}, u32[]{:S(2)}, u32[]{:S(2)}) collective-permute-start(bf16[192,256]{1,0:T(8,128)(2,1)} %get-tuple-element.100.refs_8_), channel_id=1, source_target_pairs={{0,3},{1,0},{2,1},{3,2},{4,7},{5,4},{6,5},{7,6},{8,11},{9,8},{10,9... | collective-permute-start | bytes 294920 | tf_op jit(solution)/shard_map/ppermute | solution.py:589
  123.9 4.4 %attend_forward.3 = (bf16[192,256]{1,0:T(8,128)(2,1)}, f32[3,256]{1,0:T(4,128)}) custom-call(s32[5]{0:T(128)} %stack.68.refs_0_.info_ref, bf16[4,256,256]{2,1,0:T(8,128)(2,1)} %get-tuple-element.98.refs_1_, bf16[8,256,256]{2,1,0:T(8,128)(2,1)} %get-tuple-element.93.refs_2_, bf16[8,256,256]{2,1,0:T(8,128)(2,1)} %copy-done.1, ...), custom_call_target="tpu_custom_call" | custom-call | flops 1000000 | bytes 3000 | tf_op jit(solution)/shard_map/attend_forward/pallas_call | solution.py:181
  128.4 3.9 %collective-permute-done.11.refs_2_.refs_9_ = bf16[192,256]{1,0:T(8,128)(2,1)S(1)} collective-permute-done((bf16[192,256]{1,0:T(8,128)(2,1)}, bf16[192,256]{1,0:T(8,128)(2,1)S(1)}, u32[]{:S(2)}, u32[]{:S(2)}) %collective-permute-start.11) | collective-permute-done | bytes 98336 | tf_op jit(solution)/shard_map/ppermute | solution.py:589
  132.9 15.7 %feed.1 = (bf16[256,768]{1,0:T(8,128)(2,1)}, bf16[4,192,256]{2,1,0:T(8,128)(2,1)}, f32[256,768]{1,0:T(8,128)}, bf16[768,256]{1,0:T(8,128)(2,1)}, bf16[4,256,768]...) custom-call(s32[5]{0:T(128)} %stack.68.refs_0_.info_ref, ...), custom_call_target="tpu_custom_call" | custom-call | flops 1000000 | bytes 3000 | tf_op jit(solution)/shard_map/feed/pallas_call | solution.py:470
  148.7 7.2 %weigh.2 = bf16[2,2,4,96,1792]{4,3,2,1,0:T(8,128)(2,1)} custom-call(s32[5]{0:T(128)} %stack.68.refs_0_.info_ref, bf16[768,256]{1,0:T(8,128)(2,1)} %get-tuple-element.106.refs_1_, bf16[4,256,768]{2,1,0:T(8,128)(2,1)} %get-tuple-element.112.refs_2_, bf16[4,256,768]{2,1,0:T(8,128)(2,1)} %get-tuple-element.108.refs_3_, ...), custom_call_target="tpu_custom_call" | custom-call | flops 1000000 | bytes 3000 | tf_op jit(solution)/shard_map/weigh/pallas_call | solution.py:528
  155.9 3.7 %all-to-all-start.2 = ((bf16[4,192,256]{2,1,0:T(8,128)(2,1)}), bf16[4,192,256]{2,1,0:T(8,128)(2,1)S(1)}, u32[]{:S(2)}, u32[]{:S(2)}) async-start(bf16[4,192,256]{2,1,0:T(8,128)(2,1)} %get-tuple-element.105), calls=%async_computation.2 | async-start | bytes 786432 | tf_op jit(solution)/shard_map/all_to_all | solution.py:771
  159.6 7.2 %weigh.3.refs_0_ = bf16[2,2,4,96,1792]{4,3,2,1,0:T(8,128)(2,1)} custom-call(s32[5]{0:T(128)} %stack.68.refs_0_.info_ref, bf16[768,256]{1,0:T(8,128)(2,1)} %get-tuple-element.106.refs_1_, bf16[4,256,768]{2,1,0:T(8,128)(2,1)} %get-tuple-element.112.refs_2_, bf16[4,256,768]{2,1,0:T(8,128)(2,1)} %get-tuple-element.108.refs_3_, ...), custom_call_target="tpu_custom_call" | custom-call | flops 1000000 | bytes 3000 | tf_op jit(solution)/shard_map/weigh/pallas_call | solution.py:528
  166.8 4.0 %add_blocks.3 = (bf16[4,96,1792]{2,1,0:T(8,128)(2,1)}, bf16[4,96,1792]{2,1,0:T(8,128)(2,1)}) custom-call(bf16[2,2,4,96,1792]{4,3,2,1,0:T(8,128)(2,1)} %weigh.3.refs_0_, bf16[2,2,4,96,1792]{4,3,2,1,0:T(8,128)(2,1)} %collective-permute-done.13.refs_1_), custom_call_target="tpu_custom_call" | custom-call | flops 1000000 | bytes 3000 | tf_op jit(solution)/shard_map/add_blocks/pallas_call | solution.py:623
  173.9 17.9 %attend_backward.1 = (f32[4,256,192]{2,1,0:T(8,128)}, bf16[8,256,256]{2,1,0:T(8,128)(2,1)}, bf16[4,256,256]{2,1,0:T(8,128)(2,1)}, bf16[4,256,256]{2,1,0:T(8,128)(2,1)}) custom-call(s32[5]{0:T(128)} %stack.68.refs_0_.info_ref, bf16[4,256,256]{2,1,0:T(8,128)(2,1)} %get-tuple-element.98.refs_1_, bf16[8,256,256]{2,1,0:T(8,128)(2,1)} %get-tuple-element.93.refs_2_, ...), custom_call_target="tpu_custom_call" | custom-call | flops 1000000 | bytes 3000 | tf_op jit(solution)/shard_map/attend_backward/pallas_call | solution.py:264
  192.3 1.6 collective-permute-done.14.far_k_ref
  195.5 7.0 %unproject.1 = (bf16[4,256,768]{2,1,0:T(8,128)(2,1)}, bf16[4,256,576]{2,1,0:T(8,128)(2,1)}) custom-call(s32[5]{0:T(128)} %stack.68.refs_0_.info_ref, f32[4,256,192]{2,1,0:T(8,128)} %get-tuple-element.121.dq_ref, bf16[8,256,256]{2,1,0:T(8,128)(2,1)} %get-tuple-element.122.near_k_ref.near_v_ref, bf16[4,256,256]{2,1,0:T(8,128)(2,1)} %copy-done.14, ...), custom_call_target="tpu_custom_call" | custom-call | flops 1000000 | bytes 3000 | tf_op jit(solution)/shard_map/unproject/pallas_call | solution.py:306
  202.4 4.0 %all-to-all-start.3 = ((bf16[4,256,768]{2,1,0:T(8,128)(2,1)}), bf16[4,256,768]{2,1,0:T(8,128)(2,1)S(1)}, u32[]{:S(2)}, u32[]{:S(2)}) async-start(bf16[4,256,768]{2,1,0:T(8,128)(2,1)} %get-tuple-element.125), calls=%async_computation.3 | async-start | bytes 3145728 | tf_op jit(solution)/shard_map/all_to_all | solution.py:804
  207.6 3.3 %add_blocks.4 = (bf16[2,96,1792]{2,1,0:T(8,128)(2,1)}, bf16[2,96,1792]{2,1,0:T(8,128)(2,1)}) custom-call(bf16[2,2,4,96,1792]{4,3,2,1,0:T(8,128)(2,1)} %weigh.3.refs_0_, bf16[2,2,4,96,1792]{4,3,2,1,0:T(8,128)(2,1)} %collective-permute-done.13.refs_1_, bf16[4,96,1792]{2,1,0:T(8,128)(2,1)} %copy-done.5, bf16[4,96,1792]{2,1,0:T(8,128)(2,1)} %collective-permute-done.17.refs_3_), custom_call_target="tpu_custom_call" | custom-call | flops 1000000 | bytes 3000 | tf_op jit(solution)/shard_map/add_blocks/pallas_call | solution.py:623
  211.6 3.8 %collective-permute-start.19 = (bf16[2,96,1792]{2,1,0:T(8,128)(2,1)}, bf16[2,96,1792]{2,1,0:T(8,128)(2,1)}, u32[]{:S(2)}, u32[]{:S(2)}) collective-permute-start(bf16[2,96,1792]{2,1,0:T(8,128)(2,1)} %get-tuple-element.135), channel_id=1, source_target_pairs={{0,16},{16,0},{1,17},{17,1},{2,18},{18,2},{3,19},{19,3},{4,20},{20... | collective-permute-start | bytes 2064392 | tf_op jit(solution)/shard_map/ppermute | solution.py:28
  215.4 4.1 %project_grad.1 = bf16[768,576]{1,0:T(8,128)(2,1)} custom-call(bf16[4,256,576]{2,1,0:T(8,128)(2,1)} %get-tuple-element.136.low_ref, bf16[256,768]{1,0:T(8,128)(2,1)} %copy-done.4, bf16[256,768]{1,0:T(8,128)(2,1)} %copy-done.7, bf16[256,768]{1,0:T(8,128)(2,1)} %copy-done.8, bf16[256,768]{1,0:T(8,128)(2,1)} %copy-done.6), custom_call_target="tpu_custom_call" | custom-call | flops 1000000 | bytes 3000 | tf_op jit(solution)/shard_map/project_grad/pallas_call | solution.py:332
  219.5 8.9 %collective-permute-done.18.refs_4_ = bf16[2,96,1792]{2,1,0:T(8,128)(2,1)S(1)} collective-permute-done((bf16[2,96,1792]{2,1,0:T(8,128)(2,1)}, bf16[2,96,1792]{2,1,0:T(8,128)(2,1)S(1)}, u32[]{:S(2)}, u32[]{:S(2)}) %collective-permute-start.18) | collective-permute-done | bytes 688160 | tf_op jit(solution)/shard_map/ppermute | solution.py:28
  228.4 2.5 collective-permute-done.19.refs_5_
  230.9 3.8 %add_blocks.5 = bf16[4,96,1792]{2,1,0:T(8,128)(2,1)} custom-call(bf16[2,2,4,96,1792]{4,3,2,1,0:T(8,128)(2,1)} %weigh.3.refs_0_, bf16[2,2,4,96,1792]{4,3,2,1,0:T(8,128)(2,1)} %collective-permute-done.13.refs_1_, bf16[4,96,1792]{2,1,0:T(8,128)(2,1)} %copy-done.5, bf16[4,96,1792]{2,1,0:T(8,128)(2,1)} %collective-permute-done.17.refs_3_, ...), custom_call_target="tpu_custom_call" | custom-call | flops 1000000 | bytes 3000 | tf_op jit(solution)/shard_map/add_blocks/pallas_call | solution.py:623
  234.9 1.8 collective-permute-done.20
  237.0 1.3 collective-permute-start.21
  239.5 5.5 %collective-permute-done.21 = bf16[192,576]{1,0:T(8,128)(2,1)S(1)} collective-permute-done((bf16[192,576]{1,0:T(8,128)(2,1)S(1)}, bf16[192,576]{1,0:T(8,128)(2,1)S(1)}, u32[]{:S(2)}, u32[]{:S(2)}) %collective-permute-start.21) | collective-permute-done | bytes 221216 | tf_op jit(solution)/shard_map/ppermute | solution.py:28
  248.5 5.7 %all-to-all-start.4 = ((bf16[8,256,384]{2,1,0:T(8,128)(2,1)}), bf16[8,256,384]{2,1,0:T(8,128)(2,1)S(1)}, u32[]{:S(2)}, u32[]{:S(2)}) async-start(bf16[8,256,384]{2,1,0:T(8,128)(2,1)} %bitcast.40), calls=%async_computation.4 | async-start | bytes 3145728 | tf_op jit(solution)/shard_map/all_to_all | solution.py:775
  254.3 14.4 %reduce-scatter.2.cloned.1.call-done = bf16[1,96,1792]{2,1,0:T(8,128)(2,1)} async-done(((bf16[4,96,1792]{2,1,0:T(8,128)(2,1)}), bf16[1,96,1792]{2,1,0:T(8,128)(2,1)}) %reduce-scatter.2.cloned.1.call-update) | async-done | bytes 344080 | tf_op jit(solution)/shard_map/reduce_scatter | solution.py:699
  268.7 1.9 collective-permute-start.23
  270.5 4.9 %all-to-all-done.4 = bf16[8,256,384]{2,1,0:T(8,128)(2,1)S(1)} async-done(((bf16[8,256,384]{2,1,0:T(8,128)(2,1)}), bf16[8,256,384]{2,1,0:T(8,128)(2,1)S(1)}, u32[]{:S(2)}, u32[]{:S(2)}) %all-to-all-start.4) | async-done | bytes 1572896 | tf_op jit(solution)/shard_map/all_to_all | solution.py:775
  275.8 1.9 fusion.12
  278.8 8.2 %collective-permute-done.22 = bf16[192,576]{1,0:T(8,128)(2,1)S(1)} collective-permute-done((bf16[192,576]{1,0:T(8,128)(2,1)S(1)}, bf16[192,576]{1,0:T(8,128)(2,1)S(1)}, u32[]{:S(2)}, u32[]{:S(2)}) %collective-permute-start.22) | collective-permute-done | bytes 221216 | tf_op jit(solution)/shard_map/ppermute | solution.py:28
  287.9 1.3 open_shards.1
  (125 shorter events, 30.4 us)
Async XLA Ops:
  7.2 14.7 %copy-start.16 = (bf16[2,192,512]{2,1,0:T(8,128)(2,1)S(1)}, bf16[2,192,512]{2,1,0:T(8,128)(2,1)}, u32[]{:S(2)}) copy-start(bf16[2,192,512]{2,1,0:T(8,128)(2,1)} %param.14) | copy-start | bytes 1179652
  7.2 125.1 %all-gather.3.cloned.1.call-start = ((), (), s32[]{:S(2)}) async-start(), calls=%async_computation.7 | async-start | bytes 11354112 | tf_op jit(solution)/shard_map/all_gather | solution.py:728
  9.5 12.4 %collective-permute-start = (bf16[2,192,512]{2,1,0:T(8,128)(2,1)}, bf16[2,192,512]{2,1,0:T(8,128)(2,1)S(1)}, u32[]{:S(2)}, u32[]{:S(2)}) collective-permute-start(bf16[2,192,512]{2,1,0:T(8,128)(2,1)} %param.14), channel_id=1, source_target_pairs={{0,16},{16,0},{1,17},{17,1},{2,18},{18,2},{3,19},{19,3},{4,20},{20... | collective-permute-start | bytes 1179656 | tf_op jit(solution)/shard_map/ppermute | solution.py:28
  12.5 13.3 %collective-permute-start.3 = (s32[2,512]{1,0:T(2,128)}, s32[2,512]{1,0:T(2,128)S(1)}, u32[]{:S(2)}, u32[]{:S(2)}) collective-permute-start(s32[2,512]{1,0:T(2,128)} %param.17), channel_id=1, source_target_pairs={{0,16},{16,0},{1,17},{17,1},{2,18},{18,2},{3,19},{19,3},{4,20},{20... | collective-permute-start | bytes 12296 | tf_op jit(solution)/shard_map/ppermute | solution.py:28
  22.0 1.8 copy-start.18
  22.0 1.8 copy-start.19
  22.0 1.8 copy-start.20
  22.0 3.8 %copy-start.21 = (s32[2,512]{1,0:T(2,128)S(1)}, s32[2,512]{1,0:T(2,128)}, u32[]{:S(2)}) copy-start(s32[2,512]{1,0:T(2,128)} %param.17) | copy-start | bytes 12292
  22.0 3.8 %copy-start.17 = (bf16[2,192,512]{2,1,0:T(8,128)(2,1)S(1)}, bf16[2,192,512]{2,1,0:T(8,128)(2,1)}, u32[]{:S(2)}) copy-start(bf16[2,192,512]{2,1,0:T(8,128)(2,1)} %param.15) | copy-start | bytes 1179652
  24.0 8.8 %collective-permute-start.6 = (bf16[192,576]{1,0:T(8,128)(2,1)S(1)}, bf16[192,576]{1,0:T(8,128)(2,1)S(1)}, u32[]{:S(2)}, u32[]{:S(2)}) collective-permute-start(bf16[192,576]{1,0:T(8,128)(2,1)S(1)} %pad_maximum_fusion.5), channel_id=1, source_target_pairs={{0,8},{8,0},{1,9},{9,1},{2,10},{10,2},{3,11},{11,3},{4,12},{12,4},... | collective-permute-start | bytes 663560 | tf_op jit(solution)/shard_map/ppermute | solution.py:28
  25.8 10.0 %collective-permute-start.1 = (bf16[2,192,512]{2,1,0:T(8,128)(2,1)S(1)}, bf16[2,192,512]{2,1,0:T(8,128)(2,1)S(1)}, u32[]{:S(2)}, u32[]{:S(2)}) collective-permute-start(bf16[2,192,512]{2,1,0:T(8,128)(2,1)S(1)} %copy-done.17), channel_id=1, source_target_pairs={{0,16},{16,0},{1,17},{17,1},{2,18},{18,2},{3,19},{19,3},{4,20},{20... | collective-permute-start | bytes 1179656 | tf_op jit(solution)/shard_map/ppermute | solution.py:28
  28.2 10.9 %all-to-all-start = ((bf16[4,256,192]{1,2,0:T(8,128)(2,1)}), bf16[4,256,192]{1,2,0:T(8,128)(2,1)S(1)}, u32[]{:S(2)}, u32[]{:S(2)}) async-start(bf16[4,256,192]{1,2,0:T(8,128)(2,1)} %bitcast.109), calls=%async_computation | async-start | bytes 786432 | tf_op jit(solution)/shard_map/all_to_all | solution.py:750
  33.8 16.3 %collective-permute-start.7 = (bf16[2,192,576]{2,1,0:T(8,128)(2,1)}, bf16[2,192,576]{2,1,0:T(8,128)(2,1)}, u32[]{:S(2)}, u32[]{:S(2)}) collective-permute-start(bf16[2,192,576]{2,1,0:T(8,128)(2,1)} %pad_maximum_fusion.4), channel_id=1, source_target_pairs={{0,4},{4,0},{1,5},{5,1},{2,6},{6,2},{3,7},{7,3},{8,12},{12,8},{9,1... | collective-permute-start | bytes 1327112 | tf_op jit(solution)/shard_map/ppermute | solution.py:28
  39.2 6.5 %copy-start.4 = (bf16[256,768]{1,0:T(8,128)(2,1)}, bf16[256,768]{1,0:T(8,128)(2,1)S(1)}, u32[]{:S(2)}) copy-start(bf16[256,768]{1,0:T(8,128)(2,1)S(1)} %copy.45.refs_0_.x_ref) | copy-start | bytes 1179652
  39.2 32.9 %collective-permute-start.2 = (bf16[256,768]{1,0:T(8,128)(2,1)S(1)}, bf16[256,768]{1,0:T(8,128)(2,1)S(1)}, u32[]{:S(2)}, u32[]{:S(2)}) collective-permute-start(bf16[256,768]{1,0:T(8,128)(2,1)S(1)} %copy.45.refs_0_.x_ref), channel_id=1, source_target_pairs={{0,3},{1,0},{2,1},{3,2},{4,7},{5,4},{6,5},{7,6},{8,11},{9,8},{10,9... | collective-permute-start | bytes 1179656 | tf_op jit(solution)/shard_map/ppermute | solution.py:589
  42.9 33.6 %collective-permute-start.4 = (bf16[256,768]{1,0:T(8,128)(2,1)S(1)}, bf16[256,768]{1,0:T(8,128)(2,1)S(1)}, u32[]{:S(2)}, u32[]{:S(2)}) collective-permute-start(bf16[256,768]{1,0:T(8,128)(2,1)S(1)} %copy.45.refs_0_.x_ref), channel_id=1, source_target_pairs={{0,1},{1,2},{2,3},{3,0},{4,5},{5,6},{6,7},{7,4},{8,9},{9,10},{10,1... | collective-permute-start | bytes 1179656 | tf_op jit(solution)/shard_map/ppermute | solution.py:589
  42.9 48.2 %collective-permute-start.5 = (bf16[256,768]{1,0:T(8,128)(2,1)S(1)}, bf16[256,768]{1,0:T(8,128)(2,1)S(1)}, u32[]{:S(2)}, u32[]{:S(2)}) collective-permute-start(bf16[256,768]{1,0:T(8,128)(2,1)S(1)} %copy.45.refs_0_.x_ref), channel_id=1, source_target_pairs={{0,2},{1,3},{2,0},{3,1},{4,6},{5,7},{6,4},{7,5},{8,10},{9,11},{10,... | collective-permute-start | bytes 1179656 | tf_op jit(solution)/shard_map/ppermute | solution.py:589
  46.5 10.9 %all-to-all-start.1 = ((bf16[4,256,192]{1,2,0:T(8,128)(2,1)}), bf16[4,256,192]{1,2,0:T(8,128)(2,1)S(1)}, u32[]{:S(2)}, u32[]{:S(2)}) async-start(bf16[4,256,192]{1,2,0:T(8,128)(2,1)} %bitcast.108), calls=%async_computation.1 | async-start | bytes 786432 | tf_op jit(solution)/shard_map/all_to_all | solution.py:750
  72.1 19.0 %copy-start.6 = (bf16[256,768]{1,0:T(8,128)(2,1)}, bf16[256,768]{1,0:T(8,128)(2,1)S(1)}, u32[]{:S(2)}) copy-start(bf16[256,768]{1,0:T(8,128)(2,1)S(1)} %collective-permute-done.2.refs_3_) | copy-start | bytes 1179652
  76.5 14.6 %copy-start.7 = (bf16[256,768]{1,0:T(8,128)(2,1)}, bf16[256,768]{1,0:T(8,128)(2,1)S(1)}, u32[]{:S(2)}) copy-start(bf16[256,768]{1,0:T(8,128)(2,1)S(1)} %collective-permute-done.4.refs_1_) | copy-start | bytes 1179652
  97.2 4.0 %collective-permute-start.8 = (bf16[8,256,256]{2,1,0:T(8,128)(2,1)}, bf16[8,256,256]{2,1,0:T(8,128)(2,1)S(1)}, u32[]{:S(2)}, u32[]{:S(2)}) collective-permute-start(bf16[8,256,256]{2,1,0:T(8,128)(2,1)} %get-tuple-element.93.refs_2_), channel_id=1, source_target_pairs={{0,4},{4,0},{1,5},{5,1},{2,6},{6,2},{3,7},{7,3},{8,12},{12,8},{9,1... | collective-permute-start | bytes 3145736 | tf_op jit(solution)/shard_map/ppermute | solution.py:28
  97.2 4.0 %collective-permute-start.9 = (bf16[8,192,256]{2,1,0:T(8,128)(2,1)}, bf16[8,192,256]{2,1,0:T(8,128)(2,1)S(1)}, u32[]{:S(2)}, u32[]{:S(2)}) collective-permute-start(bf16[8,192,256]{2,1,0:T(8,128)(2,1)} %get-tuple-element.94.refs_4_), channel_id=1, source_target_pairs={{0,4},{4,0},{1,5},{5,1},{2,6},{6,2},{3,7},{7,3},{8,12},{12,8},{9,1... | collective-permute-start | bytes 2359304 | tf_op jit(solution)/shard_map/ppermute | solution.py:28
  101.1 0.9 copy-start.3
  101.2 1.2 copy-start.1
  116.0 12.3 %collective-permute-start.10 = (bf16[192,256]{1,0:T(8,128)(2,1)}, bf16[192,256]{1,0:T(8,128)(2,1)S(1)}, u32[]{:S(2)}, u32[]{:S(2)}) collective-permute-start(bf16[192,256]{1,0:T(8,128)(2,1)} %get-tuple-element.100.refs_8_), channel_id=1, source_target_pairs={{0,3},{1,0},{2,1},{3,2},{4,7},{5,4},{6,5},{7,6},{8,11},{9,8},{10,9... | collective-permute-start | bytes 294920 | tf_op jit(solution)/shard_map/ppermute | solution.py:589
  122.4 9.9 %collective-permute-start.11 = (bf16[192,256]{1,0:T(8,128)(2,1)}, bf16[192,256]{1,0:T(8,128)(2,1)S(1)}, u32[]{:S(2)}, u32[]{:S(2)}) collective-permute-start(bf16[192,256]{1,0:T(8,128)(2,1)} %get-tuple-element.101.refs_9_), channel_id=1, source_target_pairs={{0,2},{1,3},{2,0},{3,1},{4,6},{5,7},{6,4},{7,5},{8,10},{9,11},{10,... | collective-permute-start | bytes 294920 | tf_op jit(solution)/shard_map/ppermute | solution.py:589
  122.4 9.9 %collective-permute-start.12 = (bf16[192,256]{1,0:T(8,128)(2,1)}, bf16[192,256]{1,0:T(8,128)(2,1)S(1)}, u32[]{:S(2)}, u32[]{:S(2)}) collective-permute-start(bf16[192,256]{1,0:T(8,128)(2,1)} %get-tuple-element.102.refs_10_), channel_id=1, source_target_pairs={{0,1},{1,2},{2,3},{3,0},{4,5},{5,6},{6,7},{7,4},{8,9},{9,10},{10,1... | collective-permute-start | bytes 294920 | tf_op jit(solution)/shard_map/ppermute | solution.py:589
  128.4 3.9 %copy-start.10 = (bf16[192,256]{1,0:T(8,128)(2,1)}, bf16[192,256]{1,0:T(8,128)(2,1)S(1)}, u32[]{:S(2)}) copy-start(bf16[192,256]{1,0:T(8,128)(2,1)S(1)} %collective-permute-done.10.refs_1_.refs_8_) | copy-start | bytes 294916
  155.9 10.9 %collective-permute-start.13 = (bf16[2,2,4,96,1792]{4,3,2,1,0:T(8,128)(2,1)}, bf16[2,2,4,96,1792]{4,3,2,1,0:T(8,128)(2,1)}, u32[]{:S(2)}, u32[]{:S(2)}) collective-permute-start(bf16[2,2,4,96,1792]{4,3,2,1,0:T(8,128)(2,1)} %weigh.2), channel_id=1, source_target_pairs={{0,4},{4,0},{1,5},{5,1},{2,6},{6,2},{3,7},{7,3},{8,12},{12,8},{9,1... | collective-permute-start | bytes 16515080 | tf_op jit(solution)/shard_map/ppermute | solution.py:28
  155.9 16.1 %all-to-all-start.2 = ((bf16[4,192,256]{2,1,0:T(8,128)(2,1)}), bf16[4,192,256]{2,1,0:T(8,128)(2,1)S(1)}, u32[]{:S(2)}, u32[]{:S(2)}) async-start(bf16[4,192,256]{2,1,0:T(8,128)(2,1)} %get-tuple-element.105), calls=%async_computation.2 | async-start | bytes 786432 | tf_op jit(solution)/shard_map/all_to_all | solution.py:771
  171.9 2.0 copy-start.9
  171.9 34.5 %collective-permute-start.16 = (bf16[4,96,1792]{2,1,0:T(8,128)(2,1)}, bf16[4,96,1792]{2,1,0:T(8,128)(2,1)S(1)}, u32[]{:S(2)}, u32[]{:S(2)}) collective-permute-start(bf16[4,96,1792]{2,1,0:T(8,128)(2,1)} %get-tuple-element.126), channel_id=1, source_target_pairs={{0,16},{16,0},{1,17},{17,1},{2,18},{18,2},{3,19},{19,3},{4,20},{20... | collective-permute-start | bytes 4128776 | tf_op jit(solution)/shard_map/ppermute | solution.py:28
  172.8 33.7 %collective-permute-start.17 = (bf16[4,96,1792]{2,1,0:T(8,128)(2,1)}, bf16[4,96,1792]{2,1,0:T(8,128)(2,1)}, u32[]{:S(2)}, u32[]{:S(2)}) collective-permute-start(bf16[4,96,1792]{2,1,0:T(8,128)(2,1)} %get-tuple-element.127), channel_id=1, source_target_pairs={{0,8},{8,0},{1,9},{9,1},{2,10},{10,2},{3,11},{11,3},{4,12},{12,4},... | collective-permute-start | bytes 4128776 | tf_op jit(solution)/shard_map/ppermute | solution.py:28
  191.8 2.1 collective-permute-start.14
  191.8 2.9 collective-permute-start.15
  202.4 42.7 %all-to-all-start.3 = ((bf16[4,256,768]{2,1,0:T(8,128)(2,1)}), bf16[4,256,768]{2,1,0:T(8,128)(2,1)S(1)}, u32[]{:S(2)}, u32[]{:S(2)}) async-start(bf16[4,256,768]{2,1,0:T(8,128)(2,1)} %get-tuple-element.125), calls=%async_computation.3 | async-start | bytes 3145728 | tf_op jit(solution)/shard_map/all_to_all | solution.py:804
  206.5 62.2 %reduce-scatter.2.cloned.1.call-start = ((), (), s32[]{:S(2)}) async-start(), calls=%async_computation.6 | async-start | bytes 1720320 | tf_op jit(solution)/shard_map/reduce_scatter | solution.py:699
  206.5 1.1 copy-start.5
  210.9 17.5 %collective-permute-start.18 = (bf16[2,96,1792]{2,1,0:T(8,128)(2,1)}, bf16[2,96,1792]{2,1,0:T(8,128)(2,1)S(1)}, u32[]{:S(2)}, u32[]{:S(2)}) collective-permute-start(bf16[2,96,1792]{2,1,0:T(8,128)(2,1)} %get-tuple-element.134), channel_id=1, source_target_pairs={{0,8},{8,0},{1,9},{9,1},{2,10},{10,2},{3,11},{11,3},{4,12},{12,4},... | collective-permute-start | bytes 2064392 | tf_op jit(solution)/shard_map/ppermute | solution.py:28
  211.6 19.3 %collective-permute-start.19 = (bf16[2,96,1792]{2,1,0:T(8,128)(2,1)}, bf16[2,96,1792]{2,1,0:T(8,128)(2,1)}, u32[]{:S(2)}, u32[]{:S(2)}) collective-permute-start(bf16[2,96,1792]{2,1,0:T(8,128)(2,1)} %get-tuple-element.135), channel_id=1, source_target_pairs={{0,16},{16,0},{1,17},{17,1},{2,18},{18,2},{3,19},{19,3},{4,20},{20... | collective-permute-start | bytes 2064392 | tf_op jit(solution)/shard_map/ppermute | solution.py:28
  219.5 15.3 %copy-start.2 = (bf16[768,576]{1,0:T(8,128)(2,1)S(1)}, bf16[768,576]{1,0:T(8,128)(2,1)}, u32[]{:S(2)}) copy-start(bf16[768,576]{1,0:T(8,128)(2,1)} %project_grad.1) | copy-start | bytes 2654212
  228.4 2.6 copy-start.13
  234.8 1.9 collective-permute-start.20
  237.0 8.1 %collective-permute-start.21 = (bf16[192,576]{1,0:T(8,128)(2,1)S(1)}, bf16[192,576]{1,0:T(8,128)(2,1)S(1)}, u32[]{:S(2)}, u32[]{:S(2)}) collective-permute-start(bf16[192,576]{1,0:T(8,128)(2,1)S(1)} %select_bitcast_fusion.7), channel_id=1, source_target_pairs={{0,8},{8,0},{1,9},{9,1},{2,10},{10,2},{3,11},{11,3},{4,12},{12,4},... | collective-permute-start | bytes 663560 | tf_op jit(solution)/shard_map/ppermute | solution.py:28
  248.5 26.9 %all-to-all-start.4 = ((bf16[8,256,384]{2,1,0:T(8,128)(2,1)}), bf16[8,256,384]{2,1,0:T(8,128)(2,1)S(1)}, u32[]{:S(2)}, u32[]{:S(2)}) async-start(bf16[8,256,384]{2,1,0:T(8,128)(2,1)} %bitcast.40), calls=%async_computation.4 | async-start | bytes 3145728 | tf_op jit(solution)/shard_map/all_to_all | solution.py:775
  268.7 19.3 %collective-permute-start.23 = (bf16[96,1792]{1,0:T(8,128)(2,1)}, bf16[96,1792]{1,0:T(8,128)(2,1)S(1)}, u32[]{:S(2)}, u32[]{:S(2)}) collective-permute-start(bf16[96,1792]{1,0:T(8,128)(2,1)} %bitcast.110), channel_id=1, source_target_pairs={{0,16},{16,0},{1,17},{17,1},{2,18},{18,2},{3,19},{19,3},{4,20},{20... | collective-permute-start | bytes 1032200 | tf_op jit(solution)/shard_map/ppermute | solution.py:28
  275.4 11.6 %collective-permute-start.22 = (bf16[192,576]{1,0:T(8,128)(2,1)S(1)}, bf16[192,576]{1,0:T(8,128)(2,1)S(1)}, u32[]{:S(2)}, u32[]{:S(2)}) collective-permute-start(bf16[192,576]{1,0:T(8,128)(2,1)S(1)} %fusion.31), channel_id=1, source_target_pairs={{0,16},{16,0},{1,17},{17,1},{2,18},{18,2},{3,19},{19,3},{4,20},{20... | collective-permute-start | bytes 663560 | tf_op jit(solution)/shard_map/ppermute | solution.py:28
  277.8 10.1 %copy-start = (bf16[1,96,1792]{2,1,0:T(8,128)(2,1)S(1)}, bf16[1,96,1792]{2,1,0:T(8,128)(2,1)}, u32[]{:S(2)}) copy-start(bf16[1,96,1792]{2,1,0:T(8,128)(2,1)} %reduce-scatter.2.cloned.1.call-done) | copy-start | bytes 1032196
  (5 other events, 3.7 us)
Sparse Core Ops, SparseCore 0:
  10.9 115.3 all-gather.2
  235.0 33.5 reduce-scatter.1

commit v6 on v5

--- a/solution.py
+++ b/solution.py
@@ -362,9 +362,11 @@
 def feed_kernel(info_ref, x_ref, cot_ref, w_ref, *refs):
     parts, _, columns, slab, _ = w_ref.shape
     att_refs, refs = refs[:columns], refs[columns:]
-    result_ref, grad_att_ref, *refs = refs
-    grad_one_ref, hidden_ref, act_ref, gin_ref, gtwo_ref, gone_ref, sums_ref, w, slopes, outer, sems = refs
+    result_ref, grad_att_ref, grad_one_ref, hidden_ref, act_out, gin_out, gtwo_ref, gone_ref, sums_ref, sent_ref, *refs = refs
+    w, slopes, outer, act_ref, gin_ref, stage, sems, ends = refs
     rows, columns, quarter, _ = w.shape
+    act_copy = pltpu.make_async_copy(act_ref, act_out, ends.at[0])
+    gin_copy = pltpu.make_async_copy(gin_ref, gin_out, ends.at[1])
 
     def turned(step):
         column = info_ref[2] + step
@@ -421,6 +423,7 @@
         return carry
 
     lax.fori_loop(0, columns, forward, 0)
+    act_copy.start()
     wait(1)
 
     def combine(column, carry):
@@ -443,6 +446,7 @@
         return carry
 
     lax.fori_loop(0, columns, backward, 0)
+    gin_copy.start()
     grad_hidden = outer[...]
     grad_one = norm_backward(grad_hidden, normed_one, inverse_one, gain_one)
     grad_one_ref[...] = grad_one
@@ -457,29 +461,48 @@
         gone_ref[row] = grad_one_low[:, mine]
         sums_ref[row] = sums[:, mine].astype(bf16)
 
-
-def feed(info, attended, tokens, cot, weights):
+    copies_out = []
+    for column in range(columns):
+        slot = column % 2
+        if column > 1:
+            copies_out[column - 2].wait()
+        attended = attended_block(info_ref, att_refs, column)
+        operands = attended, act_ref[column], gin_ref[column], hidden_ref, gtwo_ref, gone_ref, sums_ref
+        weigh_block(1 - info_ref[1], info_ref, *operands, stage.at[slot])
+        copies_out.append(pltpu.make_async_copy(stage.at[slot], sent_ref.at[:, :, column], ends.at[2 + slot]))
+        copies_out[-1].start()
+    for copy in copies_out[-2:] + [act_copy, gin_copy]:
+        copy.wait()
+
+
+def feed(info, attended, tokens, cot, weights, slabs):
     own, feature = tokens.shape
     parts, rows, columns, slab, lanes = weights.shape
     quarter = parts * slab
     hidden_cols = feature
     vmem, smem = pl.BlockSpec(memory_space=pltpu.VMEM), pl.BlockSpec(memory_space=pltpu.SMEM)
+    hbm = pl.BlockSpec(memory_space=pltpu.HBM)
     wide = jax.ShapeDtypeStruct((columns, own, hidden_cols), bf16)
     flat = lambda kind: jax.ShapeDtypeStruct((own, feature), kind)
     tall = jax.ShapeDtypeStruct((feature, own), bf16)
     return pl.pallas_call(
         feed_kernel,
         in_specs=[smem, vmem, vmem, pl.BlockSpec(memory_space=pltpu.HBM)] + [vmem] * columns,
-        out_specs=[vmem] * 9,
+        out_specs=[vmem] * 4 + [hbm] * 2 + [vmem] * 3 + [hbm],
         out_shape=[
             flat(bf16), jax.ShapeDtypeStruct((columns, quarter, own), bf16), flat(f32), tall, wide, wide, tall,
             jax.ShapeDtypeStruct((rows, own, quarter), bf16), jax.ShapeDtypeStruct((rows, 4, quarter), bf16),
+            jax.ShapeDtypeStruct((2, slabs, columns, quarter // slabs, lanes), bf16),
         ],
         scratch_shapes=[
             pltpu.VMEM((rows, columns, quarter, lanes), bf16),
             pltpu.VMEM((columns, own, hidden_cols), f32),
             pltpu.VMEM((own, feature), f32),
+            pltpu.VMEM(wide.shape, bf16),
+            pltpu.VMEM(wide.shape, bf16),
+            pltpu.VMEM((2, 2, slabs, quarter // slabs, lanes), bf16),
             pltpu.SemaphoreType.DMA((3, parts)),
+            pltpu.SemaphoreType.DMA((4,)),
         ],
         compiler_params=pltpu.CompilerParams(vmem_limit_bytes=60 << 20),
         cost_estimate=cost(0.001),
@@ -487,25 +510,17 @@
     )(info, tokens, cot, weights, *attended)
 
 
-def weigh_kernel(twin, info_ref, hidden_ref, act_ref, gin_ref, gtwo_ref, gone_ref, sums_ref, *refs):
-    att_refs, out_ref = refs[:-1], refs[-1]
-    _, slabs, _, slab, lanes = out_ref.shape
+def weigh_block(core, info_ref, attended, act, gin, hidden_ref, gtwo_ref, gone_ref, sums_ref, out):
+    _, slabs, slab, lanes = out.shape
     quarter = slabs * slab
-    hidden_cols = act_ref.shape[2]
-    columns = len(att_refs)
-    step = pl.program_id(0) - info_ref[2]
-    step = jnp.where(step < 0, step + columns, step)
-    attended = att_refs[0][...]
-    for index in range(1, columns):
-        attended = jnp.where(step == index, att_refs[index][...], attended)
-    core = 1 - info_ref[1] if twin else info_ref[1]
+    hidden_cols = act.shape[1]
     eye = unit(quarter)
     away = lambda index, mine: jnp.where(index == mine, 0, 1)
     for pair in range(2):
         row = 2 * pair + core
         mine = pl.ds(pl.multiple_of(row * quarter, quarter), quarter)
-        inner = jnp.dot(hidden_ref[mine, :], gin_ref[0], preferred_element_type=f32).astype(bf16)
-        outer = jnp.dot(gtwo_ref[mine, :], act_ref[0], preferred_element_type=f32).astype(bf16)
+        inner = jnp.dot(hidden_ref[mine, :], gin, preferred_element_type=f32).astype(bf16)
+        outer = jnp.dot(gtwo_ref[mine, :], act, preferred_element_type=f32).astype(bf16)
         mixed = jnp.dot(attended, gone_ref[row], preferred_element_type=f32).astype(bf16)
         vector = contract(eye, sums_ref[row], (1, 1)).astype(bf16)
         rest = jnp.zeros((quarter, lanes - 2 * hidden_cols - quarter - 4), bf16)
@@ -514,19 +529,35 @@
         for part in range(slabs):
             place = away(part, info_ref[4]) if slabs > 1 else 0
             rows = slice(part * slab, (part + 1) * slab)
-            out_ref[far, place, 0, :, 0:hidden_cols] = inner[rows]
-            out_ref[far, place, 0, :, hidden_cols : 2 * hidden_cols] = outer[rows]
-            out_ref[far, place, 0, :, 2 * hidden_cols :] = tail[rows]
-
-
-def weigh(twin, info, attended, hidden, act, gin, gtwo, gone, sums, lanes, slabs):
+            out[far, place, :, 0:hidden_cols] = inner[rows]
+            out[far, place, :, hidden_cols : 2 * hidden_cols] = outer[rows]
+            out[far, place, :, 2 * hidden_cols :] = tail[rows]
+
+
+def attended_block(info_ref, att_refs, column):
+    step = column - info_ref[2]
+    step = jnp.where(step < 0, step + len(att_refs), step)
+    attended = att_refs[0][...]
+    for index in range(1, len(att_refs)):
+        attended = jnp.where(step == index, att_refs[index][...], attended)
+    return attended
+
+
+def weigh_kernel(info_ref, hidden_ref, act_ref, gin_ref, gtwo_ref, gone_ref, sums_ref, *refs):
+    att_refs, out_ref = refs[:-1], refs[-1]
+    attended = attended_block(info_ref, att_refs, pl.program_id(0))
+    operands = attended, act_ref[0], gin_ref[0], hidden_ref, gtwo_ref, gone_ref, sums_ref
+    weigh_block(info_ref[1], info_ref, *operands, out_ref.at[:, :, 0])
+
+
+def weigh(info, attended, hidden, act, gin, gtwo, gone, sums, lanes, slabs):
     columns = act.shape[0]
     quarter = attended[0].shape[0]
     whole = lambda a: pl.BlockSpec(a.shape, lambda i, s: (0,) * a.ndim)
     piece = pl.BlockSpec((1,) + act.shape[1:], lambda i, s: (i, 0, 0))
     slab = quarter // slabs
     return pl.pallas_call(
-        lambda *refs: weigh_kernel(twin, *refs),
+        weigh_kernel,
         grid_spec=pltpu.PrefetchScalarGridSpec(
             num_scalar_prefetch=1,
             grid=(columns,),
@@ -637,34 +668,43 @@
     )(*arrays)
 
 
-def open_kernel(swapped_ref, mine_ref, other_ref, *outs):
-    slab = mine_ref.shape[0]
-    hidden_cols, quarter = outs[0].shape[1], outs[2].shape[1]
+def open_kernel(hidden_cols, part_ref, mine_ref, other_ref, *outs):
+    *outs, sums_ref, query_ref, key_ref, value_ref = outs
+    slab, quarter = mine_ref.shape[0], outs[2].shape[1]
     spans = (0, hidden_cols), (hidden_cols, hidden_cols), (2 * hidden_cols, quarter)
+    lanes = mine_ref.shape[1] - 6 * quarter
 
     def write(first, second):
         for (start, size), out in zip(spans, outs):
             out[0:slab, :] = first[:, start : start + size].astype(f32)
             out[slab : 2 * slab, :] = second[:, start : start + size].astype(f32)
-        last = jnp.concatenate([first[:, 2 * hidden_cols + quarter :], second[:, 2 * hidden_cols + quarter :]], 0)
-        outs[3][...] = contract(last[:, 0:4], unit(2 * slab), (0, 0))
-
-    @pl.when(swapped_ref[0] == 0)
+        start = 2 * hidden_cols + quarter
+        last = jnp.concatenate([first[:, start:lanes], second[:, start:lanes]], 0)
+        sums_ref[...] = contract(last[:, 0:4], unit(2 * slab), (0, 0))
+
+    @pl.when(part_ref[0] == 0)
     def _():
         write(mine_ref[...], other_ref[...])
 
-    @pl.when(swapped_ref[0] != 0)
+    @pl.when(part_ref[0] != 0)
     def _():
         write(other_ref[...], mine_ref[...])
 
+    total = mine_ref[:, lanes:].astype(f32) + other_ref[:, lanes:].astype(f32)
+    for index, ref in enumerate((query_ref, key_ref, value_ref)):
+        for half in range(2):
+            start = (3 * half + index) * quarter
+            ref[half * slab : (half + 1) * slab, :] = total[:, start : start + quarter]
+
 
 def open_shards(part, mine, other, hidden_cols, quarter):
     vmem, smem = pl.BlockSpec(memory_space=pltpu.VMEM), pl.BlockSpec(memory_space=pltpu.SMEM)
-    lanes = hidden_cols, hidden_cols, quarter
+    rows = hidden_cols, hidden_cols, quarter
+    shape = lambda *dims: jax.ShapeDtypeStruct(dims, f32)
     return pl.pallas_call(
-        open_kernel,
+        lambda *refs: open_kernel(hidden_cols, *refs),
         in_specs=[smem, vmem, vmem],
-        out_shape=[jax.ShapeDtypeStruct((quarter, a), f32) for a in lanes] + [jax.ShapeDtypeStruct((4, quarter), f32)],
+        out_shape=[shape(quarter, a) for a in rows] + [shape(4, quarter)] + [shape(quarter, quarter)] * 3,
         compiler_params=pltpu.CompilerParams(vmem_limit_bytes=16 << 20),
         cost_estimate=cost(0.001),
         name="open_shards",
@@ -697,8 +737,7 @@
             (own,) = add_blocks(pair + (dp, ya, low_ya, high_dp), (columns,), [(0, 0, low), (0, middle, high)])
             own, mark = tie(own, mark)
             mine = lax.psum_scatter(own, "col", scatter_dimension=0, tiled=False)
-            other = swap(mine, "dp")
-            return (mine, other), mark
+            return mine, mark
 
         return mark, finish
 
@@ -750,7 +789,7 @@
         return lax.all_to_all(dealt.reshape(4, own, quarter), ROWS, split_axis=0, concat_axis=0, tiled=True)
 
     dealt = deal(wide_in)
-    cotangent, query_weight, dealt = tie(cotangent, query_weight, dealt)
+    cotangent, dealt = tie(cotangent, dealt)
     tokens = to_tokens(dealt).transpose(1, 0, 2).reshape(own, feature)
     wide_cot, tokens = tie(spread_dp(cotangent), tokens)
     blocks = [shift(tokens, step) for step in range(columns)]
@@ -767,7 +806,7 @@
     mixed, lses = last[0] + mixed, last[1] + lses
     attended = [shift(mixed[step], -step) for step in range(columns)]
 
-    result, grad_att, grad_one, hidden, act, gin, gtwo, gone, sums = feed(info, attended, tokens, cot, everywhere)
+    result, grad_att, grad_one, *pieces, sent = feed(info, attended, tokens, cot, everywhere, slabs)
     grad_att = lax.all_to_all(grad_att, "col", split_axis=0, concat_axis=0, tiled=True)
     def to_loader(*rows):
         cut = jnp.concatenate([a.astype(bf16).reshape(own, 4, quarter).transpose(1, 0, 2) for a in rows], 2)
@@ -784,10 +823,7 @@
         order = jnp.argsort(anchors.reshape(-1))
         spots_in = jnp.searchsorted(anchors.reshape(-1)[order], wanted)
         settle = lambda wide: wide[order[spots_in]].T
-    pieces = (hidden, act, gin, gtwo, gone, sums)
-    sent = weigh(True, info, attended, *pieces, lanes, slabs)
-    act, sent = tie(act, sent)
-    kept = weigh(False, info, attended, hidden, act, *pieces[2:], lanes, slabs)
+    kept = weigh(info, attended, *pieces, lanes, slabs)
     if slabs == 2:
         grad_att, sides = sum_shards(kept, sent, grad_att)
     else:
@@ -820,6 +856,7 @@
     grad_tokens, grad_qkv = tie(grad_tokens, grad_qkv)
     if slabs == 1:
         grad_qkv = over_dp(grad_qkv)
+        sum_qkv = [grad_qkv[:, i * width : (i + 1) * width] for i in range(3)]
         sum_inner, sum_outer = summed[:, :hidden_cols], summed[:, hidden_cols : 2 * hidden_cols]
         sum_output = summed[:, 2 * hidden_cols : 2 * hidden_cols + quarter]
         sum_vectors = summed[:, 2 * hidden_cols + quarter : 2 * hidden_cols + quarter + 4].T
@@ -827,14 +864,16 @@
     shape = lambda a: a.reshape(quarter, micro, share).transpose(1, 0, 2)
     moved = to_loader(result, grad_tokens)
     if slabs == 2:
-        (mine, other), (moved, mine, grad_qkv) = summed, tie(moved, summed[0], grad_qkv)
-        grad_qkv = over_dp(grad_qkv)
+        slab = quarter // 2
+        mine = jnp.concatenate([summed, grad_qkv[:slab], grad_qkv[slab:]], 1)
+        other = swap(mine, "dp")
+        moved, summed = tie(moved, summed)
         part = jnp.reshape(me, (1,)).astype(jnp.int32)
-        sum_inner, sum_outer, sum_output, sum_vectors = open_shards(part, mine, other, hidden_cols, quarter)
+        sum_inner, sum_outer, sum_output, sum_vectors, *sum_qkv = open_shards(part, mine, other, hidden_cols, quarter)
     settled = settle(moved)
     final_out, final_grad = shape(settled[:quarter]), shape(settled[quarter:])
     return (
-        final_out, final_grad, grad_qkv[:, :width], grad_qkv[:, width : 2 * width], grad_qkv[:, 2 * width :],
+        final_out, final_grad, *sum_qkv,
         sum_output, sum_inner, sum_outer, sum_vectors[0], sum_vectors[1], sum_vectors[2], sum_vectors[3],
     )
 

time: 298 us -> 299 us (level)
  starting transfers between devices: 49.9 us -> 56.7 us
  local copies, waits for them, and re-layouts: 16.6 us -> 13.6 us
    pallas_call x3 -> x2, Pallas kernels: 15.7 us -> 8.68 us  [the longest x1 7.15 us: weigh(): pl.pallas_call(weigh_kernel, grid_spec=pltpu.PrefetchScalarGridSpec(num_s...]
    all_to_all x1, starting transfers between devices: 5.73 us -> 11.3 us  [to_loader(): lax.all_to_all(cut, ('dp',) + ROWS, split_axis=0, concat_axis=0, tiled=True)]
    reduce_scatter x1, waiting for transfers between devices: 14.4 us -> 9.15 us  [finish(): mine = lax.psum_scatter(own, 'col', scatter_dimension=0, tiled=False)]
    pallas_call x1, Pallas kernels: 15.7 us -> 19.9 us  [feed(): pl.pallas_call(feed_kernel, in_specs=[smem, vmem, vmem, pl.BlockSpec(memo...]
    ppermute x18 -> x17, starting transfers between devices: 17.6 us -> 20.4 us  [swap(): return lax.ppermute(values, axis, SWAP)]
    ppermute x18 -> x17, waiting for transfers between devices: 38 us -> 37.7 us  [swap(): return lax.ppermute(values, axis, SWAP)]
  transfers between devices with their start and end apart: 31 -> 30, of which waited for: 20 -> 19; matrix products, arithmetic and copies ran while one was open for 8% -> 8% of each run, Pallas kernels for 24% -> 24%
where the time goes in v6:
time: 299 us; the launch traced here: 298 us
  waiting for transfers between devices  104 us (35%)
  Pallas kernels  94.2 us (32%)
  starting transfers between devices  56.7 us (19%)
  between operations  15.8 us (5%)
  local copies, waits for them, and re-layouts  13.6 us (5%)
  other arithmetic  7.72 us (3%)
  matrix products  5.5 us (2%)
    ppermute x6, waiting for transfers between devices, shift(): lax.ppermute(values, 'col', [(i, (i + step) % columns) for i in range(col...  40.2 us
    ppermute x17, waiting for transfers between devices, swap(): return lax.ppermute(values, axis, SWAP)  37.7 us
    ppermute x17, starting transfers between devices, swap(): return lax.ppermute(values, axis, SWAP)  20.4 us
    pallas_call x1, Pallas kernels, feed(): pl.pallas_call(feed_kernel, in_specs=[smem, vmem, vmem, pl.BlockSpec(memo...  19.9 us
    pallas_call x1, Pallas kernels, attend_backward(): pl.pallas_call(lambda *refs: backward_kernel(columns, share, *refs), in_s...  18 us
    pallas_call x2, Pallas kernels, attend_forward(): pl.pallas_call(lambda *refs: forward_kernel(first, share, *refs), grid_sp...  17.9 us
    all_to_all x1, starting transfers between devices, to_loader(): lax.all_to_all(cut, ('dp',) + ROWS, split_axis=0, concat_axis=0, tiled=True)  11.3 us
    pallas_call x3, Pallas kernels, add_blocks(): pl.pallas_call(lambda *refs: add_kernel(len(lengths), sums, *refs), in_sp...  11.1 us
  transfers between devices with their start and end apart: 30, of which 19 were waited for; matrix products, arithmetic and copies ran while one was open for 8% of the time, Pallas kernels for 24%

profile of v6, /device:TPU:0, one launch (start us, length us, event | category | flops | bytes accessed | tf_op | source)
XLA Modules:
  0.0 297.9 jit_solution(13748139662356198948)
XLA Ops:
  7.3 2.2 parcel.1
  9.5 3.0 %collective-permute-start = (bf16[2,192,512]{2,1,0:T(8,128)(2,1)}, bf16[2,192,512]{2,1,0:T(8,128)(2,1)S(1)}, u32[]{:S(2)}, u32[]{:S(2)}) collective-permute-start(bf16[2,192,512]{2,1,0:T(8,128)(2,1)} %param.14), channel_id=1, source_target_pairs={{0,16},{16,0},{1,17},{17,1},{2,18},{18,2},{3,19},{19,3},{4,20},{20... | collective-permute-start | bytes 1179656 | tf_op jit(solution)/shard_map/ppermute | solution.py:28
  13.7 2.1 collective-permute-start.6
  18.0 3.0 %fusion.30 = (f32[4,256,128]{2,1,0:T(8,128)}, f32[4,256,128]{2,1,0:T(8,128)}) fusion(f32[128]{0:T(128)S(1)} %compare_select_fusion.2, f32[128]{0:T(128)S(1)} %mul.76, f32[4,256]{1,0:T(4,128)S(1)} %subtract_convert_fusion), kind=kLoop, calls=%fused_computation.28 | loop fusion | flops 262144 | bytes 1053696 | tf_op jit(solution)/shard_map/mul | solution.py:778
  22.1 1.8 fusion.24
  23.9 1.8 collective-permute-start.1
  27.5 3.5 %all-to-all-start = ((bf16[4,256,192]{1,2,0:T(8,128)(2,1)}), bf16[4,256,192]{1,2,0:T(8,128)(2,1)S(1)}, u32[]{:S(2)}, u32[]{:S(2)}) async-start(bf16[4,256,192]{1,2,0:T(8,128)(2,1)} %bitcast.109), calls=%async_computation | async-start | bytes 786432 | tf_op jit(solution)/shard_map/all_to_all | solution.py:789
  31.0 4.9 %collective-permute-done.1 = bf16[2,192,512]{2,1,0:T(8,128)(2,1)S(1)} collective-permute-done((bf16[2,192,512]{2,1,0:T(8,128)(2,1)S(1)}, bf16[2,192,512]{2,1,0:T(8,128)(2,1)S(1)}, u32[]{:S(2)}, u32[]{:S(2)}) %collective-permute-start.1) | collective-permute-done | bytes 393248 | tf_op jit(solution)/shard_map/ppermute | solution.py:28
  36.0 2.4 all-to-all-done
  38.6 3.7 %collective-permute-start.2 = (bf16[256,768]{1,0:T(8,128)(2,1)S(1)}, bf16[256,768]{1,0:T(8,128)(2,1)S(1)}, u32[]{:S(2)}, u32[]{:S(2)}) collective-permute-start(bf16[256,768]{1,0:T(8,128)(2,1)S(1)} %copy.43.refs_0_.x_ref), channel_id=1, source_target_pairs={{0,3},{1,0},{2,1},{3,2},{4,7},{5,4},{6,5},{7,6},{8,11},{9,8},{10,9... | collective-permute-start | bytes 1179656 | tf_op jit(solution)/shard_map/ppermute | solution.py:620
  43.3 1.8 fusion.21
  45.8 3.6 %all-to-all-start.1 = ((bf16[4,256,192]{1,2,0:T(8,128)(2,1)}), bf16[4,256,192]{1,2,0:T(8,128)(2,1)S(1)}, u32[]{:S(2)}, u32[]{:S(2)}) async-start(bf16[4,256,192]{1,2,0:T(8,128)(2,1)} %bitcast.108), calls=%async_computation.1 | async-start | bytes 786432 | tf_op jit(solution)/shard_map/all_to_all | solution.py:789
  50.8 5.9 %all-to-all-done.1 = bf16[4,256,192]{1,2,0:T(8,128)(2,1)S(1)} async-done(((bf16[4,256,192]{1,2,0:T(8,128)(2,1)}), bf16[4,256,192]{1,2,0:T(8,128)(2,1)S(1)}, u32[]{:S(2)}, u32[]{:S(2)}) %all-to-all-start.1) | async-done | bytes 393248 | tf_op jit(solution)/shard_map/all_to_all | solution.py:789
  56.7 13.5 %collective-permute-done.2.refs_3_ = bf16[256,768]{1,0:T(8,128)(2,1)S(1)} collective-permute-done((bf16[256,768]{1,0:T(8,128)(2,1)S(1)}, bf16[256,768]{1,0:T(8,128)(2,1)S(1)}, u32[]{:S(2)}, u32[]{:S(2)}) %collective-permute-start.2) | collective-permute-done | bytes 393248 | tf_op jit(solution)/shard_map/ppermute | solution.py:620
  70.2 4.7 %collective-permute-done.4.refs_1_ = bf16[256,768]{1,0:T(8,128)(2,1)S(1)} collective-permute-done((bf16[256,768]{1,0:T(8,128)(2,1)S(1)}, bf16[256,768]{1,0:T(8,128)(2,1)S(1)}, u32[]{:S(2)}, u32[]{:S(2)}) %collective-permute-start.4) | collective-permute-done | bytes 393248 | tf_op jit(solution)/shard_map/ppermute | solution.py:620
  74.9 15.6 %collective-permute-done.5.refs_2_ = bf16[256,768]{1,0:T(8,128)(2,1)} collective-permute-done((bf16[256,768]{1,0:T(8,128)(2,1)S(1)}, bf16[256,768]{1,0:T(8,128)(2,1)}, u32[]{:S(2)}, u32[]{:S(2)}) %collective-permute-start.5) | collective-permute-done | bytes 393248 | tf_op jit(solution)/shard_map/ppermute | solution.py:620
  90.5 5.3 %project.1 = (bf16[4,256,256]{2,1,0:T(8,128)(2,1)}, bf16[8,256,256]{2,1,0:T(8,128)(2,1)}, bf16[8,192,256]{2,1,0:T(8,128)(2,1)}) custom-call(bf16[256,768]{1,0:T(8,128)(2,1)} %copy-done.3, bf16[256,768]{1,0:T(8,128)(2,1)} %copy-done.5, bf16[256,768]{1,0:T(8,128)(2,1)} %collective-permute-done.5.refs_2_, bf16[256,768]{1,0:T(8,128)(2,1)} %copy-done.4, ...), custom_call_target="tpu_custom_call" | custom-call | flops 1000000 | bytes 3000 | tf_op jit(solution)/shard_map/project/pallas_call | solution.py:76
  96.9 2.9 collective-permute-done.9.refs_5_
  101.0 13.6 %attend_forward.2 = (bf16[192,256]{1,0:T(8,128)(2,1)}, bf16[192,256]{1,0:T(8,128)(2,1)}, bf16[192,256]{1,0:T(8,128)(2,1)}, f32[3,256]{1,0:T(4,128)}, f32[3,256]{1,0:T(4,128)}, /*index=5*/f32[3,256]{1,0:T(4,128)}) custom-call(s32[5]{0:T(128)} %stack.68.refs_0_.info_ref, bf16[4,256,256]{2,1,0:T(8,128)(2,1)} %get-tuple-element.96.refs_1_, ...), custom_call_target="tpu_custom_call" | custom-call | flops 1000000 | bytes 3000 | tf_op jit(solution)/shard_map/attend_forward/pallas_call | solution.py:181
  114.6 4.7 %collective-permute-start.10 = (bf16[192,256]{1,0:T(8,128)(2,1)}, bf16[192,256]{1,0:T(8,128)(2,1)S(1)}, u32[]{:S(2)}, u32[]{:S(2)}) collective-permute-start(bf16[192,256]{1,0:T(8,128)(2,1)} %get-tuple-element.98.refs_8_), channel_id=1, source_target_pairs={{0,3},{1,0},{2,1},{3,2},{4,7},{5,4},{6,5},{7,6},{8,11},{9,8},{10,9... | collective-permute-start | bytes 294920 | tf_op jit(solution)/shard_map/ppermute | solution.py:620
  120.9 4.3 %attend_forward.3 = (bf16[192,256]{1,0:T(8,128)(2,1)}, f32[3,256]{1,0:T(4,128)}) custom-call(s32[5]{0:T(128)} %stack.68.refs_0_.info_ref, bf16[4,256,256]{2,1,0:T(8,128)(2,1)} %get-tuple-element.96.refs_1_, bf16[8,256,256]{2,1,0:T(8,128)(2,1)} %get-tuple-element.91.refs_2_, bf16[8,256,256]{2,1,0:T(8,128)(2,1)} %copy-done, ...), custom_call_target="tpu_custom_call" | custom-call | flops 1000000 | bytes 3000 | tf_op jit(solution)/shard_map/attend_forward/pallas_call | solution.py:181
  125.3 6.4 %collective-permute-done.11.refs_2_ = bf16[192,256]{1,0:T(8,128)(2,1)S(1)} collective-permute-done((bf16[192,256]{1,0:T(8,128)(2,1)}, bf16[192,256]{1,0:T(8,128)(2,1)S(1)}, u32[]{:S(2)}, u32[]{:S(2)}) %collective-permute-start.11) | collective-permute-done | bytes 98336 | tf_op jit(solution)/shard_map/ppermute | solution.py:620
  132.4 19.9 %feed.1 = (bf16[256,768]{1,0:T(8,128)(2,1)}, bf16[4,192,256]{2,1,0:T(8,128)(2,1)}, f32[256,768]{1,0:T(8,128)}, bf16[768,256]{1,0:T(8,128)(2,1)}, bf16[4,256,768]...) custom-call(s32[5]{0:T(128)} %stack.68.refs_0_.info_ref, ...), custom_call_target="tpu_custom_call" | custom-call | flops 1000000 | bytes 3000 | tf_op jit(solution)/shard_map/feed/pallas_call | solution.py:488
  152.4 3.7 %all-to-all-start.2 = ((bf16[4,192,256]{2,1,0:T(8,128)(2,1)}), bf16[4,192,256]{2,1,0:T(8,128)(2,1)S(1)}, u32[]{:S(2)}, u32[]{:S(2)}) async-start(bf16[4,192,256]{2,1,0:T(8,128)(2,1)} %get-tuple-element.103), calls=%async_computation.2 | async-start | bytes 786432 | tf_op jit(solution)/shard_map/all_to_all | solution.py:810
  156.1 7.1 %weigh.1.refs_0_ = bf16[2,2,4,96,1792]{4,3,2,1,0:T(8,128)(2,1)} custom-call(s32[5]{0:T(128)} %stack.68.refs_0_.info_ref, bf16[768,256]{1,0:T(8,128)(2,1)} %get-tuple-element.104.hidden_ref, bf16[4,256,768]{2,1,0:T(8,128)(2,1)} %get-tuple-element.105.act_ref, bf16[4,256,768]{2,1,0:T(8,128)(2,1)} %get-tuple-element.106.gin_ref, ...), custom_call_target="tpu_custom_call" | custom-call | flops 1000000 | bytes 3000 | tf_op jit(solution)/shard_map/weigh/pallas_call | solution.py:559
  163.3 4.0 %add_blocks.3 = (bf16[4,96,1792]{2,1,0:T(8,128)(2,1)}, bf16[4,96,1792]{2,1,0:T(8,128)(2,1)}) custom-call(bf16[2,2,4,96,1792]{4,3,2,1,0:T(8,128)(2,1)} %weigh.1.refs_0_, bf16[2,2,4,96,1792]{4,3,2,1,0:T(8,128)(2,1)} %collective-permute-done.13.refs_1_), custom_call_target="tpu_custom_call" | custom-call | flops 1000000 | bytes 3000 | tf_op jit(solution)/shard_map/add_blocks/pallas_call | solution.py:654
  168.4 2.4 collective-permute-start.16
  171.5 18.0 %attend_backward.1 = (f32[4,256,192]{2,1,0:T(8,128)}, bf16[8,256,256]{2,1,0:T(8,128)(2,1)}, bf16[4,256,256]{2,1,0:T(8,128)(2,1)}, bf16[4,256,256]{2,1,0:T(8,128)(2,1)}) custom-call(s32[5]{0:T(128)} %stack.68.refs_0_.info_ref, bf16[4,256,256]{2,1,0:T(8,128)(2,1)} %get-tuple-element.96.refs_1_, bf16[8,256,256]{2,1,0:T(8,128)(2,1)} %get-tuple-element.91.refs_2_, ...), custom_call_target="tpu_custom_call" | custom-call | flops 1000000 | bytes 3000 | tf_op jit(solution)/shard_map/attend_backward/pallas_call | solution.py:264
  190.0 1.6 collective-permute-done.14.far_k_ref
  193.1 7.0 %unproject.1 = (bf16[4,256,768]{2,1,0:T(8,128)(2,1)}, bf16[4,256,576]{2,1,0:T(8,128)(2,1)}) custom-call(s32[5]{0:T(128)} %stack.68.refs_0_.info_ref, f32[4,256,192]{2,1,0:T(8,128)} %get-tuple-element.118.dq_ref, bf16[8,256,256]{2,1,0:T(8,128)(2,1)} %get-tuple-element.119.near_k_ref.near_v_ref, bf16[4,256,256]{2,1,0:T(8,128)(2,1)} %copy-done.8, ...), custom_call_target="tpu_custom_call" | custom-call | flops 1000000 | bytes 3000 | tf_op jit(solution)/shard_map/unproject/pallas_call | solution.py:306
  200.1 4.0 %all-to-all-start.3 = ((bf16[4,256,768]{2,1,0:T(8,128)(2,1)}), bf16[4,256,768]{2,1,0:T(8,128)(2,1)S(1)}, u32[]{:S(2)}, u32[]{:S(2)}) async-start(bf16[4,256,768]{2,1,0:T(8,128)(2,1)} %get-tuple-element.122), calls=%async_computation.3 | async-start | bytes 3145728 | tf_op jit(solution)/shard_map/all_to_all | solution.py:840
  204.1 3.3 %add_blocks.4 = (bf16[2,96,1792]{2,1,0:T(8,128)(2,1)}, bf16[2,96,1792]{2,1,0:T(8,128)(2,1)}) custom-call(bf16[2,2,4,96,1792]{4,3,2,1,0:T(8,128)(2,1)} %weigh.1.refs_0_, bf16[2,2,4,96,1792]{4,3,2,1,0:T(8,128)(2,1)} %collective-permute-done.13.refs_1_, bf16[4,96,1792]{2,1,0:T(8,128)(2,1)} %collective-permute-done.16.refs_2_, ...), custom_call_target="tpu_custom_call" | custom-call | flops 1000000 | bytes 3000 | tf_op jit(solution)/shard_map/add_blocks/pallas_call | solution.py:654
  207.4 1.4 collective-permute-start.18
  208.9 3.1 %collective-permute-start.19 = (bf16[2,96,1792]{2,1,0:T(8,128)(2,1)}, bf16[2,96,1792]{2,1,0:T(8,128)(2,1)}, u32[]{:S(2)}, u32[]{:S(2)}) collective-permute-start(bf16[2,96,1792]{2,1,0:T(8,128)(2,1)} %get-tuple-element.132), channel_id=1, source_target_pairs={{0,16},{16,0},{1,17},{17,1},{2,18},{18,2},{3,19},{19,3},{4,20},{20... | collective-permute-start | bytes 2064392 | tf_op jit(solution)/shard_map/ppermute | solution.py:28
  212.0 4.1 %project_grad.1 = bf16[768,576]{1,0:T(8,128)(2,1)} custom-call(bf16[4,256,576]{2,1,0:T(8,128)(2,1)} %get-tuple-element.133.low_ref, bf16[256,768]{1,0:T(8,128)(2,1)} %copy-done.3, bf16[256,768]{1,0:T(8,128)(2,1)} %copy-done.5, bf16[256,768]{1,0:T(8,128)(2,1)} %collective-permute-done.5.refs_2_, bf16[256,768]{1,0:T(8,128)(2,1)} %copy-done.4), custom_call_target="tpu_custom_call" | custom-call | flops 1000000 | bytes 3000 | tf_op jit(solution)/shard_map/project_grad/pallas_call | solution.py:332
  216.1 8.8 %collective-permute-done.18.refs_4_ = bf16[2,96,1792]{2,1,0:T(8,128)(2,1)S(1)} collective-permute-done((bf16[2,96,1792]{2,1,0:T(8,128)(2,1)}, bf16[2,96,1792]{2,1,0:T(8,128)(2,1)S(1)}, u32[]{:S(2)}, u32[]{:S(2)}) %collective-permute-start.18) | collective-permute-done | bytes 688160 | tf_op jit(solution)/shard_map/ppermute | solution.py:28
  224.9 2.8 collective-permute-done.19.refs_5_
  227.8 3.8 %add_blocks.5 = bf16[4,96,1792]{2,1,0:T(8,128)(2,1)} custom-call(bf16[2,2,4,96,1792]{4,3,2,1,0:T(8,128)(2,1)} %weigh.1.refs_0_, bf16[2,2,4,96,1792]{4,3,2,1,0:T(8,128)(2,1)} %collective-permute-done.13.refs_1_, bf16[4,96,1792]{2,1,0:T(8,128)(2,1)} %collective-permute-done.16.refs_2_, bf16[4,96,1792]{2,1,0:T(8,128)(2,1)} %collective-permute-done.17.refs_3_, ...), custom_call_target="tpu_custom_call" | custom-call | flops 1000000 | bytes 3000 | tf_op jit(solution)/shard_map/add_blocks/pallas_call | solution.py:654
  231.8 1.8 collective-permute-done.20
  233.9 1.7 collective-permute-start.21
  236.7 5.2 %collective-permute-done.21 = bf16[192,576]{1,0:T(8,128)(2,1)S(1)} collective-permute-done((bf16[192,576]{1,0:T(8,128)(2,1)S(1)}, bf16[192,576]{1,0:T(8,128)(2,1)S(1)}, u32[]{:S(2)}, u32[]{:S(2)}) %collective-permute-start.21) | collective-permute-done | bytes 221216 | tf_op jit(solution)/shard_map/ppermute | solution.py:28
  245.4 11.3 %all-to-all-start.4 = ((bf16[8,256,384]{2,1,0:T(8,128)(2,1)}), bf16[8,256,384]{2,1,0:T(8,128)(2,1)S(1)}, u32[]{:S(2)}, u32[]{:S(2)}) async-start(bf16[8,256,384]{2,1,0:T(8,128)(2,1)} %bitcast.40), calls=%async_computation.4 | async-start | bytes 3145728 | tf_op jit(solution)/shard_map/all_to_all | solution.py:814
  256.8 9.2 %reduce-scatter.2.cloned.1.call-done = bf16[1,96,1792]{2,1,0:T(8,128)(2,1)} async-done(((bf16[4,96,1792]{2,1,0:T(8,128)(2,1)}), bf16[1,96,1792]{2,1,0:T(8,128)(2,1)}) %reduce-scatter.2.cloned.1.call-update) | async-done | bytes 344080 | tf_op jit(solution)/shard_map/reduce_scatter | solution.py:739
  267.1 3.0 %collective-permute-start.22 = (bf16[96,2944]{1,0:T(8,128)(2,1)S(1)}, bf16[96,2944]{1,0:T(8,128)(2,1)S(1)}, u32[]{:S(2)}, u32[]{:S(2)}) collective-permute-start(bf16[96,2944]{1,0:T(8,128)(2,1)S(1)} %concatenate.11.refs_1_), channel_id=1, source_target_pairs={{0,16},{16,0},{1,17},{17,1},{2,18},{18,2},{3,19},{19,3},{4,20},{20... | collective-permute-start | bytes 1695752 | tf_op jit(solution)/shard_map/ppermute | solution.py:28
  270.1 7.7 %all-to-all-done.4 = bf16[8,256,384]{2,1,0:T(8,128)(2,1)S(1)} async-done(((bf16[8,256,384]{2,1,0:T(8,128)(2,1)}), bf16[8,256,384]{2,1,0:T(8,128)(2,1)S(1)}, u32[]{:S(2)}, u32[]{:S(2)}) %all-to-all-start.4) | async-done | bytes 1572896 | tf_op jit(solution)/shard_map/all_to_all | solution.py:814
  277.9 1.9 fusion.12
  280.8 8.1 %collective-permute-done.22.refs_2_ = bf16[96,2944]{1,0:T(8,128)(2,1)S(1)} collective-permute-done((bf16[96,2944]{1,0:T(8,128)(2,1)S(1)}, bf16[96,2944]{1,0:T(8,128)(2,1)S(1)}, u32[]{:S(2)}, u32[]{:S(2)}) %collective-permute-start.22) | collective-permute-done | bytes 565280 | tf_op jit(solution)/shard_map/ppermute | solution.py:28
  289.0 1.5 open_shards.1
  (118 shorter events, 24.6 us)
Async XLA Ops:
  7.2 14.7 %copy-start.13 = (bf16[2,192,512]{2,1,0:T(8,128)(2,1)S(1)}, bf16[2,192,512]{2,1,0:T(8,128)(2,1)}, u32[]{:S(2)}) copy-start(bf16[2,192,512]{2,1,0:T(8,128)(2,1)} %param.14) | copy-start | bytes 1179652
  7.2 8.8 %copy-start.18 = (s32[2,512]{1,0:T(2,128)S(1)}, s32[2,512]{1,0:T(2,128)}, u32[]{:S(2)}) copy-start(s32[2,512]{1,0:T(2,128)} %param.17) | copy-start | bytes 12292
  7.2 8.8 %copy-start.19 = (s32[1,2]{1,0:T(1,128)S(1)}, s32[1,2]{1,0:T(1,128)}, u32[]{:S(2)}) copy-start(s32[1,2]{1,0:T(1,128)} %param.16) | copy-start | bytes 28
  7.2 124.5 %all-gather.3.cloned.1.call-start = ((), (), s32[]{:S(2)}) async-start(), calls=%async_computation.7 | async-start | bytes 11354112 | tf_op jit(solution)/shard_map/all_gather | solution.py:767
  9.5 12.4 %collective-permute-start = (bf16[2,192,512]{2,1,0:T(8,128)(2,1)}, bf16[2,192,512]{2,1,0:T(8,128)(2,1)S(1)}, u32[]{:S(2)}, u32[]{:S(2)}) collective-permute-start(bf16[2,192,512]{2,1,0:T(8,128)(2,1)} %param.14), channel_id=1, source_target_pairs={{0,16},{16,0},{1,17},{17,1},{2,18},{18,2},{3,19},{19,3},{4,20},{20... | collective-permute-start | bytes 1179656 | tf_op jit(solution)/shard_map/ppermute | solution.py:28
  12.5 9.4 %collective-permute-start.3 = (s32[2,512]{1,0:T(2,128)}, s32[2,512]{1,0:T(2,128)S(1)}, u32[]{:S(2)}, u32[]{:S(2)}) collective-permute-start(s32[2,512]{1,0:T(2,128)} %param.17), channel_id=1, source_target_pairs={{0,16},{16,0},{1,17},{17,1},{2,18},{18,2},{3,19},{19,3},{4,20},{20... | collective-permute-start | bytes 12296 | tf_op jit(solution)/shard_map/ppermute | solution.py:28
  13.7 12.1 %collective-permute-start.6 = (bf16[192,576]{1,0:T(8,128)(2,1)S(1)}, bf16[192,576]{1,0:T(8,128)(2,1)S(1)}, u32[]{:S(2)}, u32[]{:S(2)}) collective-permute-start(bf16[192,576]{1,0:T(8,128)(2,1)S(1)} %pad_maximum_fusion.5), channel_id=1, source_target_pairs={{0,8},{8,0},{1,9},{9,1},{2,10},{10,2},{3,11},{11,3},{4,12},{12,4},... | collective-permute-start | bytes 663560 | tf_op jit(solution)/shard_map/ppermute | solution.py:28
  22.1 1.8 copy-start.14
  22.1 3.6 %copy-start.15 = (bf16[192,192]{1,0:T(8,128)(2,1)S(1)}, bf16[192,192]{1,0:T(8,128)(2,1)}, u32[]{:S(2)}) copy-start(bf16[192,192]{1,0:T(8,128)(2,1)} %param.20) | copy-start | bytes 221188
  22.1 3.6 %copy-start.16 = (bf16[192,192]{1,0:T(8,128)(2,1)S(1)}, bf16[192,192]{1,0:T(8,128)(2,1)}, u32[]{:S(2)}) copy-start(bf16[192,192]{1,0:T(8,128)(2,1)} %param.19) | copy-start | bytes 221188
  22.1 3.6 %copy-start.17 = (bf16[192,192]{1,0:T(8,128)(2,1)S(1)}, bf16[192,192]{1,0:T(8,128)(2,1)}, u32[]{:S(2)}) copy-start(bf16[192,192]{1,0:T(8,128)(2,1)} %param.18) | copy-start | bytes 221188
  23.9 12.0 %collective-permute-start.1 = (bf16[2,192,512]{2,1,0:T(8,128)(2,1)S(1)}, bf16[2,192,512]{2,1,0:T(8,128)(2,1)S(1)}, u32[]{:S(2)}, u32[]{:S(2)}) collective-permute-start(bf16[2,192,512]{2,1,0:T(8,128)(2,1)S(1)} %copy-done.14), channel_id=1, source_target_pairs={{0,16},{16,0},{1,17},{17,1},{2,18},{18,2},{3,19},{19,3},{4,20},{20... | collective-permute-start | bytes 1179656 | tf_op jit(solution)/shard_map/ppermute | solution.py:28
  26.8 22.7 %collective-permute-start.7 = (bf16[2,192,576]{2,1,0:T(8,128)(2,1)}, bf16[2,192,576]{2,1,0:T(8,128)(2,1)S(1)}, u32[]{:S(2)}, u32[]{:S(2)}) collective-permute-start(bf16[2,192,576]{2,1,0:T(8,128)(2,1)} %pad_maximum_fusion.4), channel_id=1, source_target_pairs={{0,4},{4,0},{1,5},{5,1},{2,6},{6,2},{3,7},{7,3},{8,12},{12,8},{9,1... | collective-permute-start | bytes 1327112 | tf_op jit(solution)/shard_map/ppermute | solution.py:28
  27.5 10.9 %all-to-all-start = ((bf16[4,256,192]{1,2,0:T(8,128)(2,1)}), bf16[4,256,192]{1,2,0:T(8,128)(2,1)S(1)}, u32[]{:S(2)}, u32[]{:S(2)}) async-start(bf16[4,256,192]{1,2,0:T(8,128)(2,1)} %bitcast.109), calls=%async_computation | async-start | bytes 786432 | tf_op jit(solution)/shard_map/all_to_all | solution.py:789
  38.6 6.5 %copy-start.3 = (bf16[256,768]{1,0:T(8,128)(2,1)}, bf16[256,768]{1,0:T(8,128)(2,1)S(1)}, u32[]{:S(2)}) copy-start(bf16[256,768]{1,0:T(8,128)(2,1)S(1)} %copy.43.refs_0_.x_ref) | copy-start | bytes 1179652
  38.6 31.6 %collective-permute-start.2 = (bf16[256,768]{1,0:T(8,128)(2,1)S(1)}, bf16[256,768]{1,0:T(8,128)(2,1)S(1)}, u32[]{:S(2)}, u32[]{:S(2)}) collective-permute-start(bf16[256,768]{1,0:T(8,128)(2,1)S(1)} %copy.43.refs_0_.x_ref), channel_id=1, source_target_pairs={{0,3},{1,0},{2,1},{3,2},{4,7},{5,4},{6,5},{7,6},{8,11},{9,8},{10,9... | collective-permute-start | bytes 1179656 | tf_op jit(solution)/shard_map/ppermute | solution.py:620
  42.3 32.6 %collective-permute-start.4 = (bf16[256,768]{1,0:T(8,128)(2,1)S(1)}, bf16[256,768]{1,0:T(8,128)(2,1)S(1)}, u32[]{:S(2)}, u32[]{:S(2)}) collective-permute-start(bf16[256,768]{1,0:T(8,128)(2,1)S(1)} %copy.43.refs_0_.x_ref), channel_id=1, source_target_pairs={{0,1},{1,2},{2,3},{3,0},{4,5},{5,6},{6,7},{7,4},{8,9},{9,10},{10,1... | collective-permute-start | bytes 1179656 | tf_op jit(solution)/shard_map/ppermute | solution.py:620
  42.3 48.2 %collective-permute-start.5 = (bf16[256,768]{1,0:T(8,128)(2,1)S(1)}, bf16[256,768]{1,0:T(8,128)(2,1)}, u32[]{:S(2)}, u32[]{:S(2)}) collective-permute-start(bf16[256,768]{1,0:T(8,128)(2,1)S(1)} %copy.43.refs_0_.x_ref), channel_id=1, source_target_pairs={{0,2},{1,3},{2,0},{3,1},{4,6},{5,7},{6,4},{7,5},{8,10},{9,11},{10,... | collective-permute-start | bytes 1179656 | tf_op jit(solution)/shard_map/ppermute | solution.py:620
  45.8 10.9 %all-to-all-start.1 = ((bf16[4,256,192]{1,2,0:T(8,128)(2,1)}), bf16[4,256,192]{1,2,0:T(8,128)(2,1)S(1)}, u32[]{:S(2)}, u32[]{:S(2)}) async-start(bf16[4,256,192]{1,2,0:T(8,128)(2,1)} %bitcast.108), calls=%async_computation.1 | async-start | bytes 786432 | tf_op jit(solution)/shard_map/all_to_all | solution.py:789
  70.2 20.3 %copy-start.4 = (bf16[256,768]{1,0:T(8,128)(2,1)}, bf16[256,768]{1,0:T(8,128)(2,1)S(1)}, u32[]{:S(2)}) copy-start(bf16[256,768]{1,0:T(8,128)(2,1)S(1)} %collective-permute-done.2.refs_3_) | copy-start | bytes 1179652
  74.9 15.6 %copy-start.5 = (bf16[256,768]{1,0:T(8,128)(2,1)}, bf16[256,768]{1,0:T(8,128)(2,1)S(1)}, u32[]{:S(2)}) copy-start(bf16[256,768]{1,0:T(8,128)(2,1)S(1)} %collective-permute-done.4.refs_1_) | copy-start | bytes 1179652
  95.8 4.0 %collective-permute-start.8 = (bf16[8,256,256]{2,1,0:T(8,128)(2,1)}, bf16[8,256,256]{2,1,0:T(8,128)(2,1)S(1)}, u32[]{:S(2)}, u32[]{:S(2)}) collective-permute-start(bf16[8,256,256]{2,1,0:T(8,128)(2,1)} %get-tuple-element.91.refs_2_), channel_id=1, source_target_pairs={{0,4},{4,0},{1,5},{5,1},{2,6},{6,2},{3,7},{7,3},{8,12},{12,8},{9,1... | collective-permute-start | bytes 3145736 | tf_op jit(solution)/shard_map/ppermute | solution.py:28
  95.8 4.0 %collective-permute-start.9 = (bf16[8,192,256]{2,1,0:T(8,128)(2,1)}, bf16[8,192,256]{2,1,0:T(8,128)(2,1)S(1)}, u32[]{:S(2)}, u32[]{:S(2)}) collective-permute-start(bf16[8,192,256]{2,1,0:T(8,128)(2,1)} %get-tuple-element.92.refs_4_), channel_id=1, source_target_pairs={{0,4},{4,0},{1,5},{5,1},{2,6},{6,2},{3,7},{7,3},{8,12},{12,8},{9,1... | collective-permute-start | bytes 2359304 | tf_op jit(solution)/shard_map/ppermute | solution.py:28
  99.8 0.9 copy-start.2
  99.8 1.2 copy-start
  114.6 10.6 %collective-permute-start.10 = (bf16[192,256]{1,0:T(8,128)(2,1)}, bf16[192,256]{1,0:T(8,128)(2,1)S(1)}, u32[]{:S(2)}, u32[]{:S(2)}) collective-permute-start(bf16[192,256]{1,0:T(8,128)(2,1)} %get-tuple-element.98.refs_8_), channel_id=1, source_target_pairs={{0,3},{1,0},{2,1},{3,2},{4,7},{5,4},{6,5},{7,6},{8,11},{9,8},{10,9... | collective-permute-start | bytes 294920 | tf_op jit(solution)/shard_map/ppermute | solution.py:620
  119.4 12.3 %collective-permute-start.11 = (bf16[192,256]{1,0:T(8,128)(2,1)}, bf16[192,256]{1,0:T(8,128)(2,1)S(1)}, u32[]{:S(2)}, u32[]{:S(2)}) collective-permute-start(bf16[192,256]{1,0:T(8,128)(2,1)} %get-tuple-element.99.refs_9_), channel_id=1, source_target_pairs={{0,2},{1,3},{2,0},{3,1},{4,6},{5,7},{6,4},{7,5},{8,10},{9,11},{10,... | collective-permute-start | bytes 294920 | tf_op jit(solution)/shard_map/ppermute | solution.py:620
  119.4 12.3 %collective-permute-start.12 = (bf16[192,256]{1,0:T(8,128)(2,1)}, bf16[192,256]{1,0:T(8,128)(2,1)S(1)}, u32[]{:S(2)}, u32[]{:S(2)}) collective-permute-start(bf16[192,256]{1,0:T(8,128)(2,1)} %get-tuple-element.100.refs_10_), channel_id=1, source_target_pairs={{0,1},{1,2},{2,3},{3,0},{4,5},{5,6},{6,7},{7,4},{8,9},{9,10},{10,1... | collective-permute-start | bytes 294920 | tf_op jit(solution)/shard_map/ppermute | solution.py:620
  125.2 6.5 %copy-start.10 = (bf16[192,256]{1,0:T(8,128)(2,1)}, bf16[192,256]{1,0:T(8,128)(2,1)S(1)}, u32[]{:S(2)}) copy-start(bf16[192,256]{1,0:T(8,128)(2,1)S(1)} %collective-permute-done.10.refs_1_) | copy-start | bytes 294916
  152.3 11.0 %collective-permute-start.13 = (bf16[2,2,4,96,1792]{4,3,2,1,0:T(8,128)(2,1)}, bf16[2,2,4,96,1792]{4,3,2,1,0:T(8,128)(2,1)}, u32[]{:S(2)}, u32[]{:S(2)}) collective-permute-start(bf16[2,2,4,96,1792]{4,3,2,1,0:T(8,128)(2,1)} %get-tuple-element.110), channel_id=1, source_target_pairs={{0,4},{4,0},{1,5},{5,1},{2,6},{6,2},{3,7},{7,3},{8,12},{12,8},{9,1... | collective-permute-start | bytes 16515080 | tf_op jit(solution)/shard_map/ppermute | solution.py:28
  152.4 16.1 %all-to-all-start.2 = ((bf16[4,192,256]{2,1,0:T(8,128)(2,1)}), bf16[4,192,256]{2,1,0:T(8,128)(2,1)S(1)}, u32[]{:S(2)}, u32[]{:S(2)}) async-start(bf16[4,192,256]{2,1,0:T(8,128)(2,1)} %get-tuple-element.103), calls=%async_computation.2 | async-start | bytes 786432 | tf_op jit(solution)/shard_map/all_to_all | solution.py:810
  168.4 3.0 %copy-start.6 = (bf16[4,192,256]{2,1,0:T(8,128)(2,1)}, bf16[4,192,256]{2,1,0:T(8,128)(2,1)S(1)}, u32[]{:S(2)}) copy-start(bf16[4,192,256]{2,1,0:T(8,128)(2,1)S(1)} %all-to-all-done.2.refs_6_) | copy-start | bytes 1179652
  168.4 35.7 %collective-permute-start.16 = (bf16[4,96,1792]{2,1,0:T(8,128)(2,1)}, bf16[4,96,1792]{2,1,0:T(8,128)(2,1)}, u32[]{:S(2)}, u32[]{:S(2)}) collective-permute-start(bf16[4,96,1792]{2,1,0:T(8,128)(2,1)} %get-tuple-element.123), channel_id=1, source_target_pairs={{0,16},{16,0},{1,17},{17,1},{2,18},{18,2},{3,19},{19,3},{4,20},{20... | collective-permute-start | bytes 4128776 | tf_op jit(solution)/shard_map/ppermute | solution.py:28
  170.9 33.3 %collective-permute-start.17 = (bf16[4,96,1792]{2,1,0:T(8,128)(2,1)}, bf16[4,96,1792]{2,1,0:T(8,128)(2,1)}, u32[]{:S(2)}, u32[]{:S(2)}) collective-permute-start(bf16[4,96,1792]{2,1,0:T(8,128)(2,1)} %get-tuple-element.124), channel_id=1, source_target_pairs={{0,8},{8,0},{1,9},{9,1},{2,10},{10,2},{3,11},{11,3},{4,12},{12,4},... | collective-permute-start | bytes 4128776 | tf_op jit(solution)/shard_map/ppermute | solution.py:28
  189.5 2.1 collective-permute-start.14
  189.5 2.9 collective-permute-start.15
  191.6 0.8 copy-start.8
  192.3 0.8 copy-start.9
  200.1 41.9 %all-to-all-start.3 = ((bf16[4,256,768]{2,1,0:T(8,128)(2,1)}), bf16[4,256,768]{2,1,0:T(8,128)(2,1)S(1)}, u32[]{:S(2)}, u32[]{:S(2)}) async-start(bf16[4,256,768]{2,1,0:T(8,128)(2,1)} %get-tuple-element.122), calls=%async_computation.3 | async-start | bytes 3145728 | tf_op jit(solution)/shard_map/all_to_all | solution.py:840
  204.1 61.8 %reduce-scatter.2.cloned.1.call-start = ((), (), s32[]{:S(2)}) async-start(), calls=%async_computation.6 | async-start | bytes 1720320 | tf_op jit(solution)/shard_map/reduce_scatter | solution.py:739
  207.4 17.5 %collective-permute-start.18 = (bf16[2,96,1792]{2,1,0:T(8,128)(2,1)}, bf16[2,96,1792]{2,1,0:T(8,128)(2,1)S(1)}, u32[]{:S(2)}, u32[]{:S(2)}) collective-permute-start(bf16[2,96,1792]{2,1,0:T(8,128)(2,1)} %get-tuple-element.131), channel_id=1, source_target_pairs={{0,8},{8,0},{1,9},{9,1},{2,10},{10,2},{3,11},{11,3},{4,12},{12,4},... | collective-permute-start | bytes 2064392 | tf_op jit(solution)/shard_map/ppermute | solution.py:28
  208.9 18.9 %collective-permute-start.19 = (bf16[2,96,1792]{2,1,0:T(8,128)(2,1)}, bf16[2,96,1792]{2,1,0:T(8,128)(2,1)}, u32[]{:S(2)}, u32[]{:S(2)}) collective-permute-start(bf16[2,96,1792]{2,1,0:T(8,128)(2,1)} %get-tuple-element.132), channel_id=1, source_target_pairs={{0,16},{16,0},{1,17},{17,1},{2,18},{18,2},{3,19},{19,3},{4,20},{20... | collective-permute-start | bytes 2064392 | tf_op jit(solution)/shard_map/ppermute | solution.py:28
  216.1 15.5 %copy-start.1 = (bf16[768,576]{1,0:T(8,128)(2,1)S(1)}, bf16[768,576]{1,0:T(8,128)(2,1)}, u32[]{:S(2)}) copy-start(bf16[768,576]{1,0:T(8,128)(2,1)} %project_grad.1) | copy-start | bytes 2654212
  224.9 2.9 copy-start.7
  231.7 1.9 collective-permute-start.20
  233.9 8.1 %collective-permute-start.21 = (bf16[192,576]{1,0:T(8,128)(2,1)S(1)}, bf16[192,576]{1,0:T(8,128)(2,1)S(1)}, u32[]{:S(2)}, u32[]{:S(2)}) collective-permute-start(bf16[192,576]{1,0:T(8,128)(2,1)S(1)} %select_bitcast_fusion.7), channel_id=1, source_target_pairs={{0,8},{8,0},{1,9},{9,1},{2,10},{10,2},{3,11},{11,3},{4,12},{12,4},... | collective-permute-start | bytes 663560 | tf_op jit(solution)/shard_map/ppermute | solution.py:28
  245.4 32.5 %all-to-all-start.4 = ((bf16[8,256,384]{2,1,0:T(8,128)(2,1)}), bf16[8,256,384]{2,1,0:T(8,128)(2,1)S(1)}, u32[]{:S(2)}, u32[]{:S(2)}) async-start(bf16[8,256,384]{2,1,0:T(8,128)(2,1)} %bitcast.40), calls=%async_computation.4 | async-start | bytes 3145728 | tf_op jit(solution)/shard_map/all_to_all | solution.py:814
  267.1 21.9 %collective-permute-start.22 = (bf16[96,2944]{1,0:T(8,128)(2,1)S(1)}, bf16[96,2944]{1,0:T(8,128)(2,1)S(1)}, u32[]{:S(2)}, u32[]{:S(2)}) collective-permute-start(bf16[96,2944]{1,0:T(8,128)(2,1)S(1)} %concatenate.11.refs_1_), channel_id=1, source_target_pairs={{0,16},{16,0},{1,17},{17,1},{2,18},{18,2},{3,19},{19,3},{4,20},{20... | collective-permute-start | bytes 1695752 | tf_op jit(solution)/shard_map/ppermute | solution.py:28
  (2 other events, 1.3 us)
Sparse Core Ops, SparseCore 0:
  10.9 118.7 all-gather.2
  231.9 33.9 reduce-scatter.1

commit v7 on v6

--- a/solution.py
+++ b/solution.py
@@ -140,22 +140,23 @@
     def visit(key_block, same):
         keys = jnp.concatenate([k0_ref[key_block], k1_ref[key_block]], 0)
         values = jnp.concatenate([vt0_ref[key_block], vt1_ref[key_block]], 1)
-        for head in range(heads):
-            rows = pl.ds(head * DH, DH)
-            line = pl.ds(head, 1)
-            scores = contract(keys, parts[head], (1, 1)) * scaling
-            if same is not None:
-                scores = jnp.where(same, scores, MASKED)
-            before = top[line, :]
-            highest = jnp.maximum(before, jnp.max(scores, 0, keepdims=True))
-            fade = jnp.exp2(before - highest)
-            raised = jnp.exp2(scores - highest)
-            if same is not None:
-                raised = jnp.where(same, raised, 0.0)
-            top[line, :] = highest
-            total[line, :] = total[line, :] * fade + jnp.sum(raised, 0, keepdims=True)
-            product = jnp.dot(values[head * DH : (head + 1) * DH], raised.astype(bf16), preferred_element_type=f32)
-            sums[rows, :] = sums[rows, :] * fade + product
+        scores = [contract(keys, parts[head], (1, 1)) * scaling for head in range(heads)]
+        if same is not None:
+            scores = [jnp.where(same, each, MASKED) for each in scores]
+        before = top[...]
+        highest = jnp.maximum(before, jnp.concatenate([jnp.max(each, 0, keepdims=True) for each in scores], 0))
+        fade = jnp.exp2(before - highest)
+        raised = [jnp.exp2(each - highest[head : head + 1]) for head, each in enumerate(scores)]
+        if same is not None:
+            raised = [jnp.where(same, each, 0.0) for each in raised]
+        top[...] = highest
+        total[...] = total[...] * fade + jnp.concatenate([jnp.sum(each, 0, keepdims=True) for each in raised], 0)
+        products = [
+            jnp.dot(values[head * DH : (head + 1) * DH], each.astype(bf16), preferred_element_type=f32)
+            for head, each in enumerate(raised)
+        ]
+        fades = [jnp.broadcast_to(fade[head : head + 1], (DH, fade.shape[1])) for head in range(heads)]
+        sums[...] = sums[...] * jnp.concatenate(fades, 0) + jnp.concatenate(products, 0)
 
     for index in range(count):
         for head in range(heads):
@@ -276,7 +277,7 @@
             pltpu.VMEM((columns, share, padded), f32),
             pltpu.VMEM((columns, share, padded), f32),
         ],
-        compiler_params=pltpu.CompilerParams(vmem_limit_bytes=60 << 20),
+        compiler_params=pltpu.CompilerParams(vmem_limit_bytes=48 << 20),
         cost_estimate=cost(0.001),
         name="attend_backward",
     )(info, *operands)
@@ -313,7 +314,7 @@
             out_specs=[pl.BlockSpec((1, own, feature), place), block(low, 0)],
         ),
         out_shape=[jax.ShapeDtypeStruct((columns, own, feature), bf16), low],
-        compiler_params=pltpu.CompilerParams(vmem_limit_bytes=60 << 20),
+        compiler_params=pltpu.CompilerParams(vmem_limit_bytes=40 << 20),
         cost_estimate=cost(0.001),
         name="unproject",
     )(info, dq, near, far_k, near, far_v, weight, cosine, sine)
@@ -332,7 +333,7 @@
     return pl.pallas_call(
         project_grad_kernel,
         out_shape=jax.ShapeDtypeStruct((blocks[0].shape[1], low.shape[2]), bf16),
-        compiler_params=pltpu.CompilerParams(vmem_limit_bytes=60 << 20),
+        compiler_params=pltpu.CompilerParams(vmem_limit_bytes=40 << 20),
         cost_estimate=cost(0.001),
         name="project_grad",
     )(low, *blocks)
@@ -516,11 +517,12 @@
     hidden_cols = act.shape[1]
     eye = unit(quarter)
     away = lambda index, mine: jnp.where(index == mine, 0, 1)
-    for pair in range(2):
-        row = 2 * pair + core
-        mine = pl.ds(pl.multiple_of(row * quarter, quarter), quarter)
-        inner = jnp.dot(hidden_ref[mine, :], gin, preferred_element_type=f32).astype(bf16)
-        outer = jnp.dot(gtwo_ref[mine, :], act, preferred_element_type=f32).astype(bf16)
+    rows = [2 * pair + core for pair in range(2)]
+    spans = [pl.ds(pl.multiple_of(row * quarter, quarter), quarter) for row in rows]
+    both = lambda ref: jnp.concatenate([ref[span, :] for span in spans], 0)
+    inner = jnp.dot(both(hidden_ref), gin, preferred_element_type=f32).astype(bf16)
+    outer = jnp.dot(both(gtwo_ref), act, preferred_element_type=f32).astype(bf16)
+    for pair, row in enumerate(rows):
         mixed = jnp.dot(attended, gone_ref[row], preferred_element_type=f32).astype(bf16)
         vector = contract(eye, sums_ref[row], (1, 1)).astype(bf16)
         rest = jnp.zeros((quarter, lanes - 2 * hidden_cols - quarter - 4), bf16)
@@ -528,10 +530,10 @@
         far = away(pair, info_ref[3])
         for part in range(slabs):
             place = away(part, info_ref[4]) if slabs > 1 else 0
-            rows = slice(part * slab, (part + 1) * slab)
-            out[far, place, :, 0:hidden_cols] = inner[rows]
-            out[far, place, :, hidden_cols : 2 * hidden_cols] = outer[rows]
-            out[far, place, :, 2 * hidden_cols :] = tail[rows]
+            low = pair * quarter + part * slab
+            out[far, place, :, 0:hidden_cols] = inner[low : low + slab]
+            out[far, place, :, hidden_cols : 2 * hidden_cols] = outer[low : low + slab]
+            out[far, place, :, 2 * hidden_cols :] = tail[part * slab : (part + 1) * slab]
 
 
 def attended_block(info_ref, att_refs, column):

time: 299 us -> 300 us (level); the launches traced: 298 us -> 294 us
  Pallas kernels: 94.2 us -> 86.7 us
  waiting for transfers between devices: 104 us -> 108 us
    ppermute x17, waiting for transfers between devices: 37.7 us -> 44.3 us  [swap(): return lax.ppermute(values, axis, SWAP)]
  transfers between devices with their start and end apart: 30 -> 30, of which waited for: 19 -> 21; matrix products, arithmetic and copies ran while one was open for 8% -> 8% of each run, Pallas kernels for 24% -> 21%
where the time goes in v7:
time: 300 us; the launch traced here: 294 us
  waiting for transfers between devices  108 us (36%)
  Pallas kernels  86.7 us (29%)
  starting transfers between devices  56.1 us (19%)
  between operations  16.3 us (5%)
  local copies, waits for them, and re-layouts  13.7 us (5%)
  other arithmetic  8.11 us (3%)
  matrix products  5.53 us (2%)
    ppermute x17, waiting for transfers between devices, swap(): return lax.ppermute(values, axis, SWAP)  44.3 us
    ppermute x6, waiting for transfers between devices, shift(): lax.ppermute(values, 'col', [(i, (i + step) % columns) for i in range(col...  37.6 us
    pallas_call x1, Pallas kernels, feed(): pl.pallas_call(feed_kernel, in_specs=[smem, vmem, vmem, pl.BlockSpec(memo...  20.4 us
    ppermute x17, starting transfers between devices, swap(): return lax.ppermute(values, axis, SWAP)  18.4 us
    pallas_call x2, Pallas kernels, attend_forward(): pl.pallas_call(lambda *refs: forward_kernel(first, share, *refs), grid_sp...  17.1 us
    pallas_call x1, Pallas kernels, attend_backward(): pl.pallas_call(lambda *refs: backward_kernel(columns, share, *refs), in_s...  15.9 us
    pallas_call x3, Pallas kernels, add_blocks(): pl.pallas_call(lambda *refs: add_kernel(len(lengths), sums, *refs), in_sp...  11.3 us
    all_to_all x1, starting transfers between devices, to_loader(): lax.all_to_all(cut, ('dp',) + ROWS, split_axis=0, concat_axis=0, tiled=True)  11.2 us
  transfers between devices with their start and end apart: 30, of which 21 were waited for; matrix products, arithmetic and copies ran while one was open for 8% of the time, Pallas kernels for 21%

profile of v7, /device:TPU:0, one launch (start us, length us, event | category | flops | bytes accessed | tf_op | source)
XLA Modules:
  0.0 294.5 jit_solution(5465888685306130135)
XLA Ops:
  7.3 2.2 parcel.1
  9.5 3.0 %collective-permute-start = (bf16[2,192,512]{2,1,0:T(8,128)(2,1)}, bf16[2,192,512]{2,1,0:T(8,128)(2,1)S(1)}, u32[]{:S(2)}, u32[]{:S(2)}) collective-permute-start(bf16[2,192,512]{2,1,0:T(8,128)(2,1)} %param.14), channel_id=1, source_target_pairs={{0,16},{16,0},{1,17},{17,1},{2,18},{18,2},{3,19},{19,3},{4,20},{20... | collective-permute-start | bytes 1179656 | tf_op jit(solution)/shard_map/ppermute | solution.py:28
  13.7 2.0 collective-permute-start.6
  18.0 3.0 %fusion.30 = (f32[4,256,128]{2,1,0:T(8,128)}, f32[4,256,128]{2,1,0:T(8,128)}) fusion(f32[128]{0:T(128)S(1)} %compare_select_fusion.2, f32[128]{0:T(128)S(1)} %mul.76, f32[4,256]{1,0:T(4,128)S(1)} %subtract_convert_fusion), kind=kLoop, calls=%fused_computation.28 | loop fusion | flops 262144 | bytes 1053696 | tf_op jit(solution)/shard_map/mul | solution.py:780
  22.1 1.8 fusion.24
  23.9 1.8 collective-permute-start.1
  27.6 3.5 %all-to-all-start = ((bf16[4,256,192]{1,2,0:T(8,128)(2,1)}), bf16[4,256,192]{1,2,0:T(8,128)(2,1)S(1)}, u32[]{:S(2)}, u32[]{:S(2)}) async-start(bf16[4,256,192]{1,2,0:T(8,128)(2,1)} %bitcast.109), calls=%async_computation | async-start | bytes 786432 | tf_op jit(solution)/shard_map/all_to_all | solution.py:791
  31.0 4.9 %collective-permute-done.1 = bf16[2,192,512]{2,1,0:T(8,128)(2,1)S(1)} collective-permute-done((bf16[2,192,512]{2,1,0:T(8,128)(2,1)S(1)}, bf16[2,192,512]{2,1,0:T(8,128)(2,1)S(1)}, u32[]{:S(2)}, u32[]{:S(2)}) %collective-permute-start.1) | collective-permute-done | bytes 393248 | tf_op jit(solution)/shard_map/ppermute | solution.py:28
  36.0 2.4 all-to-all-done
  38.6 3.6 %collective-permute-start.2 = (bf16[256,768]{1,0:T(8,128)(2,1)S(1)}, bf16[256,768]{1,0:T(8,128)(2,1)S(1)}, u32[]{:S(2)}, u32[]{:S(2)}) collective-permute-start(bf16[256,768]{1,0:T(8,128)(2,1)S(1)} %copy.43.refs_0_.x_ref), channel_id=1, source_target_pairs={{0,3},{1,0},{2,1},{3,2},{4,7},{5,4},{6,5},{7,6},{8,11},{9,8},{10,9... | collective-permute-start | bytes 1179656 | tf_op jit(solution)/shard_map/ppermute | solution.py:622
  43.3 1.8 fusion.21
  45.9 4.4 %all-to-all-start.1 = ((bf16[4,256,192]{1,2,0:T(8,128)(2,1)}), bf16[4,256,192]{1,2,0:T(8,128)(2,1)}, u32[]{:S(2)}, u32[]{:S(2)}) async-start(bf16[4,256,192]{1,2,0:T(8,128)(2,1)} %bitcast.108), calls=%async_computation.1 | async-start | bytes 786432 | tf_op jit(solution)/shard_map/all_to_all | solution.py:791
  51.7 6.1 %all-to-all-done.1 = bf16[4,256,192]{1,2,0:T(8,128)(2,1)} async-done(((bf16[4,256,192]{1,2,0:T(8,128)(2,1)}), bf16[4,256,192]{1,2,0:T(8,128)(2,1)}, u32[]{:S(2)}, u32[]{:S(2)}) %all-to-all-start.1) | async-done | bytes 393248 | tf_op jit(solution)/shard_map/all_to_all | solution.py:791
  57.8 12.4 %collective-permute-done.2.refs_3_ = bf16[256,768]{1,0:T(8,128)(2,1)S(1)} collective-permute-done((bf16[256,768]{1,0:T(8,128)(2,1)S(1)}, bf16[256,768]{1,0:T(8,128)(2,1)S(1)}, u32[]{:S(2)}, u32[]{:S(2)}) %collective-permute-start.2) | collective-permute-done | bytes 393248 | tf_op jit(solution)/shard_map/ppermute | solution.py:622
  70.2 4.7 %collective-permute-done.4.refs_1_ = bf16[256,768]{1,0:T(8,128)(2,1)S(1)} collective-permute-done((bf16[256,768]{1,0:T(8,128)(2,1)S(1)}, bf16[256,768]{1,0:T(8,128)(2,1)S(1)}, u32[]{:S(2)}, u32[]{:S(2)}) %collective-permute-start.4) | collective-permute-done | bytes 393248 | tf_op jit(solution)/shard_map/ppermute | solution.py:622
  74.9 15.5 %collective-permute-done.5.refs_2_ = bf16[256,768]{1,0:T(8,128)(2,1)S(1)} collective-permute-done((bf16[256,768]{1,0:T(8,128)(2,1)S(1)}, bf16[256,768]{1,0:T(8,128)(2,1)S(1)}, u32[]{:S(2)}, u32[]{:S(2)}) %collective-permute-start.5) | collective-permute-done | bytes 393248 | tf_op jit(solution)/shard_map/ppermute | solution.py:622
  91.1 5.4 %project.1 = (bf16[4,256,256]{2,1,0:T(8,128)(2,1)}, bf16[8,256,256]{2,1,0:T(8,128)(2,1)}, bf16[8,192,256]{2,1,0:T(8,128)(2,1)}) custom-call(bf16[256,768]{1,0:T(8,128)(2,1)} %copy-done.4, bf16[256,768]{1,0:T(8,128)(2,1)} %copy-done.11, bf16[256,768]{1,0:T(8,128)(2,1)} %copy-done.13, bf16[256,768]{1,0:T(8,128)(2,1)} %copy-done.9, bf16[768,576]{1,0:T(8,128)(2,1)} %bitcast.110, ...), custom_call_target="tpu_custom_call" | custom-call | flops 1000000 | bytes 3000 | tf_op jit(solution)/shard_map/project/pallas_call | solution.py:76
  97.6 2.9 collective-permute-done.9.refs_5_
  101.8 12.7 %attend_forward.2 = (bf16[192,256]{1,0:T(8,128)(2,1)}, bf16[192,256]{1,0:T(8,128)(2,1)}, bf16[192,256]{1,0:T(8,128)(2,1)}, f32[3,256]{1,0:T(4,128)}, f32[3,256]{1,0:T(4,128)}, /*index=5*/f32[3,256]{1,0:T(4,128)}) custom-call(s32[5]{0:T(128)} %stack.68.refs_0_.info_ref, bf16[4,256,256]{2,1,0:T(8,128)(2,1)} %get-tuple-element.96.refs_1_, ...), custom_call_target="tpu_custom_call" | custom-call | flops 1000000 | bytes 3000 | tf_op jit(solution)/shard_map/attend_forward/pallas_call | solution.py:182
  114.5 4.8 %collective-permute-start.10 = (bf16[192,256]{1,0:T(8,128)(2,1)}, bf16[192,256]{1,0:T(8,128)(2,1)S(1)}, u32[]{:S(2)}, u32[]{:S(2)}) collective-permute-start(bf16[192,256]{1,0:T(8,128)(2,1)} %get-tuple-element.98.refs_8_), channel_id=1, source_target_pairs={{0,3},{1,0},{2,1},{3,2},{4,7},{5,4},{6,5},{7,6},{8,11},{9,8},{10,9... | collective-permute-start | bytes 294920 | tf_op jit(solution)/shard_map/ppermute | solution.py:622
  120.4 1.9 copy.44.cot_ref
  122.4 4.3 %attend_forward.3 = (bf16[192,256]{1,0:T(8,128)(2,1)}, f32[3,256]{1,0:T(4,128)}) custom-call(s32[5]{0:T(128)} %stack.68.refs_0_.info_ref, bf16[4,256,256]{2,1,0:T(8,128)(2,1)} %get-tuple-element.96.refs_1_, bf16[8,256,256]{2,1,0:T(8,128)(2,1)} %get-tuple-element.91.refs_2_, bf16[8,256,256]{2,1,0:T(8,128)(2,1)} %copy-done.24, ...), custom_call_target="tpu_custom_call" | custom-call | flops 1000000 | bytes 3000 | tf_op jit(solution)/shard_map/attend_forward/pallas_call | solution.py:182
  126.7 4.9 %collective-permute-done.11.refs_2_ = bf16[192,256]{1,0:T(8,128)(2,1)S(1)} collective-permute-done((bf16[192,256]{1,0:T(8,128)(2,1)}, bf16[192,256]{1,0:T(8,128)(2,1)S(1)}, u32[]{:S(2)}, u32[]{:S(2)}) %collective-permute-start.11) | collective-permute-done | bytes 98336 | tf_op jit(solution)/shard_map/ppermute | solution.py:622
  132.3 20.4 %feed.1 = (bf16[256,768]{1,0:T(8,128)(2,1)}, bf16[4,192,256]{2,1,0:T(8,128)(2,1)}, f32[256,768]{1,0:T(8,128)}, bf16[768,256]{1,0:T(8,128)(2,1)}, bf16[4,256,768]...) custom-call(s32[5]{0:T(128)} %stack.68.refs_0_.info_ref, ...), custom_call_target="tpu_custom_call" | custom-call | flops 1000000 | bytes 3000 | tf_op jit(solution)/shard_map/feed/pallas_call | solution.py:489
  152.8 3.6 %all-to-all-start.2 = ((bf16[4,192,256]{2,1,0:T(8,128)(2,1)}), bf16[4,192,256]{2,1,0:T(8,128)(2,1)S(1)}, u32[]{:S(2)}, u32[]{:S(2)}) async-start(bf16[4,192,256]{2,1,0:T(8,128)(2,1)} %get-tuple-element.103), calls=%async_computation.2 | async-start | bytes 786432 | tf_op jit(solution)/shard_map/all_to_all | solution.py:812
  156.4 7.2 %weigh.1.refs_0_ = bf16[2,2,4,96,1792]{4,3,2,1,0:T(8,128)(2,1)} custom-call(s32[5]{0:T(128)} %stack.68.refs_0_.info_ref, bf16[768,256]{1,0:T(8,128)(2,1)} %get-tuple-element.104.hidden_ref, bf16[4,256,768]{2,1,0:T(8,128)(2,1)} %get-tuple-element.105.act_ref, bf16[4,256,768]{2,1,0:T(8,128)(2,1)} %get-tuple-element.106.gin_ref, ...), custom_call_target="tpu_custom_call" | custom-call | flops 1000000 | bytes 3000 | tf_op jit(solution)/shard_map/weigh/pallas_call | solution.py:561
  163.7 4.1 %add_blocks.3 = (bf16[4,96,1792]{2,1,0:T(8,128)(2,1)}, bf16[4,96,1792]{2,1,0:T(8,128)(2,1)}) custom-call(bf16[2,2,4,96,1792]{4,3,2,1,0:T(8,128)(2,1)} %weigh.1.refs_0_, bf16[2,2,4,96,1792]{4,3,2,1,0:T(8,128)(2,1)} %collective-permute-done.13.refs_1_), custom_call_target="tpu_custom_call" | custom-call | flops 1000000 | bytes 3000 | tf_op jit(solution)/shard_map/add_blocks/pallas_call | solution.py:656
  169.0 2.7 collective-permute-start.16
  172.2 15.9 %attend_backward.1 = (f32[4,256,192]{2,1,0:T(8,128)S(1)}, bf16[8,256,256]{2,1,0:T(8,128)(2,1)S(1)}, bf16[4,256,256]{2,1,0:T(8,128)(2,1)S(1)}, bf16[4,256,256]{2,1,0:T(8,128)(2,1)S(1)}) custom-call(s32[5]{0:T(128)S(1)} %copy-done.19, bf16[4,256,256]{2,1,0:T(8,128)(2,1)S(1)} %copy-done.8, bf16[8,256,256]{2,1,0:T(8,128)(2,1)} %get-tuple-element.91.refs_2_, ...), custom_call_target="tpu_custom_call" | custom-call | flops 1000000 | bytes 3000 | tf_op jit(solution)/shard_map/attend_backward/pallas_call | solution.py:265
  190.8 4.4 %unproject.1 = (bf16[4,256,768]{2,1,0:T(8,128)(2,1)}, bf16[4,256,576]{2,1,0:T(8,128)(2,1)S(1)}) custom-call(s32[5]{0:T(128)S(1)} %copy-done.19, f32[4,256,192]{2,1,0:T(8,128)S(1)} %get-tuple-element.118.dq_ref, bf16[8,256,256]{2,1,0:T(8,128)(2,1)S(1)} %get-tuple-element.119.near_k_ref.near_v_ref, bf16[4,256,256]{2,1,0:T(8,128)(2,1)S(1)} %collective-permute-done.14.far_k_ref, ...), custom_call_target="tpu_custom_call" | custom-call | flops 1000000 | bytes 3000 | tf_op jit(solution)/shard_map/unproject/pallas_call | solution.py:307
  195.2 4.4 %all-to-all-start.3 = ((bf16[4,256,768]{2,1,0:T(8,128)(2,1)}), bf16[4,256,768]{2,1,0:T(8,128)(2,1)}, u32[]{:S(2)}, u32[]{:S(2)}) async-start(bf16[4,256,768]{2,1,0:T(8,128)(2,1)} %get-tuple-element.122), calls=%async_computation.3 | async-start | bytes 3145728 | tf_op jit(solution)/shard_map/all_to_all | solution.py:842
  199.6 2.2 collective-permute-done.16.refs_2_
  201.8 1.5 collective-permute-done.17.refs_3_
  203.3 3.4 %add_blocks.4 = (bf16[2,96,1792]{2,1,0:T(8,128)(2,1)}, bf16[2,96,1792]{2,1,0:T(8,128)(2,1)}) custom-call(bf16[2,2,4,96,1792]{4,3,2,1,0:T(8,128)(2,1)} %weigh.1.refs_0_, bf16[2,2,4,96,1792]{4,3,2,1,0:T(8,128)(2,1)} %collective-permute-done.13.refs_1_, bf16[4,96,1792]{2,1,0:T(8,128)(2,1)} %collective-permute-done.16.refs_2_, ...), custom_call_target="tpu_custom_call" | custom-call | flops 1000000 | bytes 3000 | tf_op jit(solution)/shard_map/add_blocks/pallas_call | solution.py:656
  207.4 1.7 collective-permute-start.19
  210.6 12.0 %collective-permute-done.18.refs_4_ = bf16[2,96,1792]{2,1,0:T(8,128)(2,1)} collective-permute-done((bf16[2,96,1792]{2,1,0:T(8,128)(2,1)}, bf16[2,96,1792]{2,1,0:T(8,128)(2,1)}, u32[]{:S(2)}, u32[]{:S(2)}) %collective-permute-start.18) | collective-permute-done | bytes 688160 | tf_op jit(solution)/shard_map/ppermute | solution.py:28
  224.0 3.8 %add_blocks.5 = bf16[4,96,1792]{2,1,0:T(8,128)(2,1)} custom-call(bf16[2,2,4,96,1792]{4,3,2,1,0:T(8,128)(2,1)} %weigh.1.refs_0_, bf16[2,2,4,96,1792]{4,3,2,1,0:T(8,128)(2,1)} %collective-permute-done.13.refs_1_, bf16[4,96,1792]{2,1,0:T(8,128)(2,1)} %collective-permute-done.16.refs_2_, bf16[4,96,1792]{2,1,0:T(8,128)(2,1)} %collective-permute-done.17.refs_3_, ...), custom_call_target="tpu_custom_call" | custom-call | flops 1000000 | bytes 3000 | tf_op jit(solution)/shard_map/add_blocks/pallas_call | solution.py:656
  228.0 1.8 collective-permute-done.20
  230.1 1.7 collective-permute-start.21
  232.0 6.1 %collective-permute-done.21 = bf16[192,576]{1,0:T(8,128)(2,1)S(1)} collective-permute-done((bf16[192,576]{1,0:T(8,128)(2,1)S(1)}, bf16[192,576]{1,0:T(8,128)(2,1)S(1)}, u32[]{:S(2)}, u32[]{:S(2)}) %collective-permute-start.21) | collective-permute-done | bytes 221216 | tf_op jit(solution)/shard_map/ppermute | solution.py:28
  238.3 1.7 convert_reduce_fusion
  242.0 11.2 %all-to-all-start.4 = ((bf16[8,256,384]{2,1,0:T(8,128)(2,1)}), bf16[8,256,384]{2,1,0:T(8,128)(2,1)S(1)}, u32[]{:S(2)}, u32[]{:S(2)}) async-start(bf16[8,256,384]{2,1,0:T(8,128)(2,1)} %bitcast.40), calls=%async_computation.4 | async-start | bytes 3145728 | tf_op jit(solution)/shard_map/all_to_all | solution.py:816
  253.2 8.8 %reduce-scatter.2.cloned.1.call-done = bf16[1,96,1792]{2,1,0:T(8,128)(2,1)} async-done(((bf16[4,96,1792]{2,1,0:T(8,128)(2,1)}), bf16[1,96,1792]{2,1,0:T(8,128)(2,1)}) %reduce-scatter.2.cloned.1.call-update) | async-done | bytes 344080 | tf_op jit(solution)/shard_map/reduce_scatter | solution.py:741
  263.2 3.0 %collective-permute-start.22 = (bf16[96,2944]{1,0:T(8,128)(2,1)S(1)}, bf16[96,2944]{1,0:T(8,128)(2,1)S(1)}, u32[]{:S(2)}, u32[]{:S(2)}) collective-permute-start(bf16[96,2944]{1,0:T(8,128)(2,1)S(1)} %concatenate.11.refs_1_), channel_id=1, source_target_pairs={{0,16},{16,0},{1,17},{17,1},{2,18},{18,2},{3,19},{19,3},{4,20},{20... | collective-permute-start | bytes 1695752 | tf_op jit(solution)/shard_map/ppermute | solution.py:28
  266.2 7.7 %all-to-all-done.4 = bf16[8,256,384]{2,1,0:T(8,128)(2,1)S(1)} async-done(((bf16[8,256,384]{2,1,0:T(8,128)(2,1)}), bf16[8,256,384]{2,1,0:T(8,128)(2,1)S(1)}, u32[]{:S(2)}, u32[]{:S(2)}) %all-to-all-start.4) | async-done | bytes 1572896 | tf_op jit(solution)/shard_map/all_to_all | solution.py:816
  273.9 2.0 fusion.12
  276.9 8.4 %collective-permute-done.22.refs_2_ = bf16[96,2944]{1,0:T(8,128)(2,1)S(1)} collective-permute-done((bf16[96,2944]{1,0:T(8,128)(2,1)S(1)}, bf16[96,2944]{1,0:T(8,128)(2,1)S(1)}, u32[]{:S(2)}, u32[]{:S(2)}) %collective-permute-start.22) | collective-permute-done | bytes 565280 | tf_op jit(solution)/shard_map/ppermute | solution.py:28
  285.3 1.5 open_shards.1
  (152 shorter events, 26.9 us)
Async XLA Ops:
  7.2 14.7 %copy-start.30 = (bf16[2,192,512]{2,1,0:T(8,128)(2,1)S(1)}, bf16[2,192,512]{2,1,0:T(8,128)(2,1)}, u32[]{:S(2)}) copy-start(bf16[2,192,512]{2,1,0:T(8,128)(2,1)} %param.14) | copy-start | bytes 1179652
  7.2 8.8 %copy-start.35 = (s32[2,512]{1,0:T(2,128)S(1)}, s32[2,512]{1,0:T(2,128)}, u32[]{:S(2)}) copy-start(s32[2,512]{1,0:T(2,128)} %param.17) | copy-start | bytes 12292
  7.2 8.8 %copy-start.36 = (s32[1,2]{1,0:T(1,128)S(1)}, s32[1,2]{1,0:T(1,128)}, u32[]{:S(2)}) copy-start(s32[1,2]{1,0:T(1,128)} %param.16) | copy-start | bytes 28
  7.2 124.4 %all-gather.3.cloned.1.call-start = ((), (), s32[]{:S(2)}) async-start(), calls=%async_computation.7 | async-start | bytes 11354112 | tf_op jit(solution)/shard_map/all_gather | solution.py:769
  9.5 12.4 %collective-permute-start = (bf16[2,192,512]{2,1,0:T(8,128)(2,1)}, bf16[2,192,512]{2,1,0:T(8,128)(2,1)S(1)}, u32[]{:S(2)}, u32[]{:S(2)}) collective-permute-start(bf16[2,192,512]{2,1,0:T(8,128)(2,1)} %param.14), channel_id=1, source_target_pairs={{0,16},{16,0},{1,17},{17,1},{2,18},{18,2},{3,19},{19,3},{4,20},{20... | collective-permute-start | bytes 1179656 | tf_op jit(solution)/shard_map/ppermute | solution.py:28
  12.5 9.4 %collective-permute-start.3 = (s32[2,512]{1,0:T(2,128)}, s32[2,512]{1,0:T(2,128)S(1)}, u32[]{:S(2)}, u32[]{:S(2)}) collective-permute-start(s32[2,512]{1,0:T(2,128)} %param.17), channel_id=1, source_target_pairs={{0,16},{16,0},{1,17},{17,1},{2,18},{18,2},{3,19},{19,3},{4,20},{20... | collective-permute-start | bytes 12296 | tf_op jit(solution)/shard_map/ppermute | solution.py:28
  13.7 12.1 %collective-permute-start.6 = (bf16[192,576]{1,0:T(8,128)(2,1)S(1)}, bf16[192,576]{1,0:T(8,128)(2,1)S(1)}, u32[]{:S(2)}, u32[]{:S(2)}) collective-permute-start(bf16[192,576]{1,0:T(8,128)(2,1)S(1)} %pad_maximum_fusion.5), channel_id=1, source_target_pairs={{0,8},{8,0},{1,9},{9,1},{2,10},{10,2},{3,11},{11,3},{4,12},{12,4},... | collective-permute-start | bytes 663560 | tf_op jit(solution)/shard_map/ppermute | solution.py:28
  23.9 12.0 %collective-permute-start.1 = (bf16[2,192,512]{2,1,0:T(8,128)(2,1)S(1)}, bf16[2,192,512]{2,1,0:T(8,128)(2,1)S(1)}, u32[]{:S(2)}, u32[]{:S(2)}) collective-permute-start(bf16[2,192,512]{2,1,0:T(8,128)(2,1)S(1)} %copy-done.31), channel_id=1, source_target_pairs={{0,16},{16,0},{1,17},{17,1},{2,18},{18,2},{3,19},{19,3},{4,20},{20... | collective-permute-start | bytes 1179656 | tf_op jit(solution)/shard_map/ppermute | solution.py:28
  26.8 23.5 %collective-permute-start.7 = (bf16[2,192,576]{2,1,0:T(8,128)(2,1)}, bf16[2,192,576]{2,1,0:T(8,128)(2,1)S(1)}, u32[]{:S(2)}, u32[]{:S(2)}) collective-permute-start(bf16[2,192,576]{2,1,0:T(8,128)(2,1)} %pad_maximum_fusion.4), channel_id=1, source_target_pairs={{0,4},{4,0},{1,5},{5,1},{2,6},{6,2},{3,7},{7,3},{8,12},{12,8},{9,1... | collective-permute-start | bytes 1327112 | tf_op jit(solution)/shard_map/ppermute | solution.py:28
  27.6 10.9 %all-to-all-start = ((bf16[4,256,192]{1,2,0:T(8,128)(2,1)}), bf16[4,256,192]{1,2,0:T(8,128)(2,1)S(1)}, u32[]{:S(2)}, u32[]{:S(2)}) async-start(bf16[4,256,192]{1,2,0:T(8,128)(2,1)} %bitcast.109), calls=%async_computation | async-start | bytes 786432 | tf_op jit(solution)/shard_map/all_to_all | solution.py:791
  38.6 31.6 %collective-permute-start.2 = (bf16[256,768]{1,0:T(8,128)(2,1)S(1)}, bf16[256,768]{1,0:T(8,128)(2,1)S(1)}, u32[]{:S(2)}, u32[]{:S(2)}) collective-permute-start(bf16[256,768]{1,0:T(8,128)(2,1)S(1)} %copy.43.refs_0_.x_ref), channel_id=1, source_target_pairs={{0,3},{1,0},{2,1},{3,2},{4,7},{5,4},{6,5},{7,6},{8,11},{9,8},{10,9... | collective-permute-start | bytes 1179656 | tf_op jit(solution)/shard_map/ppermute | solution.py:622
  42.3 32.6 %collective-permute-start.4 = (bf16[256,768]{1,0:T(8,128)(2,1)S(1)}, bf16[256,768]{1,0:T(8,128)(2,1)S(1)}, u32[]{:S(2)}, u32[]{:S(2)}) collective-permute-start(bf16[256,768]{1,0:T(8,128)(2,1)S(1)} %copy.43.refs_0_.x_ref), channel_id=1, source_target_pairs={{0,1},{1,2},{2,3},{3,0},{4,5},{5,6},{6,7},{7,4},{8,9},{9,10},{10,1... | collective-permute-start | bytes 1179656 | tf_op jit(solution)/shard_map/ppermute | solution.py:622
  42.3 48.1 %collective-permute-start.5 = (bf16[256,768]{1,0:T(8,128)(2,1)S(1)}, bf16[256,768]{1,0:T(8,128)(2,1)S(1)}, u32[]{:S(2)}, u32[]{:S(2)}) collective-permute-start(bf16[256,768]{1,0:T(8,128)(2,1)S(1)} %copy.43.refs_0_.x_ref), channel_id=1, source_target_pairs={{0,2},{1,3},{2,0},{3,1},{4,6},{5,7},{6,4},{7,5},{8,10},{9,11},{10,... | collective-permute-start | bytes 1179656 | tf_op jit(solution)/shard_map/ppermute | solution.py:622
  45.9 11.9 %all-to-all-start.1 = ((bf16[4,256,192]{1,2,0:T(8,128)(2,1)}), bf16[4,256,192]{1,2,0:T(8,128)(2,1)}, u32[]{:S(2)}, u32[]{:S(2)}) async-start(bf16[4,256,192]{1,2,0:T(8,128)(2,1)} %bitcast.108), calls=%async_computation.1 | async-start | bytes 786432 | tf_op jit(solution)/shard_map/all_to_all | solution.py:791
  70.2 20.2 %copy-start.9 = (bf16[256,768]{1,0:T(8,128)(2,1)}, bf16[256,768]{1,0:T(8,128)(2,1)S(1)}, u32[]{:S(2)}) copy-start(bf16[256,768]{1,0:T(8,128)(2,1)S(1)} %collective-permute-done.2.refs_3_) | copy-start | bytes 1179652
  74.9 15.5 %copy-start.11 = (bf16[256,768]{1,0:T(8,128)(2,1)}, bf16[256,768]{1,0:T(8,128)(2,1)S(1)}, u32[]{:S(2)}) copy-start(bf16[256,768]{1,0:T(8,128)(2,1)S(1)} %collective-permute-done.4.refs_1_) | copy-start | bytes 1179652
  96.5 4.0 %collective-permute-start.8 = (bf16[8,256,256]{2,1,0:T(8,128)(2,1)}, bf16[8,256,256]{2,1,0:T(8,128)(2,1)S(1)}, u32[]{:S(2)}, u32[]{:S(2)}) collective-permute-start(bf16[8,256,256]{2,1,0:T(8,128)(2,1)} %get-tuple-element.91.refs_2_), channel_id=1, source_target_pairs={{0,4},{4,0},{1,5},{5,1},{2,6},{6,2},{3,7},{7,3},{8,12},{12,8},{9,1... | collective-permute-start | bytes 3145736 | tf_op jit(solution)/shard_map/ppermute | solution.py:28
  96.5 4.0 %collective-permute-start.9 = (bf16[8,192,256]{2,1,0:T(8,128)(2,1)}, bf16[8,192,256]{2,1,0:T(8,128)(2,1)S(1)}, u32[]{:S(2)}, u32[]{:S(2)}) collective-permute-start(bf16[8,192,256]{2,1,0:T(8,128)(2,1)} %get-tuple-element.92.refs_4_), channel_id=1, source_target_pairs={{0,4},{4,0},{1,5},{5,1},{2,6},{6,2},{3,7},{7,3},{8,12},{12,8},{9,1... | collective-permute-start | bytes 2359304 | tf_op jit(solution)/shard_map/ppermute | solution.py:28
  114.5 12.2 %collective-permute-start.10 = (bf16[192,256]{1,0:T(8,128)(2,1)}, bf16[192,256]{1,0:T(8,128)(2,1)S(1)}, u32[]{:S(2)}, u32[]{:S(2)}) collective-permute-start(bf16[192,256]{1,0:T(8,128)(2,1)} %get-tuple-element.98.refs_8_), channel_id=1, source_target_pairs={{0,3},{1,0},{2,1},{3,2},{4,7},{5,4},{6,5},{7,6},{8,11},{9,8},{10,9... | collective-permute-start | bytes 294920 | tf_op jit(solution)/shard_map/ppermute | solution.py:622
  119.3 12.3 %collective-permute-start.11 = (bf16[192,256]{1,0:T(8,128)(2,1)}, bf16[192,256]{1,0:T(8,128)(2,1)S(1)}, u32[]{:S(2)}, u32[]{:S(2)}) collective-permute-start(bf16[192,256]{1,0:T(8,128)(2,1)} %get-tuple-element.99.refs_9_), channel_id=1, source_target_pairs={{0,2},{1,3},{2,0},{3,1},{4,6},{5,7},{6,4},{7,5},{8,10},{9,11},{10,... | collective-permute-start | bytes 294920 | tf_op jit(solution)/shard_map/ppermute | solution.py:622
  119.3 12.3 %collective-permute-start.12 = (bf16[192,256]{1,0:T(8,128)(2,1)}, bf16[192,256]{1,0:T(8,128)(2,1)S(1)}, u32[]{:S(2)}, u32[]{:S(2)}) collective-permute-start(bf16[192,256]{1,0:T(8,128)(2,1)} %get-tuple-element.100.refs_10_), channel_id=1, source_target_pairs={{0,1},{1,2},{2,3},{3,0},{4,5},{5,6},{6,7},{7,4},{8,9},{9,10},{10,1... | collective-permute-start | bytes 294920 | tf_op jit(solution)/shard_map/ppermute | solution.py:622
  152.7 11.0 %collective-permute-start.13 = (bf16[2,2,4,96,1792]{4,3,2,1,0:T(8,128)(2,1)}, bf16[2,2,4,96,1792]{4,3,2,1,0:T(8,128)(2,1)}, u32[]{:S(2)}, u32[]{:S(2)}) collective-permute-start(bf16[2,2,4,96,1792]{4,3,2,1,0:T(8,128)(2,1)} %get-tuple-element.110), channel_id=1, source_target_pairs={{0,4},{4,0},{1,5},{5,1},{2,6},{6,2},{3,7},{7,3},{8,12},{12,8},{9,1... | collective-permute-start | bytes 16515080 | tf_op jit(solution)/shard_map/ppermute | solution.py:28
  152.8 16.2 %all-to-all-start.2 = ((bf16[4,192,256]{2,1,0:T(8,128)(2,1)}), bf16[4,192,256]{2,1,0:T(8,128)(2,1)S(1)}, u32[]{:S(2)}, u32[]{:S(2)}) async-start(bf16[4,192,256]{2,1,0:T(8,128)(2,1)} %get-tuple-element.103), calls=%async_computation.2 | async-start | bytes 786432 | tf_op jit(solution)/shard_map/all_to_all | solution.py:812
  163.6 8.5 %copy-start.1 = (bf16[8,192,256]{2,1,0:T(8,128)(2,1)S(1)}, bf16[8,192,256]{2,1,0:T(8,128)(2,1)}, u32[]{:S(2)}) copy-start(bf16[8,192,256]{2,1,0:T(8,128)(2,1)} %get-tuple-element.92.refs_4_) | copy-start | bytes 2359300
  163.6 8.5 %copy-start.3 = (bf16[8,192,256]{2,1,0:T(8,128)(2,1)S(1)}, bf16[8,192,256]{2,1,0:T(8,128)(2,1)}, u32[]{:S(2)}) copy-start(bf16[8,192,256]{2,1,0:T(8,128)(2,1)} %copy-done.2) | copy-start | bytes 2359300
  163.6 8.5 %copy-start.8 = (bf16[4,256,256]{2,1,0:T(8,128)(2,1)S(1)}, bf16[4,256,256]{2,1,0:T(8,128)(2,1)}, u32[]{:S(2)}) copy-start(bf16[4,256,256]{2,1,0:T(8,128)(2,1)} %get-tuple-element.96.refs_1_) | copy-start | bytes 1572868
  163.6 8.5 %copy-start.15 = (bf16[192,256]{1,0:T(8,128)(2,1)S(1)}, bf16[192,256]{1,0:T(8,128)(2,1)}, u32[]{:S(2)}) copy-start(bf16[192,256]{1,0:T(8,128)(2,1)} %get-tuple-element.97.refs_0_.refs_7_) | copy-start | bytes 294916
  163.6 8.5 %copy-start.16 = (bf16[192,256]{1,0:T(8,128)(2,1)S(1)}, bf16[192,256]{1,0:T(8,128)(2,1)}, u32[]{:S(2)}) copy-start(bf16[192,256]{1,0:T(8,128)(2,1)} %get-tuple-element.98.refs_8_) | copy-start | bytes 294916
  163.6 8.5 %copy-start.17 = (bf16[192,256]{1,0:T(8,128)(2,1)S(1)}, bf16[192,256]{1,0:T(8,128)(2,1)}, u32[]{:S(2)}) copy-start(bf16[192,256]{1,0:T(8,128)(2,1)} %get-tuple-element.99.refs_9_) | copy-start | bytes 294916
  163.6 8.5 %copy-start.18 = (bf16[192,256]{1,0:T(8,128)(2,1)S(1)}, bf16[192,256]{1,0:T(8,128)(2,1)}, u32[]{:S(2)}) copy-start(bf16[192,256]{1,0:T(8,128)(2,1)} %get-tuple-element.100.refs_10_) | copy-start | bytes 294916
  163.7 8.4 %copy-start.19 = (s32[5]{0:T(128)S(1)}, s32[5]{0:T(128)}, u32[]{:S(2)}) copy-start(s32[5]{0:T(128)} %stack.68.refs_0_.info_ref) | copy-start | bytes 64
  163.7 8.4 %copy-start.20 = (f32[3,256]{1,0:T(4,128)S(1)}, f32[3,256]{1,0:T(4,128)}, u32[]{:S(2)}) copy-start(f32[3,256]{1,0:T(4,128)} %get-tuple-element.115.refs_12_) | copy-start | bytes 9220
  163.7 8.4 %copy-start.21 = (f32[3,256]{1,0:T(4,128)S(1)}, f32[3,256]{1,0:T(4,128)}, u32[]{:S(2)}) copy-start(f32[3,256]{1,0:T(4,128)} %get-tuple-element.116.refs_13_) | copy-start | bytes 9220
  169.0 32.8 %collective-permute-start.16 = (bf16[4,96,1792]{2,1,0:T(8,128)(2,1)}, bf16[4,96,1792]{2,1,0:T(8,128)(2,1)}, u32[]{:S(2)}, u32[]{:S(2)}) collective-permute-start(bf16[4,96,1792]{2,1,0:T(8,128)(2,1)} %get-tuple-element.123), channel_id=1, source_target_pairs={{0,16},{16,0},{1,17},{17,1},{2,18},{18,2},{3,19},{19,3},{4,20},{20... | collective-permute-start | bytes 4128776 | tf_op jit(solution)/shard_map/ppermute | solution.py:28
  171.7 31.5 %collective-permute-start.17 = (bf16[4,96,1792]{2,1,0:T(8,128)(2,1)}, bf16[4,96,1792]{2,1,0:T(8,128)(2,1)}, u32[]{:S(2)}, u32[]{:S(2)}) collective-permute-start(bf16[4,96,1792]{2,1,0:T(8,128)(2,1)} %get-tuple-element.124), channel_id=1, source_target_pairs={{0,8},{8,0},{1,9},{9,1},{2,10},{10,2},{3,11},{11,3},{4,12},{12,4},... | collective-permute-start | bytes 4128776 | tf_op jit(solution)/shard_map/ppermute | solution.py:28
  172.2 18.6 %copy-start = (bf16[2,2,192,576]{3,2,1,0:T(8,128)(2,1)S(1)}, bf16[2,2,192,576]{3,2,1,0:T(8,128)(2,1)}, u32[]{:S(2)}) copy-start(bf16[2,2,192,576]{3,2,1,0:T(8,128)(2,1)} %copy.41) | copy-start | bytes 2654212
  172.2 18.6 %copy-start.6 = (f32[4,256,128]{2,1,0:T(8,128)S(1)}, f32[4,256,128]{2,1,0:T(8,128)}, u32[]{:S(2)}) copy-start(f32[4,256,128]{2,1,0:T(8,128)} %get-tuple-element.89.refs_6_.sin_ref) | copy-start | bytes 1572868
  172.2 18.6 %copy-start.7 = (f32[4,256,128]{2,1,0:T(8,128)S(1)}, f32[4,256,128]{2,1,0:T(8,128)}, u32[]{:S(2)}) copy-start(f32[4,256,128]{2,1,0:T(8,128)} %get-tuple-element.88.refs_5_.cos_ref) | copy-start | bytes 1572868
  188.1 2.0 collective-permute-start.14
  188.2 2.6 collective-permute-start.15
  195.2 43.1 %all-to-all-start.3 = ((bf16[4,256,768]{2,1,0:T(8,128)(2,1)}), bf16[4,256,768]{2,1,0:T(8,128)(2,1)}, u32[]{:S(2)}, u32[]{:S(2)}) async-start(bf16[4,256,768]{2,1,0:T(8,128)(2,1)} %get-tuple-element.122), calls=%async_computation.3 | async-start | bytes 3145728 | tf_op jit(solution)/shard_map/all_to_all | solution.py:842
  199.5 62.5 %reduce-scatter.2.cloned.1.call-start = ((), (), s32[]{:S(2)}) async-start(), calls=%async_computation.6 | async-start | bytes 1720320 | tf_op jit(solution)/shard_map/reduce_scatter | solution.py:741
  206.7 15.9 %collective-permute-start.18 = (bf16[2,96,1792]{2,1,0:T(8,128)(2,1)}, bf16[2,96,1792]{2,1,0:T(8,128)(2,1)}, u32[]{:S(2)}, u32[]{:S(2)}) collective-permute-start(bf16[2,96,1792]{2,1,0:T(8,128)(2,1)} %get-tuple-element.131), channel_id=1, source_target_pairs={{0,8},{8,0},{1,9},{9,1},{2,10},{10,2},{3,11},{11,3},{4,12},{12,4},... | collective-permute-start | bytes 2064392 | tf_op jit(solution)/shard_map/ppermute | solution.py:28
  207.4 16.6 %collective-permute-start.19 = (bf16[2,96,1792]{2,1,0:T(8,128)(2,1)}, bf16[2,96,1792]{2,1,0:T(8,128)(2,1)}, u32[]{:S(2)}, u32[]{:S(2)}) collective-permute-start(bf16[2,96,1792]{2,1,0:T(8,128)(2,1)} %get-tuple-element.132), channel_id=1, source_target_pairs={{0,16},{16,0},{1,17},{17,1},{2,18},{18,2},{3,19},{19,3},{4,20},{20... | collective-permute-start | bytes 2064392 | tf_op jit(solution)/shard_map/ppermute | solution.py:28
  227.9 1.9 collective-permute-start.20
  230.1 8.1 %collective-permute-start.21 = (bf16[192,576]{1,0:T(8,128)(2,1)S(1)}, bf16[192,576]{1,0:T(8,128)(2,1)S(1)}, u32[]{:S(2)}, u32[]{:S(2)}) collective-permute-start(bf16[192,576]{1,0:T(8,128)(2,1)S(1)} %select_bitcast_fusion.7), channel_id=1, source_target_pairs={{0,8},{8,0},{1,9},{9,1},{2,10},{10,2},{3,11},{11,3},{4,12},{12,4},... | collective-permute-start | bytes 663560 | tf_op jit(solution)/shard_map/ppermute | solution.py:28
  242.0 31.9 %all-to-all-start.4 = ((bf16[8,256,384]{2,1,0:T(8,128)(2,1)}), bf16[8,256,384]{2,1,0:T(8,128)(2,1)S(1)}, u32[]{:S(2)}, u32[]{:S(2)}) async-start(bf16[8,256,384]{2,1,0:T(8,128)(2,1)} %bitcast.40), calls=%async_computation.4 | async-start | bytes 3145728 | tf_op jit(solution)/shard_map/all_to_all | solution.py:816
  263.2 22.1 %collective-permute-start.22 = (bf16[96,2944]{1,0:T(8,128)(2,1)S(1)}, bf16[96,2944]{1,0:T(8,128)(2,1)S(1)}, u32[]{:S(2)}, u32[]{:S(2)}) collective-permute-start(bf16[96,2944]{1,0:T(8,128)(2,1)S(1)} %concatenate.11.refs_1_), channel_id=1, source_target_pairs={{0,16},{16,0},{1,17},{17,1},{2,18},{18,2},{3,19},{19,3},{4,20},{20... | collective-permute-start | bytes 1695752 | tf_op jit(solution)/shard_map/ppermute | solution.py:28
  (19 other events, 80.7 us)
Sparse Core Ops, SparseCore 0:
  10.9 117.9 all-gather.2
  228.2 33.8 reduce-scatter.1

commit v8 on v7

--- a/solution.py
+++ b/solution.py
@@ -462,18 +462,26 @@
         gone_ref[row] = grad_one_low[:, mine]
         sums_ref[row] = sums[:, mine].astype(bf16)
 
-    copies_out = []
-    for column in range(columns):
+    def leave(column):
         slot = column % 2
-        if column > 1:
-            copies_out[column - 2].wait()
+        return pltpu.make_async_copy(stage.at[slot], sent_ref.at[:, :, column], ends.at[2 + slot])
+
+    def send(column, carry):
+        @pl.when(column > 1)
+        def _():
+            leave(column - 2).wait()
+
         attended = attended_block(info_ref, att_refs, column)
         operands = attended, act_ref[column], gin_ref[column], hidden_ref, gtwo_ref, gone_ref, sums_ref
-        weigh_block(1 - info_ref[1], info_ref, *operands, stage.at[slot])
-        copies_out.append(pltpu.make_async_copy(stage.at[slot], sent_ref.at[:, :, column], ends.at[2 + slot]))
-        copies_out[-1].start()
-    for copy in copies_out[-2:] + [act_copy, gin_copy]:
-        copy.wait()
+        weigh_block(1 - info_ref[1], info_ref, *operands, stage.at[column % 2])
+        leave(column).start()
+        return carry
+
+    lax.fori_loop(0, columns, send, 0)
+    for column in (columns - 2, columns - 1):
+        leave(column).wait()
+    act_copy.wait()
+    gin_copy.wait()
 
 
 def feed(info, attended, tokens, cot, weights, slabs):

time: 300 us -> 294 us (0.980); the launches traced: 294 us -> 293 us
  no operation moved by 1% of the time
where the time goes in v8:
time: 294 us; the launch traced here: 293 us
  waiting for transfers between devices  109 us (37%)
  Pallas kernels  86.3 us (29%)
  starting transfers between devices  54.1 us (18%)
  between operations  16.1 us (5%)
  local copies, waits for them, and re-layouts  13.8 us (5%)
  other arithmetic  8.1 us (3%)
  matrix products  5.52 us (2%)
    ppermute x17, waiting for transfers between devices, swap(): return lax.ppermute(values, axis, SWAP)  44.1 us
    ppermute x6, waiting for transfers between devices, shift(): lax.ppermute(values, 'col', [(i, (i + step) % columns) for i in range(col...  38.4 us
    pallas_call x1, Pallas kernels, feed(): pl.pallas_call(feed_kernel, in_specs=[smem, vmem, vmem, pl.BlockSpec(memo...  20.2 us
    ppermute x17, starting transfers between devices, swap(): return lax.ppermute(values, axis, SWAP)  17.9 us
    pallas_call x2, Pallas kernels, attend_forward(): pl.pallas_call(lambda *refs: forward_kernel(first, share, *refs), grid_sp...  16.9 us
    pallas_call x1, Pallas kernels, attend_backward(): pl.pallas_call(lambda *refs: backward_kernel(columns, share, *refs), in_s...  15.9 us
    pallas_call x3, Pallas kernels, add_blocks(): pl.pallas_call(lambda *refs: add_kernel(len(lengths), sums, *refs), in_sp...  11.3 us
    all_to_all x1, starting transfers between devices, to_loader(): lax.all_to_all(cut, ('dp',) + ROWS, split_axis=0, concat_axis=0, tiled=True)  10.2 us
  transfers between devices with their start and end apart: 30, of which 21 were waited for; matrix products, arithmetic and copies ran while one was open for 8% of the time, Pallas kernels for 21%

profile of v8, /device:TPU:0, one launch (start us, length us, event | category | flops | bytes accessed | tf_op | source)
XLA Modules:
  0.0 292.7 jit_solution(13171416129132404266)
XLA Ops:
  7.3 2.2 parcel.1
  9.5 3.0 %collective-permute-start = (bf16[2,192,512]{2,1,0:T(8,128)(2,1)}, bf16[2,192,512]{2,1,0:T(8,128)(2,1)S(1)}, u32[]{:S(2)}, u32[]{:S(2)}) collective-permute-start(bf16[2,192,512]{2,1,0:T(8,128)(2,1)} %param.14), channel_id=1, source_target_pairs={{0,16},{16,0},{1,17},{17,1},{2,18},{18,2},{3,19},{19,3},{4,20},{20... | collective-permute-start | bytes 1179656 | tf_op jit(solution)/shard_map/ppermute | solution.py:28
  13.7 2.0 collective-permute-start.6
  18.0 3.0 %fusion.30 = (f32[4,256,128]{2,1,0:T(8,128)}, f32[4,256,128]{2,1,0:T(8,128)}) fusion(f32[128]{0:T(128)S(1)} %compare_select_fusion.2, f32[128]{0:T(128)S(1)} %mul.76, f32[4,256]{1,0:T(4,128)S(1)} %subtract_convert_fusion), kind=kLoop, calls=%fused_computation.28 | loop fusion | flops 262144 | bytes 1053696 | tf_op jit(solution)/shard_map/mul | solution.py:788
  22.1 1.8 fusion.24
  23.9 1.8 collective-permute-start.1
  27.6 3.5 %all-to-all-start = ((bf16[4,256,192]{1,2,0:T(8,128)(2,1)}), bf16[4,256,192]{1,2,0:T(8,128)(2,1)S(1)}, u32[]{:S(2)}, u32[]{:S(2)}) async-start(bf16[4,256,192]{1,2,0:T(8,128)(2,1)} %bitcast.109), calls=%async_computation | async-start | bytes 786432 | tf_op jit(solution)/shard_map/all_to_all | solution.py:799
  31.0 4.9 %collective-permute-done.1 = bf16[2,192,512]{2,1,0:T(8,128)(2,1)S(1)} collective-permute-done((bf16[2,192,512]{2,1,0:T(8,128)(2,1)S(1)}, bf16[2,192,512]{2,1,0:T(8,128)(2,1)S(1)}, u32[]{:S(2)}, u32[]{:S(2)}) %collective-permute-start.1) | collective-permute-done | bytes 393248 | tf_op jit(solution)/shard_map/ppermute | solution.py:28
  36.0 2.4 all-to-all-done
  38.6 3.6 %collective-permute-start.2 = (bf16[256,768]{1,0:T(8,128)(2,1)S(1)}, bf16[256,768]{1,0:T(8,128)(2,1)S(1)}, u32[]{:S(2)}, u32[]{:S(2)}) collective-permute-start(bf16[256,768]{1,0:T(8,128)(2,1)S(1)} %copy.43.refs_0_.x_ref), channel_id=1, source_target_pairs={{0,3},{1,0},{2,1},{3,2},{4,7},{5,4},{6,5},{7,6},{8,11},{9,8},{10,9... | collective-permute-start | bytes 1179656 | tf_op jit(solution)/shard_map/ppermute | solution.py:630
  43.3 1.8 fusion.21
  45.9 4.3 %all-to-all-start.1 = ((bf16[4,256,192]{1,2,0:T(8,128)(2,1)}), bf16[4,256,192]{1,2,0:T(8,128)(2,1)}, u32[]{:S(2)}, u32[]{:S(2)}) async-start(bf16[4,256,192]{1,2,0:T(8,128)(2,1)} %bitcast.108), calls=%async_computation.1 | async-start | bytes 786432 | tf_op jit(solution)/shard_map/all_to_all | solution.py:799
  51.5 5.9 %all-to-all-done.1 = bf16[4,256,192]{1,2,0:T(8,128)(2,1)} async-done(((bf16[4,256,192]{1,2,0:T(8,128)(2,1)}), bf16[4,256,192]{1,2,0:T(8,128)(2,1)}, u32[]{:S(2)}, u32[]{:S(2)}) %all-to-all-start.1) | async-done | bytes 393248 | tf_op jit(solution)/shard_map/all_to_all | solution.py:799
  57.5 12.7 %collective-permute-done.2.refs_3_ = bf16[256,768]{1,0:T(8,128)(2,1)S(1)} collective-permute-done((bf16[256,768]{1,0:T(8,128)(2,1)S(1)}, bf16[256,768]{1,0:T(8,128)(2,1)S(1)}, u32[]{:S(2)}, u32[]{:S(2)}) %collective-permute-start.2) | collective-permute-done | bytes 393248 | tf_op jit(solution)/shard_map/ppermute | solution.py:630
  70.2 4.7 %collective-permute-done.4.refs_1_ = bf16[256,768]{1,0:T(8,128)(2,1)S(1)} collective-permute-done((bf16[256,768]{1,0:T(8,128)(2,1)S(1)}, bf16[256,768]{1,0:T(8,128)(2,1)S(1)}, u32[]{:S(2)}, u32[]{:S(2)}) %collective-permute-start.4) | collective-permute-done | bytes 393248 | tf_op jit(solution)/shard_map/ppermute | solution.py:630
  74.9 15.5 %collective-permute-done.5.refs_2_ = bf16[256,768]{1,0:T(8,128)(2,1)S(1)} collective-permute-done((bf16[256,768]{1,0:T(8,128)(2,1)S(1)}, bf16[256,768]{1,0:T(8,128)(2,1)S(1)}, u32[]{:S(2)}, u32[]{:S(2)}) %collective-permute-start.5) | collective-permute-done | bytes 393248 | tf_op jit(solution)/shard_map/ppermute | solution.py:630
  91.1 5.4 %project.1 = (bf16[4,256,256]{2,1,0:T(8,128)(2,1)}, bf16[8,256,256]{2,1,0:T(8,128)(2,1)}, bf16[8,192,256]{2,1,0:T(8,128)(2,1)}) custom-call(bf16[256,768]{1,0:T(8,128)(2,1)} %copy-done.4, bf16[256,768]{1,0:T(8,128)(2,1)} %copy-done.11, bf16[256,768]{1,0:T(8,128)(2,1)} %copy-done.13, bf16[256,768]{1,0:T(8,128)(2,1)} %copy-done.9, bf16[768,576]{1,0:T(8,128)(2,1)} %bitcast.110, ...), custom_call_target="tpu_custom_call" | custom-call | flops 1000000 | bytes 3000 | tf_op jit(solution)/shard_map/project/pallas_call | solution.py:76
  97.6 2.9 collective-permute-done.9.refs_5_
  101.8 12.7 %attend_forward.2 = (bf16[192,256]{1,0:T(8,128)(2,1)}, bf16[192,256]{1,0:T(8,128)(2,1)}, bf16[192,256]{1,0:T(8,128)(2,1)}, f32[3,256]{1,0:T(4,128)}, f32[3,256]{1,0:T(4,128)}, /*index=5*/f32[3,256]{1,0:T(4,128)}) custom-call(s32[5]{0:T(128)} %stack.68.refs_0_.info_ref, bf16[4,256,256]{2,1,0:T(8,128)(2,1)} %get-tuple-element.96.refs_1_, ...), custom_call_target="tpu_custom_call" | custom-call | flops 1000000 | bytes 3000 | tf_op jit(solution)/shard_map/attend_forward/pallas_call | solution.py:182
  114.5 4.8 %collective-permute-start.10 = (bf16[192,256]{1,0:T(8,128)(2,1)}, bf16[192,256]{1,0:T(8,128)(2,1)S(1)}, u32[]{:S(2)}, u32[]{:S(2)}) collective-permute-start(bf16[192,256]{1,0:T(8,128)(2,1)} %get-tuple-element.98.refs_8_), channel_id=1, source_target_pairs={{0,3},{1,0},{2,1},{3,2},{4,7},{5,4},{6,5},{7,6},{8,11},{9,8},{10,9... | collective-permute-start | bytes 294920 | tf_op jit(solution)/shard_map/ppermute | solution.py:630
  119.9 2.0 copy.44.cot_ref
  122.0 4.2 %attend_forward.3 = (bf16[192,256]{1,0:T(8,128)(2,1)}, f32[3,256]{1,0:T(4,128)}) custom-call(s32[5]{0:T(128)} %stack.68.refs_0_.info_ref, bf16[4,256,256]{2,1,0:T(8,128)(2,1)} %get-tuple-element.96.refs_1_, bf16[8,256,256]{2,1,0:T(8,128)(2,1)} %get-tuple-element.91.refs_2_, bf16[8,256,256]{2,1,0:T(8,128)(2,1)} %copy-done.24, ...), custom_call_target="tpu_custom_call" | custom-call | flops 1000000 | bytes 3000 | tf_op jit(solution)/shard_map/attend_forward/pallas_call | solution.py:182
  126.1 5.5 %collective-permute-done.11.refs_2_ = bf16[192,256]{1,0:T(8,128)(2,1)S(1)} collective-permute-done((bf16[192,256]{1,0:T(8,128)(2,1)}, bf16[192,256]{1,0:T(8,128)(2,1)S(1)}, u32[]{:S(2)}, u32[]{:S(2)}) %collective-permute-start.11) | collective-permute-done | bytes 98336 | tf_op jit(solution)/shard_map/ppermute | solution.py:630
  132.3 20.2 %feed.1 = (bf16[256,768]{1,0:T(8,128)(2,1)}, bf16[4,192,256]{2,1,0:T(8,128)(2,1)}, f32[256,768]{1,0:T(8,128)}, bf16[768,256]{1,0:T(8,128)(2,1)}, bf16[4,256,768]...) custom-call(s32[5]{0:T(128)} %stack.68.refs_0_.info_ref, ...), custom_call_target="tpu_custom_call" | custom-call | flops 1000000 | bytes 3000 | tf_op jit(solution)/shard_map/feed/pallas_call | solution.py:497
  152.6 3.7 %all-to-all-start.2 = ((bf16[4,192,256]{2,1,0:T(8,128)(2,1)}), bf16[4,192,256]{2,1,0:T(8,128)(2,1)S(1)}, u32[]{:S(2)}, u32[]{:S(2)}) async-start(bf16[4,192,256]{2,1,0:T(8,128)(2,1)} %get-tuple-element.103), calls=%async_computation.2 | async-start | bytes 786432 | tf_op jit(solution)/shard_map/all_to_all | solution.py:820
  156.4 7.2 %weigh.1.refs_0_ = bf16[2,2,4,96,1792]{4,3,2,1,0:T(8,128)(2,1)} custom-call(s32[5]{0:T(128)} %stack.68.refs_0_.info_ref, bf16[768,256]{1,0:T(8,128)(2,1)} %get-tuple-element.104.hidden_ref, bf16[4,256,768]{2,1,0:T(8,128)(2,1)} %get-tuple-element.105.act_ref, bf16[4,256,768]{2,1,0:T(8,128)(2,1)} %get-tuple-element.106.gin_ref, ...), custom_call_target="tpu_custom_call" | custom-call | flops 1000000 | bytes 3000 | tf_op jit(solution)/shard_map/weigh/pallas_call | solution.py:569
  163.6 4.1 %add_blocks.3 = (bf16[4,96,1792]{2,1,0:T(8,128)(2,1)}, bf16[4,96,1792]{2,1,0:T(8,128)(2,1)}) custom-call(bf16[2,2,4,96,1792]{4,3,2,1,0:T(8,128)(2,1)} %weigh.1.refs_0_, bf16[2,2,4,96,1792]{4,3,2,1,0:T(8,128)(2,1)} %collective-permute-done.13.refs_1_), custom_call_target="tpu_custom_call" | custom-call | flops 1000000 | bytes 3000 | tf_op jit(solution)/shard_map/add_blocks/pallas_call | solution.py:664
  168.7 2.3 collective-permute-start.16
  171.9 15.9 %attend_backward.1 = (f32[4,256,192]{2,1,0:T(8,128)S(1)}, bf16[8,256,256]{2,1,0:T(8,128)(2,1)S(1)}, bf16[4,256,256]{2,1,0:T(8,128)(2,1)S(1)}, bf16[4,256,256]{2,1,0:T(8,128)(2,1)S(1)}) custom-call(s32[5]{0:T(128)S(1)} %copy-done.19, bf16[4,256,256]{2,1,0:T(8,128)(2,1)S(1)} %copy-done.8, bf16[8,256,256]{2,1,0:T(8,128)(2,1)} %get-tuple-element.91.refs_2_, ...), custom_call_target="tpu_custom_call" | custom-call | flops 1000000 | bytes 3000 | tf_op jit(solution)/shard_map/attend_backward/pallas_call | solution.py:265
  190.5 4.4 %unproject.1 = (bf16[4,256,768]{2,1,0:T(8,128)(2,1)}, bf16[4,256,576]{2,1,0:T(8,128)(2,1)S(1)}) custom-call(s32[5]{0:T(128)S(1)} %copy-done.19, f32[4,256,192]{2,1,0:T(8,128)S(1)} %get-tuple-element.118.dq_ref, bf16[8,256,256]{2,1,0:T(8,128)(2,1)S(1)} %get-tuple-element.119.near_k_ref.near_v_ref, bf16[4,256,256]{2,1,0:T(8,128)(2,1)S(1)} %collective-permute-done.14.far_k_ref, ...), custom_call_target="tpu_custom_call" | custom-call | flops 1000000 | bytes 3000 | tf_op jit(solution)/shard_map/unproject/pallas_call | solution.py:307
  194.8 4.4 %all-to-all-start.3 = ((bf16[4,256,768]{2,1,0:T(8,128)(2,1)}), bf16[4,256,768]{2,1,0:T(8,128)(2,1)}, u32[]{:S(2)}, u32[]{:S(2)}) async-start(bf16[4,256,768]{2,1,0:T(8,128)(2,1)} %get-tuple-element.122), calls=%async_computation.3 | async-start | bytes 3145728 | tf_op jit(solution)/shard_map/all_to_all | solution.py:850
  199.2 2.0 collective-permute-done.16.refs_2_
  201.2 1.5 collective-permute-done.17.refs_3_
  202.7 3.4 %add_blocks.4 = (bf16[2,96,1792]{2,1,0:T(8,128)(2,1)}, bf16[2,96,1792]{2,1,0:T(8,128)(2,1)}) custom-call(bf16[2,2,4,96,1792]{4,3,2,1,0:T(8,128)(2,1)} %weigh.1.refs_0_, bf16[2,2,4,96,1792]{4,3,2,1,0:T(8,128)(2,1)} %collective-permute-done.13.refs_1_, bf16[4,96,1792]{2,1,0:T(8,128)(2,1)} %collective-permute-done.16.refs_2_, ...), custom_call_target="tpu_custom_call" | custom-call | flops 1000000 | bytes 3000 | tf_op jit(solution)/shard_map/add_blocks/pallas_call | solution.py:664
  207.3 1.7 collective-permute-start.19
  209.0 1.5 project_grad.1
  210.4 11.8 %collective-permute-done.18.refs_4_ = bf16[2,96,1792]{2,1,0:T(8,128)(2,1)} collective-permute-done((bf16[2,96,1792]{2,1,0:T(8,128)(2,1)}, bf16[2,96,1792]{2,1,0:T(8,128)(2,1)}, u32[]{:S(2)}, u32[]{:S(2)}) %collective-permute-start.18) | collective-permute-done | bytes 688160 | tf_op jit(solution)/shard_map/ppermute | solution.py:28
  223.4 3.8 %add_blocks.5 = bf16[4,96,1792]{2,1,0:T(8,128)(2,1)} custom-call(bf16[2,2,4,96,1792]{4,3,2,1,0:T(8,128)(2,1)} %weigh.1.refs_0_, bf16[2,2,4,96,1792]{4,3,2,1,0:T(8,128)(2,1)} %collective-permute-done.13.refs_1_, bf16[4,96,1792]{2,1,0:T(8,128)(2,1)} %collective-permute-done.16.refs_2_, bf16[4,96,1792]{2,1,0:T(8,128)(2,1)} %collective-permute-done.17.refs_3_, ...), custom_call_target="tpu_custom_call" | custom-call | flops 1000000 | bytes 3000 | tf_op jit(solution)/shard_map/add_blocks/pallas_call | solution.py:664
  227.4 1.8 collective-permute-done.20
  230.6 7.0 %collective-permute-done.21 = bf16[192,576]{1,0:T(8,128)(2,1)S(1)} collective-permute-done((bf16[192,576]{1,0:T(8,128)(2,1)S(1)}, bf16[192,576]{1,0:T(8,128)(2,1)S(1)}, u32[]{:S(2)}, u32[]{:S(2)}) %collective-permute-start.21) | collective-permute-done | bytes 221216 | tf_op jit(solution)/shard_map/ppermute | solution.py:28
  237.6 1.7 convert_reduce_fusion
  241.4 10.2 %all-to-all-start.4 = ((bf16[8,256,384]{2,1,0:T(8,128)(2,1)}), bf16[8,256,384]{2,1,0:T(8,128)(2,1)S(1)}, u32[]{:S(2)}, u32[]{:S(2)}) async-start(bf16[8,256,384]{2,1,0:T(8,128)(2,1)} %bitcast.40), calls=%async_computation.4 | async-start | bytes 3145728 | tf_op jit(solution)/shard_map/all_to_all | solution.py:824
  251.6 9.0 %reduce-scatter.2.cloned.1.call-done = bf16[1,96,1792]{2,1,0:T(8,128)(2,1)} async-done(((bf16[4,96,1792]{2,1,0:T(8,128)(2,1)}), bf16[1,96,1792]{2,1,0:T(8,128)(2,1)}) %reduce-scatter.2.cloned.1.call-update) | async-done | bytes 344080 | tf_op jit(solution)/shard_map/reduce_scatter | solution.py:749
  261.8 2.9 %collective-permute-start.22 = (bf16[96,2944]{1,0:T(8,128)(2,1)S(1)}, bf16[96,2944]{1,0:T(8,128)(2,1)S(1)}, u32[]{:S(2)}, u32[]{:S(2)}) collective-permute-start(bf16[96,2944]{1,0:T(8,128)(2,1)S(1)} %concatenate.11.refs_1_), channel_id=1, source_target_pairs={{0,16},{16,0},{1,17},{17,1},{2,18},{18,2},{3,19},{19,3},{4,20},{20... | collective-permute-start | bytes 1695752 | tf_op jit(solution)/shard_map/ppermute | solution.py:28
  264.8 7.9 %all-to-all-done.4 = bf16[8,256,384]{2,1,0:T(8,128)(2,1)S(1)} async-done(((bf16[8,256,384]{2,1,0:T(8,128)(2,1)}), bf16[8,256,384]{2,1,0:T(8,128)(2,1)S(1)}, u32[]{:S(2)}, u32[]{:S(2)}) %all-to-all-start.4) | async-done | bytes 1572896 | tf_op jit(solution)/shard_map/all_to_all | solution.py:824
  272.7 1.9 fusion.12
  275.7 8.1 %collective-permute-done.22.refs_2_ = bf16[96,2944]{1,0:T(8,128)(2,1)S(1)} collective-permute-done((bf16[96,2944]{1,0:T(8,128)(2,1)S(1)}, bf16[96,2944]{1,0:T(8,128)(2,1)S(1)}, u32[]{:S(2)}, u32[]{:S(2)}) %collective-permute-start.22) | collective-permute-done | bytes 565280 | tf_op jit(solution)/shard_map/ppermute | solution.py:28
  283.8 1.5 open_shards.1
  (152 shorter events, 26.2 us)
Async XLA Ops:
  7.2 14.7 %copy-start.30 = (bf16[2,192,512]{2,1,0:T(8,128)(2,1)S(1)}, bf16[2,192,512]{2,1,0:T(8,128)(2,1)}, u32[]{:S(2)}) copy-start(bf16[2,192,512]{2,1,0:T(8,128)(2,1)} %param.14) | copy-start | bytes 1179652
  7.2 8.8 %copy-start.35 = (s32[2,512]{1,0:T(2,128)S(1)}, s32[2,512]{1,0:T(2,128)}, u32[]{:S(2)}) copy-start(s32[2,512]{1,0:T(2,128)} %param.17) | copy-start | bytes 12292
  7.2 8.8 %copy-start.36 = (s32[1,2]{1,0:T(1,128)S(1)}, s32[1,2]{1,0:T(1,128)}, u32[]{:S(2)}) copy-start(s32[1,2]{1,0:T(1,128)} %param.16) | copy-start | bytes 28
  7.2 124.5 %all-gather.3.cloned.1.call-start = ((), (), s32[]{:S(2)}) async-start(), calls=%async_computation.7 | async-start | bytes 11354112 | tf_op jit(solution)/shard_map/all_gather | solution.py:777
  9.5 12.4 %collective-permute-start = (bf16[2,192,512]{2,1,0:T(8,128)(2,1)}, bf16[2,192,512]{2,1,0:T(8,128)(2,1)S(1)}, u32[]{:S(2)}, u32[]{:S(2)}) collective-permute-start(bf16[2,192,512]{2,1,0:T(8,128)(2,1)} %param.14), channel_id=1, source_target_pairs={{0,16},{16,0},{1,17},{17,1},{2,18},{18,2},{3,19},{19,3},{4,20},{20... | collective-permute-start | bytes 1179656 | tf_op jit(solution)/shard_map/ppermute | solution.py:28
  12.5 9.4 %collective-permute-start.3 = (s32[2,512]{1,0:T(2,128)}, s32[2,512]{1,0:T(2,128)S(1)}, u32[]{:S(2)}, u32[]{:S(2)}) collective-permute-start(s32[2,512]{1,0:T(2,128)} %param.17), channel_id=1, source_target_pairs={{0,16},{16,0},{1,17},{17,1},{2,18},{18,2},{3,19},{19,3},{4,20},{20... | collective-permute-start | bytes 12296 | tf_op jit(solution)/shard_map/ppermute | solution.py:28
  13.7 12.1 %collective-permute-start.6 = (bf16[192,576]{1,0:T(8,128)(2,1)S(1)}, bf16[192,576]{1,0:T(8,128)(2,1)S(1)}, u32[]{:S(2)}, u32[]{:S(2)}) collective-permute-start(bf16[192,576]{1,0:T(8,128)(2,1)S(1)} %pad_maximum_fusion.5), channel_id=1, source_target_pairs={{0,8},{8,0},{1,9},{9,1},{2,10},{10,2},{3,11},{11,3},{4,12},{12,4},... | collective-permute-start | bytes 663560 | tf_op jit(solution)/shard_map/ppermute | solution.py:28
  23.9 12.0 %collective-permute-start.1 = (bf16[2,192,512]{2,1,0:T(8,128)(2,1)S(1)}, bf16[2,192,512]{2,1,0:T(8,128)(2,1)S(1)}, u32[]{:S(2)}, u32[]{:S(2)}) collective-permute-start(bf16[2,192,512]{2,1,0:T(8,128)(2,1)S(1)} %copy-done.31), channel_id=1, source_target_pairs={{0,16},{16,0},{1,17},{17,1},{2,18},{18,2},{3,19},{19,3},{4,20},{20... | collective-permute-start | bytes 1179656 | tf_op jit(solution)/shard_map/ppermute | solution.py:28
  26.8 23.4 %collective-permute-start.7 = (bf16[2,192,576]{2,1,0:T(8,128)(2,1)}, bf16[2,192,576]{2,1,0:T(8,128)(2,1)S(1)}, u32[]{:S(2)}, u32[]{:S(2)}) collective-permute-start(bf16[2,192,576]{2,1,0:T(8,128)(2,1)} %pad_maximum_fusion.4), channel_id=1, source_target_pairs={{0,4},{4,0},{1,5},{5,1},{2,6},{6,2},{3,7},{7,3},{8,12},{12,8},{9,1... | collective-permute-start | bytes 1327112 | tf_op jit(solution)/shard_map/ppermute | solution.py:28
  27.6 10.9 %all-to-all-start = ((bf16[4,256,192]{1,2,0:T(8,128)(2,1)}), bf16[4,256,192]{1,2,0:T(8,128)(2,1)S(1)}, u32[]{:S(2)}, u32[]{:S(2)}) async-start(bf16[4,256,192]{1,2,0:T(8,128)(2,1)} %bitcast.109), calls=%async_computation | async-start | bytes 786432 | tf_op jit(solution)/shard_map/all_to_all | solution.py:799
  38.6 31.5 %collective-permute-start.2 = (bf16[256,768]{1,0:T(8,128)(2,1)S(1)}, bf16[256,768]{1,0:T(8,128)(2,1)S(1)}, u32[]{:S(2)}, u32[]{:S(2)}) collective-permute-start(bf16[256,768]{1,0:T(8,128)(2,1)S(1)} %copy.43.refs_0_.x_ref), channel_id=1, source_target_pairs={{0,3},{1,0},{2,1},{3,2},{4,7},{5,4},{6,5},{7,6},{8,11},{9,8},{10,9... | collective-permute-start | bytes 1179656 | tf_op jit(solution)/shard_map/ppermute | solution.py:630
  42.3 32.6 %collective-permute-start.4 = (bf16[256,768]{1,0:T(8,128)(2,1)S(1)}, bf16[256,768]{1,0:T(8,128)(2,1)S(1)}, u32[]{:S(2)}, u32[]{:S(2)}) collective-permute-start(bf16[256,768]{1,0:T(8,128)(2,1)S(1)} %copy.43.refs_0_.x_ref), channel_id=1, source_target_pairs={{0,1},{1,2},{2,3},{3,0},{4,5},{5,6},{6,7},{7,4},{8,9},{9,10},{10,1... | collective-permute-start | bytes 1179656 | tf_op jit(solution)/shard_map/ppermute | solution.py:630
  42.3 48.1 %collective-permute-start.5 = (bf16[256,768]{1,0:T(8,128)(2,1)S(1)}, bf16[256,768]{1,0:T(8,128)(2,1)S(1)}, u32[]{:S(2)}, u32[]{:S(2)}) collective-permute-start(bf16[256,768]{1,0:T(8,128)(2,1)S(1)} %copy.43.refs_0_.x_ref), channel_id=1, source_target_pairs={{0,2},{1,3},{2,0},{3,1},{4,6},{5,7},{6,4},{7,5},{8,10},{9,11},{10,... | collective-permute-start | bytes 1179656 | tf_op jit(solution)/shard_map/ppermute | solution.py:630
  45.9 11.6 %all-to-all-start.1 = ((bf16[4,256,192]{1,2,0:T(8,128)(2,1)}), bf16[4,256,192]{1,2,0:T(8,128)(2,1)}, u32[]{:S(2)}, u32[]{:S(2)}) async-start(bf16[4,256,192]{1,2,0:T(8,128)(2,1)} %bitcast.108), calls=%async_computation.1 | async-start | bytes 786432 | tf_op jit(solution)/shard_map/all_to_all | solution.py:799
  70.2 20.2 %copy-start.9 = (bf16[256,768]{1,0:T(8,128)(2,1)}, bf16[256,768]{1,0:T(8,128)(2,1)S(1)}, u32[]{:S(2)}) copy-start(bf16[256,768]{1,0:T(8,128)(2,1)S(1)} %collective-permute-done.2.refs_3_) | copy-start | bytes 1179652
  74.9 15.5 %copy-start.11 = (bf16[256,768]{1,0:T(8,128)(2,1)}, bf16[256,768]{1,0:T(8,128)(2,1)S(1)}, u32[]{:S(2)}) copy-start(bf16[256,768]{1,0:T(8,128)(2,1)S(1)} %collective-permute-done.4.refs_1_) | copy-start | bytes 1179652
  96.5 4.0 %collective-permute-start.8 = (bf16[8,256,256]{2,1,0:T(8,128)(2,1)}, bf16[8,256,256]{2,1,0:T(8,128)(2,1)S(1)}, u32[]{:S(2)}, u32[]{:S(2)}) collective-permute-start(bf16[8,256,256]{2,1,0:T(8,128)(2,1)} %get-tuple-element.91.refs_2_), channel_id=1, source_target_pairs={{0,4},{4,0},{1,5},{5,1},{2,6},{6,2},{3,7},{7,3},{8,12},{12,8},{9,1... | collective-permute-start | bytes 3145736 | tf_op jit(solution)/shard_map/ppermute | solution.py:28
  96.5 4.0 %collective-permute-start.9 = (bf16[8,192,256]{2,1,0:T(8,128)(2,1)}, bf16[8,192,256]{2,1,0:T(8,128)(2,1)S(1)}, u32[]{:S(2)}, u32[]{:S(2)}) collective-permute-start(bf16[8,192,256]{2,1,0:T(8,128)(2,1)} %get-tuple-element.92.refs_4_), channel_id=1, source_target_pairs={{0,4},{4,0},{1,5},{5,1},{2,6},{6,2},{3,7},{7,3},{8,12},{12,8},{9,1... | collective-permute-start | bytes 2359304 | tf_op jit(solution)/shard_map/ppermute | solution.py:28
  114.5 11.6 %collective-permute-start.10 = (bf16[192,256]{1,0:T(8,128)(2,1)}, bf16[192,256]{1,0:T(8,128)(2,1)S(1)}, u32[]{:S(2)}, u32[]{:S(2)}) collective-permute-start(bf16[192,256]{1,0:T(8,128)(2,1)} %get-tuple-element.98.refs_8_), channel_id=1, source_target_pairs={{0,3},{1,0},{2,1},{3,2},{4,7},{5,4},{6,5},{7,6},{8,11},{9,8},{10,9... | collective-permute-start | bytes 294920 | tf_op jit(solution)/shard_map/ppermute | solution.py:630
  119.3 12.3 %collective-permute-start.11 = (bf16[192,256]{1,0:T(8,128)(2,1)}, bf16[192,256]{1,0:T(8,128)(2,1)S(1)}, u32[]{:S(2)}, u32[]{:S(2)}) collective-permute-start(bf16[192,256]{1,0:T(8,128)(2,1)} %get-tuple-element.99.refs_9_), channel_id=1, source_target_pairs={{0,2},{1,3},{2,0},{3,1},{4,6},{5,7},{6,4},{7,5},{8,10},{9,11},{10,... | collective-permute-start | bytes 294920 | tf_op jit(solution)/shard_map/ppermute | solution.py:630
  119.3 12.3 %collective-permute-start.12 = (bf16[192,256]{1,0:T(8,128)(2,1)}, bf16[192,256]{1,0:T(8,128)(2,1)S(1)}, u32[]{:S(2)}, u32[]{:S(2)}) collective-permute-start(bf16[192,256]{1,0:T(8,128)(2,1)} %get-tuple-element.100.refs_10_), channel_id=1, source_target_pairs={{0,1},{1,2},{2,3},{3,0},{4,5},{5,6},{6,7},{7,4},{8,9},{9,10},{10,1... | collective-permute-start | bytes 294920 | tf_op jit(solution)/shard_map/ppermute | solution.py:630
  152.5 11.1 %collective-permute-start.13 = (bf16[2,2,4,96,1792]{4,3,2,1,0:T(8,128)(2,1)}, bf16[2,2,4,96,1792]{4,3,2,1,0:T(8,128)(2,1)}, u32[]{:S(2)}, u32[]{:S(2)}) collective-permute-start(bf16[2,2,4,96,1792]{4,3,2,1,0:T(8,128)(2,1)} %get-tuple-element.110), channel_id=1, source_target_pairs={{0,4},{4,0},{1,5},{5,1},{2,6},{6,2},{3,7},{7,3},{8,12},{12,8},{9,1... | collective-permute-start | bytes 16515080 | tf_op jit(solution)/shard_map/ppermute | solution.py:28
  152.6 16.1 %all-to-all-start.2 = ((bf16[4,192,256]{2,1,0:T(8,128)(2,1)}), bf16[4,192,256]{2,1,0:T(8,128)(2,1)S(1)}, u32[]{:S(2)}, u32[]{:S(2)}) async-start(bf16[4,192,256]{2,1,0:T(8,128)(2,1)} %get-tuple-element.103), calls=%async_computation.2 | async-start | bytes 786432 | tf_op jit(solution)/shard_map/all_to_all | solution.py:820
  163.5 8.2 %copy-start.1 = (bf16[8,192,256]{2,1,0:T(8,128)(2,1)S(1)}, bf16[8,192,256]{2,1,0:T(8,128)(2,1)}, u32[]{:S(2)}) copy-start(bf16[8,192,256]{2,1,0:T(8,128)(2,1)} %get-tuple-element.92.refs_4_) | copy-start | bytes 2359300
  163.5 8.2 %copy-start.3 = (bf16[8,192,256]{2,1,0:T(8,128)(2,1)S(1)}, bf16[8,192,256]{2,1,0:T(8,128)(2,1)}, u32[]{:S(2)}) copy-start(bf16[8,192,256]{2,1,0:T(8,128)(2,1)} %copy-done.2) | copy-start | bytes 2359300
  163.5 8.2 %copy-start.8 = (bf16[4,256,256]{2,1,0:T(8,128)(2,1)S(1)}, bf16[4,256,256]{2,1,0:T(8,128)(2,1)}, u32[]{:S(2)}) copy-start(bf16[4,256,256]{2,1,0:T(8,128)(2,1)} %get-tuple-element.96.refs_1_) | copy-start | bytes 1572868
  163.5 8.2 %copy-start.15 = (bf16[192,256]{1,0:T(8,128)(2,1)S(1)}, bf16[192,256]{1,0:T(8,128)(2,1)}, u32[]{:S(2)}) copy-start(bf16[192,256]{1,0:T(8,128)(2,1)} %get-tuple-element.97.refs_0_.refs_7_) | copy-start | bytes 294916
  163.5 8.2 %copy-start.16 = (bf16[192,256]{1,0:T(8,128)(2,1)S(1)}, bf16[192,256]{1,0:T(8,128)(2,1)}, u32[]{:S(2)}) copy-start(bf16[192,256]{1,0:T(8,128)(2,1)} %get-tuple-element.98.refs_8_) | copy-start | bytes 294916
  163.6 8.2 %copy-start.17 = (bf16[192,256]{1,0:T(8,128)(2,1)S(1)}, bf16[192,256]{1,0:T(8,128)(2,1)}, u32[]{:S(2)}) copy-start(bf16[192,256]{1,0:T(8,128)(2,1)} %get-tuple-element.99.refs_9_) | copy-start | bytes 294916
  163.6 8.2 %copy-start.18 = (bf16[192,256]{1,0:T(8,128)(2,1)S(1)}, bf16[192,256]{1,0:T(8,128)(2,1)}, u32[]{:S(2)}) copy-start(bf16[192,256]{1,0:T(8,128)(2,1)} %get-tuple-element.100.refs_10_) | copy-start | bytes 294916
  163.6 8.2 %copy-start.19 = (s32[5]{0:T(128)S(1)}, s32[5]{0:T(128)}, u32[]{:S(2)}) copy-start(s32[5]{0:T(128)} %stack.68.refs_0_.info_ref) | copy-start | bytes 64
  163.6 8.2 %copy-start.20 = (f32[3,256]{1,0:T(4,128)S(1)}, f32[3,256]{1,0:T(4,128)}, u32[]{:S(2)}) copy-start(f32[3,256]{1,0:T(4,128)} %get-tuple-element.115.refs_12_) | copy-start | bytes 9220
  168.7 32.6 %collective-permute-start.16 = (bf16[4,96,1792]{2,1,0:T(8,128)(2,1)}, bf16[4,96,1792]{2,1,0:T(8,128)(2,1)}, u32[]{:S(2)}, u32[]{:S(2)}) collective-permute-start(bf16[4,96,1792]{2,1,0:T(8,128)(2,1)} %get-tuple-element.123), channel_id=1, source_target_pairs={{0,16},{16,0},{1,17},{17,1},{2,18},{18,2},{3,19},{19,3},{4,20},{20... | collective-permute-start | bytes 4128776 | tf_op jit(solution)/shard_map/ppermute | solution.py:28
  171.0 31.7 %collective-permute-start.17 = (bf16[4,96,1792]{2,1,0:T(8,128)(2,1)}, bf16[4,96,1792]{2,1,0:T(8,128)(2,1)}, u32[]{:S(2)}, u32[]{:S(2)}) collective-permute-start(bf16[4,96,1792]{2,1,0:T(8,128)(2,1)} %get-tuple-element.124), channel_id=1, source_target_pairs={{0,8},{8,0},{1,9},{9,1},{2,10},{10,2},{3,11},{11,3},{4,12},{12,4},... | collective-permute-start | bytes 4128776 | tf_op jit(solution)/shard_map/ppermute | solution.py:28
  171.8 18.6 %copy-start = (bf16[2,2,192,576]{3,2,1,0:T(8,128)(2,1)S(1)}, bf16[2,2,192,576]{3,2,1,0:T(8,128)(2,1)}, u32[]{:S(2)}) copy-start(bf16[2,2,192,576]{3,2,1,0:T(8,128)(2,1)} %copy.41) | copy-start | bytes 2654212
  171.8 18.6 %copy-start.6 = (f32[4,256,128]{2,1,0:T(8,128)S(1)}, f32[4,256,128]{2,1,0:T(8,128)}, u32[]{:S(2)}) copy-start(f32[4,256,128]{2,1,0:T(8,128)} %get-tuple-element.89.refs_6_.sin_ref) | copy-start | bytes 1572868
  171.8 18.6 %copy-start.7 = (f32[4,256,128]{2,1,0:T(8,128)S(1)}, f32[4,256,128]{2,1,0:T(8,128)}, u32[]{:S(2)}) copy-start(f32[4,256,128]{2,1,0:T(8,128)} %get-tuple-element.88.refs_5_.cos_ref) | copy-start | bytes 1572868
  187.7 2.0 collective-permute-start.14
  187.8 2.6 collective-permute-start.15
  194.8 42.8 %all-to-all-start.3 = ((bf16[4,256,768]{2,1,0:T(8,128)(2,1)}), bf16[4,256,768]{2,1,0:T(8,128)(2,1)}, u32[]{:S(2)}, u32[]{:S(2)}) async-start(bf16[4,256,768]{2,1,0:T(8,128)(2,1)} %get-tuple-element.122), calls=%async_computation.3 | async-start | bytes 3145728 | tf_op jit(solution)/shard_map/all_to_all | solution.py:850
  199.2 61.4 %reduce-scatter.2.cloned.1.call-start = ((), (), s32[]{:S(2)}) async-start(), calls=%async_computation.6 | async-start | bytes 1720320 | tf_op jit(solution)/shard_map/reduce_scatter | solution.py:749
  206.1 16.1 %collective-permute-start.18 = (bf16[2,96,1792]{2,1,0:T(8,128)(2,1)}, bf16[2,96,1792]{2,1,0:T(8,128)(2,1)}, u32[]{:S(2)}, u32[]{:S(2)}) collective-permute-start(bf16[2,96,1792]{2,1,0:T(8,128)(2,1)} %get-tuple-element.131), channel_id=1, source_target_pairs={{0,8},{8,0},{1,9},{9,1},{2,10},{10,2},{3,11},{11,3},{4,12},{12,4},... | collective-permute-start | bytes 2064392 | tf_op jit(solution)/shard_map/ppermute | solution.py:28
  207.3 16.1 %collective-permute-start.19 = (bf16[2,96,1792]{2,1,0:T(8,128)(2,1)}, bf16[2,96,1792]{2,1,0:T(8,128)(2,1)}, u32[]{:S(2)}, u32[]{:S(2)}) collective-permute-start(bf16[2,96,1792]{2,1,0:T(8,128)(2,1)} %get-tuple-element.132), channel_id=1, source_target_pairs={{0,16},{16,0},{1,17},{17,1},{2,18},{18,2},{3,19},{19,3},{4,20},{20... | collective-permute-start | bytes 2064392 | tf_op jit(solution)/shard_map/ppermute | solution.py:28
  227.3 1.9 collective-permute-start.20
  229.5 8.1 %collective-permute-start.21 = (bf16[192,576]{1,0:T(8,128)(2,1)S(1)}, bf16[192,576]{1,0:T(8,128)(2,1)S(1)}, u32[]{:S(2)}, u32[]{:S(2)}) collective-permute-start(bf16[192,576]{1,0:T(8,128)(2,1)S(1)} %select_bitcast_fusion.7), channel_id=1, source_target_pairs={{0,8},{8,0},{1,9},{9,1},{2,10},{10,2},{3,11},{11,3},{4,12},{12,4},... | collective-permute-start | bytes 663560 | tf_op jit(solution)/shard_map/ppermute | solution.py:28
  230.6 8.8 %copy-start.25 = (f32[256,768]{1,0:T(8,128)S(1)}, f32[256,768]{1,0:T(8,128)}, u32[]{:S(2)}) copy-start(f32[256,768]{1,0:T(8,128)} %get-tuple-element.102) | copy-start | bytes 2359300
  241.4 31.3 %all-to-all-start.4 = ((bf16[8,256,384]{2,1,0:T(8,128)(2,1)}), bf16[8,256,384]{2,1,0:T(8,128)(2,1)S(1)}, u32[]{:S(2)}, u32[]{:S(2)}) async-start(bf16[8,256,384]{2,1,0:T(8,128)(2,1)} %bitcast.40), calls=%async_computation.4 | async-start | bytes 3145728 | tf_op jit(solution)/shard_map/all_to_all | solution.py:824
  261.8 22.0 %collective-permute-start.22 = (bf16[96,2944]{1,0:T(8,128)(2,1)S(1)}, bf16[96,2944]{1,0:T(8,128)(2,1)S(1)}, u32[]{:S(2)}, u32[]{:S(2)}) collective-permute-start(bf16[96,2944]{1,0:T(8,128)(2,1)S(1)} %concatenate.11.refs_1_), channel_id=1, source_target_pairs={{0,16},{16,0},{1,17},{17,1},{2,18},{18,2},{3,19},{19,3},{4,20},{20... | collective-permute-start | bytes 1695752 | tf_op jit(solution)/shard_map/ppermute | solution.py:28
  (19 other events, 81.7 us)
Sparse Core Ops, SparseCore 0:
  10.9 117.9 all-gather.2
  227.5 33.0 reduce-scatter.1

commit v9 on v8

--- a/solution.py
+++ b/solution.py
@@ -513,7 +513,7 @@
             pltpu.SemaphoreType.DMA((3, parts)),
             pltpu.SemaphoreType.DMA((4,)),
         ],
-        compiler_params=pltpu.CompilerParams(vmem_limit_bytes=60 << 20),
+        compiler_params=pltpu.CompilerParams(vmem_limit_bytes=52 << 20),
         cost_estimate=cost(0.001),
         name="feed",
     )(info, tokens, cot, weights, *attended)
@@ -575,7 +575,7 @@
             out_specs=pl.BlockSpec((2, slabs, 1, slab, lanes), lambda i, s: (0, 0, i, 0, 0)),
         ),
         out_shape=jax.ShapeDtypeStruct((2, slabs, columns, slab, lanes), bf16),
-        compiler_params=pltpu.CompilerParams(vmem_limit_bytes=60 << 20),
+        compiler_params=pltpu.CompilerParams(vmem_limit_bytes=52 << 20),
         cost_estimate=cost(0.001),
         name="weigh",
     )(info, hidden, act, gin, gtwo, gone, sums, *attended)

time: 294 us -> 296 us (level)
  no operation moved by 1% of the time
where the time goes in v9:
time: 296 us; the launch traced here: 295 us
  waiting for transfers between devices  109 us (37%)
  Pallas kernels  85.3 us (29%)
  starting transfers between devices  55.3 us (19%)
  between operations  16 us (5%)
  local copies, waits for them, and re-layouts  15.8 us (5%)
  other arithmetic  8.1 us (3%)
  matrix products  5.52 us (2%)
    ppermute x17, waiting for transfers between devices, swap(): return lax.ppermute(values, axis, SWAP)  44.8 us
    ppermute x6, waiting for transfers between devices, shift(): lax.ppermute(values, 'col', [(i, (i + step) % columns) for i in range(col...  38.3 us
    pallas_call x1, Pallas kernels, feed(): pl.pallas_call(feed_kernel, in_specs=[smem, vmem, vmem, pl.BlockSpec(memo...  19.7 us
    ppermute x17, starting transfers between devices, swap(): return lax.ppermute(values, axis, SWAP)  18.4 us
    pallas_call x2, Pallas kernels, attend_forward(): pl.pallas_call(lambda *refs: forward_kernel(first, share, *refs), grid_sp...  17.1 us
    pallas_call x1, Pallas kernels, attend_backward(): pl.pallas_call(lambda *refs: backward_kernel(columns, share, *refs), in_s...  15.9 us
    pallas_call x3, Pallas kernels, add_blocks(): pl.pallas_call(lambda *refs: add_kernel(len(lengths), sums, *refs), in_sp...  11.3 us
    all_to_all x1, starting transfers between devices, to_loader(): lax.all_to_all(cut, ('dp',) + ROWS, split_axis=0, concat_axis=0, tiled=True)  10.6 us
  transfers between devices with their start and end apart: 30, of which 21 were waited for; matrix products, arithmetic and copies ran while one was open for 8% of the time, Pallas kernels for 21%

profile of v9, /device:TPU:0, one launch (start us, length us, event | category | flops | bytes accessed | tf_op | source)
XLA Modules:
  0.0 295.0 jit_solution(2325788778179352227)
XLA Ops:
  7.3 2.2 parcel.1
  9.5 3.0 %collective-permute-start = (bf16[2,192,512]{2,1,0:T(8,128)(2,1)}, bf16[2,192,512]{2,1,0:T(8,128)(2,1)S(1)}, u32[]{:S(2)}, u32[]{:S(2)}) collective-permute-start(bf16[2,192,512]{2,1,0:T(8,128)(2,1)} %param.14), channel_id=1, source_target_pairs={{0,16},{16,0},{1,17},{17,1},{2,18},{18,2},{3,19},{19,3},{4,20},{20... | collective-permute-start | bytes 1179656 | tf_op jit(solution)/shard_map/ppermute | solution.py:28
  13.7 2.0 collective-permute-start.6
  18.0 3.0 %fusion.30 = (f32[4,256,128]{2,1,0:T(8,128)}, f32[4,256,128]{2,1,0:T(8,128)}) fusion(f32[128]{0:T(128)S(1)} %compare_select_fusion.2, f32[128]{0:T(128)S(1)} %mul.76, f32[4,256]{1,0:T(4,128)S(1)} %subtract_convert_fusion), kind=kLoop, calls=%fused_computation.28 | loop fusion | flops 262144 | bytes 1053696 | tf_op jit(solution)/shard_map/mul | solution.py:788
  22.1 1.8 fusion.24
  23.9 1.8 collective-permute-start.1
  27.6 3.5 %all-to-all-start = ((bf16[4,256,192]{1,2,0:T(8,128)(2,1)}), bf16[4,256,192]{1,2,0:T(8,128)(2,1)S(1)}, u32[]{:S(2)}, u32[]{:S(2)}) async-start(bf16[4,256,192]{1,2,0:T(8,128)(2,1)} %bitcast.109), calls=%async_computation | async-start | bytes 786432 | tf_op jit(solution)/shard_map/all_to_all | solution.py:799
  31.0 4.9 %collective-permute-done.1 = bf16[2,192,512]{2,1,0:T(8,128)(2,1)S(1)} collective-permute-done((bf16[2,192,512]{2,1,0:T(8,128)(2,1)S(1)}, bf16[2,192,512]{2,1,0:T(8,128)(2,1)S(1)}, u32[]{:S(2)}, u32[]{:S(2)}) %collective-permute-start.1) | collective-permute-done | bytes 393248 | tf_op jit(solution)/shard_map/ppermute | solution.py:28
  36.0 2.4 all-to-all-done
  38.6 3.6 %collective-permute-start.2 = (bf16[256,768]{1,0:T(8,128)(2,1)S(1)}, bf16[256,768]{1,0:T(8,128)(2,1)S(1)}, u32[]{:S(2)}, u32[]{:S(2)}) collective-permute-start(bf16[256,768]{1,0:T(8,128)(2,1)S(1)} %copy.43.refs_0_.x_ref), channel_id=1, source_target_pairs={{0,3},{1,0},{2,1},{3,2},{4,7},{5,4},{6,5},{7,6},{8,11},{9,8},{10,9... | collective-permute-start | bytes 1179656 | tf_op jit(solution)/shard_map/ppermute | solution.py:630
  43.3 1.8 fusion.21
  45.9 4.3 %all-to-all-start.1 = ((bf16[4,256,192]{1,2,0:T(8,128)(2,1)}), bf16[4,256,192]{1,2,0:T(8,128)(2,1)}, u32[]{:S(2)}, u32[]{:S(2)}) async-start(bf16[4,256,192]{1,2,0:T(8,128)(2,1)} %bitcast.108), calls=%async_computation.1 | async-start | bytes 786432 | tf_op jit(solution)/shard_map/all_to_all | solution.py:799
  51.5 5.9 %all-to-all-done.1 = bf16[4,256,192]{1,2,0:T(8,128)(2,1)} async-done(((bf16[4,256,192]{1,2,0:T(8,128)(2,1)}), bf16[4,256,192]{1,2,0:T(8,128)(2,1)}, u32[]{:S(2)}, u32[]{:S(2)}) %all-to-all-start.1) | async-done | bytes 393248 | tf_op jit(solution)/shard_map/all_to_all | solution.py:799
  57.5 12.7 %collective-permute-done.2.refs_3_ = bf16[256,768]{1,0:T(8,128)(2,1)S(1)} collective-permute-done((bf16[256,768]{1,0:T(8,128)(2,1)S(1)}, bf16[256,768]{1,0:T(8,128)(2,1)S(1)}, u32[]{:S(2)}, u32[]{:S(2)}) %collective-permute-start.2) | collective-permute-done | bytes 393248 | tf_op jit(solution)/shard_map/ppermute | solution.py:630
  70.2 4.7 %collective-permute-done.4.refs_1_ = bf16[256,768]{1,0:T(8,128)(2,1)S(1)} collective-permute-done((bf16[256,768]{1,0:T(8,128)(2,1)S(1)}, bf16[256,768]{1,0:T(8,128)(2,1)S(1)}, u32[]{:S(2)}, u32[]{:S(2)}) %collective-permute-start.4) | collective-permute-done | bytes 393248 | tf_op jit(solution)/shard_map/ppermute | solution.py:630
  74.9 15.5 %collective-permute-done.5.refs_2_ = bf16[256,768]{1,0:T(8,128)(2,1)S(1)} collective-permute-done((bf16[256,768]{1,0:T(8,128)(2,1)S(1)}, bf16[256,768]{1,0:T(8,128)(2,1)S(1)}, u32[]{:S(2)}, u32[]{:S(2)}) %collective-permute-start.5) | collective-permute-done | bytes 393248 | tf_op jit(solution)/shard_map/ppermute | solution.py:630
  91.1 5.4 %project.1 = (bf16[4,256,256]{2,1,0:T(8,128)(2,1)}, bf16[8,256,256]{2,1,0:T(8,128)(2,1)}, bf16[8,192,256]{2,1,0:T(8,128)(2,1)}) custom-call(bf16[256,768]{1,0:T(8,128)(2,1)} %copy-done.4, bf16[256,768]{1,0:T(8,128)(2,1)} %copy-done.11, bf16[256,768]{1,0:T(8,128)(2,1)} %copy-done.13, bf16[256,768]{1,0:T(8,128)(2,1)} %copy-done.9, bf16[768,576]{1,0:T(8,128)(2,1)} %bitcast.110, ...), custom_call_target="tpu_custom_call" | custom-call | flops 1000000 | bytes 3000 | tf_op jit(solution)/shard_map/project/pallas_call | solution.py:76
  97.6 2.9 collective-permute-done.9.refs_5_
  101.8 12.7 %attend_forward.2 = (bf16[192,256]{1,0:T(8,128)(2,1)}, bf16[192,256]{1,0:T(8,128)(2,1)}, bf16[192,256]{1,0:T(8,128)(2,1)}, f32[3,256]{1,0:T(4,128)}, f32[3,256]{1,0:T(4,128)}, /*index=5*/f32[3,256]{1,0:T(4,128)}) custom-call(s32[5]{0:T(128)} %stack.68.refs_0_.info_ref, bf16[4,256,256]{2,1,0:T(8,128)(2,1)} %get-tuple-element.96.refs_1_, ...), custom_call_target="tpu_custom_call" | custom-call | flops 1000000 | bytes 3000 | tf_op jit(solution)/shard_map/attend_forward/pallas_call | solution.py:182
  114.5 4.8 %collective-permute-start.10 = (bf16[192,256]{1,0:T(8,128)(2,1)}, bf16[192,256]{1,0:T(8,128)(2,1)S(1)}, u32[]{:S(2)}, u32[]{:S(2)}) collective-permute-start(bf16[192,256]{1,0:T(8,128)(2,1)} %get-tuple-element.98.refs_8_), channel_id=1, source_target_pairs={{0,3},{1,0},{2,1},{3,2},{4,7},{5,4},{6,5},{7,6},{8,11},{9,8},{10,9... | collective-permute-start | bytes 294920 | tf_op jit(solution)/shard_map/ppermute | solution.py:630
  119.9 2.0 copy.44.cot_ref
  122.0 4.3 %attend_forward.3 = (bf16[192,256]{1,0:T(8,128)(2,1)}, f32[3,256]{1,0:T(4,128)}) custom-call(s32[5]{0:T(128)} %stack.68.refs_0_.info_ref, bf16[4,256,256]{2,1,0:T(8,128)(2,1)} %get-tuple-element.96.refs_1_, bf16[8,256,256]{2,1,0:T(8,128)(2,1)} %get-tuple-element.91.refs_2_, bf16[8,256,256]{2,1,0:T(8,128)(2,1)} %copy-done.28, ...), custom_call_target="tpu_custom_call" | custom-call | flops 1000000 | bytes 3000 | tf_op jit(solution)/shard_map/attend_forward/pallas_call | solution.py:182
  126.3 5.4 %collective-permute-done.11.refs_2_ = bf16[192,256]{1,0:T(8,128)(2,1)S(1)} collective-permute-done((bf16[192,256]{1,0:T(8,128)(2,1)}, bf16[192,256]{1,0:T(8,128)(2,1)S(1)}, u32[]{:S(2)}, u32[]{:S(2)}) %collective-permute-start.11) | collective-permute-done | bytes 98336 | tf_op jit(solution)/shard_map/ppermute | solution.py:630
  132.6 19.7 %feed.1 = (bf16[256,768]{1,0:T(8,128)(2,1)S(1)}, bf16[4,192,256]{2,1,0:T(8,128)(2,1)}, f32[256,768]{1,0:T(8,128)}, bf16[768,256]{1,0:T(8,128)(2,1)S(1)}, bf16[4,...) custom-call(s32[5]{0:T(128)S(1)} %copy-done.23, ...), custom_call_target="tpu_custom_call" | custom-call | flops 1000000 | bytes 3000 | tf_op jit(solution)/shard_map/feed/pallas_call | solution.py:497
  153.0 3.7 %all-to-all-start.2 = ((bf16[4,192,256]{2,1,0:T(8,128)(2,1)}), bf16[4,192,256]{2,1,0:T(8,128)(2,1)S(1)}, u32[]{:S(2)}, u32[]{:S(2)}) async-start(bf16[4,192,256]{2,1,0:T(8,128)(2,1)} %get-tuple-element.103), calls=%async_computation.2 | async-start | bytes 786432 | tf_op jit(solution)/shard_map/all_to_all | solution.py:820
  157.7 6.5 %weigh.1.refs_0_ = bf16[2,2,4,96,1792]{4,3,2,1,0:T(8,128)(2,1)} custom-call(s32[5]{0:T(128)S(1)} %copy-done.23, bf16[768,256]{1,0:T(8,128)(2,1)S(1)} %get-tuple-element.104.hidden_ref, bf16[4,256,768]{2,1,0:T(8,128)(2,1)} %get-tuple-element.105.act_ref, bf16[4,256,768]{2,1,0:T(8,128)(2,1)} %get-tuple-element.106.gin_ref, ...), custom_call_target="tpu_custom_call" | custom-call | flops 1000000 | bytes 3000 | tf_op jit(solution)/shard_map/weigh/pallas_call | solution.py:569
  164.3 4.1 %add_blocks.3 = (bf16[4,96,1792]{2,1,0:T(8,128)(2,1)}, bf16[4,96,1792]{2,1,0:T(8,128)(2,1)}) custom-call(bf16[2,2,4,96,1792]{4,3,2,1,0:T(8,128)(2,1)} %weigh.1.refs_0_, bf16[2,2,4,96,1792]{4,3,2,1,0:T(8,128)(2,1)} %collective-permute-done.13.refs_1_), custom_call_target="tpu_custom_call" | custom-call | flops 1000000 | bytes 3000 | tf_op jit(solution)/shard_map/add_blocks/pallas_call | solution.py:664
  169.0 3.4 %collective-permute-start.16 = (bf16[4,96,1792]{2,1,0:T(8,128)(2,1)}, bf16[4,96,1792]{2,1,0:T(8,128)(2,1)}, u32[]{:S(2)}, u32[]{:S(2)}) collective-permute-start(bf16[4,96,1792]{2,1,0:T(8,128)(2,1)} %get-tuple-element.123), channel_id=1, source_target_pairs={{0,16},{16,0},{1,17},{17,1},{2,18},{18,2},{3,19},{19,3},{4,20},{20... | collective-permute-start | bytes 4128776 | tf_op jit(solution)/shard_map/ppermute | solution.py:28
  172.9 15.9 %attend_backward.1 = (f32[4,256,192]{2,1,0:T(8,128)S(1)}, bf16[8,256,256]{2,1,0:T(8,128)(2,1)S(1)}, bf16[4,256,256]{2,1,0:T(8,128)(2,1)S(1)}, bf16[4,256,256]{2,1,0:T(8,128)(2,1)S(1)}) custom-call(s32[5]{0:T(128)S(1)} %copy-done.23, bf16[4,256,256]{2,1,0:T(8,128)(2,1)S(1)} %copy-done.8, bf16[8,256,256]{2,1,0:T(8,128)(2,1)} %get-tuple-element.91.refs_2_, ...), custom_call_target="tpu_custom_call" | custom-call | flops 1000000 | bytes 3000 | tf_op jit(solution)/shard_map/attend_backward/pallas_call | solution.py:265
  191.5 4.4 %unproject.1 = (bf16[4,256,768]{2,1,0:T(8,128)(2,1)}, bf16[4,256,576]{2,1,0:T(8,128)(2,1)S(1)}) custom-call(s32[5]{0:T(128)S(1)} %copy-done.23, f32[4,256,192]{2,1,0:T(8,128)S(1)} %get-tuple-element.118.dq_ref, bf16[8,256,256]{2,1,0:T(8,128)(2,1)S(1)} %get-tuple-element.119.near_k_ref.near_v_ref, bf16[4,256,256]{2,1,0:T(8,128)(2,1)S(1)} %collective-permute-done.14.far_k_ref, ...), custom_call_target="tpu_custom_call" | custom-call | flops 1000000 | bytes 3000 | tf_op jit(solution)/shard_map/unproject/pallas_call | solution.py:307
  195.8 4.6 %all-to-all-start.3 = ((bf16[4,256,768]{2,1,0:T(8,128)(2,1)}), bf16[4,256,768]{2,1,0:T(8,128)(2,1)}, u32[]{:S(2)}, u32[]{:S(2)}) async-start(bf16[4,256,768]{2,1,0:T(8,128)(2,1)} %get-tuple-element.122), calls=%async_computation.3 | async-start | bytes 3145728 | tf_op jit(solution)/shard_map/all_to_all | solution.py:850
  200.5 2.5 collective-permute-done.16.refs_2_
  203.0 1.5 collective-permute-done.17.refs_3_
  204.5 3.4 %add_blocks.4 = (bf16[2,96,1792]{2,1,0:T(8,128)(2,1)}, bf16[2,96,1792]{2,1,0:T(8,128)(2,1)}) custom-call(bf16[2,2,4,96,1792]{4,3,2,1,0:T(8,128)(2,1)} %weigh.1.refs_0_, bf16[2,2,4,96,1792]{4,3,2,1,0:T(8,128)(2,1)} %collective-permute-done.13.refs_1_, bf16[4,96,1792]{2,1,0:T(8,128)(2,1)} %collective-permute-done.16.refs_2_, ...), custom_call_target="tpu_custom_call" | custom-call | flops 1000000 | bytes 3000 | tf_op jit(solution)/shard_map/add_blocks/pallas_call | solution.py:664
  208.7 1.7 collective-permute-start.19
  210.4 1.5 project_grad.1
  211.8 12.6 %collective-permute-done.18.refs_4_ = bf16[2,96,1792]{2,1,0:T(8,128)(2,1)} collective-permute-done((bf16[2,96,1792]{2,1,0:T(8,128)(2,1)}, bf16[2,96,1792]{2,1,0:T(8,128)(2,1)}, u32[]{:S(2)}, u32[]{:S(2)}) %collective-permute-start.18) | collective-permute-done | bytes 688160 | tf_op jit(solution)/shard_map/ppermute | solution.py:28
  225.2 3.8 %add_blocks.5 = bf16[4,96,1792]{2,1,0:T(8,128)(2,1)} custom-call(bf16[2,2,4,96,1792]{4,3,2,1,0:T(8,128)(2,1)} %weigh.1.refs_0_, bf16[2,2,4,96,1792]{4,3,2,1,0:T(8,128)(2,1)} %collective-permute-done.13.refs_1_, bf16[4,96,1792]{2,1,0:T(8,128)(2,1)} %collective-permute-done.16.refs_2_, bf16[4,96,1792]{2,1,0:T(8,128)(2,1)} %collective-permute-done.17.refs_3_, ...), custom_call_target="tpu_custom_call" | custom-call | flops 1000000 | bytes 3000 | tf_op jit(solution)/shard_map/add_blocks/pallas_call | solution.py:664
  229.2 1.8 collective-permute-done.20
  232.7 6.7 %collective-permute-done.21 = bf16[192,576]{1,0:T(8,128)(2,1)S(1)} collective-permute-done((bf16[192,576]{1,0:T(8,128)(2,1)S(1)}, bf16[192,576]{1,0:T(8,128)(2,1)S(1)}, u32[]{:S(2)}, u32[]{:S(2)}) %collective-permute-start.21) | collective-permute-done | bytes 221216 | tf_op jit(solution)/shard_map/ppermute | solution.py:28
  239.4 1.7 convert_reduce_fusion
  243.2 10.6 %all-to-all-start.4 = ((bf16[8,256,384]{2,1,0:T(8,128)(2,1)}), bf16[8,256,384]{2,1,0:T(8,128)(2,1)S(1)}, u32[]{:S(2)}, u32[]{:S(2)}) async-start(bf16[8,256,384]{2,1,0:T(8,128)(2,1)} %bitcast.40), calls=%async_computation.4 | async-start | bytes 3145728 | tf_op jit(solution)/shard_map/all_to_all | solution.py:824
  253.8 8.9 %reduce-scatter.2.cloned.1.call-done = bf16[1,96,1792]{2,1,0:T(8,128)(2,1)} async-done(((bf16[4,96,1792]{2,1,0:T(8,128)(2,1)}), bf16[1,96,1792]{2,1,0:T(8,128)(2,1)}) %reduce-scatter.2.cloned.1.call-update) | async-done | bytes 344080 | tf_op jit(solution)/shard_map/reduce_scatter | solution.py:749
  263.9 2.9 collective-permute-start.22
  266.9 8.1 %all-to-all-done.4 = bf16[8,256,384]{2,1,0:T(8,128)(2,1)S(1)} async-done(((bf16[8,256,384]{2,1,0:T(8,128)(2,1)}), bf16[8,256,384]{2,1,0:T(8,128)(2,1)S(1)}, u32[]{:S(2)}, u32[]{:S(2)}) %all-to-all-start.4) | async-done | bytes 1572896 | tf_op jit(solution)/shard_map/all_to_all | solution.py:824
  274.9 2.0 fusion.12
  277.9 8.1 %collective-permute-done.22.refs_2_ = bf16[96,2944]{1,0:T(8,128)(2,1)S(1)} collective-permute-done((bf16[96,2944]{1,0:T(8,128)(2,1)S(1)}, bf16[96,2944]{1,0:T(8,128)(2,1)S(1)}, u32[]{:S(2)}, u32[]{:S(2)}) %collective-permute-start.22) | collective-permute-done | bytes 565280 | tf_op jit(solution)/shard_map/ppermute | solution.py:28
  286.0 1.5 open_shards.1
  (152 shorter events, 26.9 us)
Async XLA Ops:
  7.2 14.7 %copy-start.30 = (bf16[2,192,512]{2,1,0:T(8,128)(2,1)S(1)}, bf16[2,192,512]{2,1,0:T(8,128)(2,1)}, u32[]{:S(2)}) copy-start(bf16[2,192,512]{2,1,0:T(8,128)(2,1)} %param.14) | copy-start | bytes 1179652
  7.2 8.8 %copy-start.35 = (s32[2,512]{1,0:T(2,128)S(1)}, s32[2,512]{1,0:T(2,128)}, u32[]{:S(2)}) copy-start(s32[2,512]{1,0:T(2,128)} %param.17) | copy-start | bytes 12292
  7.2 8.8 %copy-start.36 = (s32[1,2]{1,0:T(1,128)S(1)}, s32[1,2]{1,0:T(1,128)}, u32[]{:S(2)}) copy-start(s32[1,2]{1,0:T(1,128)} %param.16) | copy-start | bytes 28
  7.2 124.4 %all-gather.3.cloned.1.call-start = ((), (), s32[]{:S(2)}) async-start(), calls=%async_computation.7 | async-start | bytes 11354112 | tf_op jit(solution)/shard_map/all_gather | solution.py:777
  9.5 12.4 %collective-permute-start = (bf16[2,192,512]{2,1,0:T(8,128)(2,1)}, bf16[2,192,512]{2,1,0:T(8,128)(2,1)S(1)}, u32[]{:S(2)}, u32[]{:S(2)}) collective-permute-start(bf16[2,192,512]{2,1,0:T(8,128)(2,1)} %param.14), channel_id=1, source_target_pairs={{0,16},{16,0},{1,17},{17,1},{2,18},{18,2},{3,19},{19,3},{4,20},{20... | collective-permute-start | bytes 1179656 | tf_op jit(solution)/shard_map/ppermute | solution.py:28
  12.5 9.4 %collective-permute-start.3 = (s32[2,512]{1,0:T(2,128)}, s32[2,512]{1,0:T(2,128)S(1)}, u32[]{:S(2)}, u32[]{:S(2)}) collective-permute-start(s32[2,512]{1,0:T(2,128)} %param.17), channel_id=1, source_target_pairs={{0,16},{16,0},{1,17},{17,1},{2,18},{18,2},{3,19},{19,3},{4,20},{20... | collective-permute-start | bytes 12296 | tf_op jit(solution)/shard_map/ppermute | solution.py:28
  13.7 12.1 %collective-permute-start.6 = (bf16[192,576]{1,0:T(8,128)(2,1)S(1)}, bf16[192,576]{1,0:T(8,128)(2,1)S(1)}, u32[]{:S(2)}, u32[]{:S(2)}) collective-permute-start(bf16[192,576]{1,0:T(8,128)(2,1)S(1)} %pad_maximum_fusion.5), channel_id=1, source_target_pairs={{0,8},{8,0},{1,9},{9,1},{2,10},{10,2},{3,11},{11,3},{4,12},{12,4},... | collective-permute-start | bytes 663560 | tf_op jit(solution)/shard_map/ppermute | solution.py:28
  23.9 12.0 %collective-permute-start.1 = (bf16[2,192,512]{2,1,0:T(8,128)(2,1)S(1)}, bf16[2,192,512]{2,1,0:T(8,128)(2,1)S(1)}, u32[]{:S(2)}, u32[]{:S(2)}) collective-permute-start(bf16[2,192,512]{2,1,0:T(8,128)(2,1)S(1)} %copy-done.31), channel_id=1, source_target_pairs={{0,16},{16,0},{1,17},{17,1},{2,18},{18,2},{3,19},{19,3},{4,20},{20... | collective-permute-start | bytes 1179656 | tf_op jit(solution)/shard_map/ppermute | solution.py:28
  26.8 23.4 %collective-permute-start.7 = (bf16[2,192,576]{2,1,0:T(8,128)(2,1)}, bf16[2,192,576]{2,1,0:T(8,128)(2,1)S(1)}, u32[]{:S(2)}, u32[]{:S(2)}) collective-permute-start(bf16[2,192,576]{2,1,0:T(8,128)(2,1)} %pad_maximum_fusion.4), channel_id=1, source_target_pairs={{0,4},{4,0},{1,5},{5,1},{2,6},{6,2},{3,7},{7,3},{8,12},{12,8},{9,1... | collective-permute-start | bytes 1327112 | tf_op jit(solution)/shard_map/ppermute | solution.py:28
  27.6 10.9 %all-to-all-start = ((bf16[4,256,192]{1,2,0:T(8,128)(2,1)}), bf16[4,256,192]{1,2,0:T(8,128)(2,1)S(1)}, u32[]{:S(2)}, u32[]{:S(2)}) async-start(bf16[4,256,192]{1,2,0:T(8,128)(2,1)} %bitcast.109), calls=%async_computation | async-start | bytes 786432 | tf_op jit(solution)/shard_map/all_to_all | solution.py:799
  38.6 31.5 %collective-permute-start.2 = (bf16[256,768]{1,0:T(8,128)(2,1)S(1)}, bf16[256,768]{1,0:T(8,128)(2,1)S(1)}, u32[]{:S(2)}, u32[]{:S(2)}) collective-permute-start(bf16[256,768]{1,0:T(8,128)(2,1)S(1)} %copy.43.refs_0_.x_ref), channel_id=1, source_target_pairs={{0,3},{1,0},{2,1},{3,2},{4,7},{5,4},{6,5},{7,6},{8,11},{9,8},{10,9... | collective-permute-start | bytes 1179656 | tf_op jit(solution)/shard_map/ppermute | solution.py:630
  42.3 32.6 %collective-permute-start.4 = (bf16[256,768]{1,0:T(8,128)(2,1)S(1)}, bf16[256,768]{1,0:T(8,128)(2,1)S(1)}, u32[]{:S(2)}, u32[]{:S(2)}) collective-permute-start(bf16[256,768]{1,0:T(8,128)(2,1)S(1)} %copy.43.refs_0_.x_ref), channel_id=1, source_target_pairs={{0,1},{1,2},{2,3},{3,0},{4,5},{5,6},{6,7},{7,4},{8,9},{9,10},{10,1... | collective-permute-start | bytes 1179656 | tf_op jit(solution)/shard_map/ppermute | solution.py:630
  42.3 48.1 %collective-permute-start.5 = (bf16[256,768]{1,0:T(8,128)(2,1)S(1)}, bf16[256,768]{1,0:T(8,128)(2,1)S(1)}, u32[]{:S(2)}, u32[]{:S(2)}) collective-permute-start(bf16[256,768]{1,0:T(8,128)(2,1)S(1)} %copy.43.refs_0_.x_ref), channel_id=1, source_target_pairs={{0,2},{1,3},{2,0},{3,1},{4,6},{5,7},{6,4},{7,5},{8,10},{9,11},{10,... | collective-permute-start | bytes 1179656 | tf_op jit(solution)/shard_map/ppermute | solution.py:630
  45.9 11.6 %all-to-all-start.1 = ((bf16[4,256,192]{1,2,0:T(8,128)(2,1)}), bf16[4,256,192]{1,2,0:T(8,128)(2,1)}, u32[]{:S(2)}, u32[]{:S(2)}) async-start(bf16[4,256,192]{1,2,0:T(8,128)(2,1)} %bitcast.108), calls=%async_computation.1 | async-start | bytes 786432 | tf_op jit(solution)/shard_map/all_to_all | solution.py:799
  70.2 20.2 %copy-start.9 = (bf16[256,768]{1,0:T(8,128)(2,1)}, bf16[256,768]{1,0:T(8,128)(2,1)S(1)}, u32[]{:S(2)}) copy-start(bf16[256,768]{1,0:T(8,128)(2,1)S(1)} %collective-permute-done.2.refs_3_) | copy-start | bytes 1179652
  74.9 15.5 %copy-start.11 = (bf16[256,768]{1,0:T(8,128)(2,1)}, bf16[256,768]{1,0:T(8,128)(2,1)S(1)}, u32[]{:S(2)}) copy-start(bf16[256,768]{1,0:T(8,128)(2,1)S(1)} %collective-permute-done.4.refs_1_) | copy-start | bytes 1179652
  96.5 4.0 %collective-permute-start.8 = (bf16[8,256,256]{2,1,0:T(8,128)(2,1)}, bf16[8,256,256]{2,1,0:T(8,128)(2,1)S(1)}, u32[]{:S(2)}, u32[]{:S(2)}) collective-permute-start(bf16[8,256,256]{2,1,0:T(8,128)(2,1)} %get-tuple-element.91.refs_2_), channel_id=1, source_target_pairs={{0,4},{4,0},{1,5},{5,1},{2,6},{6,2},{3,7},{7,3},{8,12},{12,8},{9,1... | collective-permute-start | bytes 3145736 | tf_op jit(solution)/shard_map/ppermute | solution.py:28
  96.5 4.0 %collective-permute-start.9 = (bf16[8,192,256]{2,1,0:T(8,128)(2,1)}, bf16[8,192,256]{2,1,0:T(8,128)(2,1)S(1)}, u32[]{:S(2)}, u32[]{:S(2)}) collective-permute-start(bf16[8,192,256]{2,1,0:T(8,128)(2,1)} %get-tuple-element.92.refs_4_), channel_id=1, source_target_pairs={{0,4},{4,0},{1,5},{5,1},{2,6},{6,2},{3,7},{7,3},{8,12},{12,8},{9,1... | collective-permute-start | bytes 2359304 | tf_op jit(solution)/shard_map/ppermute | solution.py:28
  114.5 11.7 %collective-permute-start.10 = (bf16[192,256]{1,0:T(8,128)(2,1)}, bf16[192,256]{1,0:T(8,128)(2,1)S(1)}, u32[]{:S(2)}, u32[]{:S(2)}) collective-permute-start(bf16[192,256]{1,0:T(8,128)(2,1)} %get-tuple-element.98.refs_8_), channel_id=1, source_target_pairs={{0,3},{1,0},{2,1},{3,2},{4,7},{5,4},{6,5},{7,6},{8,11},{9,8},{10,9... | collective-permute-start | bytes 294920 | tf_op jit(solution)/shard_map/ppermute | solution.py:630
  119.3 12.3 %collective-permute-start.11 = (bf16[192,256]{1,0:T(8,128)(2,1)}, bf16[192,256]{1,0:T(8,128)(2,1)S(1)}, u32[]{:S(2)}, u32[]{:S(2)}) collective-permute-start(bf16[192,256]{1,0:T(8,128)(2,1)} %get-tuple-element.99.refs_9_), channel_id=1, source_target_pairs={{0,2},{1,3},{2,0},{3,1},{4,6},{5,7},{6,4},{7,5},{8,10},{9,11},{10,... | collective-permute-start | bytes 294920 | tf_op jit(solution)/shard_map/ppermute | solution.py:630
  119.3 12.3 %collective-permute-start.12 = (bf16[192,256]{1,0:T(8,128)(2,1)}, bf16[192,256]{1,0:T(8,128)(2,1)S(1)}, u32[]{:S(2)}, u32[]{:S(2)}) collective-permute-start(bf16[192,256]{1,0:T(8,128)(2,1)} %get-tuple-element.100.refs_10_), channel_id=1, source_target_pairs={{0,1},{1,2},{2,3},{3,0},{4,5},{5,6},{6,7},{7,4},{8,9},{9,10},{10,1... | collective-permute-start | bytes 294920 | tf_op jit(solution)/shard_map/ppermute | solution.py:630
  122.0 9.7 %copy-start.23 = (s32[5]{0:T(128)S(1)}, s32[5]{0:T(128)}, u32[]{:S(2)}) copy-start(s32[5]{0:T(128)} %stack.68.refs_0_.info_ref) | copy-start | bytes 64
  132.5 24.1 %copy-start.16 = (bf16[192,256]{1,0:T(8,128)(2,1)S(1)}, bf16[192,256]{1,0:T(8,128)(2,1)}, u32[]{:S(2)}) copy-start(bf16[192,256]{1,0:T(8,128)(2,1)} %get-tuple-element.97.refs_0_.refs_7_) | copy-start | bytes 294916
  153.0 11.4 %collective-permute-start.13 = (bf16[2,2,4,96,1792]{4,3,2,1,0:T(8,128)(2,1)}, bf16[2,2,4,96,1792]{4,3,2,1,0:T(8,128)(2,1)}, u32[]{:S(2)}, u32[]{:S(2)}) collective-permute-start(bf16[2,2,4,96,1792]{4,3,2,1,0:T(8,128)(2,1)} %get-tuple-element.110), channel_id=1, source_target_pairs={{0,4},{4,0},{1,5},{5,1},{2,6},{6,2},{3,7},{7,3},{8,12},{12,8},{9,1... | collective-permute-start | bytes 16515080 | tf_op jit(solution)/shard_map/ppermute | solution.py:28
  153.0 16.1 %all-to-all-start.2 = ((bf16[4,192,256]{2,1,0:T(8,128)(2,1)}), bf16[4,192,256]{2,1,0:T(8,128)(2,1)S(1)}, u32[]{:S(2)}, u32[]{:S(2)}) async-start(bf16[4,192,256]{2,1,0:T(8,128)(2,1)} %get-tuple-element.103), calls=%async_computation.2 | async-start | bytes 786432 | tf_op jit(solution)/shard_map/all_to_all | solution.py:820
  164.3 8.5 %copy-start.1 = (bf16[8,192,256]{2,1,0:T(8,128)(2,1)S(1)}, bf16[8,192,256]{2,1,0:T(8,128)(2,1)}, u32[]{:S(2)}) copy-start(bf16[8,192,256]{2,1,0:T(8,128)(2,1)} %get-tuple-element.92.refs_4_) | copy-start | bytes 2359300
  164.3 8.5 %copy-start.3 = (bf16[8,192,256]{2,1,0:T(8,128)(2,1)S(1)}, bf16[8,192,256]{2,1,0:T(8,128)(2,1)}, u32[]{:S(2)}) copy-start(bf16[8,192,256]{2,1,0:T(8,128)(2,1)} %copy-done.2) | copy-start | bytes 2359300
  164.3 8.5 %copy-start.8 = (bf16[4,256,256]{2,1,0:T(8,128)(2,1)S(1)}, bf16[4,256,256]{2,1,0:T(8,128)(2,1)}, u32[]{:S(2)}) copy-start(bf16[4,256,256]{2,1,0:T(8,128)(2,1)} %get-tuple-element.96.refs_1_) | copy-start | bytes 1572868
  164.3 8.5 %copy-start.20 = (bf16[192,256]{1,0:T(8,128)(2,1)S(1)}, bf16[192,256]{1,0:T(8,128)(2,1)}, u32[]{:S(2)}) copy-start(bf16[192,256]{1,0:T(8,128)(2,1)} %get-tuple-element.98.refs_8_) | copy-start | bytes 294916
  164.3 8.5 %copy-start.21 = (bf16[192,256]{1,0:T(8,128)(2,1)S(1)}, bf16[192,256]{1,0:T(8,128)(2,1)}, u32[]{:S(2)}) copy-start(bf16[192,256]{1,0:T(8,128)(2,1)} %get-tuple-element.99.refs_9_) | copy-start | bytes 294916
  164.3 8.5 %copy-start.22 = (bf16[192,256]{1,0:T(8,128)(2,1)S(1)}, bf16[192,256]{1,0:T(8,128)(2,1)}, u32[]{:S(2)}) copy-start(bf16[192,256]{1,0:T(8,128)(2,1)} %get-tuple-element.100.refs_10_) | copy-start | bytes 294916
  164.3 8.5 %copy-start.24 = (f32[3,256]{1,0:T(4,128)S(1)}, f32[3,256]{1,0:T(4,128)}, u32[]{:S(2)}) copy-start(f32[3,256]{1,0:T(4,128)} %get-tuple-element.115.refs_12_) | copy-start | bytes 9220
  169.0 34.0 %collective-permute-start.16 = (bf16[4,96,1792]{2,1,0:T(8,128)(2,1)}, bf16[4,96,1792]{2,1,0:T(8,128)(2,1)}, u32[]{:S(2)}, u32[]{:S(2)}) collective-permute-start(bf16[4,96,1792]{2,1,0:T(8,128)(2,1)} %get-tuple-element.123), channel_id=1, source_target_pairs={{0,16},{16,0},{1,17},{17,1},{2,18},{18,2},{3,19},{19,3},{4,20},{20... | collective-permute-start | bytes 4128776 | tf_op jit(solution)/shard_map/ppermute | solution.py:28
  172.4 32.1 %collective-permute-start.17 = (bf16[4,96,1792]{2,1,0:T(8,128)(2,1)}, bf16[4,96,1792]{2,1,0:T(8,128)(2,1)}, u32[]{:S(2)}, u32[]{:S(2)}) collective-permute-start(bf16[4,96,1792]{2,1,0:T(8,128)(2,1)} %get-tuple-element.124), channel_id=1, source_target_pairs={{0,8},{8,0},{1,9},{9,1},{2,10},{10,2},{3,11},{11,3},{4,12},{12,4},... | collective-permute-start | bytes 4128776 | tf_op jit(solution)/shard_map/ppermute | solution.py:28
  172.8 18.6 %copy-start = (bf16[2,2,192,576]{3,2,1,0:T(8,128)(2,1)S(1)}, bf16[2,2,192,576]{3,2,1,0:T(8,128)(2,1)}, u32[]{:S(2)}) copy-start(bf16[2,2,192,576]{3,2,1,0:T(8,128)(2,1)} %copy.41) | copy-start | bytes 2654212
  172.8 18.6 %copy-start.6 = (f32[4,256,128]{2,1,0:T(8,128)S(1)}, f32[4,256,128]{2,1,0:T(8,128)}, u32[]{:S(2)}) copy-start(f32[4,256,128]{2,1,0:T(8,128)} %get-tuple-element.89.refs_6_.sin_ref) | copy-start | bytes 1572868
  172.8 18.6 %copy-start.7 = (f32[4,256,128]{2,1,0:T(8,128)S(1)}, f32[4,256,128]{2,1,0:T(8,128)}, u32[]{:S(2)}) copy-start(f32[4,256,128]{2,1,0:T(8,128)} %get-tuple-element.88.refs_5_.cos_ref) | copy-start | bytes 1572868
  188.7 2.0 collective-permute-start.14
  188.8 2.6 collective-permute-start.15
  195.8 43.6 %all-to-all-start.3 = ((bf16[4,256,768]{2,1,0:T(8,128)(2,1)}), bf16[4,256,768]{2,1,0:T(8,128)(2,1)}, u32[]{:S(2)}, u32[]{:S(2)}) async-start(bf16[4,256,768]{2,1,0:T(8,128)(2,1)} %get-tuple-element.122), calls=%async_computation.3 | async-start | bytes 3145728 | tf_op jit(solution)/shard_map/all_to_all | solution.py:850
  200.5 62.3 %reduce-scatter.2.cloned.1.call-start = ((), (), s32[]{:S(2)}) async-start(), calls=%async_computation.6 | async-start | bytes 1720320 | tf_op jit(solution)/shard_map/reduce_scatter | solution.py:749
  207.9 16.5 %collective-permute-start.18 = (bf16[2,96,1792]{2,1,0:T(8,128)(2,1)}, bf16[2,96,1792]{2,1,0:T(8,128)(2,1)}, u32[]{:S(2)}, u32[]{:S(2)}) collective-permute-start(bf16[2,96,1792]{2,1,0:T(8,128)(2,1)} %get-tuple-element.131), channel_id=1, source_target_pairs={{0,8},{8,0},{1,9},{9,1},{2,10},{10,2},{3,11},{11,3},{4,12},{12,4},... | collective-permute-start | bytes 2064392 | tf_op jit(solution)/shard_map/ppermute | solution.py:28
  208.7 16.6 %collective-permute-start.19 = (bf16[2,96,1792]{2,1,0:T(8,128)(2,1)}, bf16[2,96,1792]{2,1,0:T(8,128)(2,1)}, u32[]{:S(2)}, u32[]{:S(2)}) collective-permute-start(bf16[2,96,1792]{2,1,0:T(8,128)(2,1)} %get-tuple-element.132), channel_id=1, source_target_pairs={{0,16},{16,0},{1,17},{17,1},{2,18},{18,2},{3,19},{19,3},{4,20},{20... | collective-permute-start | bytes 2064392 | tf_op jit(solution)/shard_map/ppermute | solution.py:28
  229.1 1.9 collective-permute-start.20
  231.3 8.1 %collective-permute-start.21 = (bf16[192,576]{1,0:T(8,128)(2,1)S(1)}, bf16[192,576]{1,0:T(8,128)(2,1)S(1)}, u32[]{:S(2)}, u32[]{:S(2)}) collective-permute-start(bf16[192,576]{1,0:T(8,128)(2,1)S(1)} %select_bitcast_fusion.7), channel_id=1, source_target_pairs={{0,8},{8,0},{1,9},{9,1},{2,10},{10,2},{3,11},{11,3},{4,12},{12,4},... | collective-permute-start | bytes 663560 | tf_op jit(solution)/shard_map/ppermute | solution.py:28
  232.7 8.5 %copy-start.29 = (f32[256,768]{1,0:T(8,128)S(1)}, f32[256,768]{1,0:T(8,128)}, u32[]{:S(2)}) copy-start(f32[256,768]{1,0:T(8,128)} %get-tuple-element.102) | copy-start | bytes 2359300
  243.2 31.8 %all-to-all-start.4 = ((bf16[8,256,384]{2,1,0:T(8,128)(2,1)}), bf16[8,256,384]{2,1,0:T(8,128)(2,1)S(1)}, u32[]{:S(2)}, u32[]{:S(2)}) async-start(bf16[8,256,384]{2,1,0:T(8,128)(2,1)} %bitcast.40), calls=%async_computation.4 | async-start | bytes 3145728 | tf_op jit(solution)/shard_map/all_to_all | solution.py:824
  263.9 22.1 %collective-permute-start.22 = (bf16[96,2944]{1,0:T(8,128)(2,1)S(1)}, bf16[96,2944]{1,0:T(8,128)(2,1)S(1)}, u32[]{:S(2)}, u32[]{:S(2)}) collective-permute-start(bf16[96,2944]{1,0:T(8,128)(2,1)S(1)} %concatenate.11.refs_1_), channel_id=1, source_target_pairs={{0,16},{16,0},{1,17},{17,1},{2,18},{18,2},{3,19},{19,3},{4,20},{20... | collective-permute-start | bytes 1695752 | tf_op jit(solution)/shard_map/ppermute | solution.py:28
  (19 other events, 77.1 us)
Sparse Core Ops, SparseCore 0:
  10.9 117.9 all-gather.2
  229.4 33.3 reduce-scatter.1
